TPU v7x, 256 devices: a whole 4x4x8 slice. The times are simulated.
256 devices in a mesh: gx: 16 (over z, core), gy: 4 (over x), af: 4 (over y).
Axes of the slice: x: 4, y: 4, z: 8, core: 2. Of those that a mesh axis runs over, the one named last changes fastest.
Arguments:
- features: bfloat16 [65536, 1024], P(('gx', 'gy'), 'af'), may hold values from -6 to 6
- adj_tiles: bfloat16 [512, 4, 128, 128], P(('gx', 'gy')), may hold values from -0.25 to 0.25
- col_block: int32 [512, 4], P(('gx', 'gy')), may hold values from 0 to 7, as said below
- send_rows: int32 [256, 384], P(('gx', 'gy')), may hold values from 0 to 1023
- send_counts: int32 [256], P(('gx', 'gy')), may hold values from 96 to 384, as said below
- recv_target: int32 [256, 384], P(('gx', 'gy')), may hold values from 0 to 1023
- edge_weight: float32 [256, 384], P(('gx', 'gy')), may hold values from -3 to 3
- labels: int32 [65536], P(('gx', 'gy')), may hold values from 0 to 127
- w_hidden: bfloat16 [1024, 1024], P('af'), may hold values from -0.1875 to 0.1875
- w_classes: bfloat16 [1024, 128], P('af'), may hold values from -0.5 to 0.5
Outputs:
- grad_w_hidden: float32 [1024, 1024], P('af')
- grad_w_classes: float32 [1024, 128], P('af')
Inputs may be any that keep to these rules, and one draw needn't show every extreme that they name: `send_counts`: entry 4 p + d is the number of leading live slots in row 4 p + d of send_rows; some entry equals 384. `col_block`: entry k = 0 of row t is t mod (8), the tile's own block; the 4 entries of a row are distinct. `send_rows`: rows of the sending partition; repeats possible. `recv_target`: rows of the receiving partition; repeats possible.
All inputs are finite; a program needn't handle non-finite values.
Results may differ from a plain program's by a relative error of at most 0.008.
Values may be sent and summed in bfloat16 or wider, within the bound.
No kernel may reach another device: no remote copies, remote signals or barrier semaphores. Data moves between devices by JAX's collectives and lax.ppermute only.
A program may use at most 64 MiB of HBM per device.

v0:
```python
import jax
import jax.numpy as jnp
from jax import lax
from jax.sharding import PartitionSpec as P


def with_halo(block, sides, width):
    for axis, dim in sides:
        count = lax.axis_size(axis)
        forward = [(i, i + 1) for i in range(count - 1)]
        backward = [(target, source) for source, target in forward]
        low = lax.ppermute(
            lax.slice_in_dim(block, block.shape[dim] - width, None, axis=dim), axis, forward
        )
        high = lax.ppermute(lax.slice_in_dim(block, 0, width, axis=dim), axis, backward)
        block = jnp.concatenate([low, block, high], axis=dim)
    return block


def trade_rims(to_lower_x, to_upper_x, to_lower_y, to_upper_y):
    along_x = with_halo(jnp.stack([to_lower_x, to_upper_x]), (("gx", 0),), 1)
    along_y = with_halo(jnp.stack([to_lower_y, to_upper_y]), (("gy", 0),), 1)
    return (along_x[0], along_x[3], along_y[0], along_y[3])


def aggregate(node_field, graph_parts):
    adj_tiles, col_block, send_rows, slot_live, recv_target, edge_weight = graph_parts
    feat_width = node_field.shape[1]
    blocks = adj_tiles.shape[0]
    field_blocks = node_field.reshape(blocks, -1, feat_width)
    local_sum = jnp.zeros(field_blocks.shape, jnp.float32)
    for slot in range(adj_tiles.shape[1]):
        picked = field_blocks[col_block[:, slot]]
        local_sum = local_sum + jnp.einsum(
            "bij,bjf->bif", adj_tiles[:, slot], picked, preferred_element_type=jnp.float32
        )
    local_sum = local_sum.reshape(-1, feat_width)
    outgoing = jnp.where(
        slot_live[:, :, None], node_field[send_rows], jnp.zeros((), node_field.dtype)
    )
    arrived = jnp.stack(trade_rims(outgoing[1], outgoing[0], outgoing[3], outgoing[2]))
    weighted = edge_weight[:, :, None] * arrived.astype(jnp.float32)
    return local_sum.at[recv_target.reshape(-1)].add(weighted.reshape(-1, feat_width))


def aggregate_back(grad_field, graph_parts):
    adj_tiles, col_block, send_rows, slot_live, recv_target, edge_weight = graph_parts
    feat_width = grad_field.shape[1]
    blocks = adj_tiles.shape[0]
    grad_blocks = grad_field.reshape(blocks, -1, feat_width)
    local_sum = jnp.zeros(grad_blocks.shape, jnp.float32)
    for slot in range(adj_tiles.shape[1]):
        spread = jnp.einsum(
            "bij,bif->bjf", adj_tiles[:, slot], grad_blocks, preferred_element_type=jnp.float32
        )
        local_sum = local_sum.at[col_block[:, slot]].add(spread)
    local_sum = local_sum.reshape(-1, feat_width)
    back_terms = (edge_weight[:, :, None] * grad_field[recv_target].astype(jnp.float32)).astype(
        jnp.bfloat16
    )
    came_back = trade_rims(back_terms[0], back_terms[1], back_terms[2], back_terms[3])
    returned = jnp.stack([came_back[1], came_back[0], came_back[3], came_back[2]]).astype(
        jnp.float32
    )
    returned = jnp.where(slot_live[:, :, None], returned, jnp.zeros((), jnp.float32))
    return local_sum.at[send_rows.reshape(-1)].add(returned.reshape(-1, feat_width))


def local(
    features,
    adj_tiles,
    col_block,
    send_rows,
    send_counts,
    recv_target,
    edge_weight,
    labels,
    w_hidden,
    w_classes,
):
    slot_live = jnp.arange(send_rows.shape[1], dtype=jnp.int32)[None, :] < send_counts[:, None]
    graph_parts = (adj_tiles, col_block, send_rows, slot_live, recv_target, edge_weight)
    mixed_own = aggregate(features, graph_parts).astype(jnp.bfloat16)
    mixed_all = lax.all_gather(mixed_own, "af", axis=1, tiled=True)
    w_columns = lax.all_to_all(w_hidden, "af", split_axis=1, concat_axis=0, tiled=True)
    pre_act = jnp.dot(mixed_all, w_columns, preferred_element_type=jnp.float32)
    hidden = jax.nn.silu(pre_act).astype(jnp.bfloat16)
    mixed_hidden = aggregate(hidden, graph_parts).astype(jnp.bfloat16)
    logits = lax.psum(jnp.dot(mixed_hidden, w_classes, preferred_element_type=jnp.float32), "af")
    exponent = jnp.exp(logits - jnp.max(logits, axis=1, keepdims=True))
    probability = exponent / jnp.sum(exponent, axis=1, keepdims=True)
    onehot = (labels[:, None] == jnp.arange(w_classes.shape[1], dtype=jnp.int32)[None, :]).astype(
        jnp.float32
    )
    grad_logits = ((probability - onehot) / 64.0).astype(jnp.bfloat16)
    class_term = jnp.dot(mixed_hidden.T, grad_logits, preferred_element_type=jnp.float32)
    grad_classes = lax.psum(class_term, ("gx", "gy"))
    grad_mixed = jnp.dot(grad_logits, w_classes.T, preferred_element_type=jnp.float32).astype(
        jnp.bfloat16
    )
    grad_act = aggregate_back(grad_mixed, graph_parts)
    sigmoid_act = jax.nn.sigmoid(pre_act)
    grad_pre = (grad_act * sigmoid_act * (1.0 + pre_act * (1.0 - sigmoid_act))).astype(jnp.bfloat16)
    grad_all = lax.all_gather(grad_pre, "af", axis=1, tiled=True)
    partial_grad = jnp.dot(mixed_own.T, grad_all, preferred_element_type=jnp.float32)
    grad_hidden = lax.psum(partial_grad, ("gx", "gy"))
    return (grad_hidden, grad_classes)


def solution(mesh):
    placed = (
        P(("gx", "gy"), "af"),
        P(("gx", "gy"), None, None, None),
        P(("gx", "gy"), None),
        P(("gx", "gy"), None),
        P(("gx", "gy")),
        P(("gx", "gy"), None),
        P(("gx", "gy"), None),
        P(("gx", "gy")),
        P("af", None),
        P("af", None),
    )
    return jax.shard_map(
        local, mesh=mesh, in_specs=placed, out_specs=(P("af", None), P("af", None)), check_vma=False
    )
```

profile of v0, /device:TPU:1, one launch (start us, length us, event | category | flops | bytes accessed | tf_op | source)
XLA Modules:
  0.0 475.2 jit_solution(247402482869926105)
XLA Ops:
  8.7 4.8 %gather_fusion.4 = bf16[1536,256]{1,0:T(8,128)(2,1)S(1)} fusion(bf16[1024,256]{1,0:T(8,128)(2,1)S(1)} %copy-done, s32[2048]{0:T(1024)S(1)} %pad_clamp_fusion.1), kind=kCustom, calls=%fused_computation.4 | custom fusion | bytes 1579008 | tf_op jit(solution)/shard_map/gather | solution.py:39
  14.6 4.9 %collective-permute-start = (bf16[1,384,256]{2,1,0:T(8,128)(2,1)}, bf16[1,384,256]{2,1,0:T(8,128)(2,1)S(1)}, u32[]{:S(2)}, u32[]{:S(2)}) collective-permute-start(bf16[1,384,256]{2,1,0:T(8,128)(2,1)} %get-tuple-element.12), channel_id=1, source_target_pairs={{0,16},{16,32},{32,48},{48,64},{64,80},{80,96},{96,112},{112,128},... | collective-permute-start | bytes 589832 | tf_op jit(solution)/shard_map/ppermute | solution.py:12
  19.5 1.9 collective-permute-start.1
  21.5 3.8 collective-permute-start.2
  25.3 1.3 collective-permute-start.3
  28.4 1.4 gather_fusion.2
  34.9 1.3 pad_maximum_fusion
  36.2 10.1 %scatter_custom_fusion = f32[1024,256]{1,0:T(8,128)S(1)} fusion(f32[1024,256]{1,0:T(8,128)S(1)} %bitcast.114, s32[1536]{0:T(1024)} %fusion.39, bf16[1536,256]{1,0:T(8,128)(2,1)S(1)} %bitcast.119, f32[1536]{0:T(1024)S(1)} %mul.39), kind=kCustom, calls=%fused_computation.25 | custom fusion | flops 1179648 | bytes 1843200 | tf_op jit(solution)/shard_map/scatter-add | solution.py:43
  47.8 12.4 %all_to_all.19 = bf16[256,4,256]{0,2,1:T(8,128)(2,1)S(1)} all-to-all(bf16[256,4,256]{0,2,1:T(8,128)(2,1)S(1)} %bitcast.123), channel_id=1, replica_groups=mesh['gx'=16,'gy'=4,'af'=4] {'af'}, dimensions={1} | all-to-all | bytes 1048576 | tf_op jit(solution)/shard_map/all_to_all | solution.py:85
  60.4 27.0 %all-gather.3.cloned.1.call-done = bf16[1024,1024]{1,0:T(8,128)(2,1)} async-done(((bf16[1024,256]{1,0:T(8,128)(2,1)}), bf16[1024,1024]{1,0:T(8,128)(2,1)}) %all-gather.3.cloned.1.call-update) | async-done | bytes 2097168 | tf_op jit(solution)/shard_map/all_gather | solution.py:84
  87.4 3.3 multiply_convert_fusion.1
  90.7 4.8 gather_fusion.9
  96.2 1.5 gather_fusion.6
  97.7 1.5 gather_fusion.7
  99.2 1.5 gather_fusion.8
  101.1 5.2 %collective-permute-start.4 = (bf16[1,384,256]{2,1,0:T(8,128)(2,1)S(1)}, bf16[1,384,256]{2,1,0:T(8,128)(2,1)S(1)}, u32[]{:S(2)}, u32[]{:S(2)}) collective-permute-start(bf16[1,384,256]{2,1,0:T(8,128)(2,1)S(1)} %get-tuple-element.8), channel_id=1, source_target_pairs={{0,16},{16,32},{32,48},{48,64},{64,80},{80,96},{96,112},{112,128},... | collective-permute-start | bytes 589832 | tf_op jit(solution)/shard_map/ppermute | solution.py:12
  106.3 1.9 collective-permute-start.5
  108.2 3.1 collective-permute-start.6
  111.3 1.3 collective-permute-start.7
  115.4 2.9 collective-permute-done.7
  118.3 10.3 %scatter_custom_fusion.1 = f32[1024,256]{1,0:T(8,128)S(1)} fusion(f32[1024,256]{1,0:T(8,128)S(1)} %bitcast.115, s32[1536]{0:T(1024)} %fusion.39, bf16[1536,256]{1,0:T(8,128)(2,1)S(1)} %bitcast.118, f32[1536]{0:T(1024)S(1)} %mul.39), kind=kCustom, calls=%fused_computation.23 | custom fusion | flops 1179648 | bytes 1843200 | tf_op jit(solution)/shard_map/scatter-add | solution.py:43
  130.0 48.7 %all-reduce.4.cloned.1.call-done = f32[1024,128]{1,0:T(8,128)} async-done(((f32[1024,128]{1,0:T(8,128)}), f32[1024,128]{1,0:T(8,128)}) %all-reduce.4.cloned.1.call-update) | async-done | bytes 524304 | tf_op jit(solution)/shard_map/psum | solution.py:89
  178.7 1.2 reduce_max.9
  180.0 1.4 fusion.8
  181.4 1.6 convolution_convert_fusion
  183.1 1.3 convolution_bitcast_fusion.3
  184.4 1.3 convolution_bitcast_fusion.2
  186.1 5.3 %gather_fusion.10 = bf16[1536,256]{1,0:T(8,128)(2,1)} fusion(bf16[1024,256]{1,0:T(8,128)(2,1)S(1)} %convolution_convert_fusion, s32[2048]{0:T(1024)S(1)} %pad_clamp_fusion), kind=kCustom, calls=%fused_computation.10 | custom fusion | bytes 1579008 | tf_op jit(solution)/shard_map/gather | solution.py:58
  191.4 1.4 fusion.1
  193.7 1.3 collective-permute-start.10
  195.0 4.7 collective-permute-start.11
  199.6 5.3 %collective-permute-start.8 = (bf16[1,384,256]{2,1,0:T(8,128)(2,1)}, bf16[1,384,256]{2,1,0:T(8,128)(2,1)}, u32[]{:S(2)}, u32[]{:S(2)}) collective-permute-start(bf16[1,384,256]{2,1,0:T(8,128)(2,1)} %get-tuple-element.4), channel_id=1, source_target_pairs={{16,0},{32,16},{48,32},{64,48},{80,64},{96,80},{112,96},{128,112},... | collective-permute-start | bytes 589832 | tf_op jit(solution)/shard_map/ppermute | solution.py:15
  205.0 3.1 collective-permute-start.9
  208.1 2.5 copy.43
  210.6 2.5 copy.45
  213.1 1.4 copy.47
  214.8 1.3 copy.49
  217.4 1.6 scatter_fusion
  219.0 2.5 scatter_fusion.1
  221.5 1.3 scatter_fusion.2
  222.8 2.5 scatter_fusion.3
  226.6 10.3 %scatter_custom_fusion.6 = f32[1024,256]{1,0:T(8,128)S(1)} fusion(f32[1024,256]{1,0:T(8,128)S(1)} %bitcast.113, s32[1536]{0:T(1024)S(1)} %fusion.40, bf16[1536,256]{1,0:T(8,128)(2,1)S(1)} %bitcast.117, f32[]{:T(128)} %constant.12.clone.1, pred[1536]{0:T(1024)(128)(4,1)S(1)} %lt.83), kind=kCustom, calls=%fused_computation.19 | custom fusion | flops 1179648 | bytes 1837060 | tf_op jit(solution)/shard_map/scatter-add | solution.py:66
  236.9 2.5 multiply_convert_fusion
  239.5 1.4 fusion.23
  241.0 32.5 %all-gather.5.cloned.1.call-done = bf16[1024,1024]{1,0:T(8,128)(2,1)} async-done(((bf16[1024,256]{1,0:T(8,128)(2,1)}), bf16[1024,1024]{1,0:T(8,128)(2,1)}) %all-gather.5.cloned.1.call-update) | async-done | bytes 2097168 | tf_op jit(solution)/shard_map/all_gather | solution.py:104
  273.4 3.3 fusion.48
  276.7 189.0 %all-reduce.6.cloned.1.call-done = (f32[256,1024]{1,0:T(8,128)}, f32[256,128]{1,0:T(8,128)}) async-done(((f32[256,1024]{1,0:T(8,128)}, f32[256,128]{1,0:T(8,128)}), (f32[256,1024]{1,0:T(8,128)}, f32[256,128]{1,0:T(8,128)})) %all-reduce.6.cloned.1.call-update) | async-done | bytes 1179664 | tf_op jit(solution)/shard_map/psum | solution.py:106
  465.7 2.3 copy.70
  (136 shorter events, 20.9 us)
Async XLA Ops:
  7.2 1.6 copy-start
  7.2 80.2 %all-gather.3.cloned.1.call-start = ((), (), s32[]{:S(2)}) async-start(), calls=%async_computation.1 | async-start | bytes 2621440 | tf_op jit(solution)/shard_map/all_gather | solution.py:84
  8.0 5.5 %copy-start.17 = (pred[4,384]{1,0:T(4,128)(4,1)}, pred[4,384]{1,0:T(4,128)(4,1)S(1)}, u32[]{:S(2)}) copy-start(pred[4,384]{1,0:T(4,128)(4,1)S(1)} %iota_compare_fusion.1) | copy-start | bytes 4612
  13.5 13.1 %copy-start.34 = (s32[8,4]{0,1:T(4,128)S(1)}, s32[8,4]{0,1:T(4,128)}, u32[]{:S(2)}) copy-start(s32[8,4]{0,1:T(4,128)} %param.12) | copy-start | bytes 388
  14.6 19.6 %collective-permute-start = (bf16[1,384,256]{2,1,0:T(8,128)(2,1)}, bf16[1,384,256]{2,1,0:T(8,128)(2,1)S(1)}, u32[]{:S(2)}, u32[]{:S(2)}) collective-permute-start(bf16[1,384,256]{2,1,0:T(8,128)(2,1)} %get-tuple-element.12), channel_id=1, source_target_pairs={{0,16},{16,32},{32,48},{48,64},{64,80},{80,96},{96,112},{112,128},... | collective-permute-start | bytes 589832 | tf_op jit(solution)/shard_map/ppermute | solution.py:12
  19.5 14.7 %collective-permute-start.1 = (bf16[1,384,256]{2,1,0:T(8,128)(2,1)}, bf16[1,384,256]{2,1,0:T(8,128)(2,1)}, u32[]{:S(2)}, u32[]{:S(2)}) collective-permute-start(bf16[1,384,256]{2,1,0:T(8,128)(2,1)} %get-tuple-element.15), channel_id=1, source_target_pairs={{16,0},{32,16},{48,32},{64,48},{80,64},{96,80},{112,96},{128,112},... | collective-permute-start | bytes 589832 | tf_op jit(solution)/shard_map/ppermute | solution.py:15
  21.5 12.8 %collective-permute-start.2 = (bf16[1,384,256]{2,1,0:T(8,128)(2,1)}, bf16[1,384,256]{2,1,0:T(8,128)(2,1)}, u32[]{:S(2)}, u32[]{:S(2)}) collective-permute-start(bf16[1,384,256]{2,1,0:T(8,128)(2,1)} %get-tuple-element.14), channel_id=1, source_target_pairs={{0,4},{4,8},{8,12},{1,5},{5,9},{9,13},{2,6},{6,10},{10,14},{3,7},{... | collective-permute-start | bytes 589832 | tf_op jit(solution)/shard_map/ppermute | solution.py:12
  25.3 9.6 %collective-permute-start.3 = (bf16[1,384,256]{2,1,0:T(8,128)(2,1)S(1)}, bf16[1,384,256]{2,1,0:T(8,128)(2,1)}, u32[]{:S(2)}, u32[]{:S(2)}) collective-permute-start(bf16[1,384,256]{2,1,0:T(8,128)(2,1)S(1)} %get-tuple-element.13), channel_id=1, source_target_pairs={{4,0},{8,4},{12,8},{5,1},{9,5},{13,9},{6,2},{10,6},{14,10},{7,3},{... | collective-permute-start | bytes 589832 | tf_op jit(solution)/shard_map/ppermute | solution.py:15
  26.6 3.2 copy-start.25
  26.6 3.2 copy-start.27
  26.6 3.2 copy-start.29
  26.6 3.2 copy-start.31
  26.6 3.2 copy-start.22
  26.7 3.2 copy-start.23
  27.3 3.3 copy-start.1
  28.4 1.4 copy-start.24
  46.3 1.2 copy-start.12
  47.2 131.5 %all-reduce.4.cloned.1.call-start = ((), (), s32[]{:S(2)}) async-start(), calls=%async_computation.2 | async-start | bytes 1048576 | tf_op jit(solution)/shard_map/psum | solution.py:89
  96.2 4.6 copy-start.18
  101.0 11.9 %copy-start.10 = (bf16[8,128,256]{2,1,0:T(8,128)(2,1)S(1)}, bf16[8,128,256]{2,1,0:T(8,128)(2,1)}, u32[]{:S(2)}) copy-start(bf16[8,128,256]{2,1,0:T(8,128)(2,1)} %gather_fusion.6) | copy-start | bytes 1572868
  101.1 14.3 %collective-permute-start.4 = (bf16[1,384,256]{2,1,0:T(8,128)(2,1)S(1)}, bf16[1,384,256]{2,1,0:T(8,128)(2,1)S(1)}, u32[]{:S(2)}, u32[]{:S(2)}) collective-permute-start(bf16[1,384,256]{2,1,0:T(8,128)(2,1)S(1)} %get-tuple-element.8), channel_id=1, source_target_pairs={{0,16},{16,32},{32,48},{48,64},{64,80},{80,96},{96,112},{112,128},... | collective-permute-start | bytes 589832 | tf_op jit(solution)/shard_map/ppermute | solution.py:12
  106.3 9.0 %collective-permute-start.5 = (bf16[1,384,256]{2,1,0:T(8,128)(2,1)S(1)}, bf16[1,384,256]{2,1,0:T(8,128)(2,1)S(1)}, u32[]{:S(2)}, u32[]{:S(2)}) collective-permute-start(bf16[1,384,256]{2,1,0:T(8,128)(2,1)S(1)} %get-tuple-element.11), channel_id=1, source_target_pairs={{16,0},{32,16},{48,32},{64,48},{80,64},{96,80},{112,96},{128,112},... | collective-permute-start | bytes 589832 | tf_op jit(solution)/shard_map/ppermute | solution.py:15
  108.2 7.1 %collective-permute-start.6 = (bf16[1,384,256]{2,1,0:T(8,128)(2,1)S(1)}, bf16[1,384,256]{2,1,0:T(8,128)(2,1)S(1)}, u32[]{:S(2)}, u32[]{:S(2)}) collective-permute-start(bf16[1,384,256]{2,1,0:T(8,128)(2,1)S(1)} %get-tuple-element.10), channel_id=1, source_target_pairs={{0,4},{4,8},{8,12},{1,5},{5,9},{9,13},{2,6},{6,10},{10,14},{3,7},{... | collective-permute-start | bytes 589832 | tf_op jit(solution)/shard_map/ppermute | solution.py:12
  111.3 6.9 %collective-permute-start.7 = (bf16[1,384,256]{2,1,0:T(8,128)(2,1)S(1)}, bf16[1,384,256]{2,1,0:T(8,128)(2,1)S(1)}, u32[]{:S(2)}, u32[]{:S(2)}) collective-permute-start(bf16[1,384,256]{2,1,0:T(8,128)(2,1)S(1)} %get-tuple-element.9), channel_id=1, source_target_pairs={{4,0},{8,4},{12,8},{5,1},{9,5},{13,9},{6,2},{10,6},{14,10},{7,3},{... | collective-permute-start | bytes 589832 | tf_op jit(solution)/shard_map/ppermute | solution.py:15
  115.3 13.3 %copy-start.15 = (bf16[256,128]{1,0:T(8,128)(2,1)S(1)}, bf16[256,128]{1,0:T(8,128)(2,1)}, u32[]{:S(2)}) copy-start(bf16[256,128]{1,0:T(8,128)(2,1)} %param.19) | copy-start | bytes 196612
  118.3 11.6 %copy-start.20 = (s32[4,384]{1,0:T(4,128)S(1)}, s32[4,384]{1,0:T(4,128)}, u32[]{:S(2)}) copy-start(s32[4,384]{1,0:T(4,128)} %param.15) | copy-start | bytes 18436
  118.3 11.6 %copy-start.21 = (s32[4,384]{1,0:T(4,128)S(1)}, s32[4,384]{1,0:T(4,128)}, u32[]{:S(2)}) copy-start(s32[4,384]{1,0:T(4,128)} %param.13) | copy-start | bytes 18436
  128.6 51.4 %copy-start.5 = (f32[1024,256]{1,0:T(8,128)}, f32[1024,256]{1,0:T(8,128)S(1)}, u32[]{:S(2)}) copy-start(f32[1024,256]{1,0:T(8,128)S(1)} %scatter_custom_fusion.1) | copy-start | bytes 3145732
  128.6 52.8 %copy-start.35 = (s32[1024]{0:T(1024)S(1)}, s32[1024]{0:T(1024)}, u32[]{:S(2)}) copy-start(s32[1024]{0:T(1024)} %param.17) | copy-start | bytes 12292
  129.8 143.6 %all-gather.5.cloned.1.call-start = ((), (), s32[]{:S(2)}) async-start(), calls=%async_computation.3 | async-start | bytes 2621440 | tf_op jit(solution)/shard_map/all_gather | solution.py:104
  181.4 3.0 copy-start.32
  186.1 5.4 %copy-start.16 = (f32[4,384]{1,0:T(4,128)S(1)}, f32[4,384]{1,0:T(4,128)}, u32[]{:S(2)}) copy-start(f32[4,384]{1,0:T(4,128)} %param.16) | copy-start | bytes 18436
  193.7 31.6 %collective-permute-start.10 = (bf16[1,384,256]{2,1,0:T(8,128)(2,1)}, bf16[1,384,256]{2,1,0:T(8,128)(2,1)S(1)}, u32[]{:S(2)}, u32[]{:S(2)}) collective-permute-start(bf16[1,384,256]{2,1,0:T(8,128)(2,1)} %get-tuple-element.6), channel_id=1, source_target_pairs={{4,0},{8,4},{12,8},{5,1},{9,5},{13,9},{6,2},{10,6},{14,10},{7,3},{... | collective-permute-start | bytes 589832 | tf_op jit(solution)/shard_map/ppermute | solution.py:15
  195.0 30.3 %collective-permute-start.11 = (bf16[1,384,256]{2,1,0:T(8,128)(2,1)}, bf16[1,384,256]{2,1,0:T(8,128)(2,1)}, u32[]{:S(2)}, u32[]{:S(2)}) collective-permute-start(bf16[1,384,256]{2,1,0:T(8,128)(2,1)} %get-tuple-element.5), channel_id=1, source_target_pairs={{0,4},{4,8},{8,12},{1,5},{5,9},{9,13},{2,6},{6,10},{10,14},{3,7},{... | collective-permute-start | bytes 589832 | tf_op jit(solution)/shard_map/ppermute | solution.py:12
  199.6 25.7 %collective-permute-start.8 = (bf16[1,384,256]{2,1,0:T(8,128)(2,1)}, bf16[1,384,256]{2,1,0:T(8,128)(2,1)}, u32[]{:S(2)}, u32[]{:S(2)}) collective-permute-start(bf16[1,384,256]{2,1,0:T(8,128)(2,1)} %get-tuple-element.4), channel_id=1, source_target_pairs={{16,0},{32,16},{48,32},{64,48},{80,64},{96,80},{112,96},{128,112},... | collective-permute-start | bytes 589832 | tf_op jit(solution)/shard_map/ppermute | solution.py:15
  205.0 20.4 %collective-permute-start.9 = (bf16[1,384,256]{2,1,0:T(8,128)(2,1)S(1)}, bf16[1,384,256]{2,1,0:T(8,128)(2,1)}, u32[]{:S(2)}, u32[]{:S(2)}) collective-permute-start(bf16[1,384,256]{2,1,0:T(8,128)(2,1)S(1)} %get-tuple-element.7), channel_id=1, source_target_pairs={{0,16},{16,32},{32,48},{48,64},{64,80},{80,96},{96,112},{112,128},... | collective-permute-start | bytes 589832 | tf_op jit(solution)/shard_map/ppermute | solution.py:12
  216.1 1.2 copy-start.4
  217.4 1.6 copy-start.30
  219.0 2.5 copy-start.3
  219.0 2.5 copy-start.28
  221.5 1.3 copy-start.26
  236.9 2.6 copy-start.6
  236.9 2.6 copy-start.7
  236.9 2.6 copy-start.33
  236.9 2.6 copy-start.36
  239.4 34.0 %copy-start.2 = (bf16[1024,256]{1,0:T(8,128)(2,1)S(1)}, bf16[1024,256]{1,0:T(8,128)(2,1)}, u32[]{:S(2)}) copy-start(bf16[1024,256]{1,0:T(8,128)(2,1)} %convert_element_type.50) | copy-start | bytes 1572868
  239.4 226.3 %all-reduce.6.cloned.1.call-start = ((), (), s32[]{:S(2)}) async-start(), calls=%async_computation.4 | async-start | bytes 2359296 | tf_op jit(solution)/shard_map/psum | solution.py:106
  465.7 2.3 copy-start.14
  (5 other events, 4.5 us)
Sparse Core Ops, SparseCore 0:
  47.3 40.0 all-gather.2
  129.9 48.7 all-reduce.3
  239.6 33.8 all-gather.4
  277.3 188.4 all-reduce.5
where the time goes:
time: 477 us; the launch traced here: 475 us
  waiting for transfers between devices  300 us (63%)
  other arithmetic  51.8 us (11%)
  local copies, waits for them, and re-layouts  41.9 us (9%)
  starting transfers between devices  38 us (8%)
  matrix products  16.4 us (3%)
  between operations  14.6 us (3%)
  blocking collectives  12.4 us (3%)
    psum x1, waiting for transfers between devices, local(): grad_hidden = lax.psum(partial_grad, ('gx', 'gy'))  189 us
    psum x1, waiting for transfers between devices, local(): lax.psum(jnp.dot(mixed_hidden, w_classes, preferred_element_type=jnp.floa...  48.7 us
    all_gather x1, waiting for transfers between devices, local(): grad_all = lax.all_gather(grad_pre, 'af', axis=1, tiled=True)  32.5 us
    all_gather x1, waiting for transfers between devices, local(): mixed_all = lax.all_gather(mixed_own, 'af', axis=1, tiled=True)  27 us
    ppermute x6, starting transfers between devices, with_halo(): lax.ppermute(lax.slice_in_dim(block, block.shape[dim] - width, None, axis...  24.8 us
    scatter-add x2, other arithmetic, aggregate(): local_sum.at[recv_target.reshape(-1)].add(weighted.reshape(-1, feat_width))  20.3 us
    ppermute x6, starting transfers between devices, with_halo(): lax.ppermute(lax.slice_in_dim(block, 0, width, axis=dim), axis, backward)  13 us
    all_to_all x1, blocking collectives, local(): lax.all_to_all(w_hidden, 'af', split_axis=1, concat_axis=0, tiled=True)  12.4 us
  transfers between devices with their start and end apart: 16, of which 5 were waited for; matrix products, arithmetic and copies ran while one was open for 5% of the time, Pallas kernels for 0%

commit v1 on v0

v1 whole, which is shorter than its diff:
```python
import jax
import jax.numpy as jnp
import numpy as np
from jax import lax
from jax.sharding import Mesh
from jax.sharding import PartitionSpec as P

BF = jnp.bfloat16
F32 = jnp.float32
ROWS = ("z", "core")
PLANE = ("z", "gy")


def dot(lhs, rhs, lhs_dim=1, rhs_dim=0):
    return lax.dot_general(lhs, rhs, (((lhs_dim,), (rhs_dim,)), ((), ())), preferred_element_type=F32)


def step(field, axis, move):
    count = lax.axis_size(axis)
    pairs = [(i, i + move) for i in range(count) if 0 <= i + move < count]
    return lax.ppermute(field, axis, pairs)


def turn(field, axis, move):
    count = lax.axis_size(axis)
    return lax.ppermute(field, axis, [(i, (i + move) % count) for i in range(count)])


def trade(fields, sign):
    return jnp.concatenate(
        [
            step(fields[0], ROWS, sign),
            step(fields[1], ROWS, -sign),
            step(fields[2], "gy", sign),
            step(fields[3], "gy", -sign),
        ],
        axis=0,
    )


def two_parts(values):
    high = values.astype(BF)
    low = (values - high.astype(F32)).astype(BF)
    return jnp.concatenate([high, low], axis=1)


def local(
    features,
    adj_tiles,
    col_block,
    send_rows,
    send_counts,
    recv_target,
    edge_weight,
    labels,
    w_hidden,
    w_classes,
):
    af = lax.axis_index("af")
    core = lax.axis_index("core")
    n_af = lax.axis_size("af")
    n_plane = lax.axis_size("z") * lax.axis_size("gy")
    nodes = features.shape[0]
    own = nodes // n_af
    slots = send_rows.shape[1]
    hid = w_hidden.shape[1]
    classes = w_classes.shape[1]
    w_rows = w_hidden.shape[0]
    half = w_rows // 2
    blocks, kt, tb, _ = adj_tiles.shape

    w_both = jnp.concatenate([w_hidden, w_classes], axis=1)
    w_from = [w_both] + [turn(w_both, "af", k) for k in range(1, n_af)]

    live = jnp.arange(slots, dtype=jnp.int32)[None, :] < send_counts[:, None]
    send_at = jnp.where(live, send_rows, -1).reshape(-1)
    recv_at = recv_target.reshape(-1)
    weight = edge_weight.reshape(-1, 1)
    node_ids = jnp.arange(nodes, dtype=jnp.int32)
    pick_send = (send_at[:, None] == node_ids[None, :]).astype(BF)
    pick_recv = (recv_at[:, None] == node_ids[None, :]).astype(BF)
    put_recv = (node_ids[:, None] == recv_at[None, :]).astype(BF)
    own_ids = node_ids[:own] + af * own
    put_send = (own_ids[:, None] == send_at[None, :]).astype(BF)

    block_ids = jnp.arange(blocks, dtype=jnp.int32)
    dense = jnp.zeros((blocks, tb, blocks, tb), BF)
    for k in range(kt):
        here = col_block[:, k][:, None, None, None] == block_ids[None, None, :, None]
        dense = jnp.where(here, adj_tiles[:, k][:, :, None, :], dense)
    dense = dense.reshape(nodes, nodes)

    out = dot(pick_send, features).astype(BF).reshape(4, slots, -1)
    arrived = trade(out, 1).astype(F32) * weight
    width = features.shape[1]
    spread = dot(put_recv, two_parts(arrived))
    mixed = (dot(dense, features) + spread[:, :width] + spread[:, width:]).astype(BF)

    def rows_for(k):
        return lax.dynamic_slice_in_dim(mixed, ((af + k) % n_af) * own, own, axis=0)

    mixed_from = [rows_for(0)] + [turn(rows_for(k), "af", k) for k in range(1, n_af)]
    pre_act = sum(dot(m, w[:, :hid]) for m, w in zip(mixed_from, w_from))
    sigmoid_act = jax.nn.sigmoid(pre_act)
    hidden = (pre_act * sigmoid_act).astype(BF)
    slope = sigmoid_act * (1.0 + pre_act * (1.0 - sigmoid_act))

    w_cls = [w[:, hid:] for w in w_from]
    around = [w_cls[(n_af - k) % n_af] for k in range(n_af)]
    w_cls = lax.dynamic_slice_in_dim(
        jnp.concatenate(around + around, axis=0), (n_af - af) * w_rows, n_af * w_rows, axis=0
    )

    z_own = dot(hidden, w_cls).astype(BF)
    z_all = lax.all_to_all(
        jnp.broadcast_to(z_own[None], (n_af, own, classes)), "af", 0, 0, tiled=True
    ).reshape(nodes, classes)
    out = dot(pick_send, z_all).astype(BF).reshape(4, slots, -1)
    arrived = trade(out, 1).astype(F32) * weight
    spread = dot(put_recv, two_parts(arrived))
    logits = dot(dense, z_all) + spread[:, :classes] + spread[:, classes:]

    exponent = jnp.exp(logits - jnp.max(logits, axis=1, keepdims=True))
    probability = exponent / jnp.sum(exponent, axis=1, keepdims=True)
    onehot = (labels[:, None] == jnp.arange(classes, dtype=jnp.int32)[None, :]).astype(F32)
    grad_logits = ((probability - onehot) / 64.0).astype(BF)

    back = (dot(pick_recv, grad_logits) * weight).astype(BF).reshape(4, slots, -1)
    returned = trade(back, -1)
    dense_own = lax.dynamic_slice_in_dim(dense, af * own, own, axis=1)
    grad_own = (dot(dense_own, grad_logits, 0, 0) + dot(put_send, returned)).astype(BF)
    grad_pre = (dot(grad_own, w_cls, 1, 1) * slope).astype(BF)

    def columns(which):
        return jnp.concatenate(
            [lax.dynamic_slice_in_dim(m, which * half, half, axis=1) for m in mixed_from], axis=1
        )

    def hidden_columns(which):
        return jnp.concatenate(
            [
                lax.dynamic_slice_in_dim(
                    hidden, ((af - k) % n_af) * w_rows + which * half, half, axis=1
                )
                for k in range(n_af)
            ],
            axis=1,
        )

    def terms(which):
        return jnp.concatenate(
            [dot(columns(which), grad_pre, 0, 0), dot(hidden_columns(which), grad_own, 0, 0)],
            axis=1,
        )

    theirs = lax.ppermute(terms(1 - core).astype(BF), "core", [(0, 1), (1, 0)])
    pair_sum = (terms(core) + theirs.astype(F32)).reshape(n_af, half, hid + classes)
    total = pair_sum[0]
    for k in range(1, n_af):
        total = total + turn(pair_sum[k].astype(BF), "af", -k).astype(F32)
    pieces = total.astype(BF).reshape(n_plane, half // n_plane, hid + classes)
    pieces = lax.all_to_all(pieces, PLANE, 0, 0, tiled=True)
    piece = jnp.sum(pieces.astype(F32), axis=0).astype(BF)
    mine = lax.all_to_all(
        jnp.broadcast_to(piece[None], (n_plane,) + piece.shape), PLANE, 0, 0, tiled=True
    ).reshape(half, hid + classes)
    other = lax.ppermute(mine, "core", [(0, 1), (1, 0)])
    first = jnp.where(core == 0, mine, other)
    second = jnp.where(core == 0, other, mine)
    whole = jnp.concatenate([first, second], axis=0).astype(F32)
    return (whole[:, :hid], whole[:, hid:])


def solution(mesh):
    shape = mesh.devices.shape
    split = Mesh(
        np.reshape(mesh.devices, (shape[0] // 2, 2) + shape[1:]), ("z", "core", "gy", "af")
    )
    parts = ("z", "core", "gy")
    placed = (
        P(parts, "af"),
        P(parts, None, None, None),
        P(parts, None),
        P(parts, None),
        P(parts),
        P(parts, None),
        P(parts, None),
        P(parts),
        P("af", None),
        P("af", None),
    )
    return jax.shard_map(
        local, mesh=split, in_specs=placed, out_specs=(P("af", None), P("af", None)), check_vma=False
    )
```

time: 477 us -> 188 us (0.39)
  waiting for transfers between devices: 300 us -> 51.3 us
  other arithmetic: 51.8 us -> 5.94 us
  blocking collectives: 12.4 us -> 43.5 us
  local copies, waits for them, and re-layouts: 41.9 us -> 12.2 us
  starting transfers between devices: 38 us -> 55.2 us
  between operations: 14.6 us -> 1.49 us
    psum x2 -> x0, waiting for transfers between devices: 238 us -> none  [the longest x1 189 us: local(): grad_hidden = lax.psum(partial_grad, ('gx', 'gy'))]
    all_gather x2 -> x0, waiting for transfers between devices: 59.5 us -> none  [the longest x1 32.5 us: local(): grad_all = lax.all_gather(grad_pre, 'af', axis=1, tiled=True)]
    ppermute x12 -> x23, waiting for transfers between devices: 2.88 us -> 46.4 us  [the longest x9 39.4 us: turn(): lax.ppermute(field, axis, [(i, (i + move) % count) for i in range(count)])]
    scatter-add x7 -> x0, other arithmetic: 38.5 us -> none  [the longest x2 20.3 us: aggregate(): local_sum.at[recv_target.reshape(-1)].add(weighted.reshape(-1, feat_width))]
    all_to_all x1 -> x2, blocking collectives: 12.4 us -> 43.5 us  [the longest x1 27.7 us: local(): pieces = lax.all_to_all(pieces, PLANE, 0, 0, tiled=True)]
    gather x11 -> x0, local copies, waits for them, and re-layouts: 23.3 us -> none  [the longest x2 9.51 us: aggregate(): node_field[send_rows]]
    ppermute x12 -> x23, starting transfers between devices: 37.8 us -> 51 us  [the longest x12 35.8 us: step(): return lax.ppermute(field, axis, pairs)]
    dot_general x4 -> x0, local copies, waits for them, and re-layouts: 7.72 us -> none  [aggregate_back(): jnp.einsum('bij,bif->bjf', adj_tiles[:, slot], grad_blocks, preferred_ele...]
  transfers between devices with their start and end apart: 16 -> 24, of which waited for: 5 -> 9; matrix products, arithmetic and copies ran while one was open for 5% -> 9% of each run, Pallas kernels for 0% -> 0%
where the time goes in v1:
time: 188 us; the launch traced here: 187 us
  starting transfers between devices  55.2 us (29%)
  waiting for transfers between devices  51.3 us (27%)
  blocking collectives  43.5 us (23%)
  matrix products  17.3 us (9%)
  local copies, waits for them, and re-layouts  12.2 us (6%)
  other arithmetic  5.94 us (3%)
    ppermute x9, waiting for transfers between devices, turn(): lax.ppermute(field, axis, [(i, (i + move) % count) for i in range(count)])  39.4 us
    ppermute x12, starting transfers between devices, step(): return lax.ppermute(field, axis, pairs)  35.8 us
    all_to_all x1, blocking collectives, local(): pieces = lax.all_to_all(pieces, PLANE, 0, 0, tiled=True)  27.7 us
    dot_general x19, matrix products, dot(): lax.dot_general(lhs, rhs, (((lhs_dim,), (rhs_dim,)), ((), ())), preferred...  17.3 us
    all_to_all x1, blocking collectives, local(): lax.all_to_all(jnp.broadcast_to(piece[None], (n_plane,) + piece.shape), P...  15.8 us
    ppermute x9, starting transfers between devices, turn(): lax.ppermute(field, axis, [(i, (i + move) % count) for i in range(count)])  10.9 us
    unnamed x49, local copies, waits for them, and re-layouts  6.07 us
    all_to_all x1, waiting for transfers between devices, local(): lax.all_to_all(jnp.broadcast_to(z_own[None], (n_af, own, classes)), 'af',...  4.99 us
  transfers between devices with their start and end apart: 24, of which 9 were waited for; matrix products, arithmetic and copies ran while one was open for 9% of the time, Pallas kernels for 0%

profile of v1, /device:TPU:1, one launch (start us, length us, event | category | flops | bytes accessed | tf_op | source)
XLA Modules:
  0.0 187.0 jit_solution(11162817348831255421)
XLA Ops:
  0.6 1.9 %constant_dynamic-update-slice_fusion.1 = bf16[256,1152]{1,0:T(8,128)(2,1)} fusion(bf16[256,1024]{1,0:T(8,128)(2,1)} %param.18), kind=kLoop, calls=%fused_computation.126 | loop fusion | bytes 1048576
  2.6 1.5 constant_dynamic-update-slice_fusion.3
  4.1 3.6 %collective-permute-start.9 = (bf16[256,1152]{1,0:T(8,128)(2,1)}, bf16[256,1152]{1,0:T(8,128)(2,1)S(1)}, u32[]{:S(2)}, u32[]{:S(2)}) collective-permute-start(bf16[256,1152]{1,0:T(8,128)(2,1)} %get-tuple-element.49), channel_id=1, source_target_pairs={{0,3},{1,0},{2,1},{3,2},{4,7},{5,4},{6,5},{7,6},{8,11},{9,8},{10,9... | collective-permute-start | bytes 1769480 | tf_op jit(solution)/shard_map/ppermute | solution.py:26
  7.6 0.8 fusion.87
  8.4 1.3 fusion.10
  9.7 0.9 fusion.102
  10.6 4.4 %collective-permute-start = (bf16[384,256]{1,0:T(8,128)(2,1)}, bf16[384,256]{1,0:T(8,128)(2,1)S(1)}, u32[]{:S(2)}, u32[]{:S(2)}) collective-permute-start(bf16[384,256]{1,0:T(8,128)(2,1)} %get-tuple-element.13), channel_id=1, source_target_pairs={{0,16},{16,32},{32,48},{48,64},{64,80},{80,96},{96,112},{112,128},... | collective-permute-start | bytes 589832 | tf_op jit(solution)/shard_map/ppermute | solution.py:21
  15.0 1.3 collective-permute-start.3
  16.3 4.7 %collective-permute-start.2 = (bf16[384,256]{1,0:T(8,128)(2,1)}, bf16[384,256]{1,0:T(8,128)(2,1)}, u32[]{:S(2)}, u32[]{:S(2)}) collective-permute-start(bf16[384,256]{1,0:T(8,128)(2,1)} %get-tuple-element.15), channel_id=1, source_target_pairs={{0,4},{4,8},{8,12},{1,5},{5,9},{9,13},{2,6},{6,10},{10,14},{3,7},{... | collective-permute-start | bytes 589832 | tf_op jit(solution)/shard_map/ppermute | solution.py:21
  21.0 1.9 %collective-permute-start.1 = (bf16[384,256]{1,0:T(8,128)(2,1)}, bf16[384,256]{1,0:T(8,128)(2,1)}, u32[]{:S(2)}, u32[]{:S(2)}) collective-permute-start(bf16[384,256]{1,0:T(8,128)(2,1)} %get-tuple-element.16), channel_id=1, source_target_pairs={{16,0},{32,16},{48,32},{64,48},{80,64},{96,80},{112,96},{128,112},... | collective-permute-start | bytes 589832 | tf_op jit(solution)/shard_map/ppermute | solution.py:21
  23.4 1.2 select_select_fusion
  24.6 2.0 %copy.24 = bf16[128,8,8,128]{3,1,2,0:T(8,128)(2,1)} copy(bf16[128,8,8,128]{3,2,1,0:T(8,128)(2,1)S(1)} %bitcast.42) | data formatting | bytes 4194304
  28.3 1.4 fusion.17
  29.7 1.9 %fusion.3 = f32[1024,512]{0,1:T(8,128)S(1)} fusion(s32[1536]{0:T(1024)S(1)} %eq.184, bf16[1536,256]{1,0:T(8,128)(2,1)S(1)} %get-tuple-element.12, bf16[1536,256]{1,0:T(8,128)(2,1)S(1)} %get-tuple-element.11), kind=kOutput, calls=%fused_computation.6 | convolution fusion | flops 1615331328 | bytes 3676160 | tf_op jit(solution)/shard_map/dot_general | solution.py:15
  31.6 0.8 fusion.29
  32.5 1.9 %collective-permute-start.5 = (bf16[256,256]{0,1:T(8,128)(2,1)S(1)}, bf16[256,256]{0,1:T(8,128)(2,1)S(1)}, u32[]{:S(2)}, u32[]{:S(2)}) collective-permute-start(bf16[256,256]{0,1:T(8,128)(2,1)S(1)} %get-tuple-element.29), channel_id=1, source_target_pairs={{0,2},{1,3},{2,0},{3,1},{4,6},{5,7},{6,4},{7,5},{8,10},{9,11},{10,... | collective-permute-start | bytes 393224 | tf_op jit(solution)/shard_map/ppermute | solution.py:26
  34.8 2.1 %collective-permute-start.6 = (bf16[256,256]{0,1:T(8,128)(2,1)S(1)}, bf16[256,256]{0,1:T(8,128)(2,1)S(1)}, u32[]{:S(2)}, u32[]{:S(2)}) collective-permute-start(bf16[256,256]{0,1:T(8,128)(2,1)S(1)} %get-tuple-element.30), channel_id=1, source_target_pairs={{0,3},{1,0},{2,1},{3,2},{4,7},{5,4},{6,5},{7,6},{8,11},{9,8},{10,9... | collective-permute-start | bytes 393224 | tf_op jit(solution)/shard_map/ppermute | solution.py:26
  36.9 0.7 fusion.103
  37.7 20.2 %collective-permute-done.5 = bf16[256,256]{0,1:T(8,128)(2,1)S(1)} collective-permute-done((bf16[256,256]{0,1:T(8,128)(2,1)S(1)}, bf16[256,256]{0,1:T(8,128)(2,1)S(1)}, u32[]{:S(2)}, u32[]{:S(2)}) %collective-permute-start.5) | collective-permute-done | bytes 131104 | tf_op jit(solution)/shard_map/ppermute | solution.py:26
  59.0 4.8 %collective-permute-done.4 = bf16[256,256]{0,1:T(8,128)(2,1)S(1)} collective-permute-done((bf16[256,256]{0,1:T(8,128)(2,1)S(1)}, bf16[256,256]{0,1:T(8,128)(2,1)S(1)}, u32[]{:S(2)}, u32[]{:S(2)}) %collective-permute-start.4) | collective-permute-done | bytes 131104 | tf_op jit(solution)/shard_map/ppermute | solution.py:26
  64.2 1.4 multiply_convert_fusion
  65.9 0.7 broadcast_in_dim.101
  66.6 4.2 %all-to-all-start = ((bf16[4,256,128]{2,1,0:T(8,128)(2,1)}), bf16[4,256,128]{2,1,0:T(8,128)(2,1)}, u32[]{:S(2)}, u32[]{:S(2)}) async-start(bf16[4,256,128]{2,1,0:T(8,128)(2,1)} %broadcast_in_dim.101), calls=%async_computation | async-start | bytes 524288 | tf_op jit(solution)/shard_map/all_to_all | solution.py:115
  72.1 5.0 %all-to-all-done = bf16[4,256,128]{2,1,0:T(8,128)(2,1)} async-done(((bf16[4,256,128]{2,1,0:T(8,128)(2,1)}), bf16[4,256,128]{2,1,0:T(8,128)(2,1)}, u32[]{:S(2)}, u32[]{:S(2)}) %all-to-all-start) | async-done | bytes 262176 | tf_op jit(solution)/shard_map/all_to_all | solution.py:115
  77.1 2.2 %fusion.13 = bf16[1536,128]{1,0:T(8,128)(2,1)S(1)} fusion(bf16[1024,128]{1,0:T(8,128)(2,1)} %bitcast.8, s32[1536]{0:T(1024)S(1)} %eq.187), kind=kOutput, calls=%fused_computation.16 | convolution fusion | flops 404422656 | bytes 661504 | tf_op jit(solution)/shard_map/dot_general | solution.py:15
  79.3 6.3 %collective-permute-start.10 = (bf16[384,128]{1,0:T(8,128)(2,1)S(1)}, bf16[384,128]{1,0:T(8,128)(2,1)S(1)}, u32[]{:S(2)}, u32[]{:S(2)}) collective-permute-start(bf16[384,128]{1,0:T(8,128)(2,1)S(1)} %get-tuple-element.38), channel_id=1, source_target_pairs={{0,16},{16,32},{32,48},{48,64},{64,80},{80,96},{96,112},{112,128},... | collective-permute-start | bytes 294920 | tf_op jit(solution)/shard_map/ppermute | solution.py:21
  85.7 1.3 collective-permute-start.13
  87.0 4.0 %collective-permute-start.12 = (bf16[384,128]{1,0:T(8,128)(2,1)S(1)}, bf16[384,128]{1,0:T(8,128)(2,1)S(1)}, u32[]{:S(2)}, u32[]{:S(2)}) collective-permute-start(bf16[384,128]{1,0:T(8,128)(2,1)S(1)} %get-tuple-element.40), channel_id=1, source_target_pairs={{0,4},{4,8},{8,12},{1,5},{5,9},{9,13},{2,6},{6,10},{10,14},{3,7},{... | collective-permute-start | bytes 294920 | tf_op jit(solution)/shard_map/ppermute | solution.py:21
  91.0 1.9 %collective-permute-start.11 = (bf16[384,128]{1,0:T(8,128)(2,1)S(1)}, bf16[384,128]{1,0:T(8,128)(2,1)S(1)}, u32[]{:S(2)}, u32[]{:S(2)}) collective-permute-start(bf16[384,128]{1,0:T(8,128)(2,1)S(1)} %get-tuple-element.41), channel_id=1, source_target_pairs={{16,0},{32,16},{48,32},{64,48},{80,64},{96,80},{112,96},{128,112},... | collective-permute-start | bytes 294920 | tf_op jit(solution)/shard_map/ppermute | solution.py:21
  93.1 3.8 %collective-permute-done.11 = bf16[384,128]{1,0:T(8,128)(2,1)S(1)} collective-permute-done((bf16[384,128]{1,0:T(8,128)(2,1)S(1)}, bf16[384,128]{1,0:T(8,128)(2,1)S(1)}, u32[]{:S(2)}, u32[]{:S(2)}) %collective-permute-start.11) | collective-permute-done | bytes 98336 | tf_op jit(solution)/shard_map/ppermute | solution.py:21
  97.2 1.5 fusion.2
  98.7 1.8 fusion.106
  100.6 1.3 fusion.12
  102.0 1.9 %collective-permute-start.14 = (bf16[384,128]{1,0:T(8,128)(2,1)S(1)}, bf16[384,128]{1,0:T(8,128)(2,1)S(1)}, u32[]{:S(2)}, u32[]{:S(2)}) collective-permute-start(bf16[384,128]{1,0:T(8,128)(2,1)S(1)} %get-tuple-element.34), channel_id=1, source_target_pairs={{16,0},{32,16},{48,32},{64,48},{80,64},{96,80},{112,96},{128,112},... | collective-permute-start | bytes 294920 | tf_op jit(solution)/shard_map/ppermute | solution.py:21
  103.9 2.9 %collective-permute-start.17 = (bf16[384,128]{1,0:T(8,128)(2,1)S(1)}, bf16[384,128]{1,0:T(8,128)(2,1)S(1)}, u32[]{:S(2)}, u32[]{:S(2)}) collective-permute-start(bf16[384,128]{1,0:T(8,128)(2,1)S(1)} %get-tuple-element.35), channel_id=1, source_target_pairs={{0,4},{4,8},{8,12},{1,5},{5,9},{9,13},{2,6},{6,10},{10,14},{3,7},{... | collective-permute-start | bytes 294920 | tf_op jit(solution)/shard_map/ppermute | solution.py:21
  106.8 1.3 collective-permute-start.16
  108.1 3.9 %collective-permute-start.15 = (bf16[384,128]{1,0:T(8,128)(2,1)S(1)}, bf16[384,128]{1,0:T(8,128)(2,1)S(1)}, u32[]{:S(2)}, u32[]{:S(2)}) collective-permute-start(bf16[384,128]{1,0:T(8,128)(2,1)S(1)} %get-tuple-element.37), channel_id=1, source_target_pairs={{0,16},{16,32},{32,48},{48,64},{64,80},{80,96},{96,112},{112,128},... | collective-permute-start | bytes 294920 | tf_op jit(solution)/shard_map/ppermute | solution.py:21
  112.0 1.5 fusion.43
  116.8 1.8 collective-permute-done.18
  119.0 1.0 collective-permute-start.19
  120.5 0.7 collective-permute-start.20
  121.2 6.3 %collective-permute-done.19 = bf16[128,1152]{1,0:T(8,128)(2,1)S(1)} collective-permute-done((bf16[128,1152]{1,0:T(8,128)(2,1)S(1)}, bf16[128,1152]{1,0:T(8,128)(2,1)S(1)}, u32[]{:S(2)}, u32[]{:S(2)}) %collective-permute-start.19) | collective-permute-done | bytes 294944 | tf_op jit(solution)/shard_map/ppermute | solution.py:26
  127.5 8.1 %collective-permute-done.21 = bf16[128,1152]{1,0:T(8,128)(2,1)S(1)} collective-permute-done((bf16[128,1152]{1,0:T(8,128)(2,1)S(1)}, bf16[128,1152]{1,0:T(8,128)(2,1)S(1)}, u32[]{:S(2)}, u32[]{:S(2)}) %collective-permute-start.21) | collective-permute-done | bytes 294944 | tf_op jit(solution)/shard_map/ppermute | solution.py:26
  135.8 27.7 %all_to_all.15 = bf16[32,4,1152]{2,1,0:T(4,128)(2,1)S(1)} all-to-all(bf16[32,4,1152]{2,1,0:T(4,128)(2,1)S(1)} %reshape.211), channel_id=1, replica_groups=mesh['z'=8,'core'=2,'gy'=4,'af'=4] {'z','gy'}, dimensions={0} | all-to-all | bytes 589824 | tf_op jit(solution)/shard_map/all_to_all | solution.py:162
  163.8 15.8 %all_to_all.16 = bf16[32,4,1152]{2,1,0:T(4,128)(2,1)S(1)} all-to-all(bf16[32,4,1152]{2,1,0:T(4,128)(2,1)S(1)} %broadcast_in_dim.102), channel_id=1, replica_groups=mesh['z'=8,'core'=2,'gy'=4,'af'=4] {'z','gy'}, dimensions={0} | all-to-all | bytes 589824 | tf_op jit(solution)/shard_map/all_to_all | solution.py:164
  179.7 4.2 %collective-permute-start.22 = (bf16[128,1152]{1,0:T(8,128)(2,1)S(1)}, bf16[128,1152]{1,0:T(8,128)(2,1)S(1)}, u32[]{:S(2)}, u32[]{:S(2)}) collective-permute-start(bf16[128,1152]{1,0:T(8,128)(2,1)S(1)} %reshape.212), channel_id=1, source_target_pairs={{0,16},{16,0},{1,17},{17,1},{2,18},{18,2},{3,19},{19,3},{4,20},{20... | collective-permute-start | bytes 884744 | tf_op jit(solution)/shard_map/ppermute | solution.py:167
  183.9 1.2 collective-permute-done.22
  185.9 1.1 slice.193
  (107 shorter events, 11.4 us)
Async XLA Ops:
  0.6 7.8 %copy-start = (bf16[1024,256]{1,0:T(8,128)(2,1)S(1)}, bf16[1024,256]{1,0:T(8,128)(2,1)}, u32[]{:S(2)}) copy-start(bf16[1024,256]{1,0:T(8,128)(2,1)} %param.10) | copy-start | bytes 1572868
  4.1 54.4 %collective-permute-start.9 = (bf16[256,1152]{1,0:T(8,128)(2,1)}, bf16[256,1152]{1,0:T(8,128)(2,1)S(1)}, u32[]{:S(2)}, u32[]{:S(2)}) collective-permute-start(bf16[256,1152]{1,0:T(8,128)(2,1)} %get-tuple-element.49), channel_id=1, source_target_pairs={{0,3},{1,0},{2,1},{3,2},{4,7},{5,4},{6,5},{7,6},{8,11},{9,8},{10,9... | collective-permute-start | bytes 1769480 | tf_op jit(solution)/shard_map/ppermute | solution.py:26
  8.4 14.7 %copy-start.16 = (s32[8,4]{0,1:T(4,128)S(1)}, s32[8,4]{0,1:T(4,128)}, u32[]{:S(2)}) copy-start(s32[8,4]{0,1:T(4,128)} %param.12) | copy-start | bytes 388
  8.4 14.7 %copy-start.14 = (s32[4,384]{1,0:T(4,128)S(1)}, s32[4,384]{1,0:T(4,128)}, u32[]{:S(2)}) copy-start(s32[4,384]{1,0:T(4,128)} %param.15) | copy-start | bytes 18436
  8.4 14.7 %copy-start.15 = (f32[4,384]{1,0:T(4,128)S(1)}, f32[4,384]{1,0:T(4,128)}, u32[]{:S(2)}) copy-start(f32[4,384]{1,0:T(4,128)} %param.16) | copy-start | bytes 18436
  9.7 13.4 %copy-start.2 = (bf16[8,4,128,128]{3,2,1,0:T(8,128)(2,1)S(1)}, bf16[8,4,128,128]{3,2,1,0:T(8,128)(2,1)}, u32[]{:S(2)}) copy-start(bf16[8,4,128,128]{3,2,1,0:T(8,128)(2,1)} %param.11) | copy-start | bytes 3145732
  10.6 16.5 %collective-permute-start = (bf16[384,256]{1,0:T(8,128)(2,1)}, bf16[384,256]{1,0:T(8,128)(2,1)S(1)}, u32[]{:S(2)}, u32[]{:S(2)}) collective-permute-start(bf16[384,256]{1,0:T(8,128)(2,1)} %get-tuple-element.13), channel_id=1, source_target_pairs={{0,16},{16,32},{32,48},{48,64},{64,80},{80,96},{96,112},{112,128},... | collective-permute-start | bytes 589832 | tf_op jit(solution)/shard_map/ppermute | solution.py:21
  15.0 12.5 %collective-permute-start.3 = (bf16[384,256]{1,0:T(8,128)(2,1)}, bf16[384,256]{1,0:T(8,128)(2,1)}, u32[]{:S(2)}, u32[]{:S(2)}) collective-permute-start(bf16[384,256]{1,0:T(8,128)(2,1)} %get-tuple-element.14), channel_id=1, source_target_pairs={{4,0},{8,4},{12,8},{5,1},{9,5},{13,9},{6,2},{10,6},{14,10},{7,3},{... | collective-permute-start | bytes 589832 | tf_op jit(solution)/shard_map/ppermute | solution.py:21
  16.3 11.9 %collective-permute-start.2 = (bf16[384,256]{1,0:T(8,128)(2,1)}, bf16[384,256]{1,0:T(8,128)(2,1)}, u32[]{:S(2)}, u32[]{:S(2)}) collective-permute-start(bf16[384,256]{1,0:T(8,128)(2,1)} %get-tuple-element.15), channel_id=1, source_target_pairs={{0,4},{4,8},{8,12},{1,5},{5,9},{9,13},{2,6},{6,10},{10,14},{3,7},{... | collective-permute-start | bytes 589832 | tf_op jit(solution)/shard_map/ppermute | solution.py:21
  21.0 7.3 %collective-permute-start.1 = (bf16[384,256]{1,0:T(8,128)(2,1)}, bf16[384,256]{1,0:T(8,128)(2,1)}, u32[]{:S(2)}, u32[]{:S(2)}) collective-permute-start(bf16[384,256]{1,0:T(8,128)(2,1)} %get-tuple-element.16), channel_id=1, source_target_pairs={{16,0},{32,16},{48,32},{64,48},{80,64},{96,80},{112,96},{128,112},... | collective-permute-start | bytes 589832 | tf_op jit(solution)/shard_map/ppermute | solution.py:21
  23.1 6.6 %copy-start.12 = (s32[1536]{0:T(1024)}, s32[1536]{0:T(1024)S(1)}, u32[]{:S(2)}) copy-start(s32[1536]{0:T(1024)S(1)} %eq.184) | copy-start | bytes 18436
  27.1 31.4 %collective-permute-start.8 = (bf16[256,1152]{1,0:T(8,128)(2,1)}, bf16[256,1152]{1,0:T(8,128)(2,1)S(1)}, u32[]{:S(2)}, u32[]{:S(2)}) collective-permute-start(bf16[256,1152]{1,0:T(8,128)(2,1)} %get-tuple-element.49), channel_id=1, source_target_pairs={{0,2},{1,3},{2,0},{3,1},{4,6},{5,7},{6,4},{7,5},{8,10},{9,11},{10,... | collective-permute-start | bytes 1769480 | tf_op jit(solution)/shard_map/ppermute | solution.py:26
  27.5 31.0 %collective-permute-start.7 = (bf16[256,1152]{1,0:T(8,128)(2,1)}, bf16[256,1152]{1,0:T(8,128)(2,1)S(1)}, u32[]{:S(2)}, u32[]{:S(2)}) collective-permute-start(bf16[256,1152]{1,0:T(8,128)(2,1)} %get-tuple-element.49), channel_id=1, source_target_pairs={{0,1},{1,2},{2,3},{3,0},{4,5},{5,6},{6,7},{7,4},{8,9},{9,10},{10,1... | collective-permute-start | bytes 1769480 | tf_op jit(solution)/shard_map/ppermute | solution.py:26
  31.6 2.8 %copy-start.1 = (bf16[256,1024]{1,0:T(8,128)(2,1)S(1)}, bf16[256,1024]{1,0:T(8,128)(2,1)}, u32[]{:S(2)}) copy-start(bf16[256,1024]{1,0:T(8,128)(2,1)} %param.18) | copy-start | bytes 1572868
  32.4 26.1 %copy-start.5 = (bf16[2048,128]{1,0:T(8,128)(2,1)S(1)}, bf16[2048,128]{1,0:T(8,128)(2,1)}, u32[]{:S(2)}) copy-start(bf16[2048,128]{1,0:T(8,128)(2,1)} %get-tuple-element.48) | copy-start | bytes 1572868
  32.4 26.1 %copy-start.3 = (bf16[256,128]{1,0:T(8,128)(2,1)S(1)}, bf16[256,128]{1,0:T(8,128)(2,1)}, u32[]{:S(2)}) copy-start(bf16[256,128]{1,0:T(8,128)(2,1)} %param.19) | copy-start | bytes 196612
  32.5 25.3 %collective-permute-start.5 = (bf16[256,256]{0,1:T(8,128)(2,1)S(1)}, bf16[256,256]{0,1:T(8,128)(2,1)S(1)}, u32[]{:S(2)}, u32[]{:S(2)}) collective-permute-start(bf16[256,256]{0,1:T(8,128)(2,1)S(1)} %get-tuple-element.29), channel_id=1, source_target_pairs={{0,2},{1,3},{2,0},{3,1},{4,6},{5,7},{6,4},{7,5},{8,10},{9,11},{10,... | collective-permute-start | bytes 393224 | tf_op jit(solution)/shard_map/ppermute | solution.py:26
  34.8 23.9 %collective-permute-start.6 = (bf16[256,256]{0,1:T(8,128)(2,1)S(1)}, bf16[256,256]{0,1:T(8,128)(2,1)S(1)}, u32[]{:S(2)}, u32[]{:S(2)}) collective-permute-start(bf16[256,256]{0,1:T(8,128)(2,1)S(1)} %get-tuple-element.30), channel_id=1, source_target_pairs={{0,3},{1,0},{2,1},{3,2},{4,7},{5,4},{6,5},{7,6},{8,11},{9,8},{10,9... | collective-permute-start | bytes 393224 | tf_op jit(solution)/shard_map/ppermute | solution.py:26
  57.8 6.0 %collective-permute-start.4 = (bf16[256,256]{0,1:T(8,128)(2,1)S(1)}, bf16[256,256]{0,1:T(8,128)(2,1)S(1)}, u32[]{:S(2)}, u32[]{:S(2)}) collective-permute-start(bf16[256,256]{0,1:T(8,128)(2,1)S(1)} %get-tuple-element.31), channel_id=1, source_target_pairs={{0,1},{1,2},{2,3},{3,0},{4,5},{5,6},{6,7},{7,4},{8,9},{9,10},{10,1... | collective-permute-start | bytes 393224 | tf_op jit(solution)/shard_map/ppermute | solution.py:26
  59.0 6.6 %copy-start.6 = (bf16[2048,128]{1,0:T(8,128)(2,1)}, bf16[2048,128]{1,0:T(8,128)(2,1)S(1)}, u32[]{:S(2)}) copy-start(bf16[2048,128]{1,0:T(8,128)(2,1)S(1)} %slice_dynamic-update-slice_fusion.1) | copy-start | bytes 1572868
  66.6 10.5 %all-to-all-start = ((bf16[4,256,128]{2,1,0:T(8,128)(2,1)}), bf16[4,256,128]{2,1,0:T(8,128)(2,1)}, u32[]{:S(2)}, u32[]{:S(2)}) async-start(bf16[4,256,128]{2,1,0:T(8,128)(2,1)} %broadcast_in_dim.101), calls=%async_computation | async-start | bytes 524288 | tf_op jit(solution)/shard_map/all_to_all | solution.py:115
  79.3 17.9 %copy-start.13 = (s32[1536]{0:T(1024)S(1)}, s32[1536]{0:T(1024)}, u32[]{:S(2)}) copy-start(s32[1536]{0:T(1024)} %copy-done.12) | copy-start | bytes 18436
  79.3 13.7 %collective-permute-start.10 = (bf16[384,128]{1,0:T(8,128)(2,1)S(1)}, bf16[384,128]{1,0:T(8,128)(2,1)S(1)}, u32[]{:S(2)}, u32[]{:S(2)}) collective-permute-start(bf16[384,128]{1,0:T(8,128)(2,1)S(1)} %get-tuple-element.38), channel_id=1, source_target_pairs={{0,16},{16,32},{32,48},{48,64},{64,80},{80,96},{96,112},{112,128},... | collective-permute-start | bytes 294920 | tf_op jit(solution)/shard_map/ppermute | solution.py:21
  85.7 7.4 %collective-permute-start.13 = (bf16[384,128]{1,0:T(8,128)(2,1)S(1)}, bf16[384,128]{1,0:T(8,128)(2,1)S(1)}, u32[]{:S(2)}, u32[]{:S(2)}) collective-permute-start(bf16[384,128]{1,0:T(8,128)(2,1)S(1)} %get-tuple-element.39), channel_id=1, source_target_pairs={{4,0},{8,4},{12,8},{5,1},{9,5},{13,9},{6,2},{10,6},{14,10},{7,3},{... | collective-permute-start | bytes 294920 | tf_op jit(solution)/shard_map/ppermute | solution.py:21
  87.0 6.1 %collective-permute-start.12 = (bf16[384,128]{1,0:T(8,128)(2,1)S(1)}, bf16[384,128]{1,0:T(8,128)(2,1)S(1)}, u32[]{:S(2)}, u32[]{:S(2)}) collective-permute-start(bf16[384,128]{1,0:T(8,128)(2,1)S(1)} %get-tuple-element.40), channel_id=1, source_target_pairs={{0,4},{4,8},{8,12},{1,5},{5,9},{9,13},{2,6},{6,10},{10,14},{3,7},{... | collective-permute-start | bytes 294920 | tf_op jit(solution)/shard_map/ppermute | solution.py:21
  91.0 5.9 %collective-permute-start.11 = (bf16[384,128]{1,0:T(8,128)(2,1)S(1)}, bf16[384,128]{1,0:T(8,128)(2,1)S(1)}, u32[]{:S(2)}, u32[]{:S(2)}) collective-permute-start(bf16[384,128]{1,0:T(8,128)(2,1)S(1)} %get-tuple-element.41), channel_id=1, source_target_pairs={{16,0},{32,16},{48,32},{64,48},{80,64},{96,80},{112,96},{128,112},... | collective-permute-start | bytes 294920 | tf_op jit(solution)/shard_map/ppermute | solution.py:21
  98.7 1.9 %copy-start.18 = (s32[1024]{0:T(1024)S(1)}, s32[1024]{0:T(1024)}, u32[]{:S(2)}) copy-start(s32[1024]{0:T(1024)} %param.17) | copy-start | bytes 12292
  101.9 11.7 %copy-start.17 = (s32[256]{0:T(256)S(1)}, s32[256]{0:T(256)}, u32[]{:S(2)}) copy-start(s32[256]{0:T(256)} %slice_add_fusion.3) | copy-start | bytes 3076
  102.0 11.6 %collective-permute-start.14 = (bf16[384,128]{1,0:T(8,128)(2,1)S(1)}, bf16[384,128]{1,0:T(8,128)(2,1)S(1)}, u32[]{:S(2)}, u32[]{:S(2)}) collective-permute-start(bf16[384,128]{1,0:T(8,128)(2,1)S(1)} %get-tuple-element.34), channel_id=1, source_target_pairs={{16,0},{32,16},{48,32},{64,48},{80,64},{96,80},{112,96},{128,112},... | collective-permute-start | bytes 294920 | tf_op jit(solution)/shard_map/ppermute | solution.py:21
  103.9 9.7 %collective-permute-start.17 = (bf16[384,128]{1,0:T(8,128)(2,1)S(1)}, bf16[384,128]{1,0:T(8,128)(2,1)S(1)}, u32[]{:S(2)}, u32[]{:S(2)}) collective-permute-start(bf16[384,128]{1,0:T(8,128)(2,1)S(1)} %get-tuple-element.35), channel_id=1, source_target_pairs={{0,4},{4,8},{8,12},{1,5},{5,9},{9,13},{2,6},{6,10},{10,14},{3,7},{... | collective-permute-start | bytes 294920 | tf_op jit(solution)/shard_map/ppermute | solution.py:21
  106.8 6.8 %collective-permute-start.16 = (bf16[384,128]{1,0:T(8,128)(2,1)S(1)}, bf16[384,128]{1,0:T(8,128)(2,1)S(1)}, u32[]{:S(2)}, u32[]{:S(2)}) collective-permute-start(bf16[384,128]{1,0:T(8,128)(2,1)S(1)} %get-tuple-element.36), channel_id=1, source_target_pairs={{4,0},{8,4},{12,8},{5,1},{9,5},{13,9},{6,2},{10,6},{14,10},{7,3},{... | collective-permute-start | bytes 294920 | tf_op jit(solution)/shard_map/ppermute | solution.py:21
  108.1 5.5 %collective-permute-start.15 = (bf16[384,128]{1,0:T(8,128)(2,1)S(1)}, bf16[384,128]{1,0:T(8,128)(2,1)S(1)}, u32[]{:S(2)}, u32[]{:S(2)}) collective-permute-start(bf16[384,128]{1,0:T(8,128)(2,1)S(1)} %get-tuple-element.37), channel_id=1, source_target_pairs={{0,16},{16,32},{32,48},{48,64},{64,80},{80,96},{96,112},{112,128},... | collective-permute-start | bytes 294920 | tf_op jit(solution)/shard_map/ppermute | solution.py:21
  112.0 2.1 %copy-start.7 = (bf16[2048,128]{1,0:T(8,128)(2,1)S(1)}, bf16[2048,128]{1,0:T(8,128)(2,1)}, u32[]{:S(2)}) copy-start(bf16[2048,128]{1,0:T(8,128)(2,1)} %copy-done.6) | copy-start | bytes 1572868
  112.0 2.1 %copy-start.19 = (f32[256,1024]{1,0:T(8,128)S(1)}, f32[256,1024]{1,0:T(8,128)}, u32[]{:S(2)}) copy-start(f32[256,1024]{1,0:T(8,128)} %get-tuple-element.55) | copy-start | bytes 3145732
  114.1 0.8 copy-start.8
  114.1 0.9 copy-start.9
  114.1 0.9 copy-start.10
  114.1 0.9 copy-start.11
  115.5 0.8 copy-start.4
  115.6 2.9 %collective-permute-start.18 = (bf16[512,1152]{1,0:T(8,128)(2,1)S(1)}, bf16[512,1152]{1,0:T(8,128)(2,1)S(1)}, u32[]{:S(2)}, u32[]{:S(2)}) collective-permute-start(bf16[512,1152]{1,0:T(8,128)(2,1)S(1)} %pad_maximum_fusion), channel_id=1, source_target_pairs={{0,16},{16,0},{1,17},{17,1},{2,18},{18,2},{3,19},{19,3},{4,20},{20... | collective-permute-start | bytes 3538952 | tf_op jit(solution)/shard_map/ppermute | solution.py:156
  119.0 8.5 %collective-permute-start.19 = (bf16[128,1152]{1,0:T(8,128)(2,1)S(1)}, bf16[128,1152]{1,0:T(8,128)(2,1)S(1)}, u32[]{:S(2)}, u32[]{:S(2)}) collective-permute-start(bf16[128,1152]{1,0:T(8,128)(2,1)S(1)} %get-tuple-element.4), channel_id=1, source_target_pairs={{0,3},{1,0},{2,1},{3,2},{4,7},{5,4},{6,5},{7,6},{8,11},{9,8},{10,9... | collective-permute-start | bytes 884744 | tf_op jit(solution)/shard_map/ppermute | solution.py:26
  119.9 15.7 %collective-permute-start.21 = (bf16[128,1152]{1,0:T(8,128)(2,1)S(1)}, bf16[128,1152]{1,0:T(8,128)(2,1)S(1)}, u32[]{:S(2)}, u32[]{:S(2)}) collective-permute-start(bf16[128,1152]{1,0:T(8,128)(2,1)S(1)} %get-tuple-element.5), channel_id=1, source_target_pairs={{0,1},{1,2},{2,3},{3,0},{4,5},{5,6},{6,7},{7,4},{8,9},{9,10},{10,1... | collective-permute-start | bytes 884744 | tf_op jit(solution)/shard_map/ppermute | solution.py:26
  120.5 15.1 %collective-permute-start.20 = (bf16[128,1152]{1,0:T(8,128)(2,1)S(1)}, bf16[128,1152]{1,0:T(8,128)(2,1)S(1)}, u32[]{:S(2)}, u32[]{:S(2)}) collective-permute-start(bf16[128,1152]{1,0:T(8,128)(2,1)S(1)} %get-tuple-element.6), channel_id=1, source_target_pairs={{0,2},{1,3},{2,0},{3,1},{4,6},{5,7},{6,4},{7,5},{8,10},{9,11},{10,... | collective-permute-start | bytes 884744 | tf_op jit(solution)/shard_map/ppermute | solution.py:26
  179.7 5.4 %collective-permute-start.22 = (bf16[128,1152]{1,0:T(8,128)(2,1)S(1)}, bf16[128,1152]{1,0:T(8,128)(2,1)S(1)}, u32[]{:S(2)}, u32[]{:S(2)}) collective-permute-start(bf16[128,1152]{1,0:T(8,128)(2,1)S(1)} %reshape.212), channel_id=1, source_target_pairs={{0,16},{16,0},{1,17},{17,1},{2,18},{18,2},{3,19},{19,3},{4,20},{20... | collective-permute-start | bytes 884744 | tf_op jit(solution)/shard_map/ppermute | solution.py:167

commit v2 on v1

--- a/solution.py
+++ b/solution.py
@@ -69,8 +69,19 @@
     half = w_rows // 2
     blocks, kt, tb, _ = adj_tiles.shape
 
-    w_both = jnp.concatenate([w_hidden, w_classes], axis=1)
-    w_from = [w_both] + [turn(w_both, "af", k) for k in range(1, n_af)]
+    swap = [(0, 1), (1, 0)]
+    w_both = [
+        jnp.concatenate(
+            [
+                lax.dynamic_slice_in_dim(w_hidden, part * half, half, axis=0),
+                lax.dynamic_slice_in_dim(w_classes, part * half, half, axis=0),
+            ],
+            axis=1,
+        )
+        for part in (core, 1 - core)
+    ]
+    w_mine = [w_both[0]] + [turn(w_both[0], "af", k) for k in range(1, n_af)]
+    w_other = [w_both[1]] + [lax.ppermute(w, "core", swap) for w in w_mine[1:]]
 
     live = jnp.arange(slots, dtype=jnp.int32)[None, :] < send_counts[:, None]
     send_at = jnp.where(live, send_rows, -1).reshape(-1)
@@ -95,30 +106,38 @@
     width = features.shape[1]
     spread = dot(put_recv, two_parts(arrived))
     mixed = (dot(dense, features) + spread[:, :width] + spread[:, width:]).astype(BF)
+    mixed = jnp.where(core == 0, mixed, jnp.roll(mixed, half, axis=1))
 
     def rows_for(k):
         return lax.dynamic_slice_in_dim(mixed, ((af + k) % n_af) * own, own, axis=0)
 
     mixed_from = [rows_for(0)] + [turn(rows_for(k), "af", k) for k in range(1, n_af)]
-    pre_act = sum(dot(m, w[:, :hid]) for m, w in zip(mixed_from, w_from))
+    pre_act = sum(
+        dot(m[:, :half], w[:, :hid]) + dot(m[:, half:], v[:, :hid])
+        for m, w, v in zip(mixed_from, w_mine, w_other)
+    )
     sigmoid_act = jax.nn.sigmoid(pre_act)
     hidden = (pre_act * sigmoid_act).astype(BF)
     slope = sigmoid_act * (1.0 + pre_act * (1.0 - sigmoid_act))
 
-    w_cls = [w[:, hid:] for w in w_from]
+    w_cls = []
+    for w, v in zip(w_mine, w_other):
+        w, v = w[:, hid:], v[:, hid:]
+        w_cls.append(jnp.where(core == 0, jnp.concatenate([w, v]), jnp.concatenate([v, w])))
     around = [w_cls[(n_af - k) % n_af] for k in range(n_af)]
     w_cls = lax.dynamic_slice_in_dim(
         jnp.concatenate(around + around, axis=0), (n_af - af) * w_rows, n_af * w_rows, axis=0
     )
 
-    z_own = dot(hidden, w_cls).astype(BF)
+    z_own = two_parts(dot(hidden, w_cls))
     z_all = lax.all_to_all(
-        jnp.broadcast_to(z_own[None], (n_af, own, classes)), "af", 0, 0, tiled=True
-    ).reshape(nodes, classes)
+        jnp.broadcast_to(z_own[None], (n_af,) + z_own.shape), "af", 0, 0, tiled=True
+    ).reshape(nodes, 2 * classes)
     out = dot(pick_send, z_all).astype(BF).reshape(4, slots, -1)
-    arrived = trade(out, 1).astype(F32) * weight
-    spread = dot(put_recv, two_parts(arrived))
-    logits = dot(dense, z_all) + spread[:, :classes] + spread[:, classes:]
+    arrived = trade(out, 1).astype(F32)
+    arrived = (arrived[:, :classes] + arrived[:, classes:]) * weight
+    spread = dot(put_recv, two_parts(arrived)) + dot(dense, z_all)
+    logits = spread[:, :classes] + spread[:, classes:]
 
     exponent = jnp.exp(logits - jnp.max(logits, axis=1, keepdims=True))
     probability = exponent / jnp.sum(exponent, axis=1, keepdims=True)
@@ -131,10 +150,8 @@
     grad_own = (dot(dense_own, grad_logits, 0, 0) + dot(put_send, returned)).astype(BF)
     grad_pre = (dot(grad_own, w_cls, 1, 1) * slope).astype(BF)
 
-    def columns(which):
-        return jnp.concatenate(
-            [lax.dynamic_slice_in_dim(m, which * half, half, axis=1) for m in mixed_from], axis=1
-        )
+    def columns(start):
+        return jnp.concatenate([m[:, start : start + half] for m in mixed_from], axis=1)
 
     def hidden_columns(which):
         return jnp.concatenate(
@@ -147,14 +164,14 @@
             axis=1,
         )
 
-    def terms(which):
+    def terms(start, which):
         return jnp.concatenate(
-            [dot(columns(which), grad_pre, 0, 0), dot(hidden_columns(which), grad_own, 0, 0)],
+            [dot(columns(start), grad_pre, 0, 0), dot(hidden_columns(which), grad_own, 0, 0)],
             axis=1,
         )
 
-    theirs = lax.ppermute(terms(1 - core).astype(BF), "core", [(0, 1), (1, 0)])
-    pair_sum = (terms(core) + theirs.astype(F32)).reshape(n_af, half, hid + classes)
+    theirs = lax.ppermute(terms(half, 1 - core).astype(BF), "core", swap)
+    pair_sum = (terms(0, core) + theirs.astype(F32)).reshape(n_af, half, hid + classes)
     total = pair_sum[0]
     for k in range(1, n_af):
         total = total + turn(pair_sum[k].astype(BF), "af", -k).astype(F32)
@@ -164,7 +181,7 @@
     mine = lax.all_to_all(
         jnp.broadcast_to(piece[None], (n_plane,) + piece.shape), PLANE, 0, 0, tiled=True
     ).reshape(half, hid + classes)
-    other = lax.ppermute(mine, "core", [(0, 1), (1, 0)])
+    other = lax.ppermute(mine, "core", swap)
     first = jnp.where(core == 0, mine, other)
     second = jnp.where(core == 0, other, mine)
     whole = jnp.concatenate([first, second], axis=0).astype(F32)

time: 188 us -> 174 us (0.926)
  waiting for transfers between devices: 51.3 us -> 36.3 us
  blocking collectives: 43.5 us -> 38.2 us
  other arithmetic: 5.94 us -> 9.28 us
    ppermute x9, waiting for transfers between devices: 39.4 us -> 21.6 us  [turn(): lax.ppermute(field, axis, [(i, (i + move) % count) for i in range(count)])]
    all_to_all x1, blocking collectives: 27.7 us -> 22.8 us  [local(): pieces = lax.all_to_all(pieces, PLANE, 0, 0, tiled=True)]
    slice x0 -> x11, local copies, waits for them, and re-layouts: none -> 3.84 us  [the longest x3 3 us: columns(): m[:, start:start + half]]
    dynamic_slice x4 -> x2, local copies, waits for them, and re-layouts: 2.67 us -> 0.04 us  [the longest x1 0.03 us: local(): lax.dynamic_slice_in_dim(w_hidden, part * half, half, axis=0)]
    unnamed x49 -> x53, local copies, waits for them, and re-layouts: 6.07 us -> 4.38 us
    dot_general x19 -> x23, matrix products: 17.3 us -> 17.8 us  [dot(): lax.dot_general(lhs, rhs, (((lhs_dim,), (rhs_dim,)), ((), ())), preferred...]
    ppermute x2 -> x5, starting transfers between devices: 4.32 us -> 4.21 us  [the longest x1 3.69 us: local(): other = lax.ppermute(mine, 'core', swap)]
  transfers between devices with their start and end apart: 24 -> 27, of which waited for: 9 -> 12; matrix products, arithmetic and copies ran while one was open for 9% -> 12% of each run, Pallas kernels for 0% -> 0%
where the time goes in v2:
time: 174 us; the launch traced here: 173 us
  starting transfers between devices  56.5 us (32%)
  blocking collectives  38.2 us (22%)
  waiting for transfers between devices  36.3 us (21%)
  matrix products  17.8 us (10%)
  local copies, waits for them, and re-layouts  13.3 us (8%)
  other arithmetic  9.28 us (5%)
    ppermute x12, starting transfers between devices, step(): return lax.ppermute(field, axis, pairs)  37.6 us
    all_to_all x1, blocking collectives, local(): pieces = lax.all_to_all(pieces, PLANE, 0, 0, tiled=True)  22.8 us
    ppermute x9, waiting for transfers between devices, turn(): lax.ppermute(field, axis, [(i, (i + move) % count) for i in range(count)])  21.6 us
    dot_general x23, matrix products, dot(): lax.dot_general(lhs, rhs, (((lhs_dim,), (rhs_dim,)), ((), ())), preferred...  17.8 us
    all_to_all x1, blocking collectives, local(): lax.all_to_all(jnp.broadcast_to(piece[None], (n_plane,) + piece.shape), P...  15.3 us
    ppermute x9, starting transfers between devices, turn(): lax.ppermute(field, axis, [(i, (i + move) % count) for i in range(count)])  10.4 us
    all_to_all x1, waiting for transfers between devices, local(): lax.all_to_all(jnp.broadcast_to(z_own[None], (n_af,) + z_own.shape), 'af'...  6.24 us
    ppermute x12, waiting for transfers between devices, step(): return lax.ppermute(field, axis, pairs)  5.19 us
  transfers between devices with their start and end apart: 27, of which 12 were waited for; matrix products, arithmetic and copies ran while one was open for 12% of the time, Pallas kernels for 0%

profile of v2, /device:TPU:1, one launch (start us, length us, event | category | flops | bytes accessed | tf_op | source)
XLA Modules:
  0.0 172.8 jit_solution(11582671964964507861)
XLA Ops:
  1.7 1.3 fusion.10
  3.0 0.9 fusion.118
  3.9 4.9 %collective-permute-start = (bf16[384,256]{1,0:T(8,128)(2,1)}, bf16[384,256]{1,0:T(8,128)(2,1)}, u32[]{:S(2)}, u32[]{:S(2)}) collective-permute-start(bf16[384,256]{1,0:T(8,128)(2,1)} %get-tuple-element.21), channel_id=1, source_target_pairs={{0,16},{16,32},{32,48},{48,64},{64,80},{80,96},{96,112},{112,128},... | collective-permute-start | bytes 589832 | tf_op jit(solution)/shard_map/ppermute | solution.py:21
  8.8 2.1 %collective-permute-start.1 = (bf16[384,256]{1,0:T(8,128)(2,1)}, bf16[384,256]{1,0:T(8,128)(2,1)}, u32[]{:S(2)}, u32[]{:S(2)}) collective-permute-start(bf16[384,256]{1,0:T(8,128)(2,1)} %get-tuple-element.24), channel_id=1, source_target_pairs={{16,0},{32,16},{48,32},{64,48},{80,64},{96,80},{112,96},{128,112},... | collective-permute-start | bytes 589832 | tf_op jit(solution)/shard_map/ppermute | solution.py:21
  11.0 3.6 %collective-permute-start.2 = (bf16[384,256]{1,0:T(8,128)(2,1)}, bf16[384,256]{1,0:T(8,128)(2,1)}, u32[]{:S(2)}, u32[]{:S(2)}) collective-permute-start(bf16[384,256]{1,0:T(8,128)(2,1)} %get-tuple-element.23), channel_id=1, source_target_pairs={{0,4},{4,8},{8,12},{1,5},{5,9},{9,13},{2,6},{6,10},{10,14},{3,7},{... | collective-permute-start | bytes 589832 | tf_op jit(solution)/shard_map/ppermute | solution.py:21
  14.6 1.3 collective-permute-start.3
  16.7 1.3 collective-permute-start.7
  19.6 2.1 %select_select_fusion = bf16[8,128,8,128]{3,2,1,0:T(8,128)(2,1)S(1)} fusion(pred[8,8]{1,0:T(8,128)(4,1)S(1)} %get-tuple-element.60, pred[8,8]{1,0:T(8,128)(4,1)S(1)} %get-tuple-element.61, pred[8,8]{1,0:T(8,128)(4,1)S(1)} %get-tuple-element.62, pred[8,8]{1,0:T(8,128)(4,1)S(1)} %get-tuple-element.63, bf16[8,128,128]{2,1,0:T(8,128)(2,1)} %get-tuple-element.13, ...), kind=kLoop, calls=%fused_computation.19 | loop fusion | flops 4194304 | bytes 3145984 | tf_op jit(solution)/shard_map/jit(_where)/select_n | solution.py:101
  21.8 2.0 %copy.23 = bf16[128,8,8,128]{3,1,2,0:T(8,128)(2,1)} copy(bf16[128,8,8,128]{3,2,1,0:T(8,128)(2,1)S(1)} %bitcast.41) | data formatting | bytes 4194304
  25.0 2.6 %collective-permute-start.9 = (bf16[128,1152]{1,0:T(8,128)(2,1)}, bf16[128,1152]{1,0:T(8,128)(2,1)S(1)}, u32[]{:S(2)}, u32[]{:S(2)}) collective-permute-start(bf16[128,1152]{1,0:T(8,128)(2,1)} %pad_maximum_fusion.2), channel_id=1, source_target_pairs={{0,2},{1,3},{2,0},{3,1},{4,6},{5,7},{6,4},{7,5},{8,10},{9,11},{10,... | collective-permute-start | bytes 884744 | tf_op jit(solution)/shard_map/ppermute | solution.py:26
  27.6 1.1 collective-permute-start.11
  28.7 1.5 fusion.17
  30.2 1.9 %fusion.3 = f32[1024,512]{0,1:T(8,128)S(1)} fusion(s32[1536]{0:T(1024)S(1)} %copy-done.18, bf16[1536,256]{1,0:T(8,128)(2,1)S(1)} %get-tuple-element.16, bf16[1536,256]{1,0:T(8,128)(2,1)S(1)} %get-tuple-element.15), kind=kOutput, calls=%fused_computation.6 | convolution fusion | flops 1615331328 | bytes 3676160 | tf_op jit(solution)/shard_map/dot_general | solution.py:15
  35.3 1.7 collective-permute-start.6
  37.8 3.4 %collective-permute-done.11 = bf16[128,1152]{1,0:T(8,128)(2,1)S(1)} collective-permute-done((bf16[128,1152]{1,0:T(8,128)(2,1)}, bf16[128,1152]{1,0:T(8,128)(2,1)S(1)}, u32[]{:S(2)}, u32[]{:S(2)}) %collective-permute-start.11) | collective-permute-done | bytes 294944 | tf_op jit(solution)/shard_map/ppermute | solution.py:26
  41.1 1.5 collective-permute-done.4
  43.1 1.3 fusion.57
  44.7 1.1 collective-permute-done.6
  47.1 1.4 multiply_convert_fusion
  50.6 4.2 %all-to-all-start = ((bf16[4,256,256]{2,1,0:T(8,128)(2,1)}), bf16[4,256,256]{2,1,0:T(8,128)(2,1)S(1)}, u32[]{:S(2)}, u32[]{:S(2)}) async-start(bf16[4,256,256]{2,1,0:T(8,128)(2,1)} %broadcast_in_dim.101), calls=%async_computation | async-start | bytes 1048576 | tf_op jit(solution)/shard_map/all_to_all | solution.py:133
  54.8 1.5 fusion.122
  56.3 1.5 fusion.123
  57.8 6.2 %all-to-all-done = bf16[4,256,256]{2,1,0:T(8,128)(2,1)S(1)} async-done(((bf16[4,256,256]{2,1,0:T(8,128)(2,1)}), bf16[4,256,256]{2,1,0:T(8,128)(2,1)S(1)}, u32[]{:S(2)}, u32[]{:S(2)}) %all-to-all-start) | async-done | bytes 524320 | tf_op jit(solution)/shard_map/all_to_all | solution.py:133
  64.0 1.3 fusion.11
  65.4 5.0 %collective-permute-start.13 = (bf16[384,256]{1,0:T(8,128)(2,1)S(1)}, bf16[384,256]{1,0:T(8,128)(2,1)S(1)}, u32[]{:S(2)}, u32[]{:S(2)}) collective-permute-start(bf16[384,256]{1,0:T(8,128)(2,1)S(1)} %get-tuple-element.17), channel_id=1, source_target_pairs={{0,16},{16,32},{32,48},{48,64},{64,80},{80,96},{96,112},{112,128},... | collective-permute-start | bytes 589832 | tf_op jit(solution)/shard_map/ppermute | solution.py:21
  70.4 1.9 %collective-permute-start.14 = (bf16[384,256]{1,0:T(8,128)(2,1)S(1)}, bf16[384,256]{1,0:T(8,128)(2,1)S(1)}, u32[]{:S(2)}, u32[]{:S(2)}) collective-permute-start(bf16[384,256]{1,0:T(8,128)(2,1)S(1)} %get-tuple-element.20), channel_id=1, source_target_pairs={{16,0},{32,16},{48,32},{64,48},{80,64},{96,80},{112,96},{128,112},... | collective-permute-start | bytes 589832 | tf_op jit(solution)/shard_map/ppermute | solution.py:21
  72.4 4.0 %collective-permute-start.15 = (bf16[384,256]{1,0:T(8,128)(2,1)S(1)}, bf16[384,256]{1,0:T(8,128)(2,1)S(1)}, u32[]{:S(2)}, u32[]{:S(2)}) collective-permute-start(bf16[384,256]{1,0:T(8,128)(2,1)S(1)} %get-tuple-element.19), channel_id=1, source_target_pairs={{0,4},{4,8},{8,12},{1,5},{5,9},{9,13},{2,6},{6,10},{10,14},{3,7},{... | collective-permute-start | bytes 589832 | tf_op jit(solution)/shard_map/ppermute | solution.py:21
  76.4 1.3 collective-permute-start.16
  77.9 1.1 collective-permute-done.15
  78.9 3.9 %collective-permute-done.16 = bf16[384,256]{1,0:T(8,128)(2,1)S(1)} collective-permute-done((bf16[384,256]{1,0:T(8,128)(2,1)S(1)}, bf16[384,256]{1,0:T(8,128)(2,1)S(1)}, u32[]{:S(2)}, u32[]{:S(2)}) %collective-permute-start.16) | collective-permute-done | bytes 196640 | tf_op jit(solution)/shard_map/ppermute | solution.py:21
  83.7 1.5 fusion.2
  86.8 1.7 fusion.13
  88.6 2.1 %collective-permute-start.17 = (bf16[384,128]{1,0:T(8,128)(2,1)S(1)}, bf16[384,128]{1,0:T(8,128)(2,1)S(1)}, u32[]{:S(2)}, u32[]{:S(2)}) collective-permute-start(bf16[384,128]{1,0:T(8,128)(2,1)S(1)} %get-tuple-element.42), channel_id=1, source_target_pairs={{16,0},{32,16},{48,32},{64,48},{80,64},{96,80},{112,96},{128,112},... | collective-permute-start | bytes 294920 | tf_op jit(solution)/shard_map/ppermute | solution.py:21
  90.7 6.1 %collective-permute-start.18 = (bf16[384,128]{1,0:T(8,128)(2,1)S(1)}, bf16[384,128]{1,0:T(8,128)(2,1)S(1)}, u32[]{:S(2)}, u32[]{:S(2)}) collective-permute-start(bf16[384,128]{1,0:T(8,128)(2,1)S(1)} %get-tuple-element.45), channel_id=1, source_target_pairs={{0,16},{16,32},{32,48},{48,64},{64,80},{80,96},{96,112},{112,128},... | collective-permute-start | bytes 294920 | tf_op jit(solution)/shard_map/ppermute | solution.py:21
  96.8 1.3 collective-permute-start.19
  98.1 4.0 %collective-permute-start.20 = (bf16[384,128]{1,0:T(8,128)(2,1)S(1)}, bf16[384,128]{1,0:T(8,128)(2,1)S(1)}, u32[]{:S(2)}, u32[]{:S(2)}) collective-permute-start(bf16[384,128]{1,0:T(8,128)(2,1)S(1)} %get-tuple-element.43), channel_id=1, source_target_pairs={{0,4},{4,8},{8,12},{1,5},{5,9},{9,13},{2,6},{6,10},{10,14},{3,7},{... | collective-permute-start | bytes 294920 | tf_op jit(solution)/shard_map/ppermute | solution.py:21
  102.1 1.4 fusion.40
  106.8 2.1 %collective-permute-done.21 = bf16[512,1152]{1,0:T(8,128)(2,1)S(1)} collective-permute-done((bf16[512,1152]{1,0:T(8,128)(2,1)S(1)}, bf16[512,1152]{1,0:T(8,128)(2,1)S(1)}, u32[]{:S(2)}, u32[]{:S(2)}) %collective-permute-start.21) | collective-permute-done | bytes 1179680 | tf_op jit(solution)/shard_map/ppermute | solution.py:173
  109.3 1.2 collective-permute-start.22
  110.5 1.2 collective-permute-start.23
  111.7 6.4 %collective-permute-done.22 = bf16[128,1152]{1,0:T(8,128)(2,1)S(1)} collective-permute-done((bf16[128,1152]{1,0:T(8,128)(2,1)S(1)}, bf16[128,1152]{1,0:T(8,128)(2,1)S(1)}, u32[]{:S(2)}, u32[]{:S(2)}) %collective-permute-start.22) | collective-permute-done | bytes 294944 | tf_op jit(solution)/shard_map/ppermute | solution.py:26
  118.0 2.2 %collective-permute-done.23 = bf16[128,1152]{1,0:T(8,128)(2,1)S(1)} collective-permute-done((bf16[128,1152]{1,0:T(8,128)(2,1)S(1)}, bf16[128,1152]{1,0:T(8,128)(2,1)S(1)}, u32[]{:S(2)}, u32[]{:S(2)}) %collective-permute-start.23) | collective-permute-done | bytes 294944 | tf_op jit(solution)/shard_map/ppermute | solution.py:26
  120.2 7.1 %collective-permute-done.24 = bf16[128,1152]{1,0:T(8,128)(2,1)S(1)} collective-permute-done((bf16[128,1152]{1,0:T(8,128)(2,1)S(1)}, bf16[128,1152]{1,0:T(8,128)(2,1)S(1)}, u32[]{:S(2)}, u32[]{:S(2)}) %collective-permute-start.24) | collective-permute-done | bytes 294944 | tf_op jit(solution)/shard_map/ppermute | solution.py:26
  127.5 22.8 %all_to_all.15 = bf16[32,4,1152]{2,1,0:T(4,128)(2,1)S(1)} all-to-all(bf16[32,4,1152]{2,1,0:T(4,128)(2,1)S(1)} %reshape.211), channel_id=1, replica_groups=mesh['z'=8,'core'=2,'gy'=4,'af'=4] {'z','gy'}, dimensions={0} | all-to-all | bytes 589824 | tf_op jit(solution)/shard_map/all_to_all | solution.py:179
  150.6 15.3 %all_to_all.16 = bf16[32,4,1152]{2,1,0:T(4,128)(2,1)S(1)} all-to-all(bf16[32,4,1152]{2,1,0:T(4,128)(2,1)S(1)} %broadcast_in_dim.102), channel_id=1, replica_groups=mesh['z'=8,'core'=2,'gy'=4,'af'=4] {'z','gy'}, dimensions={0} | all-to-all | bytes 589824 | tf_op jit(solution)/shard_map/all_to_all | solution.py:181
  166.0 3.7 %collective-permute-start.25 = (bf16[128,1152]{1,0:T(8,128)(2,1)S(1)}, bf16[128,1152]{1,0:T(8,128)(2,1)S(1)}, u32[]{:S(2)}, u32[]{:S(2)}) collective-permute-start(bf16[128,1152]{1,0:T(8,128)(2,1)S(1)} %reshape.212), channel_id=1, source_target_pairs={{0,16},{16,0},{1,17},{17,1},{2,18},{18,2},{3,19},{19,3},{4,20},{20... | collective-permute-start | bytes 884744 | tf_op jit(solution)/shard_map/ppermute | solution.py:184
  169.7 1.2 collective-permute-done.25
  171.7 1.1 slice.291
  (144 shorter events, 20.2 us)
Async XLA Ops:
  0.6 1.1 copy-start
  3.0 12.9 %copy-start.4 = (bf16[256,1024]{1,0:T(8,128)(2,1)S(1)}, bf16[256,1024]{1,0:T(8,128)(2,1)}, u32[]{:S(2)}) copy-start(bf16[256,1024]{1,0:T(8,128)(2,1)} %param.18) | copy-start | bytes 1572868
  3.0 12.9 %copy-start.15 = (bf16[256,128]{1,0:T(8,128)(2,1)S(1)}, bf16[256,128]{1,0:T(8,128)(2,1)}, u32[]{:S(2)}) copy-start(bf16[256,128]{1,0:T(8,128)(2,1)} %param.19) | copy-start | bytes 196612
  3.0 15.0 %copy-start.20 = (f32[4,384]{1,0:T(4,128)S(1)}, f32[4,384]{1,0:T(4,128)}, u32[]{:S(2)}) copy-start(f32[4,384]{1,0:T(4,128)} %param.16) | copy-start | bytes 18436
  3.0 15.0 %copy-start.21 = (s32[4,384]{1,0:T(4,128)S(1)}, s32[4,384]{1,0:T(4,128)}, u32[]{:S(2)}) copy-start(s32[4,384]{1,0:T(4,128)} %param.15) | copy-start | bytes 18436
  3.0 15.6 %copy-start.23 = (s32[8,4]{0,1:T(4,128)S(1)}, s32[8,4]{0,1:T(4,128)}, u32[]{:S(2)}) copy-start(s32[8,4]{0,1:T(4,128)} %param.12) | copy-start | bytes 388
  3.0 15.6 %copy-start.3 = (bf16[8,4,128,128]{3,2,1,0:T(8,128)(2,1)S(1)}, bf16[8,4,128,128]{3,2,1,0:T(8,128)(2,1)}, u32[]{:S(2)}) copy-start(bf16[8,4,128,128]{3,2,1,0:T(8,128)(2,1)} %param.11) | copy-start | bytes 3145732
  3.9 21.1 %collective-permute-start = (bf16[384,256]{1,0:T(8,128)(2,1)}, bf16[384,256]{1,0:T(8,128)(2,1)}, u32[]{:S(2)}, u32[]{:S(2)}) collective-permute-start(bf16[384,256]{1,0:T(8,128)(2,1)} %get-tuple-element.21), channel_id=1, source_target_pairs={{0,16},{16,32},{32,48},{48,64},{64,80},{80,96},{96,112},{112,128},... | collective-permute-start | bytes 589832 | tf_op jit(solution)/shard_map/ppermute | solution.py:21
  8.8 18.8 %collective-permute-start.1 = (bf16[384,256]{1,0:T(8,128)(2,1)}, bf16[384,256]{1,0:T(8,128)(2,1)}, u32[]{:S(2)}, u32[]{:S(2)}) collective-permute-start(bf16[384,256]{1,0:T(8,128)(2,1)} %get-tuple-element.24), channel_id=1, source_target_pairs={{16,0},{32,16},{48,32},{64,48},{80,64},{96,80},{112,96},{128,112},... | collective-permute-start | bytes 589832 | tf_op jit(solution)/shard_map/ppermute | solution.py:21
  11.0 17.7 %collective-permute-start.2 = (bf16[384,256]{1,0:T(8,128)(2,1)}, bf16[384,256]{1,0:T(8,128)(2,1)}, u32[]{:S(2)}, u32[]{:S(2)}) collective-permute-start(bf16[384,256]{1,0:T(8,128)(2,1)} %get-tuple-element.23), channel_id=1, source_target_pairs={{0,4},{4,8},{8,12},{1,5},{5,9},{9,13},{2,6},{6,10},{10,14},{3,7},{... | collective-permute-start | bytes 589832 | tf_op jit(solution)/shard_map/ppermute | solution.py:21
  14.6 14.1 %collective-permute-start.3 = (bf16[384,256]{1,0:T(8,128)(2,1)}, bf16[384,256]{1,0:T(8,128)(2,1)}, u32[]{:S(2)}, u32[]{:S(2)}) collective-permute-start(bf16[384,256]{1,0:T(8,128)(2,1)} %get-tuple-element.22), channel_id=1, source_target_pairs={{4,0},{8,4},{12,8},{5,1},{9,5},{13,9},{6,2},{10,6},{14,10},{7,3},{... | collective-permute-start | bytes 589832 | tf_op jit(solution)/shard_map/ppermute | solution.py:21
  16.7 18.6 %collective-permute-start.7 = (bf16[128,1152]{1,0:T(8,128)(2,1)}, bf16[128,1152]{1,0:T(8,128)(2,1)}, u32[]{:S(2)}, u32[]{:S(2)}) collective-permute-start(bf16[128,1152]{1,0:T(8,128)(2,1)} %pad_maximum_fusion.2), channel_id=1, source_target_pairs={{0,1},{1,2},{2,3},{3,0},{4,5},{5,6},{6,7},{7,4},{8,9},{9,10},{10,1... | collective-permute-start | bytes 884744 | tf_op jit(solution)/shard_map/ppermute | solution.py:26
  23.7 6.5 %copy-start.18 = (s32[1536]{0:T(1024)S(1)}, s32[1536]{0:T(1024)}, u32[]{:S(2)}) copy-start(s32[1536]{0:T(1024)} %eq.189) | copy-start | bytes 18436
  25.0 12.8 %collective-permute-start.9 = (bf16[128,1152]{1,0:T(8,128)(2,1)}, bf16[128,1152]{1,0:T(8,128)(2,1)S(1)}, u32[]{:S(2)}, u32[]{:S(2)}) collective-permute-start(bf16[128,1152]{1,0:T(8,128)(2,1)} %pad_maximum_fusion.2), channel_id=1, source_target_pairs={{0,2},{1,3},{2,0},{3,1},{4,6},{5,7},{6,4},{7,5},{8,10},{9,11},{10,... | collective-permute-start | bytes 884744 | tf_op jit(solution)/shard_map/ppermute | solution.py:26
  27.6 13.5 %collective-permute-start.11 = (bf16[128,1152]{1,0:T(8,128)(2,1)}, bf16[128,1152]{1,0:T(8,128)(2,1)S(1)}, u32[]{:S(2)}, u32[]{:S(2)}) collective-permute-start(bf16[128,1152]{1,0:T(8,128)(2,1)} %pad_maximum_fusion.2), channel_id=1, source_target_pairs={{0,3},{1,0},{2,1},{3,2},{4,7},{5,4},{6,5},{7,6},{8,11},{9,8},{10,9... | collective-permute-start | bytes 884744 | tf_op jit(solution)/shard_map/ppermute | solution.py:26
  33.1 1.8 %copy-start.5 = (bf16[256,1024]{1,0:T(8,128)(2,1)S(1)}, bf16[256,1024]{1,0:T(8,128)(2,1)}, u32[]{:S(2)}) copy-start(bf16[256,1024]{1,0:T(8,128)(2,1)} %param.18) | copy-start | bytes 1572868
  33.2 9.5 %collective-permute-start.4 = (bf16[256,256]{0,1:T(8,128)(2,1)S(1)}, bf16[256,256]{0,1:T(8,128)(2,1)S(1)}, u32[]{:S(2)}, u32[]{:S(2)}) collective-permute-start(bf16[256,256]{0,1:T(8,128)(2,1)S(1)} %get-tuple-element.37), channel_id=1, source_target_pairs={{0,1},{1,2},{2,3},{3,0},{4,5},{5,6},{6,7},{7,4},{8,9},{9,10},{10,1... | collective-permute-start | bytes 393224 | tf_op jit(solution)/shard_map/ppermute | solution.py:26
  33.7 1.5 copy-start.10
  34.1 10.3 %collective-permute-start.5 = (bf16[256,256]{0,1:T(8,128)(2,1)S(1)}, bf16[256,256]{0,1:T(8,128)(2,1)S(1)}, u32[]{:S(2)}, u32[]{:S(2)}) collective-permute-start(bf16[256,256]{0,1:T(8,128)(2,1)S(1)} %get-tuple-element.36), channel_id=1, source_target_pairs={{0,2},{1,3},{2,0},{3,1},{4,6},{5,7},{6,4},{7,5},{8,10},{9,11},{10,... | collective-permute-start | bytes 393224 | tf_op jit(solution)/shard_map/ppermute | solution.py:26
  35.3 10.5 %collective-permute-start.6 = (bf16[256,256]{0,1:T(8,128)(2,1)S(1)}, bf16[256,256]{0,1:T(8,128)(2,1)S(1)}, u32[]{:S(2)}, u32[]{:S(2)}) collective-permute-start(bf16[256,256]{0,1:T(8,128)(2,1)S(1)} %get-tuple-element.35), channel_id=1, source_target_pairs={{0,3},{1,0},{2,1},{3,2},{4,7},{5,4},{6,5},{7,6},{8,11},{9,8},{10,9... | collective-permute-start | bytes 393224 | tf_op jit(solution)/shard_map/ppermute | solution.py:26
  37.7 8.5 %collective-permute-start.8 = (bf16[128,1152]{1,0:T(8,128)(2,1)}, bf16[128,1152]{1,0:T(8,128)(2,1)S(1)}, u32[]{:S(2)}, u32[]{:S(2)}) collective-permute-start(bf16[128,1152]{1,0:T(8,128)(2,1)} %collective-permute-done.7), channel_id=1, source_target_pairs={{0,16},{16,0},{1,17},{17,1},{2,18},{18,2},{3,19},{19,3},{4,20},{20... | collective-permute-start | bytes 884744 | tf_op jit(solution)/shard_map/ppermute | solution.py:84
  41.1 5.0 %collective-permute-start.10 = (bf16[128,1152]{1,0:T(8,128)(2,1)S(1)}, bf16[128,1152]{1,0:T(8,128)(2,1)S(1)}, u32[]{:S(2)}, u32[]{:S(2)}) collective-permute-start(bf16[128,1152]{1,0:T(8,128)(2,1)S(1)} %collective-permute-done.9), channel_id=1, source_target_pairs={{0,16},{16,0},{1,17},{17,1},{2,18},{18,2},{3,19},{19,3},{4,20},{20... | collective-permute-start | bytes 884744 | tf_op jit(solution)/shard_map/ppermute | solution.py:84
  42.7 3.7 %copy-start.6 = (bf16[256,256]{0,1:T(8,128)(2,1)}, bf16[256,256]{0,1:T(8,128)(2,1)S(1)}, u32[]{:S(2)}) copy-start(bf16[256,256]{0,1:T(8,128)(2,1)S(1)} %collective-permute-done.4) | copy-start | bytes 393220
  42.7 3.4 %collective-permute-start.12 = (bf16[128,1152]{1,0:T(8,128)(2,1)S(1)}, bf16[128,1152]{1,0:T(8,128)(2,1)S(1)}, u32[]{:S(2)}, u32[]{:S(2)}) collective-permute-start(bf16[128,1152]{1,0:T(8,128)(2,1)S(1)} %collective-permute-done.11), channel_id=1, source_target_pairs={{0,16},{16,0},{1,17},{17,1},{2,18},{18,2},{3,19},{19,3},{4,20},{20... | collective-permute-start | bytes 884744 | tf_op jit(solution)/shard_map/ppermute | solution.py:84
  44.3 1.8 %copy-start.12 = (bf16[2048,128]{1,0:T(8,128)(2,1)S(1)}, bf16[2048,128]{1,0:T(8,128)(2,1)}, u32[]{:S(2)}) copy-start(bf16[2048,128]{1,0:T(8,128)(2,1)} %constant_dynamic-update-slice_fusion.7) | copy-start | bytes 1572868
  44.4 2.4 %copy-start.7 = (bf16[256,256]{0,1:T(8,128)(2,1)}, bf16[256,256]{0,1:T(8,128)(2,1)S(1)}, u32[]{:S(2)}) copy-start(bf16[256,256]{0,1:T(8,128)(2,1)S(1)} %collective-permute-done.5) | copy-start | bytes 393220
  45.8 1.3 copy-start.8
  46.4 2.1 %copy-start.13 = (bf16[2048,128]{1,0:T(8,128)(2,1)}, bf16[2048,128]{1,0:T(8,128)(2,1)S(1)}, u32[]{:S(2)}) copy-start(bf16[2048,128]{1,0:T(8,128)(2,1)S(1)} %constant_dynamic-update-slice_fusion) | copy-start | bytes 1572868
  50.6 13.4 %all-to-all-start = ((bf16[4,256,256]{2,1,0:T(8,128)(2,1)}), bf16[4,256,256]{2,1,0:T(8,128)(2,1)S(1)}, u32[]{:S(2)}, u32[]{:S(2)}) async-start(bf16[4,256,256]{2,1,0:T(8,128)(2,1)} %broadcast_in_dim.101), calls=%async_computation | async-start | bytes 1048576 | tf_op jit(solution)/shard_map/all_to_all | solution.py:133
  65.3 12.4 %copy-start.9 = (bf16[256,256]{0,1:T(8,128)(2,1)S(1)}, bf16[256,256]{0,1:T(8,128)(2,1)}, u32[]{:S(2)}) copy-start(bf16[256,256]{0,1:T(8,128)(2,1)} %copy-done.8) | copy-start | bytes 393220
  65.3 12.4 %copy-start.2 = (bf16[256,1024]{1,0:T(8,128)(2,1)S(1)}, bf16[256,1024]{1,0:T(8,128)(2,1)}, u32[]{:S(2)}) copy-start(bf16[256,1024]{1,0:T(8,128)(2,1)} %copy-done.1) | copy-start | bytes 1572868
  65.4 12.5 %collective-permute-start.13 = (bf16[384,256]{1,0:T(8,128)(2,1)S(1)}, bf16[384,256]{1,0:T(8,128)(2,1)S(1)}, u32[]{:S(2)}, u32[]{:S(2)}) collective-permute-start(bf16[384,256]{1,0:T(8,128)(2,1)S(1)} %get-tuple-element.17), channel_id=1, source_target_pairs={{0,16},{16,32},{32,48},{48,64},{64,80},{80,96},{96,112},{112,128},... | collective-permute-start | bytes 589832 | tf_op jit(solution)/shard_map/ppermute | solution.py:21
  70.4 7.5 %collective-permute-start.14 = (bf16[384,256]{1,0:T(8,128)(2,1)S(1)}, bf16[384,256]{1,0:T(8,128)(2,1)S(1)}, u32[]{:S(2)}, u32[]{:S(2)}) collective-permute-start(bf16[384,256]{1,0:T(8,128)(2,1)S(1)} %get-tuple-element.20), channel_id=1, source_target_pairs={{16,0},{32,16},{48,32},{64,48},{80,64},{96,80},{112,96},{128,112},... | collective-permute-start | bytes 589832 | tf_op jit(solution)/shard_map/ppermute | solution.py:21
  72.4 6.6 %collective-permute-start.15 = (bf16[384,256]{1,0:T(8,128)(2,1)S(1)}, bf16[384,256]{1,0:T(8,128)(2,1)S(1)}, u32[]{:S(2)}, u32[]{:S(2)}) collective-permute-start(bf16[384,256]{1,0:T(8,128)(2,1)S(1)} %get-tuple-element.19), channel_id=1, source_target_pairs={{0,4},{4,8},{8,12},{1,5},{5,9},{9,13},{2,6},{6,10},{10,14},{3,7},{... | collective-permute-start | bytes 589832 | tf_op jit(solution)/shard_map/ppermute | solution.py:21
  76.4 6.5 %collective-permute-start.16 = (bf16[384,256]{1,0:T(8,128)(2,1)S(1)}, bf16[384,256]{1,0:T(8,128)(2,1)S(1)}, u32[]{:S(2)}, u32[]{:S(2)}) collective-permute-start(bf16[384,256]{1,0:T(8,128)(2,1)S(1)} %get-tuple-element.18), channel_id=1, source_target_pairs={{4,0},{8,4},{12,8},{5,1},{9,5},{13,9},{6,2},{10,6},{14,10},{7,3},{... | collective-permute-start | bytes 589832 | tf_op jit(solution)/shard_map/ppermute | solution.py:21
  88.6 15.2 %copy-start.24 = (s32[256]{0:T(256)S(1)}, s32[256]{0:T(256)}, u32[]{:S(2)}) copy-start(s32[256]{0:T(256)} %slice_add_fusion.5) | copy-start | bytes 3076
  88.6 15.6 %copy-start.14 = (bf16[2048,128]{1,0:T(8,128)(2,1)S(1)}, bf16[2048,128]{1,0:T(8,128)(2,1)}, u32[]{:S(2)}) copy-start(bf16[2048,128]{1,0:T(8,128)(2,1)} %copy-done.13) | copy-start | bytes 1572868
  88.6 15.6 %copy-start.25 = (f32[256,1024]{1,0:T(8,128)S(1)}, f32[256,1024]{1,0:T(8,128)}, u32[]{:S(2)}) copy-start(f32[256,1024]{1,0:T(8,128)} %get-tuple-element.59) | copy-start | bytes 3145732
  88.6 14.9 %collective-permute-start.17 = (bf16[384,128]{1,0:T(8,128)(2,1)S(1)}, bf16[384,128]{1,0:T(8,128)(2,1)S(1)}, u32[]{:S(2)}, u32[]{:S(2)}) collective-permute-start(bf16[384,128]{1,0:T(8,128)(2,1)S(1)} %get-tuple-element.42), channel_id=1, source_target_pairs={{16,0},{32,16},{48,32},{64,48},{80,64},{96,80},{112,96},{128,112},... | collective-permute-start | bytes 294920 | tf_op jit(solution)/shard_map/ppermute | solution.py:21
  90.7 12.9 %collective-permute-start.18 = (bf16[384,128]{1,0:T(8,128)(2,1)S(1)}, bf16[384,128]{1,0:T(8,128)(2,1)S(1)}, u32[]{:S(2)}, u32[]{:S(2)}) collective-permute-start(bf16[384,128]{1,0:T(8,128)(2,1)S(1)} %get-tuple-element.45), channel_id=1, source_target_pairs={{0,16},{16,32},{32,48},{48,64},{64,80},{80,96},{96,112},{112,128},... | collective-permute-start | bytes 294920 | tf_op jit(solution)/shard_map/ppermute | solution.py:21
  96.8 6.7 %collective-permute-start.19 = (bf16[384,128]{1,0:T(8,128)(2,1)S(1)}, bf16[384,128]{1,0:T(8,128)(2,1)S(1)}, u32[]{:S(2)}, u32[]{:S(2)}) collective-permute-start(bf16[384,128]{1,0:T(8,128)(2,1)S(1)} %get-tuple-element.44), channel_id=1, source_target_pairs={{4,0},{8,4},{12,8},{5,1},{9,5},{13,9},{6,2},{10,6},{14,10},{7,3},{... | collective-permute-start | bytes 294920 | tf_op jit(solution)/shard_map/ppermute | solution.py:21
  98.1 5.6 %collective-permute-start.20 = (bf16[384,128]{1,0:T(8,128)(2,1)S(1)}, bf16[384,128]{1,0:T(8,128)(2,1)S(1)}, u32[]{:S(2)}, u32[]{:S(2)}) collective-permute-start(bf16[384,128]{1,0:T(8,128)(2,1)S(1)} %get-tuple-element.43), channel_id=1, source_target_pairs={{0,4},{4,8},{8,12},{1,5},{5,9},{9,13},{2,6},{6,10},{10,14},{3,7},{... | collective-permute-start | bytes 294920 | tf_op jit(solution)/shard_map/ppermute | solution.py:21
  104.2 0.9 copy-start.17
  105.9 2.9 %collective-permute-start.21 = (bf16[512,1152]{1,0:T(8,128)(2,1)S(1)}, bf16[512,1152]{1,0:T(8,128)(2,1)S(1)}, u32[]{:S(2)}, u32[]{:S(2)}) collective-permute-start(bf16[512,1152]{1,0:T(8,128)(2,1)S(1)} %pad_maximum_fusion), channel_id=1, source_target_pairs={{0,16},{16,0},{1,17},{17,1},{2,18},{18,2},{3,19},{19,3},{4,20},{20... | collective-permute-start | bytes 3538952 | tf_op jit(solution)/shard_map/ppermute | solution.py:173
  109.3 8.7 %collective-permute-start.22 = (bf16[128,1152]{1,0:T(8,128)(2,1)S(1)}, bf16[128,1152]{1,0:T(8,128)(2,1)S(1)}, u32[]{:S(2)}, u32[]{:S(2)}) collective-permute-start(bf16[128,1152]{1,0:T(8,128)(2,1)S(1)} %get-tuple-element.8), channel_id=1, source_target_pairs={{0,3},{1,0},{2,1},{3,2},{4,7},{5,4},{6,5},{7,6},{8,11},{9,8},{10,9... | collective-permute-start | bytes 884744 | tf_op jit(solution)/shard_map/ppermute | solution.py:26
  110.5 9.7 %collective-permute-start.23 = (bf16[128,1152]{1,0:T(8,128)(2,1)S(1)}, bf16[128,1152]{1,0:T(8,128)(2,1)S(1)}, u32[]{:S(2)}, u32[]{:S(2)}) collective-permute-start(bf16[128,1152]{1,0:T(8,128)(2,1)S(1)} %get-tuple-element.10), channel_id=1, source_target_pairs={{0,2},{1,3},{2,0},{3,1},{4,6},{5,7},{6,4},{7,5},{8,10},{9,11},{10,... | collective-permute-start | bytes 884744 | tf_op jit(solution)/shard_map/ppermute | solution.py:26
  111.7 15.6 %collective-permute-start.24 = (bf16[128,1152]{1,0:T(8,128)(2,1)S(1)}, bf16[128,1152]{1,0:T(8,128)(2,1)S(1)}, u32[]{:S(2)}, u32[]{:S(2)}) collective-permute-start(bf16[128,1152]{1,0:T(8,128)(2,1)S(1)} %get-tuple-element.9), channel_id=1, source_target_pairs={{0,1},{1,2},{2,3},{3,0},{4,5},{5,6},{6,7},{7,4},{8,9},{9,10},{10,1... | collective-permute-start | bytes 884744 | tf_op jit(solution)/shard_map/ppermute | solution.py:26
  166.0 4.9 %collective-permute-start.25 = (bf16[128,1152]{1,0:T(8,128)(2,1)S(1)}, bf16[128,1152]{1,0:T(8,128)(2,1)S(1)}, u32[]{:S(2)}, u32[]{:S(2)}) collective-permute-start(bf16[128,1152]{1,0:T(8,128)(2,1)S(1)} %reshape.212), channel_id=1, source_target_pairs={{0,16},{16,0},{1,17},{17,1},{2,18},{18,2},{3,19},{19,3},{4,20},{20... | collective-permute-start | bytes 884744 | tf_op jit(solution)/shard_map/ppermute | solution.py:184
  (5 other events, 3.9 us)

commit v3 on v2

--- a/solution.py
+++ b/solution.py
@@ -39,9 +39,8 @@
 
 
 def two_parts(values):
-    high = values.astype(BF)
-    low = (values - high.astype(F32)).astype(BF)
-    return jnp.concatenate([high, low], axis=1)
+    high = lax.reduce_precision(values, 8, 7)
+    return jnp.concatenate([high.astype(BF), (values - high).astype(BF)], axis=1)
 
 
 def local(
@@ -61,7 +60,6 @@
     n_af = lax.axis_size("af")
     n_plane = lax.axis_size("z") * lax.axis_size("gy")
     nodes = features.shape[0]
-    own = nodes // n_af
     slots = send_rows.shape[1]
     hid = w_hidden.shape[1]
     classes = w_classes.shape[1]
@@ -91,8 +89,7 @@
     pick_send = (send_at[:, None] == node_ids[None, :]).astype(BF)
     pick_recv = (recv_at[:, None] == node_ids[None, :]).astype(BF)
     put_recv = (node_ids[:, None] == recv_at[None, :]).astype(BF)
-    own_ids = node_ids[:own] + af * own
-    put_send = (own_ids[:, None] == send_at[None, :]).astype(BF)
+    put_send = (node_ids[:, None] == send_at[None, :]).astype(BF)
 
     block_ids = jnp.arange(blocks, dtype=jnp.int32)
     dense = jnp.zeros((blocks, tb, blocks, tb), BF)
@@ -108,14 +105,16 @@
     mixed = (dot(dense, features) + spread[:, :width] + spread[:, width:]).astype(BF)
     mixed = jnp.where(core == 0, mixed, jnp.roll(mixed, half, axis=1))
 
-    def rows_for(k):
-        return lax.dynamic_slice_in_dim(mixed, ((af + k) % n_af) * own, own, axis=0)
+    top = nodes // 2
+    below = turn(mixed, "af", 1)
+    above = turn(mixed, "af", -1)
+    across = [turn(below[:top], "af", 1), turn(above[top:], "af", -1)]
 
-    mixed_from = [rows_for(0)] + [turn(rows_for(k), "af", k) for k in range(1, n_af)]
-    pre_act = sum(
-        dot(m[:, :half], w[:, :hid]) + dot(m[:, half:], v[:, :hid])
-        for m, w, v in zip(mixed_from, w_mine, w_other)
-    )
+    def product(rows, k):
+        return dot(rows[:, :half], w_mine[k][:, :hid]) + dot(rows[:, half:], w_other[k][:, :hid])
+
+    pre_act = product(mixed, 0) + product(below, 1) + product(above, 3)
+    pre_act = pre_act + jnp.concatenate([product(rows, 2) for rows in across], axis=0)
     sigmoid_act = jax.nn.sigmoid(pre_act)
     hidden = (pre_act * sigmoid_act).astype(BF)
     slope = sigmoid_act * (1.0 + pre_act * (1.0 - sigmoid_act))
@@ -129,14 +128,10 @@
         jnp.concatenate(around + around, axis=0), (n_af - af) * w_rows, n_af * w_rows, axis=0
     )
 
-    z_own = two_parts(dot(hidden, w_cls))
-    z_all = lax.all_to_all(
-        jnp.broadcast_to(z_own[None], (n_af,) + z_own.shape), "af", 0, 0, tiled=True
-    ).reshape(nodes, 2 * classes)
-    out = dot(pick_send, z_all).astype(BF).reshape(4, slots, -1)
-    arrived = trade(out, 1).astype(F32)
-    arrived = (arrived[:, :classes] + arrived[:, classes:]) * weight
-    spread = dot(put_recv, two_parts(arrived)) + dot(dense, z_all)
+    z_pair = two_parts(dot(hidden, w_cls))
+    out = dot(pick_send, z_pair[:, :classes]).astype(BF).reshape(4, slots, -1)
+    arrived = trade(out, 1).astype(F32) * weight
+    spread = dot(put_recv, two_parts(arrived)) + dot(dense, z_pair)
     logits = spread[:, :classes] + spread[:, classes:]
 
     exponent = jnp.exp(logits - jnp.max(logits, axis=1, keepdims=True))
@@ -146,35 +141,18 @@
 
     back = (dot(pick_recv, grad_logits) * weight).astype(BF).reshape(4, slots, -1)
     returned = trade(back, -1)
-    dense_own = lax.dynamic_slice_in_dim(dense, af * own, own, axis=1)
-    grad_own = (dot(dense_own, grad_logits, 0, 0) + dot(put_send, returned)).astype(BF)
-    grad_pre = (dot(grad_own, w_cls, 1, 1) * slope).astype(BF)
-
-    def columns(start):
-        return jnp.concatenate([m[:, start : start + half] for m in mixed_from], axis=1)
-
-    def hidden_columns(which):
-        return jnp.concatenate(
-            [
-                lax.dynamic_slice_in_dim(
-                    hidden, ((af - k) % n_af) * w_rows + which * half, half, axis=1
-                )
-                for k in range(n_af)
-            ],
-            axis=1,
-        )
+    grad_mix = (dot(dense, grad_logits, 0, 0) + dot(put_send, returned)).astype(BF)
+    grad_pre = (dot(grad_mix, w_cls, 1, 1) * slope).astype(BF)
 
     def terms(start, which):
+        units = lax.dynamic_slice_in_dim(hidden, af * w_rows + which * half, half, axis=1)
         return jnp.concatenate(
-            [dot(columns(start), grad_pre, 0, 0), dot(hidden_columns(which), grad_own, 0, 0)],
+            [dot(mixed[:, start : start + half], grad_pre, 0, 0), dot(units, grad_mix, 0, 0)],
             axis=1,
         )
 
     theirs = lax.ppermute(terms(half, 1 - core).astype(BF), "core", swap)
-    pair_sum = (terms(0, core) + theirs.astype(F32)).reshape(n_af, half, hid + classes)
-    total = pair_sum[0]
-    for k in range(1, n_af):
-        total = total + turn(pair_sum[k].astype(BF), "af", -k).astype(F32)
+    total = terms(0, core) + theirs.astype(F32)
     pieces = total.astype(BF).reshape(n_plane, half // n_plane, hid + classes)
     pieces = lax.all_to_all(pieces, PLANE, 0, 0, tiled=True)
     piece = jnp.sum(pieces.astype(F32), axis=0).astype(BF)

time: 174 us -> 164 us (0.943)
  matrix products: 17.8 us -> 35.4 us
  waiting for transfers between devices: 36.3 us -> 21.5 us
  local copies, waits for them, and re-layouts: 13.3 us -> 5.86 us
  starting transfers between devices: 56.5 us -> 50.5 us
  blocking collectives: 38.2 us -> 41.6 us
  other arithmetic: 9.28 us -> 6.33 us
    dot_general x23 -> x25, matrix products: 17.8 us -> 35.4 us  [dot(): lax.dot_general(lhs, rhs, (((lhs_dim,), (rhs_dim,)), ((), ())), preferred...]
    ppermute x9 -> x7, waiting for transfers between devices: 21.6 us -> 12.2 us  [turn(): lax.ppermute(field, axis, [(i, (i + move) % count) for i in range(count)])]
    all_to_all x1 -> x0, waiting for transfers between devices: 6.24 us -> none  [local(): lax.all_to_all(jnp.broadcast_to(z_own[None], (n_af,) + z_own.shape), 'af'...]
    all_to_all x1 -> x0, starting transfers between devices: 4.19 us -> none  [local(): lax.all_to_all(jnp.broadcast_to(z_own[None], (n_af,) + z_own.shape), 'af'...]
    all_to_all x1, blocking collectives: 22.8 us -> 26.3 us  [local(): pieces = lax.all_to_all(pieces, PLANE, 0, 0, tiled=True)]
    slice x5 -> x2, local copies, waits for them, and re-layouts: 3.09 us -> 0.04 us  [local(): across = [turn(below[:top], 'af', 1), turn(above[top:], 'af', -1)]]
    unnamed x53 -> x38, local copies, waits for them, and re-layouts: 4.38 us -> 1.87 us
    ppermute x9 -> x7, starting transfers between devices: 10.4 us -> 9.88 us  [turn(): lax.ppermute(field, axis, [(i, (i + move) % count) for i in range(count)])]
  transfers between devices with their start and end apart: 27 -> 24, of which waited for: 12 -> 9; matrix products, arithmetic and copies ran while one was open for 12% -> 12% of each run, Pallas kernels for 0% -> 0%
where the time goes in v3:
time: 164 us; the launch traced here: 163 us
  starting transfers between devices  50.5 us (31%)
  blocking collectives  41.6 us (25%)
  matrix products  35.4 us (22%)
  waiting for transfers between devices  21.5 us (13%)
  other arithmetic  6.33 us (4%)
  local copies, waits for them, and re-layouts  5.86 us (4%)
    ppermute x12, starting transfers between devices, step(): return lax.ppermute(field, axis, pairs)  36 us
    dot_general x25, matrix products, dot(): lax.dot_general(lhs, rhs, (((lhs_dim,), (rhs_dim,)), ((), ())), preferred...  35.4 us
    all_to_all x1, blocking collectives, local(): pieces = lax.all_to_all(pieces, PLANE, 0, 0, tiled=True)  26.3 us
    all_to_all x1, blocking collectives, local(): lax.all_to_all(jnp.broadcast_to(piece[None], (n_plane,) + piece.shape), P...  15.2 us
    ppermute x7, waiting for transfers between devices, turn(): lax.ppermute(field, axis, [(i, (i + move) % count) for i in range(count)])  12.2 us
    ppermute x7, starting transfers between devices, turn(): lax.ppermute(field, axis, [(i, (i + move) % count) for i in range(count)])  9.88 us
    ppermute x12, waiting for transfers between devices, step(): return lax.ppermute(field, axis, pairs)  6.81 us
    ppermute x1, starting transfers between devices, local(): other = lax.ppermute(mine, 'core', swap)  3.69 us
  transfers between devices with their start and end apart: 24, of which 9 were waited for; matrix products, arithmetic and copies ran while one was open for 12% of the time, Pallas kernels for 0%

profile of v3, /device:TPU:1, one launch (start us, length us, event | category | flops | bytes accessed | tf_op | source)
XLA Modules:
  0.0 162.6 jit_solution(3613882195151854894)
XLA Ops:
  0.7 1.0 copy-done
  1.7 0.8 constant_dynamic-slice_fusion
  3.2 3.7 %collective-permute-start.11 = (bf16[128,1152]{1,0:T(8,128)(2,1)}, bf16[128,1152]{1,0:T(8,128)(2,1)}, u32[]{:S(2)}, u32[]{:S(2)}) collective-permute-start(bf16[128,1152]{1,0:T(8,128)(2,1)} %pad_maximum_fusion.2), channel_id=1, source_target_pairs={{0,2},{1,3},{2,0},{3,1},{4,6},{5,7},{6,4},{7,5},{8,10},{9,11},{10,... | collective-permute-start | bytes 884744 | tf_op jit(solution)/shard_map/ppermute | solution.py:26
  7.0 0.8 fusion.87
  7.7 2.3 %fusion.12 = bf16[1536,256]{1,0:T(8,128)(2,1)S(1)} fusion(bf16[1024,256]{1,0:T(8,128)(2,1)} %param.10, s32[1536]{0:T(1024)S(1)} %eq.179), kind=kOutput, calls=%fused_computation.20 | convolution fusion | flops 807272448 | bytes 1316864 | tf_op jit(solution)/shard_map/dot_general | solution.py:15
  10.1 0.8 fusion.98
  10.9 4.4 %collective-permute-start = (bf16[384,256]{1,0:T(8,128)(2,1)}, bf16[384,256]{1,0:T(8,128)(2,1)S(1)}, u32[]{:S(2)}, u32[]{:S(2)}) collective-permute-start(bf16[384,256]{1,0:T(8,128)(2,1)} %get-tuple-element.8), channel_id=1, source_target_pairs={{0,16},{16,32},{32,48},{48,64},{64,80},{80,96},{96,112},{112,128},... | collective-permute-start | bytes 589832 | tf_op jit(solution)/shard_map/ppermute | solution.py:21
  15.3 1.3 collective-permute-start.3
  16.6 4.7 %collective-permute-start.2 = (bf16[384,256]{1,0:T(8,128)(2,1)}, bf16[384,256]{1,0:T(8,128)(2,1)}, u32[]{:S(2)}, u32[]{:S(2)}) collective-permute-start(bf16[384,256]{1,0:T(8,128)(2,1)} %get-tuple-element.10), channel_id=1, source_target_pairs={{0,4},{4,8},{8,12},{1,5},{5,9},{9,13},{2,6},{6,10},{10,14},{3,7},{... | collective-permute-start | bytes 589832 | tf_op jit(solution)/shard_map/ppermute | solution.py:21
  21.3 1.9 %collective-permute-start.1 = (bf16[384,256]{1,0:T(8,128)(2,1)S(1)}, bf16[384,256]{1,0:T(8,128)(2,1)}, u32[]{:S(2)}, u32[]{:S(2)}) collective-permute-start(bf16[384,256]{1,0:T(8,128)(2,1)S(1)} %get-tuple-element.11), channel_id=1, source_target_pairs={{16,0},{32,16},{48,32},{64,48},{80,64},{96,80},{112,96},{128,112},... | collective-permute-start | bytes 589832 | tf_op jit(solution)/shard_map/ppermute | solution.py:21
  23.5 1.2 select_select_fusion
  24.8 0.9 collective-permute-start.8
  26.3 2.2 %collective-permute-done.1 = bf16[384,256]{1,0:T(8,128)(2,1)} collective-permute-done((bf16[384,256]{1,0:T(8,128)(2,1)S(1)}, bf16[384,256]{1,0:T(8,128)(2,1)}, u32[]{:S(2)}, u32[]{:S(2)}) %collective-permute-start.1) | collective-permute-done | bytes 196640 | tf_op jit(solution)/shard_map/ppermute | solution.py:21
  28.6 1.4 reduce-precision_convert_fusion
  30.0 1.9 %fusion.3 = f32[1024,512]{0,1:T(8,128)S(1)} fusion(s32[1536]{0:T(1024)S(1)} %eq.176, bf16[1536,256]{1,0:T(8,128)(2,1)S(1)} %get-tuple-element.7, bf16[1536,256]{1,0:T(8,128)(2,1)S(1)} %get-tuple-element.6), kind=kOutput, calls=%fused_computation.7 | convolution fusion | flops 1615331328 | bytes 3676160 | tf_op jit(solution)/shard_map/dot_general | solution.py:15
  33.0 0.9 collective-permute-start.7
  38.2 5.6 %collective-permute-done.7 = bf16[1024,256]{0,1:T(8,128)(2,1)S(1)} collective-permute-done((bf16[1024,256]{0,1:T(8,128)(2,1)S(1)}, bf16[1024,256]{0,1:T(8,128)(2,1)S(1)}, u32[]{:S(2)}, u32[]{:S(2)}) %collective-permute-start.7) | collective-permute-done | bytes 524320 | tf_op jit(solution)/shard_map/ppermute | solution.py:26
  43.8 3.0 %collective-permute-start.13 = (bf16[512,256]{0,1:T(8,128)(2,1)S(1)}, bf16[512,256]{0,1:T(8,128)(2,1)S(1)}, u32[]{:S(2)}, u32[]{:S(2)}) collective-permute-start(bf16[512,256]{0,1:T(8,128)(2,1)S(1)} %slice.249), channel_id=1, source_target_pairs={{0,3},{1,0},{2,1},{3,2},{4,7},{5,4},{6,5},{7,6},{8,11},{9,8},{10,9... | collective-permute-start | bytes 786440 | tf_op jit(solution)/shard_map/ppermute | solution.py:26
  49.3 6.4 %collective-permute-done.10 = bf16[512,256]{0,1:T(8,128)(2,1)S(1)} collective-permute-done((bf16[512,256]{0,1:T(8,128)(2,1)S(1)}, bf16[512,256]{0,1:T(8,128)(2,1)S(1)}, u32[]{:S(2)}, u32[]{:S(2)}) %collective-permute-start.10) | collective-permute-done | bytes 262176 | tf_op jit(solution)/shard_map/ppermute | solution.py:26
  55.7 1.4 fusion.72
  57.1 1.9 %convolution_add_fusion.1 = f32[512,1024]{1,0:T(8,128)} fusion(f32[512,1024]{1,0:T(8,128)S(1)} %fusion.72, bf16[128,1152]{1,0:T(8,128)(2,1)S(1)} %collective-permute-done.12, bf16[512,256]{0,1:T(8,128)(2,1)S(1)} %collective-permute-done.10), kind=kOutput, calls=%fused_computation.34 | convolution fusion | flops 134742016 | bytes 4587520 | tf_op jit(solution)/shard_map/dot_general | solution.py:15
  59.0 1.4 fusion.70
  60.4 1.9 %convolution_add_fusion = f32[512,1024]{1,0:T(8,128)} fusion(f32[512,1024]{1,0:T(8,128)S(1)} %fusion.70, bf16[128,1152]{1,0:T(8,128)(2,1)S(1)} %collective-permute-done.12, bf16[512,256]{0,1:T(8,128)(2,1)S(1)} %collective-permute-done.13), kind=kOutput, calls=%fused_computation.33 | convolution fusion | flops 134742016 | bytes 4587520 | tf_op jit(solution)/shard_map/dot_general | solution.py:15
  62.3 5.6 %multiply_convert_fusion.1 = (bf16[1024,1024]{1,0:T(8,128)(2,1)}, f32[1024,1024]{1,0:T(8,128)}) fusion(f32[512,1024]{1,0:T(8,128)} %convolution_add_fusion, f32[512,1024]{1,0:T(8,128)} %convolution_add_fusion.1, f32[1024,1024]{1,0:T(8,128)S(1)} %fusion.54, bf16[128,1152]{1,0:T(8,128)(2,1)S(1)} %copy-done.7, ...), kind=kOutput, calls=%fused_computation.12 | convolution fusion | flops 281018368 | bytes 31981568 | tf_op jit(solution)/shard_map/dot_general | solution.py:15
  67.9 2.4 %fusion.40 = (bf16[1024,128]{0,1:T(8,128)(2,1)S(1)}, bf16[1024,128]{0,1:T(8,128)(2,1)S(1)}) fusion(bf16[1024,1024]{1,0:T(8,128)(2,1)} %get-tuple-element.34, bf16[2048,128]{1,0:T(8,128)(2,1)} %copy-done.10, s32[]{:T(128)S(6)} %select_n.100), kind=kOutput, calls=%fused_computation.64 | convolution fusion | flops 268959744 | bytes 2883588 | tf_op jit(solution)/shard_map/dot_general | solution.py:15
  70.3 1.2 fusion.15
  71.6 6.2 %collective-permute-start.14 = (bf16[384,128]{1,0:T(8,128)(2,1)S(1)}, bf16[384,128]{1,0:T(8,128)(2,1)S(1)}, u32[]{:S(2)}, u32[]{:S(2)}) collective-permute-start(bf16[384,128]{1,0:T(8,128)(2,1)S(1)} %get-tuple-element.24), channel_id=1, source_target_pairs={{0,16},{16,32},{32,48},{48,64},{64,80},{80,96},{96,112},{112,128},... | collective-permute-start | bytes 294920 | tf_op jit(solution)/shard_map/ppermute | solution.py:21
  77.8 1.3 collective-permute-start.17
  79.1 4.0 %collective-permute-start.16 = (bf16[384,128]{1,0:T(8,128)(2,1)S(1)}, bf16[384,128]{1,0:T(8,128)(2,1)S(1)}, u32[]{:S(2)}, u32[]{:S(2)}) collective-permute-start(bf16[384,128]{1,0:T(8,128)(2,1)S(1)} %get-tuple-element.26), channel_id=1, source_target_pairs={{0,4},{4,8},{8,12},{1,5},{5,9},{9,13},{2,6},{6,10},{10,14},{3,7},{... | collective-permute-start | bytes 294920 | tf_op jit(solution)/shard_map/ppermute | solution.py:21
  83.1 2.1 %collective-permute-start.15 = (bf16[384,128]{1,0:T(8,128)(2,1)S(1)}, bf16[384,128]{1,0:T(8,128)(2,1)S(1)}, u32[]{:S(2)}, u32[]{:S(2)}) collective-permute-start(bf16[384,128]{1,0:T(8,128)(2,1)S(1)} %get-tuple-element.27), channel_id=1, source_target_pairs={{16,0},{32,16},{48,32},{64,48},{80,64},{96,80},{112,96},{128,112},... | collective-permute-start | bytes 294920 | tf_op jit(solution)/shard_map/ppermute | solution.py:21
  85.3 3.8 %collective-permute-done.15 = bf16[384,128]{1,0:T(8,128)(2,1)S(1)} collective-permute-done((bf16[384,128]{1,0:T(8,128)(2,1)S(1)}, bf16[384,128]{1,0:T(8,128)(2,1)S(1)}, u32[]{:S(2)}, u32[]{:S(2)}) %collective-permute-start.15) | collective-permute-done | bytes 98336 | tf_op jit(solution)/shard_map/ppermute | solution.py:21
  89.4 1.5 fusion.2
  92.6 1.7 %fusion.14 = bf16[1536,128]{1,0:T(8,128)(2,1)S(1)} fusion(bf16[1024,128]{0,1:T(8,128)(2,1)S(1)} %multiply_convert_fusion.2, s32[1536]{0:T(1024)S(1)} %copy-done.13, f32[1536]{0:T(1024)S(1)} %mul.53), kind=kOutput, calls=%fused_computation.22 | convolution fusion | flops 404619264 | bytes 667648 | tf_op jit(solution)/shard_map/dot_general | solution.py:15
  94.3 1.9 %collective-permute-start.18 = (bf16[384,128]{1,0:T(8,128)(2,1)S(1)}, bf16[384,128]{1,0:T(8,128)(2,1)S(1)}, u32[]{:S(2)}, u32[]{:S(2)}) collective-permute-start(bf16[384,128]{1,0:T(8,128)(2,1)S(1)} %get-tuple-element.20), channel_id=1, source_target_pairs={{16,0},{32,16},{48,32},{64,48},{80,64},{96,80},{112,96},{128,112},... | collective-permute-start | bytes 294920 | tf_op jit(solution)/shard_map/ppermute | solution.py:21
  96.2 2.9 %collective-permute-start.21 = (bf16[384,128]{1,0:T(8,128)(2,1)S(1)}, bf16[384,128]{1,0:T(8,128)(2,1)S(1)}, u32[]{:S(2)}, u32[]{:S(2)}) collective-permute-start(bf16[384,128]{1,0:T(8,128)(2,1)S(1)} %get-tuple-element.21), channel_id=1, source_target_pairs={{0,4},{4,8},{8,12},{1,5},{5,9},{9,13},{2,6},{6,10},{10,14},{3,7},{... | collective-permute-start | bytes 294920 | tf_op jit(solution)/shard_map/ppermute | solution.py:21
  99.1 1.3 collective-permute-start.20
  100.4 3.9 %collective-permute-start.19 = (bf16[384,128]{1,0:T(8,128)(2,1)S(1)}, bf16[384,128]{1,0:T(8,128)(2,1)S(1)}, u32[]{:S(2)}, u32[]{:S(2)}) collective-permute-start(bf16[384,128]{1,0:T(8,128)(2,1)S(1)} %get-tuple-element.23), channel_id=1, source_target_pairs={{0,16},{16,32},{32,48},{48,64},{64,80},{80,96},{96,112},{112,128},... | collective-permute-start | bytes 294920 | tf_op jit(solution)/shard_map/ppermute | solution.py:21
  105.2 0.8 collective-permute-done.19
  106.0 1.2 fusion.33
  107.4 1.7 %multiply_convert_fusion = bf16[1024,1024]{1,0:T(8,128)(2,1)S(1)} fusion(f32[1024,1024]{1,0:T(8,128)S(1)} %copy-done.2, bf16[1024,128]{1,0:T(8,128)(2,1)S(1)} %fusion.33, bf16[2048,128]{1,0:T(8,128)(2,1)S(1)} %copy-done.11, s32[]{:T(128)S(6)} %select_n.100), kind=kOutput, calls=%fused_computation.11 | convolution fusion | flops 277872640 | bytes 6815748 | tf_op jit(solution)/shard_map/dot_general | solution.py:15
  109.1 1.2 convolution_convert_fusion.1
  110.4 1.2 fusion.64
  112.6 1.1 collective-permute-done.22
  113.9 26.3 %all_to_all.10 = bf16[32,4,1152]{2,1,0:T(4,128)(2,1)S(1)} all-to-all(bf16[32,4,1152]{2,1,0:T(4,128)(2,1)S(1)} %reshape.168), channel_id=1, replica_groups=mesh['z'=8,'core'=2,'gy'=4,'af'=4] {'z','gy'}, dimensions={0} | all-to-all | bytes 589824 | tf_op jit(solution)/shard_map/all_to_all | solution.py:157
  140.4 15.2 %all_to_all.11 = bf16[32,4,1152]{2,1,0:T(4,128)(2,1)S(1)} all-to-all(bf16[32,4,1152]{2,1,0:T(4,128)(2,1)S(1)} %broadcast_in_dim.95), channel_id=1, replica_groups=mesh['z'=8,'core'=2,'gy'=4,'af'=4] {'z','gy'}, dimensions={0} | all-to-all | bytes 589824 | tf_op jit(solution)/shard_map/all_to_all | solution.py:159
  155.7 3.7 %collective-permute-start.23 = (bf16[128,1152]{1,0:T(8,128)(2,1)S(1)}, bf16[128,1152]{1,0:T(8,128)(2,1)S(1)}, u32[]{:S(2)}, u32[]{:S(2)}) collective-permute-start(bf16[128,1152]{1,0:T(8,128)(2,1)S(1)} %reshape.169), channel_id=1, source_target_pairs={{0,16},{16,0},{1,17},{17,1},{2,18},{18,2},{3,19},{19,3},{4,20},{20... | collective-permute-start | bytes 884744 | tf_op jit(solution)/shard_map/ppermute | solution.py:162
  159.4 1.2 collective-permute-done.23
  161.5 1.1 slice.268
  (113 shorter events, 14.7 us)
Async XLA Ops:
  0.6 1.1 copy-start
  2.5 22.2 %copy-start.8 = (bf16[128,128]{1,0:T(8,128)(2,1)}, bf16[128,128]{1,0:T(8,128)(2,1)S(1)}, u32[]{:S(2)}) copy-start(bf16[128,128]{1,0:T(8,128)(2,1)S(1)} %get-tuple-element.28) | copy-start | bytes 98308
  3.2 32.0 %collective-permute-start.11 = (bf16[128,1152]{1,0:T(8,128)(2,1)}, bf16[128,1152]{1,0:T(8,128)(2,1)}, u32[]{:S(2)}, u32[]{:S(2)}) collective-permute-start(bf16[128,1152]{1,0:T(8,128)(2,1)} %pad_maximum_fusion.2), channel_id=1, source_target_pairs={{0,2},{1,3},{2,0},{3,1},{4,6},{5,7},{6,4},{7,5},{8,10},{9,11},{10,... | collective-permute-start | bytes 884744 | tf_op jit(solution)/shard_map/ppermute | solution.py:26
  7.7 15.5 %copy-start.17 = (s32[8,4]{0,1:T(4,128)S(1)}, s32[8,4]{0,1:T(4,128)}, u32[]{:S(2)}) copy-start(s32[8,4]{0,1:T(4,128)} %param.12) | copy-start | bytes 388
  10.1 13.2 %copy-start.5 = (bf16[8,4,128,128]{3,2,1,0:T(8,128)(2,1)S(1)}, bf16[8,4,128,128]{3,2,1,0:T(8,128)(2,1)}, u32[]{:S(2)}) copy-start(bf16[8,4,128,128]{3,2,1,0:T(8,128)(2,1)} %param.11) | copy-start | bytes 3145732
  10.9 13.9 %collective-permute-start = (bf16[384,256]{1,0:T(8,128)(2,1)}, bf16[384,256]{1,0:T(8,128)(2,1)S(1)}, u32[]{:S(2)}, u32[]{:S(2)}) collective-permute-start(bf16[384,256]{1,0:T(8,128)(2,1)} %get-tuple-element.8), channel_id=1, source_target_pairs={{0,16},{16,32},{32,48},{48,64},{64,80},{80,96},{96,112},{112,128},... | collective-permute-start | bytes 589832 | tf_op jit(solution)/shard_map/ppermute | solution.py:21
  15.3 10.3 %collective-permute-start.3 = (bf16[384,256]{1,0:T(8,128)(2,1)}, bf16[384,256]{1,0:T(8,128)(2,1)}, u32[]{:S(2)}, u32[]{:S(2)}) collective-permute-start(bf16[384,256]{1,0:T(8,128)(2,1)} %get-tuple-element.9), channel_id=1, source_target_pairs={{4,0},{8,4},{12,8},{5,1},{9,5},{13,9},{6,2},{10,6},{14,10},{7,3},{... | collective-permute-start | bytes 589832 | tf_op jit(solution)/shard_map/ppermute | solution.py:21
  16.6 9.7 %collective-permute-start.2 = (bf16[384,256]{1,0:T(8,128)(2,1)}, bf16[384,256]{1,0:T(8,128)(2,1)}, u32[]{:S(2)}, u32[]{:S(2)}) collective-permute-start(bf16[384,256]{1,0:T(8,128)(2,1)} %get-tuple-element.10), channel_id=1, source_target_pairs={{0,4},{4,8},{8,12},{1,5},{5,9},{9,13},{2,6},{6,10},{10,14},{3,7},{... | collective-permute-start | bytes 589832 | tf_op jit(solution)/shard_map/ppermute | solution.py:21
  21.3 7.3 %collective-permute-start.1 = (bf16[384,256]{1,0:T(8,128)(2,1)S(1)}, bf16[384,256]{1,0:T(8,128)(2,1)}, u32[]{:S(2)}, u32[]{:S(2)}) collective-permute-start(bf16[384,256]{1,0:T(8,128)(2,1)S(1)} %get-tuple-element.11), channel_id=1, source_target_pairs={{16,0},{32,16},{48,32},{64,48},{80,64},{96,80},{112,96},{128,112},... | collective-permute-start | bytes 589832 | tf_op jit(solution)/shard_map/ppermute | solution.py:21
  23.3 1.4 copy-start.14
  23.3 1.4 copy-start.15
  24.6 7.3 %copy-start.3 = (bf16[8,128,8,128]{3,2,1,0:T(8,128)(2,1)}, bf16[8,128,8,128]{3,2,1,0:T(8,128)(2,1)S(1)}, u32[]{:S(2)}) copy-start(bf16[8,128,8,128]{3,2,1,0:T(8,128)(2,1)S(1)} %select_select_fusion) | copy-start | bytes 6291460
  24.7 7.3 %copy-start.12 = (s32[1536]{0:T(1024)}, s32[1536]{0:T(1024)S(1)}, u32[]{:S(2)}) copy-start(s32[1536]{0:T(1024)S(1)} %eq.176) | copy-start | bytes 18436
  24.8 10.6 %collective-permute-start.8 = (bf16[128,1152]{1,0:T(8,128)(2,1)}, bf16[128,1152]{1,0:T(8,128)(2,1)S(1)}, u32[]{:S(2)}, u32[]{:S(2)}) collective-permute-start(bf16[128,1152]{1,0:T(8,128)(2,1)} %pad_maximum_fusion.2), channel_id=1, source_target_pairs={{0,3},{1,0},{2,1},{3,2},{4,7},{5,4},{6,5},{7,6},{8,11},{9,8},{10,9... | collective-permute-start | bytes 884744 | tf_op jit(solution)/shard_map/ppermute | solution.py:26
  25.6 10.3 %collective-permute-start.5 = (bf16[128,1152]{1,0:T(8,128)(2,1)}, bf16[128,1152]{1,0:T(8,128)(2,1)S(1)}, u32[]{:S(2)}, u32[]{:S(2)}) collective-permute-start(bf16[128,1152]{1,0:T(8,128)(2,1)} %pad_maximum_fusion.2), channel_id=1, source_target_pairs={{0,1},{1,2},{2,3},{3,0},{4,5},{5,6},{6,7},{7,4},{8,9},{9,10},{10,1... | collective-permute-start | bytes 884744 | tf_op jit(solution)/shard_map/ppermute | solution.py:26
  30.0 2.0 %copy-start.18 = (bf16[1024,256]{1,0:T(8,128)(2,1)S(1)}, bf16[1024,256]{1,0:T(8,128)(2,1)}, u32[]{:S(2)}) copy-start(bf16[1024,256]{1,0:T(8,128)(2,1)} %param.10) | copy-start | bytes 1572868
  33.0 10.8 %collective-permute-start.7 = (bf16[1024,256]{0,1:T(8,128)(2,1)S(1)}, bf16[1024,256]{0,1:T(8,128)(2,1)S(1)}, u32[]{:S(2)}, u32[]{:S(2)}) collective-permute-start(bf16[1024,256]{0,1:T(8,128)(2,1)S(1)} %maximum_select_fusion), channel_id=1, source_target_pairs={{0,3},{1,0},{2,1},{3,2},{4,7},{5,4},{6,5},{7,6},{8,11},{9,8},{10,9... | collective-permute-start | bytes 1572872 | tf_op jit(solution)/shard_map/ppermute | solution.py:26
  33.8 13.1 %collective-permute-start.4 = (bf16[1024,256]{0,1:T(8,128)(2,1)S(1)}, bf16[1024,256]{0,1:T(8,128)(2,1)S(1)}, u32[]{:S(2)}, u32[]{:S(2)}) collective-permute-start(bf16[1024,256]{0,1:T(8,128)(2,1)S(1)} %maximum_select_fusion), channel_id=1, source_target_pairs={{0,1},{1,2},{2,3},{3,0},{4,5},{5,6},{6,7},{7,4},{8,9},{9,10},{10,1... | collective-permute-start | bytes 1572872 | tf_op jit(solution)/shard_map/ppermute | solution.py:26
  35.3 2.8 %copy-start.9 = (bf16[128,128]{1,0:T(8,128)(2,1)S(1)}, bf16[128,128]{1,0:T(8,128)(2,1)}, u32[]{:S(2)}) copy-start(bf16[128,128]{1,0:T(8,128)(2,1)} %copy-done.8) | copy-start | bytes 98308
  35.3 2.4 %collective-permute-start.12 = (bf16[128,1152]{1,0:T(8,128)(2,1)}, bf16[128,1152]{1,0:T(8,128)(2,1)S(1)}, u32[]{:S(2)}, u32[]{:S(2)}) collective-permute-start(bf16[128,1152]{1,0:T(8,128)(2,1)} %collective-permute-done.11), channel_id=1, source_target_pairs={{0,16},{16,0},{1,17},{17,1},{2,18},{18,2},{3,19},{19,3},{4,20},{20... | collective-permute-start | bytes 884744 | tf_op jit(solution)/shard_map/ppermute | solution.py:82
  35.4 2.3 %collective-permute-start.9 = (bf16[128,1152]{1,0:T(8,128)(2,1)S(1)}, bf16[128,1152]{1,0:T(8,128)(2,1)S(1)}, u32[]{:S(2)}, u32[]{:S(2)}) collective-permute-start(bf16[128,1152]{1,0:T(8,128)(2,1)S(1)} %collective-permute-done.8), channel_id=1, source_target_pairs={{0,16},{16,0},{1,17},{17,1},{2,18},{18,2},{3,19},{19,3},{4,20},{20... | collective-permute-start | bytes 884744 | tf_op jit(solution)/shard_map/ppermute | solution.py:82
  35.9 2.1 %collective-permute-start.6 = (bf16[128,1152]{1,0:T(8,128)(2,1)S(1)}, bf16[128,1152]{1,0:T(8,128)(2,1)S(1)}, u32[]{:S(2)}, u32[]{:S(2)}) collective-permute-start(bf16[128,1152]{1,0:T(8,128)(2,1)S(1)} %collective-permute-done.5), channel_id=1, source_target_pairs={{0,16},{16,0},{1,17},{17,1},{2,18},{18,2},{3,19},{19,3},{4,20},{20... | collective-permute-start | bytes 884744 | tf_op jit(solution)/shard_map/ppermute | solution.py:82
  37.7 10.1 %copy-start.6 = (bf16[128,1152]{1,0:T(8,128)(2,1)}, bf16[128,1152]{1,0:T(8,128)(2,1)S(1)}, u32[]{:S(2)}) copy-start(bf16[128,1152]{1,0:T(8,128)(2,1)S(1)} %collective-permute-done.9) | copy-start | bytes 884740
  38.2 9.6 %copy-start.10 = (bf16[2048,128]{1,0:T(8,128)(2,1)}, bf16[2048,128]{1,0:T(8,128)(2,1)S(1)}, u32[]{:S(2)}) copy-start(bf16[2048,128]{1,0:T(8,128)(2,1)S(1)} %constant_dynamic-update-slice_fusion) | copy-start | bytes 1572868
  43.8 15.2 %collective-permute-start.13 = (bf16[512,256]{0,1:T(8,128)(2,1)S(1)}, bf16[512,256]{0,1:T(8,128)(2,1)S(1)}, u32[]{:S(2)}, u32[]{:S(2)}) collective-permute-start(bf16[512,256]{0,1:T(8,128)(2,1)S(1)} %slice.249), channel_id=1, source_target_pairs={{0,3},{1,0},{2,1},{3,2},{4,7},{5,4},{6,5},{7,6},{8,11},{9,8},{10,9... | collective-permute-start | bytes 786440 | tf_op jit(solution)/shard_map/ppermute | solution.py:26
  47.0 8.7 %collective-permute-start.10 = (bf16[512,256]{0,1:T(8,128)(2,1)S(1)}, bf16[512,256]{0,1:T(8,128)(2,1)S(1)}, u32[]{:S(2)}, u32[]{:S(2)}) collective-permute-start(bf16[512,256]{0,1:T(8,128)(2,1)S(1)} %slice.244), channel_id=1, source_target_pairs={{0,1},{1,2},{2,3},{3,0},{4,5},{5,6},{6,7},{7,4},{8,9},{9,10},{10,1... | collective-permute-start | bytes 786440 | tf_op jit(solution)/shard_map/ppermute | solution.py:26
  60.4 1.9 %copy-start.7 = (bf16[128,1152]{1,0:T(8,128)(2,1)S(1)}, bf16[128,1152]{1,0:T(8,128)(2,1)}, u32[]{:S(2)}) copy-start(bf16[128,1152]{1,0:T(8,128)(2,1)} %copy-done.6) | copy-start | bytes 884740
  70.3 19.0 %copy-start.13 = (s32[1536]{0:T(1024)S(1)}, s32[1536]{0:T(1024)}, u32[]{:S(2)}) copy-start(s32[1536]{0:T(1024)} %copy-done.12) | copy-start | bytes 18436
  71.6 13.7 %collective-permute-start.14 = (bf16[384,128]{1,0:T(8,128)(2,1)S(1)}, bf16[384,128]{1,0:T(8,128)(2,1)S(1)}, u32[]{:S(2)}, u32[]{:S(2)}) collective-permute-start(bf16[384,128]{1,0:T(8,128)(2,1)S(1)} %get-tuple-element.24), channel_id=1, source_target_pairs={{0,16},{16,32},{32,48},{48,64},{64,80},{80,96},{96,112},{112,128},... | collective-permute-start | bytes 294920 | tf_op jit(solution)/shard_map/ppermute | solution.py:21
  77.8 7.5 %collective-permute-start.17 = (bf16[384,128]{1,0:T(8,128)(2,1)S(1)}, bf16[384,128]{1,0:T(8,128)(2,1)S(1)}, u32[]{:S(2)}, u32[]{:S(2)}) collective-permute-start(bf16[384,128]{1,0:T(8,128)(2,1)S(1)} %get-tuple-element.25), channel_id=1, source_target_pairs={{4,0},{8,4},{12,8},{5,1},{9,5},{13,9},{6,2},{10,6},{14,10},{7,3},{... | collective-permute-start | bytes 294920 | tf_op jit(solution)/shard_map/ppermute | solution.py:21
  79.1 6.2 %collective-permute-start.16 = (bf16[384,128]{1,0:T(8,128)(2,1)S(1)}, bf16[384,128]{1,0:T(8,128)(2,1)S(1)}, u32[]{:S(2)}, u32[]{:S(2)}) collective-permute-start(bf16[384,128]{1,0:T(8,128)(2,1)S(1)} %get-tuple-element.26), channel_id=1, source_target_pairs={{0,4},{4,8},{8,12},{1,5},{5,9},{9,13},{2,6},{6,10},{10,14},{3,7},{... | collective-permute-start | bytes 294920 | tf_op jit(solution)/shard_map/ppermute | solution.py:21
  83.1 5.9 %collective-permute-start.15 = (bf16[384,128]{1,0:T(8,128)(2,1)S(1)}, bf16[384,128]{1,0:T(8,128)(2,1)S(1)}, u32[]{:S(2)}, u32[]{:S(2)}) collective-permute-start(bf16[384,128]{1,0:T(8,128)(2,1)S(1)} %get-tuple-element.27), channel_id=1, source_target_pairs={{16,0},{32,16},{48,32},{64,48},{80,64},{96,80},{112,96},{128,112},... | collective-permute-start | bytes 294920 | tf_op jit(solution)/shard_map/ppermute | solution.py:21
  89.3 1.6 copy-start.4
  91.7 0.7 copy-start.16
  94.3 10.8 %collective-permute-start.18 = (bf16[384,128]{1,0:T(8,128)(2,1)S(1)}, bf16[384,128]{1,0:T(8,128)(2,1)S(1)}, u32[]{:S(2)}, u32[]{:S(2)}) collective-permute-start(bf16[384,128]{1,0:T(8,128)(2,1)S(1)} %get-tuple-element.20), channel_id=1, source_target_pairs={{16,0},{32,16},{48,32},{64,48},{80,64},{96,80},{112,96},{128,112},... | collective-permute-start | bytes 294920 | tf_op jit(solution)/shard_map/ppermute | solution.py:21
  96.2 8.9 %collective-permute-start.21 = (bf16[384,128]{1,0:T(8,128)(2,1)S(1)}, bf16[384,128]{1,0:T(8,128)(2,1)S(1)}, u32[]{:S(2)}, u32[]{:S(2)}) collective-permute-start(bf16[384,128]{1,0:T(8,128)(2,1)S(1)} %get-tuple-element.21), channel_id=1, source_target_pairs={{0,4},{4,8},{8,12},{1,5},{5,9},{9,13},{2,6},{6,10},{10,14},{3,7},{... | collective-permute-start | bytes 294920 | tf_op jit(solution)/shard_map/ppermute | solution.py:21
  99.1 6.0 %collective-permute-start.20 = (bf16[384,128]{1,0:T(8,128)(2,1)S(1)}, bf16[384,128]{1,0:T(8,128)(2,1)S(1)}, u32[]{:S(2)}, u32[]{:S(2)}) collective-permute-start(bf16[384,128]{1,0:T(8,128)(2,1)S(1)} %get-tuple-element.22), channel_id=1, source_target_pairs={{4,0},{8,4},{12,8},{5,1},{9,5},{13,9},{6,2},{10,6},{14,10},{7,3},{... | collective-permute-start | bytes 294920 | tf_op jit(solution)/shard_map/ppermute | solution.py:21
  100.4 5.5 %collective-permute-start.19 = (bf16[384,128]{1,0:T(8,128)(2,1)S(1)}, bf16[384,128]{1,0:T(8,128)(2,1)S(1)}, u32[]{:S(2)}, u32[]{:S(2)}) collective-permute-start(bf16[384,128]{1,0:T(8,128)(2,1)S(1)} %get-tuple-element.23), channel_id=1, source_target_pairs={{0,16},{16,32},{32,48},{48,64},{64,80},{80,96},{96,112},{112,128},... | collective-permute-start | bytes 294920 | tf_op jit(solution)/shard_map/ppermute | solution.py:21
  105.1 2.2 %copy-start.2 = (f32[1024,1024]{1,0:T(8,128)S(1)}, f32[1024,1024]{1,0:T(8,128)}, u32[]{:S(2)}) copy-start(f32[1024,1024]{1,0:T(8,128)} %get-tuple-element.35) | copy-start | bytes 12582916
  105.1 2.3 %copy-start.11 = (bf16[2048,128]{1,0:T(8,128)(2,1)S(1)}, bf16[2048,128]{1,0:T(8,128)(2,1)}, u32[]{:S(2)}) copy-start(bf16[2048,128]{1,0:T(8,128)(2,1)} %copy-done.10) | copy-start | bytes 1572868
  112.1 1.7 %collective-permute-start.22 = (bf16[128,1152]{1,0:T(8,128)(2,1)S(1)}, bf16[128,1152]{1,0:T(8,128)(2,1)S(1)}, u32[]{:S(2)}, u32[]{:S(2)}) collective-permute-start(bf16[128,1152]{1,0:T(8,128)(2,1)S(1)} %pad_maximum_fusion.3), channel_id=1, source_target_pairs={{0,16},{16,0},{1,17},{17,1},{2,18},{18,2},{3,19},{19,3},{4,20},{20... | collective-permute-start | bytes 884744 | tf_op jit(solution)/shard_map/ppermute | solution.py:154
  155.7 4.9 %collective-permute-start.23 = (bf16[128,1152]{1,0:T(8,128)(2,1)S(1)}, bf16[128,1152]{1,0:T(8,128)(2,1)S(1)}, u32[]{:S(2)}, u32[]{:S(2)}) collective-permute-start(bf16[128,1152]{1,0:T(8,128)(2,1)S(1)} %reshape.169), channel_id=1, source_target_pairs={{0,16},{16,0},{1,17},{17,1},{2,18},{18,2},{3,19},{19,3},{4,20},{20... | collective-permute-start | bytes 884744 | tf_op jit(solution)/shard_map/ppermute | solution.py:162
  160.7 1.9 %copy-start.1 = (bf16[256,1024]{1,0:T(8,128)(2,1)S(1)}, bf16[256,1024]{1,0:T(8,128)(2,1)}, u32[]{:S(2)}) copy-start(bf16[256,1024]{1,0:T(8,128)(2,1)} %param.18) | copy-start | bytes 1572868

commit v4 on v3

v4 whole, which is shorter than its diff:
```python
import jax
import jax.numpy as jnp
import numpy as np
from jax import lax
from jax.experimental import pallas as pl
from jax.experimental.pallas import tpu as pltpu
from jax.sharding import Mesh
from jax.sharding import PartitionSpec as P

BF = jnp.bfloat16
F32 = jnp.float32
ROWS = ("z", "core")
PLANE = ("z", "gy")
LANES = 128
INTERPRET = False


def dot(lhs, rhs, lhs_dim=1, rhs_dim=0):
    return lax.dot_general(lhs, rhs, (((lhs_dim,), (rhs_dim,)), ((), ())), preferred_element_type=F32)


def turn(field, axis, move):
    count = lax.axis_size(axis)
    return lax.ppermute(field, axis, [(i, (i + move) % count) for i in range(count)])


def pairs_at(count, first):
    pairs = []
    for i in range(first, count - 1, 2):
        pairs += [(i, i + 1), (i + 1, i)]
    return pairs


def trade(fields):
    rows, cols = lax.axis_size(ROWS), lax.axis_size("gy")
    return (
        lax.ppermute(fields[0], "core", [(0, 1), (1, 0)]),
        lax.ppermute(fields[1], ROWS, pairs_at(rows, 1)),
        lax.ppermute(fields[2], "gy", pairs_at(cols, 0)),
        lax.ppermute(fields[3], "gy", pairs_at(cols, 1)),
    )


def send_order(meta):
    core, odd = meta[0], lax.rem(meta[1], 2)
    return (core, 1 - core, 2 + odd, 3 - odd)


def recv_order(meta):
    core, odd = meta[0], lax.rem(meta[1], 2)
    return (1 - core, core, 3 - odd, 2 + odd)


def down(row):
    return jnp.transpose(jnp.broadcast_to(row.astype(F32), (LANES, LANES)))


def pick(row, nodes, out_ref):
    lane = lax.broadcasted_iota(jnp.int32, (LANES, LANES), 1).astype(F32)
    for b in range(row.shape[1] // LANES):
        at = down(row[:, b * LANES : (b + 1) * LANES])
        for j in range(nodes // LANES):
            out_ref[b * LANES : (b + 1) * LANES, j * LANES : (j + 1) * LANES] = jnp.where(
                at == lane + float(j * LANES), 1.0, 0.0
            ).astype(BF)


def put(row, nodes):
    ids = lax.broadcasted_iota(jnp.int32, (nodes, row.shape[1]), 0)
    return jnp.where(ids == row, 1.0, 0.0).astype(BF)


def live_row(send_ref, counts, d):
    row = send_ref[pl.ds(d, 1), :]
    slot = lax.broadcasted_iota(jnp.int32, row.shape, 1)
    return jnp.where(slot < counts[d], row, -1)


def weigh(arrived, weight_row, rhs_ref, base):
    width = arrived.shape[1]
    for b in range(weight_row.shape[1] // LANES):
        w = down(weight_row[:, b * LANES : (b + 1) * LANES])
        w = jnp.concatenate([w] * (width // LANES), axis=1)
        value = arrived[b * LANES : (b + 1) * LANES, :].astype(F32) * w
        high = value.astype(BF)
        low = (value - high.astype(F32)).astype(BF)
        rhs_ref[pl.ds(base + b * LANES, LANES), :width] = high
        rhs_ref[pl.ds(base + b * LANES, LANES), width:] = low


def send_kernel(meta, counts, feat, send, w_hid, w_cls, o0, o1, o2, o3, mine, other, hot):
    nodes = feat.shape[0]
    half, hid = w_hid.shape[0] // 2, w_hid.shape[1]
    for ref, part in ((mine, meta[0]), (other, 1 - meta[0])):
        at = pl.multiple_of(part * half, half)
        ref[:, :hid] = w_hid[pl.ds(at, half), :]
        ref[:, hid:] = w_cls[pl.ds(at, half), :]
    for d, out in zip(send_order(meta), (o0, o1, o2, o3)):
        pick(live_row(send, counts, d), nodes, hot)
        out[...] = dot(hot[...], feat[...]).astype(BF)


def near(tiles, col, field, block, tb):
    lhs = jnp.concatenate([tiles[block, k] for k in range(tiles.shape[1])], axis=1)
    rhs = jnp.concatenate(
        [
            field[pl.ds(pl.multiple_of(col[block, k] * tb, tb), tb), :]
            for k in range(tiles.shape[1])
        ],
        axis=0,
    )
    return dot(lhs, rhs)


def mix_kernel(meta, col, feat, tiles, r0, r1, r2, r3, recv, weight, top, bottom, hot, rhs):
    nodes, width = feat.shape
    slots, tb = recv.shape[1], tiles.shape[2]
    for m, (d, arrived) in enumerate(zip(recv_order(meta), (r0, r1, r2, r3))):
        hot[:, m * slots : (m + 1) * slots] = put(recv[pl.ds(d, 1), :], nodes)
        weigh(arrived[...], weight[pl.ds(d, 1), :], rhs, m * slots)
    part = nodes // 2
    first = meta[0] == 0
    for h, out in enumerate((top, bottom)):
        far = dot(hot[h * part : (h + 1) * part, :], rhs[...])
        far = far[:, :width] + far[:, width:]
        for b in range(part // tb):
            got = near(tiles, col, feat, h * (part // tb) + b, tb) + far[b * tb : (b + 1) * tb, :]
            turned = jnp.concatenate([got[:, width // 2 :], got[:, : width // 2]], axis=1)
            out[b * tb : (b + 1) * tb, :] = jnp.where(first, got, turned).astype(BF)


def hidden_kernel(
    meta, counts, send, own_t, own_b, lo_t, lo_b, hi_t, hi_b, far_t, far_b,
    m0, m1, m2, m3, v0, v1, v2, v3,
    hidden, slope, z_pair, w_cls, o0, o1, o2, o3, w_all, hot,
):
    nodes = z_pair.shape[0]
    half = m0.shape[0]
    hid = w_all.shape[1]
    classes = w_cls.shape[1]
    n_af = w_cls.shape[0] // (2 * half)
    for i, (k, mine, other) in enumerate(((0, m0, v0), (1, m1, v1), (3, m3, v3), (2, m2, v2))):
        w_all[2 * i * half : (2 * i + 1) * half, :] = mine[:, :hid]
        w_all[(2 * i + 1) * half : (2 * i + 2) * half, :] = other[:, :hid]
        base = lax.rem(meta[2] + n_af - k, n_af) * 2
        w_cls[pl.ds(pl.multiple_of((base + meta[0]) * half, half), half), :] = mine[:, hid:]
        w_cls[pl.ds(pl.multiple_of((base + 1 - meta[0]) * half, half), half), :] = other[:, hid:]
    part = nodes // 2
    rows = 256
    for h, refs in enumerate(((own_t, lo_t, hi_t, far_t), (own_b, lo_b, hi_b, far_b))):

        def block(i, carry, h=h, refs=refs):
            at = pl.multiple_of(i * rows, rows)
            to = pl.multiple_of(h * part + i * rows, rows)
            lhs = jnp.concatenate([ref[pl.ds(at, rows), :] for ref in refs], axis=1)
            pre = dot(lhs, w_all[...])
            sig = jax.nn.sigmoid(pre)
            act = (pre * sig).astype(BF)
            slope[pl.ds(to, rows), :] = (sig * (1.0 + pre * (1.0 - sig))).astype(BF)
            for j in range(hid // LANES):
                hidden[j, pl.ds(to, rows), :] = act[:, j * LANES : (j + 1) * LANES]
            z = dot(act, w_cls[...])
            high = z.astype(BF)
            z_pair[pl.ds(to, rows), :classes] = high
            z_pair[pl.ds(to, rows), classes:] = (z - high.astype(F32)).astype(BF)
            return carry

        lax.fori_loop(0, part // rows, block, 0)
    for d, out in zip(send_order(meta), (o0, o1, o2, o3)):
        pick(live_row(send, counts, d), nodes, hot)
        out[...] = dot(hot[...], z_pair[:, :classes]).astype(BF)


def loss_kernel(
    meta, col, tiles, z_pair, r0, r1, r2, r3, recv, weight, labels,
    grad, b0, b1, b2, b3, hot, rhs, cols,
):
    nodes, classes = grad.shape
    slots, tb = recv.shape[1], tiles.shape[2]
    order = recv_order(meta)
    for m, (d, arrived) in enumerate(zip(order, (r0, r1, r2, r3))):
        hot[:, m * slots : (m + 1) * slots] = put(recv[pl.ds(d, 1), :], nodes)
        weigh(arrived[...], weight[pl.ds(d, 1), :], rhs, m * slots)
    part = nodes // 2
    lane = lax.broadcasted_iota(jnp.int32, (tb, classes), 1).astype(F32)
    for h in range(2):
        far = dot(hot[h * part : (h + 1) * part, :], rhs[...])
        for b in range(part // tb):
            r = h * (part // tb) + b
            logit = near(tiles, col, z_pair, r, tb) + far[b * tb : (b + 1) * tb, :]
            logit = logit[:, :classes] + logit[:, classes:]
            exponent = jnp.exp(logit - jnp.max(logit, axis=1, keepdims=True))
            probability = exponent / jnp.sum(exponent, axis=1, keepdims=True)
            onehot = jnp.where(down(labels[r : r + 1, :]) == lane, 1.0, 0.0)
            grad[r * tb : (r + 1) * tb, :] = ((probability - onehot) * (1.0 / 64.0)).astype(BF)
    for d, out in zip(order, (b0, b1, b2, b3)):
        pick(recv[pl.ds(d, 1), :], nodes, cols)
        taken = dot(cols[...], grad[...])
        row = weight[pl.ds(d, 1), :]
        for b in range(slots // LANES):
            at = slice(b * LANES, (b + 1) * LANES)
            out[at, :] = (taken[at, :] * down(row[:, at])).astype(BF)


def grads_kernel(
    meta, col, counts, pick_hid, tiles, grad, t0, t1, t2, t3, send, w_cls, slope, top, bottom,
    units_m, units_o, theirs, mine, hot, back, acc, mix, pre,
):
    nodes, classes = grad.shape
    slots, tb, kt = send.shape[1], tiles.shape[2], tiles.shape[1]
    hid = slope.shape[1]
    for m, (d, returned) in enumerate(zip(send_order(meta), (t0, t1, t2, t3))):
        hot[:, m * slots : (m + 1) * slots] = put(live_row(send, counts, d), nodes)
        back[m * slots : (m + 1) * slots, :] = returned[...]
    acc[...] = dot(hot[...], back[...])
    for r in range(tiles.shape[0]):
        lhs = jnp.concatenate([tiles[r, k] for k in range(kt)], axis=1)
        spread = dot(lhs, grad[r * tb : (r + 1) * tb, :], 0, 0)
        for k in range(kt):
            at = pl.ds(pl.multiple_of(col[r, k] * tb, tb), tb)
            acc[at, :] += spread[k * tb : (k + 1) * tb, :]
    mix[...] = acc[...].astype(BF)
    rows = 256

    def block(i, carry):
        at = pl.ds(pl.multiple_of(i * rows, rows), rows)
        act = dot(mix[at, :], w_cls[...], 1, 1)
        pre[at, :] = (act * slope[at, :].astype(F32)).astype(BF)
        return carry

    lax.fori_loop(0, nodes // rows, block, 0)
    lhs = jnp.concatenate([top[...], bottom[...]], axis=0)
    both = dot(lhs, pre[...], 0, 0)
    half = both.shape[0] // 2
    mine[:, :hid] = both[:half]
    theirs[:, :hid] = both[half:].astype(BF)
    mine[:, hid:] = dot(units_m[0], mix[...], 0, 0)
    theirs[:, hid:] = dot(units_o[0], mix[...], 0, 0).astype(BF)


def call(kernel, scalars, arrays, outs, scratch, specs=None):
    def whole(x):
        return pl.BlockSpec(x.shape, lambda *_, n=len(x.shape): (0,) * n)

    specs = specs or {}
    outs = [jax.ShapeDtypeStruct(s, t) for s, t in outs]
    return pl.pallas_call(
        kernel,
        grid_spec=pltpu.PrefetchScalarGridSpec(
            num_scalar_prefetch=len(scalars),
            grid=(1,),
            in_specs=[specs.get(i, whole(x)) for i, x in enumerate(arrays)],
            out_specs=[whole(x) for x in outs],
            scratch_shapes=[pltpu.VMEM(s, t) for s, t in scratch],
        ),
        out_shape=outs,
        interpret=INTERPRET,
        name=kernel.__name__,
    )(*scalars, *arrays)


def local(
    features,
    adj_tiles,
    col_block,
    send_rows,
    send_counts,
    recv_target,
    edge_weight,
    labels,
    w_hidden,
    w_classes,
):
    nodes, width = features.shape
    slots = send_rows.shape[1]
    hid, classes = w_hidden.shape[1], w_classes.shape[1]
    half = w_hidden.shape[0] // 2
    n_af = lax.axis_size("af")
    n_plane = lax.axis_size("z") * lax.axis_size("gy")
    core = lax.axis_index("core")
    af = lax.axis_index("af")
    meta = jnp.stack([core, lax.axis_index("gy"), af]).astype(jnp.int32)
    swap = [(0, 1), (1, 0)]
    both = hid + classes
    part = nodes // 2

    *out, w_mine, w_other = call(
        send_kernel,
        (meta, send_counts),
        (features, send_rows, w_hidden, w_classes),
        [((slots, width), BF)] * 4 + [((half, both), BF)] * 2,
        [((slots, nodes), BF)],
    )
    arrived = trade(out)
    w_mine = [w_mine] + [turn(w_mine, "af", k) for k in range(1, n_af)]
    w_other = [w_other] + [lax.ppermute(w, "core", swap) for w in w_mine[1:]]
    top, bottom = call(
        mix_kernel,
        (meta, col_block),
        (features, adj_tiles, *arrived, recv_target, edge_weight),
        [((part, width), BF)] * 2,
        [((nodes, 4 * slots), BF), ((4 * slots, 2 * width), BF)],
    )
    lo_t, hi_b = turn(top, "af", 1), turn(bottom, "af", -1)
    lo_b, hi_t = turn(bottom, "af", 1), turn(top, "af", -1)
    far_t, far_b = turn(lo_t, "af", 1), turn(hi_b, "af", -1)
    hidden, slope, z_pair, w_cls, *out = call(
        hidden_kernel,
        (meta, send_counts),
        (send_rows, top, bottom, lo_t, lo_b, hi_t, hi_b, far_t, far_b, *w_mine, *w_other),
        [
            ((hid // LANES, nodes, LANES), BF),
            ((nodes, hid), BF),
            ((nodes, 2 * classes), BF),
            ((hid, classes), BF),
        ]
        + [((slots, classes), BF)] * 4,
        [((n_af * 2 * half, hid), BF), ((slots, nodes), BF)],
    )
    arrived = trade(out)
    grad, *out = call(
        loss_kernel,
        (meta, col_block),
        (adj_tiles, z_pair, *arrived, recv_target, edge_weight, labels.reshape(-1, LANES)),
        [((nodes, classes), BF)] + [((slots, classes), BF)] * 4,
        [((nodes, 4 * slots), BF), ((4 * slots, 2 * classes), BF), ((slots, nodes), BF)],
    )
    returned = trade(out)
    pick_hid = jnp.stack([af * 2 + core, af * 2 + 1 - core]).astype(jnp.int32)
    theirs, mine = call(
        grads_kernel,
        (meta, col_block, send_counts, pick_hid),
        (adj_tiles, grad, *returned, send_rows, w_cls, slope, top, bottom, hidden, hidden),
        [((half, both), BF), ((half, both), F32)],
        [
            ((nodes, 4 * slots), BF),
            ((4 * slots, classes), BF),
            ((nodes, classes), F32),
            ((nodes, classes), BF),
            ((nodes, hid), BF),
        ],
        {
            11: pl.BlockSpec((1, nodes, LANES), lambda i, a, b, c, s: (s[0], 0, 0)),
            12: pl.BlockSpec((1, nodes, LANES), lambda i, a, b, c, s: (s[1], 0, 0)),
        },
    )
    total = mine + lax.ppermute(theirs, "core", swap).astype(F32)
    pieces = total.astype(BF).reshape(n_plane, half // n_plane, both)
    pieces = lax.all_to_all(pieces, PLANE, 0, 0, tiled=True)
    piece = jnp.sum(pieces.astype(F32), axis=0).astype(BF)
    mine = lax.all_to_all(
        jnp.broadcast_to(piece[None], (n_plane,) + piece.shape), PLANE, 0, 0, tiled=True
    ).reshape(half, both)
    other = lax.ppermute(mine, "core", swap)
    first = jnp.where(core == 0, mine, other)
    second = jnp.where(core == 0, other, mine)
    whole = jnp.concatenate([first, second], axis=0).astype(F32)
    return (whole[:, :hid], whole[:, hid:])


def solution(mesh):
    shape = mesh.devices.shape
    split = Mesh(
        np.reshape(mesh.devices, (shape[0] // 2, 2) + shape[1:]), ("z", "core", "gy", "af")
    )
    parts = ("z", "core", "gy")
    placed = (
        P(parts, "af"),
        P(parts, None, None, None),
        P(parts, None),
        P(parts, None),
        P(parts),
        P(parts, None),
        P(parts, None),
        P(parts),
        P("af", None),
        P("af", None),
    )
    return jax.shard_map(
        local, mesh=split, in_specs=placed, out_specs=(P("af", None), P("af", None)), check_vma=False
    )
```

time: 164 us -> 148 us (0.902)
  matrix products: 35.4 us -> 0 us
  Pallas kernels: 0 us -> 33.4 us
  starting transfers between devices: 50.5 us -> 36.5 us
  waiting for transfers between devices: 21.5 us -> 26.2 us
  other arithmetic: 6.33 us -> 3.28 us
    dot_general x25 -> x0, matrix products: 35.4 us -> none  [dot(): lax.dot_general(lhs, rhs, (((lhs_dim,), (rhs_dim,)), ((), ())), preferred...]
    pallas_call x0 -> x5, Pallas kernels: none -> 33.4 us  [call(): pl.pallas_call(kernel, grid_spec=pltpu.PrefetchScalarGridSpec(num_scalar_...]
    ppermute x16, starting transfers between devices: 36.9 us -> 26.1 us  [the longest x3 10.5 us: trade(): lax.ppermute(fields[1], ROWS, pairs_at(rows, 1))]
    ppermute x7 -> x9, waiting for transfers between devices: 12.2 us -> 19.1 us  [turn(): lax.ppermute(field, axis, [(i, (i + move) % count) for i in range(count)])]
    ppermute x7 -> x9, starting transfers between devices: 9.88 us -> 6.73 us  [turn(): lax.ppermute(field, axis, [(i, (i + move) % count) for i in range(count)])]
    unnamed x38 -> x49, local copies, waits for them, and re-layouts: 1.87 us -> 4.71 us
    ppermute x16, waiting for transfers between devices: 8.15 us -> 5.92 us  [the longest x3 2.22 us: trade(): lax.ppermute(fields[2], 'gy', pairs_at(cols, 0))]
    select_n x3 -> x0, other arithmetic: 2.12 us -> none  [the longest x1 1.16 us: local(): dense = jnp.where(here, adj_tiles[:, k][:, :, None, :], dense)]
  transfers between devices with their start and end apart: 24 -> 26, of which waited for: 9 -> 11; matrix products, arithmetic and copies ran while one was open for 12% -> 1% of each run, Pallas kernels for 0% -> 4%
where the time goes in v4:
time: 148 us; the launch traced here: 147 us
  blocking collectives  40.5 us (27%)
  starting transfers between devices  36.5 us (25%)
  Pallas kernels  33.4 us (23%)
  waiting for transfers between devices  26.2 us (18%)
  local copies, waits for them, and re-layouts  6.03 us (4%)
  other arithmetic  3.28 us (2%)
    pallas_call x5, Pallas kernels, call(): pl.pallas_call(kernel, grid_spec=pltpu.PrefetchScalarGridSpec(num_scalar_...  33.4 us
    all_to_all x1, blocking collectives, local(): pieces = lax.all_to_all(pieces, PLANE, 0, 0, tiled=True)  25.3 us
    ppermute x9, waiting for transfers between devices, turn(): lax.ppermute(field, axis, [(i, (i + move) % count) for i in range(count)])  19.1 us
    all_to_all x1, blocking collectives, local(): lax.all_to_all(jnp.broadcast_to(piece[None], (n_plane,) + piece.shape), P...  15.2 us
    ppermute x3, starting transfers between devices, trade(): lax.ppermute(fields[1], ROWS, pairs_at(rows, 1))  10.5 us
    ppermute x3, starting transfers between devices, trade(): lax.ppermute(fields[2], 'gy', pairs_at(cols, 0))  8 us
    ppermute x9, starting transfers between devices, turn(): lax.ppermute(field, axis, [(i, (i + move) % count) for i in range(count)])  6.73 us
    unnamed x49, local copies, waits for them, and re-layouts  4.71 us
  transfers between devices with their start and end apart: 26, of which 11 were waited for; matrix products, arithmetic and copies ran while one was open for 1% of the time, Pallas kernels for 4%

profile of v4, /device:TPU:1, one launch (start us, length us, event | category | flops | bytes accessed | tf_op | source)
XLA Modules:
  0.0 147.0 jit_solution(17615234462892368595)
XLA Ops:
  0.6 0.6 pad_add_fusion.meta
  1.2 4.3 %send_kernel.1 = (bf16[384,256]{1,0:T(8,128)(2,1)}, bf16[384,256]{1,0:T(8,128)(2,1)}, bf16[384,256]{1,0:T(8,128)(2,1)}, bf16[384,256]{1,0:T(8,128)(2,1)}, bf16[1...) custom-call(s32[3]{0:T(128)} %pad_add_fusion.meta, s32[4]{0:T(128)} %counts.5, bf16[1024,256]{1,0:T(8,128)(2,1)} %feat.3, ...), custom_call_target="tpu_custom_call" | custom-call | tf_op jit(solution)/shard_map/send_kernel/pallas_call | solution.py:247
  5.6 3.2 %collective-permute-start = (bf16[384,256]{1,0:T(8,128)(2,1)}, bf16[384,256]{1,0:T(8,128)(2,1)S(1)}, u32[]{:S(2)}, u32[]{:S(2)}) collective-permute-start(bf16[384,256]{1,0:T(8,128)(2,1)} %get-tuple-element.25), channel_id=1, source_target_pairs={{0,16},{16,0},{1,17},{17,1},{2,18},{18,2},{3,19},{19,3},{4,20},{20... | collective-permute-start | bytes 589832 | tf_op jit(solution)/shard_map/ppermute | solution.py:37
  8.8 1.0 collective-permute-start.12
  9.8 0.3 collective-permute-start.11
  10.2 4.0 %collective-permute-start.1 = (bf16[384,256]{1,0:T(8,128)(2,1)}, bf16[384,256]{1,0:T(8,128)(2,1)S(1)}, u32[]{:S(2)}, u32[]{:S(2)}) collective-permute-start(bf16[384,256]{1,0:T(8,128)(2,1)} %get-tuple-element.26), channel_id=1, source_target_pairs={{16,32},{32,16},{48,64},{64,48},{80,96},{96,80},{112,128},{128,112... | collective-permute-start | bytes 589832 | tf_op jit(solution)/shard_map/ppermute | solution.py:38
  14.2 1.3 collective-permute-start.2
  15.5 0.7 collective-permute-start.3
  16.2 1.9 %collective-permute-done.1.r1 = bf16[384,256]{1,0:T(8,128)(2,1)S(1)} collective-permute-done((bf16[384,256]{1,0:T(8,128)(2,1)}, bf16[384,256]{1,0:T(8,128)(2,1)S(1)}, u32[]{:S(2)}, u32[]{:S(2)}) %collective-permute-start.1) | collective-permute-done | bytes 196640 | tf_op jit(solution)/shard_map/ppermute | solution.py:38
  18.0 0.4 collective-permute-start.10
  18.4 1.3 copy.14.col
  19.8 0.7 copy-done.14
  20.5 0.7 copy-done.15
  21.2 5.6 %mix_kernel.1 = (bf16[512,256]{1,0:T(8,128)(2,1)}, bf16[512,256]{1,0:T(8,128)(2,1)}) custom-call(s32[3]{0:T(128)} %pad_add_fusion.meta, s32[8,4]{1,0:T(8,128)} %copy.14.col, bf16[1024,256]{1,0:T(8,128)(2,1)} %feat.3, bf16[8,4,128,128]{3,2,1,0:T(8,128)(2,1)} %tiles.5, bf16[384,256]{1,0:T(8,128)(2,1)} %copy-done.12, bf16[384,256]{1,0:T(8,128)(2,1)} %copy-done.13, ...), custom_call_target="tpu_custom_call" | custom-call | tf_op jit(solution)/shard_map/mix_kernel/pallas_call | solution.py:247
  26.7 2.3 %collective-permute-start.6 = (bf16[512,256]{1,0:T(8,128)(2,1)}, bf16[512,256]{1,0:T(8,128)(2,1)S(1)}, u32[]{:S(2)}, u32[]{:S(2)}) collective-permute-start(bf16[512,256]{1,0:T(8,128)(2,1)} %get-tuple-element.29.own_t.top), channel_id=1, source_target_pairs={{0,3},{1,0},{2,1},{3,2},{4,7},{5,4},{6,5},{7,6},{8,11},{9,8},{10,9... | collective-permute-start | bytes 786440 | tf_op jit(solution)/shard_map/ppermute | solution.py:24
  29.0 2.7 %collective-permute-start.7 = (bf16[512,256]{1,0:T(8,128)(2,1)}, bf16[512,256]{1,0:T(8,128)(2,1)S(1)}, u32[]{:S(2)}, u32[]{:S(2)}) collective-permute-start(bf16[512,256]{1,0:T(8,128)(2,1)} %get-tuple-element.30.own_b.bottom), channel_id=1, source_target_pairs={{0,3},{1,0},{2,1},{3,2},{4,7},{5,4},{6,5},{7,6},{8,11},{9,8},{10,9... | collective-permute-start | bytes 786440 | tf_op jit(solution)/shard_map/ppermute | solution.py:24
  31.7 0.3 collective-permute-start.15
  32.0 3.5 %collective-permute-done.6.hi_t = bf16[512,256]{1,0:T(8,128)(2,1)S(1)} collective-permute-done((bf16[512,256]{1,0:T(8,128)(2,1)}, bf16[512,256]{1,0:T(8,128)(2,1)S(1)}, u32[]{:S(2)}, u32[]{:S(2)}) %collective-permute-start.6) | collective-permute-done | bytes 262176 | tf_op jit(solution)/shard_map/ppermute | solution.py:24
  35.4 3.2 %collective-permute-done.4.lo_t = bf16[512,256]{1,0:T(8,128)(2,1)S(1)} collective-permute-done((bf16[512,256]{1,0:T(8,128)(2,1)}, bf16[512,256]{1,0:T(8,128)(2,1)S(1)}, u32[]{:S(2)}, u32[]{:S(2)}) %collective-permute-start.4) | collective-permute-done | bytes 262176 | tf_op jit(solution)/shard_map/ppermute | solution.py:24
  38.7 0.6 collective-permute-start.13
  39.2 1.6 %collective-permute-done.7.hi_b = bf16[512,256]{1,0:T(8,128)(2,1)S(1)} collective-permute-done((bf16[512,256]{1,0:T(8,128)(2,1)}, bf16[512,256]{1,0:T(8,128)(2,1)S(1)}, u32[]{:S(2)}, u32[]{:S(2)}) %collective-permute-start.7) | collective-permute-done | bytes 262176 | tf_op jit(solution)/shard_map/ppermute | solution.py:24
  40.9 3.4 %collective-permute-done.5.lo_b = bf16[512,256]{1,0:T(8,128)(2,1)S(1)} collective-permute-done((bf16[512,256]{1,0:T(8,128)(2,1)}, bf16[512,256]{1,0:T(8,128)(2,1)S(1)}, u32[]{:S(2)}, u32[]{:S(2)}) %collective-permute-start.5) | collective-permute-done | bytes 262176 | tf_op jit(solution)/shard_map/ppermute | solution.py:24
  44.3 5.9 %collective-permute-done.8.far_t = bf16[512,256]{1,0:T(8,128)(2,1)S(1)} collective-permute-done((bf16[512,256]{1,0:T(8,128)(2,1)S(1)}, bf16[512,256]{1,0:T(8,128)(2,1)S(1)}, u32[]{:S(2)}, u32[]{:S(2)}) %collective-permute-start.8) | collective-permute-done | bytes 262176 | tf_op jit(solution)/shard_map/ppermute | solution.py:24
  50.3 1.4 collective-permute-done.9.far_b
  51.8 0.6 copy-done.11
  52.4 9.4 %hidden_kernel.1 = (bf16[8,1024,128]{2,1,0:T(8,128)(2,1)}, bf16[1024,1024]{1,0:T(8,128)(2,1)}, bf16[1024,256]{1,0:T(8,128)(2,1)}, bf16[1024,128]{1,0:T(8,128)(2,...) custom-call(s32[3]{0:T(128)} %pad_add_fusion.meta, ...), custom_call_target="tpu_custom_call" | custom-call | tf_op jit(solution)/shard_map/hidden_kernel/pallas_call | solution.py:247
  61.8 1.4 collective-permute-start.16
  63.2 2.3 %collective-permute-start.17 = (bf16[384,128]{1,0:T(8,128)(2,1)}, bf16[384,128]{1,0:T(8,128)(2,1)S(1)}, u32[]{:S(2)}, u32[]{:S(2)}) collective-permute-start(bf16[384,128]{1,0:T(8,128)(2,1)} %get-tuple-element.35), channel_id=1, source_target_pairs={{16,32},{32,16},{48,64},{64,48},{80,96},{96,80},{112,128},{128,112... | collective-permute-start | bytes 294920 | tf_op jit(solution)/shard_map/ppermute | solution.py:38
  65.5 3.1 %collective-permute-start.18 = (bf16[384,128]{1,0:T(8,128)(2,1)}, bf16[384,128]{1,0:T(8,128)(2,1)S(1)}, u32[]{:S(2)}, u32[]{:S(2)}) collective-permute-start(bf16[384,128]{1,0:T(8,128)(2,1)} %get-tuple-element.36), channel_id=1, source_target_pairs={{0,4},{4,0},{8,12},{12,8},{1,5},{5,1},{9,13},{13,9},{2,6},{6,2},{1... | collective-permute-start | bytes 294920 | tf_op jit(solution)/shard_map/ppermute | solution.py:39
  68.6 0.7 collective-permute-start.19
  69.3 1.5 %collective-permute-done.18.r2 = bf16[384,128]{1,0:T(8,128)(2,1)S(1)} collective-permute-done((bf16[384,128]{1,0:T(8,128)(2,1)}, bf16[384,128]{1,0:T(8,128)(2,1)S(1)}, u32[]{:S(2)}, u32[]{:S(2)}) %collective-permute-start.18) | collective-permute-done | bytes 98336 | tf_op jit(solution)/shard_map/ppermute | solution.py:39
  70.9 0.6 copy-done.22
  71.6 6.4 %loss_kernel.1 = (bf16[1024,128]{1,0:T(8,128)(2,1)}, bf16[384,128]{1,0:T(8,128)(2,1)}, bf16[384,128]{1,0:T(8,128)(2,1)}, bf16[384,128]{1,0:T(8,128)(2,1)}, bf16[384,128]{1,0:T(8,128)(2,1)}) custom-call(s32[3]{0:T(128)} %pad_add_fusion.meta, s32[8,4]{1,0:T(8,128)} %copy.14.col, bf16[8,4,128,128]{3,2,1,0:T(8,128)(2,1)} %tiles.5, ...), custom_call_target="tpu_custom_call" | custom-call | tf_op jit(solution)/shard_map/loss_kernel/pallas_call | solution.py:247
  77.9 4.2 %collective-permute-start.21 = (bf16[384,128]{1,0:T(8,128)(2,1)}, bf16[384,128]{1,0:T(8,128)(2,1)S(1)}, u32[]{:S(2)}, u32[]{:S(2)}) collective-permute-start(bf16[384,128]{1,0:T(8,128)(2,1)} %get-tuple-element.40), channel_id=1, source_target_pairs={{16,32},{32,16},{48,64},{64,48},{80,96},{96,80},{112,128},{128,112... | collective-permute-start | bytes 294920 | tf_op jit(solution)/shard_map/ppermute | solution.py:38
  82.2 3.6 %collective-permute-start.22 = (bf16[384,128]{1,0:T(8,128)(2,1)}, bf16[384,128]{1,0:T(8,128)(2,1)S(1)}, u32[]{:S(2)}, u32[]{:S(2)}) collective-permute-start(bf16[384,128]{1,0:T(8,128)(2,1)} %get-tuple-element.41), channel_id=1, source_target_pairs={{0,4},{4,0},{8,12},{12,8},{1,5},{5,1},{9,13},{13,9},{2,6},{6,2},{1... | collective-permute-start | bytes 294920 | tf_op jit(solution)/shard_map/ppermute | solution.py:39
  85.7 0.9 collective-permute-start.23
  86.6 0.6 pad_add_fusion.1.pick_hid
  87.2 0.7 collective-permute-done.22.t2
  88.0 0.6 copy-done.18
  88.6 7.7 %grads_kernel.1 = (bf16[128,1152]{1,0:T(8,128)(2,1)}, f32[128,1152]{1,0:T(8,128)}) custom-call(s32[3]{0:T(128)} %pad_add_fusion.meta, s32[8,4]{1,0:T(8,128)} %copy.14.col, s32[4]{0:T(128)} %counts.5, s32[2]{0:T(128)} %pad_add_fusion.1.pick_hid, bf16[8,4,128,128]{3,2,1,0:T(8,128)(2,1)} %tiles.5, bf16[1024,128]{1,0:T(8,128)(2,1)} %get-tuple-element.38.grad, ...), custom_call_target="tpu_custom_call" | custom-call | tf_op jit(solution)/shard_map/grads_kernel/pallas_call | solution.py:247
  96.3 1.8 %collective-permute-done.24 = bf16[128,1152]{1,0:T(8,128)(2,1)S(1)} collective-permute-done((bf16[128,1152]{1,0:T(8,128)(2,1)}, bf16[128,1152]{1,0:T(8,128)(2,1)S(1)}, u32[]{:S(2)}, u32[]{:S(2)}) %collective-permute-start.24) | collective-permute-done | bytes 294944 | tf_op jit(solution)/shard_map/ppermute | solution.py:347
  98.1 1.1 add_convert_fusion
  99.3 25.3 %all_to_all.10 = bf16[32,4,1152]{2,1,0:T(4,128)(2,1)S(1)} all-to-all(bf16[32,4,1152]{2,1,0:T(4,128)(2,1)S(1)} %reshape.15), channel_id=1, replica_groups=mesh['z'=8,'core'=2,'gy'=4,'af'=4] {'z','gy'}, dimensions={0} | all-to-all | bytes 589824 | tf_op jit(solution)/shard_map/all_to_all | solution.py:349
  124.9 15.2 %all_to_all.11 = bf16[32,4,1152]{2,1,0:T(4,128)(2,1)S(1)} all-to-all(bf16[32,4,1152]{2,1,0:T(4,128)(2,1)S(1)} %broadcast_in_dim.2), channel_id=1, replica_groups=mesh['z'=8,'core'=2,'gy'=4,'af'=4] {'z','gy'}, dimensions={0} | all-to-all | bytes 589824 | tf_op jit(solution)/shard_map/all_to_all | solution.py:351
  140.2 3.7 %collective-permute-start.25 = (bf16[128,1152]{1,0:T(8,128)(2,1)S(1)}, bf16[128,1152]{1,0:T(8,128)(2,1)S(1)}, u32[]{:S(2)}, u32[]{:S(2)}) collective-permute-start(bf16[128,1152]{1,0:T(8,128)(2,1)S(1)} %reshape.16), channel_id=1, source_target_pairs={{0,16},{16,0},{1,17},{17,1},{2,18},{18,2},{3,19},{19,3},{4,20},{20... | collective-permute-start | bytes 884744 | tf_op jit(solution)/shard_map/ppermute | solution.py:354
  143.9 1.2 collective-permute-done.25
  145.1 0.7 maximum_convert_fusion.1
  145.9 1.1 slice.8
  (71 shorter events, 0.7 us)
Async XLA Ops:
  5.6 9.9 %collective-permute-start = (bf16[384,256]{1,0:T(8,128)(2,1)}, bf16[384,256]{1,0:T(8,128)(2,1)S(1)}, u32[]{:S(2)}, u32[]{:S(2)}) collective-permute-start(bf16[384,256]{1,0:T(8,128)(2,1)} %get-tuple-element.25), channel_id=1, source_target_pairs={{0,16},{16,0},{1,17},{17,1},{2,18},{18,2},{3,19},{19,3},{4,20},{20... | collective-permute-start | bytes 589832 | tf_op jit(solution)/shard_map/ppermute | solution.py:37
  8.8 20.2 %collective-permute-start.12 = (bf16[128,1152]{1,0:T(8,128)(2,1)}, bf16[128,1152]{1,0:T(8,128)(2,1)S(1)}, u32[]{:S(2)}, u32[]{:S(2)}) collective-permute-start(bf16[128,1152]{1,0:T(8,128)(2,1)} %get-tuple-element.31.m0), channel_id=1, source_target_pairs={{0,3},{1,0},{2,1},{3,2},{4,7},{5,4},{6,5},{7,6},{8,11},{9,8},{10,9... | collective-permute-start | bytes 884744 | tf_op jit(solution)/shard_map/ppermute | solution.py:24
  9.8 21.9 %collective-permute-start.11 = (bf16[128,1152]{1,0:T(8,128)(2,1)}, bf16[128,1152]{1,0:T(8,128)(2,1)S(1)}, u32[]{:S(2)}, u32[]{:S(2)}) collective-permute-start(bf16[128,1152]{1,0:T(8,128)(2,1)} %get-tuple-element.31.m0), channel_id=1, source_target_pairs={{0,2},{1,3},{2,0},{3,1},{4,6},{5,7},{6,4},{7,5},{8,10},{9,11},{10,... | collective-permute-start | bytes 884744 | tf_op jit(solution)/shard_map/ppermute | solution.py:24
  10.2 7.9 %collective-permute-start.1 = (bf16[384,256]{1,0:T(8,128)(2,1)}, bf16[384,256]{1,0:T(8,128)(2,1)S(1)}, u32[]{:S(2)}, u32[]{:S(2)}) collective-permute-start(bf16[384,256]{1,0:T(8,128)(2,1)} %get-tuple-element.26), channel_id=1, source_target_pairs={{16,32},{32,16},{48,64},{64,48},{80,96},{96,80},{112,128},{128,112... | collective-permute-start | bytes 589832 | tf_op jit(solution)/shard_map/ppermute | solution.py:38
  14.2 5.6 %collective-permute-start.2 = (bf16[384,256]{1,0:T(8,128)(2,1)}, bf16[384,256]{1,0:T(8,128)(2,1)S(1)}, u32[]{:S(2)}, u32[]{:S(2)}) collective-permute-start(bf16[384,256]{1,0:T(8,128)(2,1)} %get-tuple-element.27), channel_id=1, source_target_pairs={{0,4},{4,0},{8,12},{12,8},{1,5},{5,1},{9,13},{13,9},{2,6},{6,2},{1... | collective-permute-start | bytes 589832 | tf_op jit(solution)/shard_map/ppermute | solution.py:39
  15.5 4.3 %copy-start.12 = (bf16[384,256]{1,0:T(8,128)(2,1)}, bf16[384,256]{1,0:T(8,128)(2,1)S(1)}, u32[]{:S(2)}) copy-start(bf16[384,256]{1,0:T(8,128)(2,1)S(1)} %collective-permute-done.r0) | copy-start | bytes 589828
  15.5 4.3 %collective-permute-start.3 = (bf16[384,256]{1,0:T(8,128)(2,1)}, bf16[384,256]{1,0:T(8,128)(2,1)S(1)}, u32[]{:S(2)}, u32[]{:S(2)}) collective-permute-start(bf16[384,256]{1,0:T(8,128)(2,1)} %get-tuple-element.28), channel_id=1, source_target_pairs={{4,8},{8,4},{5,9},{9,5},{6,10},{10,6},{7,11},{11,7},{20,24},{24,20... | collective-permute-start | bytes 589832 | tf_op jit(solution)/shard_map/ppermute | solution.py:40
  18.0 1.8 %copy-start.13 = (bf16[384,256]{1,0:T(8,128)(2,1)}, bf16[384,256]{1,0:T(8,128)(2,1)S(1)}, u32[]{:S(2)}) copy-start(bf16[384,256]{1,0:T(8,128)(2,1)S(1)} %collective-permute-done.1.r1) | copy-start | bytes 589828
  18.0 13.7 %collective-permute-start.10 = (bf16[128,1152]{1,0:T(8,128)(2,1)}, bf16[128,1152]{1,0:T(8,128)(2,1)S(1)}, u32[]{:S(2)}, u32[]{:S(2)}) collective-permute-start(bf16[128,1152]{1,0:T(8,128)(2,1)} %get-tuple-element.31.m0), channel_id=1, source_target_pairs={{0,1},{1,2},{2,3},{3,0},{4,5},{5,6},{6,7},{7,4},{8,9},{9,10},{10,1... | collective-permute-start | bytes 884744 | tf_op jit(solution)/shard_map/ppermute | solution.py:24
  19.8 0.7 copy-start.14
  20.5 0.7 copy-start.15
  26.7 8.7 %collective-permute-start.6 = (bf16[512,256]{1,0:T(8,128)(2,1)}, bf16[512,256]{1,0:T(8,128)(2,1)S(1)}, u32[]{:S(2)}, u32[]{:S(2)}) collective-permute-start(bf16[512,256]{1,0:T(8,128)(2,1)} %get-tuple-element.29.own_t.top), channel_id=1, source_target_pairs={{0,3},{1,0},{2,1},{3,2},{4,7},{5,4},{6,5},{7,6},{8,11},{9,8},{10,9... | collective-permute-start | bytes 786440 | tf_op jit(solution)/shard_map/ppermute | solution.py:24
  29.0 9.7 %collective-permute-start.4 = (bf16[512,256]{1,0:T(8,128)(2,1)}, bf16[512,256]{1,0:T(8,128)(2,1)S(1)}, u32[]{:S(2)}, u32[]{:S(2)}) collective-permute-start(bf16[512,256]{1,0:T(8,128)(2,1)} %get-tuple-element.29.own_t.top), channel_id=1, source_target_pairs={{0,1},{1,2},{2,3},{3,0},{4,5},{5,6},{6,7},{7,4},{8,9},{9,10},{10,1... | collective-permute-start | bytes 786440 | tf_op jit(solution)/shard_map/ppermute | solution.py:24
  29.0 22.7 %copy-start = (bf16[128,1152]{1,0:T(8,128)(2,1)}, bf16[128,1152]{1,0:T(8,128)(2,1)S(1)}, u32[]{:S(2)}) copy-start(bf16[128,1152]{1,0:T(8,128)(2,1)S(1)} %collective-permute-done.12.m3) | copy-start | bytes 884740
  29.0 11.8 %collective-permute-start.7 = (bf16[512,256]{1,0:T(8,128)(2,1)}, bf16[512,256]{1,0:T(8,128)(2,1)S(1)}, u32[]{:S(2)}, u32[]{:S(2)}) collective-permute-start(bf16[512,256]{1,0:T(8,128)(2,1)} %get-tuple-element.30.own_b.bottom), channel_id=1, source_target_pairs={{0,3},{1,0},{2,1},{3,2},{4,7},{5,4},{6,5},{7,6},{8,11},{9,8},{10,9... | collective-permute-start | bytes 786440 | tf_op jit(solution)/shard_map/ppermute | solution.py:24
  31.7 20.0 %copy-start.1 = (bf16[128,1152]{1,0:T(8,128)(2,1)}, bf16[128,1152]{1,0:T(8,128)(2,1)S(1)}, u32[]{:S(2)}) copy-start(bf16[128,1152]{1,0:T(8,128)(2,1)S(1)} %collective-permute-done.11.m2) | copy-start | bytes 884740
  31.7 12.6 %collective-permute-start.5 = (bf16[512,256]{1,0:T(8,128)(2,1)}, bf16[512,256]{1,0:T(8,128)(2,1)S(1)}, u32[]{:S(2)}, u32[]{:S(2)}) collective-permute-start(bf16[512,256]{1,0:T(8,128)(2,1)} %get-tuple-element.30.own_b.bottom), channel_id=1, source_target_pairs={{0,1},{1,2},{2,3},{3,0},{4,5},{5,6},{6,7},{7,4},{8,9},{9,10},{10,1... | collective-permute-start | bytes 786440 | tf_op jit(solution)/shard_map/ppermute | solution.py:24
  31.7 20.0 %copy-start.2 = (bf16[128,1152]{1,0:T(8,128)(2,1)}, bf16[128,1152]{1,0:T(8,128)(2,1)S(1)}, u32[]{:S(2)}) copy-start(bf16[128,1152]{1,0:T(8,128)(2,1)S(1)} %collective-permute-done.10.m1) | copy-start | bytes 884740
  31.7 12.6 %collective-permute-start.15 = (bf16[128,1152]{1,0:T(8,128)(2,1)S(1)}, bf16[128,1152]{1,0:T(8,128)(2,1)S(1)}, u32[]{:S(2)}, u32[]{:S(2)}) collective-permute-start(bf16[128,1152]{1,0:T(8,128)(2,1)S(1)} %collective-permute-done.12.m3), channel_id=1, source_target_pairs={{0,16},{16,0},{1,17},{17,1},{2,18},{18,2},{3,19},{19,3},{4,20},{20... | collective-permute-start | bytes 884744 | tf_op jit(solution)/shard_map/ppermute | solution.py:296
  35.4 16.2 %copy-start.6 = (bf16[512,256]{1,0:T(8,128)(2,1)}, bf16[512,256]{1,0:T(8,128)(2,1)S(1)}, u32[]{:S(2)}) copy-start(bf16[512,256]{1,0:T(8,128)(2,1)S(1)} %collective-permute-done.6.hi_t) | copy-start | bytes 786436
  35.4 8.9 %collective-permute-start.14 = (bf16[128,1152]{1,0:T(8,128)(2,1)S(1)}, bf16[128,1152]{1,0:T(8,128)(2,1)S(1)}, u32[]{:S(2)}, u32[]{:S(2)}) collective-permute-start(bf16[128,1152]{1,0:T(8,128)(2,1)S(1)} %collective-permute-done.11.m2), channel_id=1, source_target_pairs={{0,16},{16,0},{1,17},{17,1},{2,18},{18,2},{3,19},{19,3},{4,20},{20... | collective-permute-start | bytes 884744 | tf_op jit(solution)/shard_map/ppermute | solution.py:296
  38.7 13.0 %copy-start.7 = (bf16[512,256]{1,0:T(8,128)(2,1)}, bf16[512,256]{1,0:T(8,128)(2,1)S(1)}, u32[]{:S(2)}) copy-start(bf16[512,256]{1,0:T(8,128)(2,1)S(1)} %collective-permute-done.4.lo_t) | copy-start | bytes 786436
  38.7 5.7 %collective-permute-start.13 = (bf16[128,1152]{1,0:T(8,128)(2,1)S(1)}, bf16[128,1152]{1,0:T(8,128)(2,1)S(1)}, u32[]{:S(2)}, u32[]{:S(2)}) collective-permute-start(bf16[128,1152]{1,0:T(8,128)(2,1)S(1)} %collective-permute-done.10.m1), channel_id=1, source_target_pairs={{0,16},{16,0},{1,17},{17,1},{2,18},{18,2},{3,19},{19,3},{4,20},{20... | collective-permute-start | bytes 884744 | tf_op jit(solution)/shard_map/ppermute | solution.py:296
  40.9 10.8 %copy-start.8 = (bf16[512,256]{1,0:T(8,128)(2,1)}, bf16[512,256]{1,0:T(8,128)(2,1)S(1)}, u32[]{:S(2)}) copy-start(bf16[512,256]{1,0:T(8,128)(2,1)S(1)} %collective-permute-done.7.hi_b) | copy-start | bytes 786436
  40.9 9.4 %collective-permute-start.8 = (bf16[512,256]{1,0:T(8,128)(2,1)S(1)}, bf16[512,256]{1,0:T(8,128)(2,1)S(1)}, u32[]{:S(2)}, u32[]{:S(2)}) collective-permute-start(bf16[512,256]{1,0:T(8,128)(2,1)S(1)} %collective-permute-done.4.lo_t), channel_id=1, source_target_pairs={{0,1},{1,2},{2,3},{3,0},{4,5},{5,6},{6,7},{7,4},{8,9},{9,10},{10,1... | collective-permute-start | bytes 786440 | tf_op jit(solution)/shard_map/ppermute | solution.py:24
  44.3 7.4 %copy-start.9 = (bf16[512,256]{1,0:T(8,128)(2,1)}, bf16[512,256]{1,0:T(8,128)(2,1)S(1)}, u32[]{:S(2)}) copy-start(bf16[512,256]{1,0:T(8,128)(2,1)S(1)} %collective-permute-done.5.lo_b) | copy-start | bytes 786436
  44.3 7.4 %collective-permute-start.9 = (bf16[512,256]{1,0:T(8,128)(2,1)S(1)}, bf16[512,256]{1,0:T(8,128)(2,1)S(1)}, u32[]{:S(2)}, u32[]{:S(2)}) collective-permute-start(bf16[512,256]{1,0:T(8,128)(2,1)S(1)} %collective-permute-done.7.hi_b), channel_id=1, source_target_pairs={{0,3},{1,0},{2,1},{3,2},{4,7},{5,4},{6,5},{7,6},{8,11},{9,8},{10,9... | collective-permute-start | bytes 786440 | tf_op jit(solution)/shard_map/ppermute | solution.py:24
  44.3 7.4 %copy-start.3 = (bf16[128,1152]{1,0:T(8,128)(2,1)}, bf16[128,1152]{1,0:T(8,128)(2,1)S(1)}, u32[]{:S(2)}) copy-start(bf16[128,1152]{1,0:T(8,128)(2,1)S(1)} %collective-permute-done.15.v3) | copy-start | bytes 884740
  44.3 7.4 %copy-start.4 = (bf16[128,1152]{1,0:T(8,128)(2,1)}, bf16[128,1152]{1,0:T(8,128)(2,1)S(1)}, u32[]{:S(2)}) copy-start(bf16[128,1152]{1,0:T(8,128)(2,1)S(1)} %collective-permute-done.14.v2) | copy-start | bytes 884740
  44.3 7.4 %copy-start.5 = (bf16[128,1152]{1,0:T(8,128)(2,1)}, bf16[128,1152]{1,0:T(8,128)(2,1)S(1)}, u32[]{:S(2)}) copy-start(bf16[128,1152]{1,0:T(8,128)(2,1)S(1)} %collective-permute-done.13.v1) | copy-start | bytes 884740
  50.3 1.5 %copy-start.10 = (bf16[512,256]{1,0:T(8,128)(2,1)}, bf16[512,256]{1,0:T(8,128)(2,1)S(1)}, u32[]{:S(2)}) copy-start(bf16[512,256]{1,0:T(8,128)(2,1)S(1)} %collective-permute-done.8.far_t) | copy-start | bytes 786436
  51.7 0.7 copy-start.11
  61.8 7.5 %collective-permute-start.16 = (bf16[384,128]{1,0:T(8,128)(2,1)}, bf16[384,128]{1,0:T(8,128)(2,1)S(1)}, u32[]{:S(2)}, u32[]{:S(2)}) collective-permute-start(bf16[384,128]{1,0:T(8,128)(2,1)} %get-tuple-element.34), channel_id=1, source_target_pairs={{0,16},{16,0},{1,17},{17,1},{2,18},{18,2},{3,19},{19,3},{4,20},{20... | collective-permute-start | bytes 294920 | tf_op jit(solution)/shard_map/ppermute | solution.py:37
  63.2 6.1 %collective-permute-start.17 = (bf16[384,128]{1,0:T(8,128)(2,1)}, bf16[384,128]{1,0:T(8,128)(2,1)S(1)}, u32[]{:S(2)}, u32[]{:S(2)}) collective-permute-start(bf16[384,128]{1,0:T(8,128)(2,1)} %get-tuple-element.35), channel_id=1, source_target_pairs={{16,32},{32,16},{48,64},{64,48},{80,96},{96,80},{112,128},{128,112... | collective-permute-start | bytes 294920 | tf_op jit(solution)/shard_map/ppermute | solution.py:38
  65.5 5.4 %collective-permute-start.18 = (bf16[384,128]{1,0:T(8,128)(2,1)}, bf16[384,128]{1,0:T(8,128)(2,1)S(1)}, u32[]{:S(2)}, u32[]{:S(2)}) collective-permute-start(bf16[384,128]{1,0:T(8,128)(2,1)} %get-tuple-element.36), channel_id=1, source_target_pairs={{0,4},{4,0},{8,12},{12,8},{1,5},{5,1},{9,13},{13,9},{2,6},{6,2},{1... | collective-permute-start | bytes 294920 | tf_op jit(solution)/shard_map/ppermute | solution.py:39
  68.6 2.2 %collective-permute-start.19 = (bf16[384,128]{1,0:T(8,128)(2,1)}, bf16[384,128]{1,0:T(8,128)(2,1)S(1)}, u32[]{:S(2)}, u32[]{:S(2)}) collective-permute-start(bf16[384,128]{1,0:T(8,128)(2,1)} %get-tuple-element.37), channel_id=1, source_target_pairs={{4,8},{8,4},{5,9},{9,5},{6,10},{10,6},{7,11},{11,7},{20,24},{24,20... | collective-permute-start | bytes 294920 | tf_op jit(solution)/shard_map/ppermute | solution.py:40
  69.3 1.5 %copy-start.20 = (bf16[384,128]{1,0:T(8,128)(2,1)}, bf16[384,128]{1,0:T(8,128)(2,1)S(1)}, u32[]{:S(2)}) copy-start(bf16[384,128]{1,0:T(8,128)(2,1)S(1)} %collective-permute-done.16.r0) | copy-start | bytes 294916
  69.3 1.5 %copy-start.21 = (bf16[384,128]{1,0:T(8,128)(2,1)}, bf16[384,128]{1,0:T(8,128)(2,1)S(1)}, u32[]{:S(2)}) copy-start(bf16[384,128]{1,0:T(8,128)(2,1)S(1)} %collective-permute-done.17.r1) | copy-start | bytes 294916
  70.9 0.7 copy-start.23
  77.9 9.3 %collective-permute-start.20 = (bf16[384,128]{1,0:T(8,128)(2,1)}, bf16[384,128]{1,0:T(8,128)(2,1)S(1)}, u32[]{:S(2)}, u32[]{:S(2)}) collective-permute-start(bf16[384,128]{1,0:T(8,128)(2,1)} %get-tuple-element.39), channel_id=1, source_target_pairs={{0,16},{16,0},{1,17},{17,1},{2,18},{18,2},{3,19},{19,3},{4,20},{20... | collective-permute-start | bytes 294920 | tf_op jit(solution)/shard_map/ppermute | solution.py:37
  77.9 9.3 %collective-permute-start.21 = (bf16[384,128]{1,0:T(8,128)(2,1)}, bf16[384,128]{1,0:T(8,128)(2,1)S(1)}, u32[]{:S(2)}, u32[]{:S(2)}) collective-permute-start(bf16[384,128]{1,0:T(8,128)(2,1)} %get-tuple-element.40), channel_id=1, source_target_pairs={{16,32},{32,16},{48,64},{64,48},{80,96},{96,80},{112,128},{128,112... | collective-permute-start | bytes 294920 | tf_op jit(solution)/shard_map/ppermute | solution.py:38
  82.2 5.8 %collective-permute-start.22 = (bf16[384,128]{1,0:T(8,128)(2,1)}, bf16[384,128]{1,0:T(8,128)(2,1)S(1)}, u32[]{:S(2)}, u32[]{:S(2)}) collective-permute-start(bf16[384,128]{1,0:T(8,128)(2,1)} %get-tuple-element.41), channel_id=1, source_target_pairs={{0,4},{4,0},{8,12},{12,8},{1,5},{5,1},{9,13},{13,9},{2,6},{6,2},{1... | collective-permute-start | bytes 294920 | tf_op jit(solution)/shard_map/ppermute | solution.py:39
  85.7 2.2 %collective-permute-start.23 = (bf16[384,128]{1,0:T(8,128)(2,1)}, bf16[384,128]{1,0:T(8,128)(2,1)S(1)}, u32[]{:S(2)}, u32[]{:S(2)}) collective-permute-start(bf16[384,128]{1,0:T(8,128)(2,1)} %get-tuple-element.42), channel_id=1, source_target_pairs={{4,8},{8,4},{5,9},{9,5},{6,10},{10,6},{7,11},{11,7},{20,24},{24,20... | collective-permute-start | bytes 294920 | tf_op jit(solution)/shard_map/ppermute | solution.py:40
  87.2 0.7 copy-start.16
  87.2 0.7 copy-start.17
  87.9 0.7 copy-start.19
  96.3 1.8 %collective-permute-start.24 = (bf16[128,1152]{1,0:T(8,128)(2,1)}, bf16[128,1152]{1,0:T(8,128)(2,1)S(1)}, u32[]{:S(2)}, u32[]{:S(2)}) collective-permute-start(bf16[128,1152]{1,0:T(8,128)(2,1)} %get-tuple-element.47), channel_id=1, source_target_pairs={{0,16},{16,0},{1,17},{17,1},{2,18},{18,2},{3,19},{19,3},{4,20},{20... | collective-permute-start | bytes 884744 | tf_op jit(solution)/shard_map/ppermute | solution.py:347
  140.2 4.9 %collective-permute-start.25 = (bf16[128,1152]{1,0:T(8,128)(2,1)S(1)}, bf16[128,1152]{1,0:T(8,128)(2,1)S(1)}, u32[]{:S(2)}, u32[]{:S(2)}) collective-permute-start(bf16[128,1152]{1,0:T(8,128)(2,1)S(1)} %reshape.16), channel_id=1, source_target_pairs={{0,16},{16,0},{1,17},{17,1},{2,18},{18,2},{3,19},{19,3},{4,20},{20... | collective-permute-start | bytes 884744 | tf_op jit(solution)/shard_map/ppermute | solution.py:354
  (2 other events, 1.3 us)

commit v5 on v4

--- a/solution.py
+++ b/solution.py
@@ -203,10 +203,10 @@
 
 
 def grads_kernel(
-    meta, col, counts, pick_hid, tiles, grad, t0, t1, t2, t3, send, w_cls, slope, top, bottom,
+    meta, col, counts, tiles, grad, t0, t1, t2, t3, send, w_cls, slope, top, bottom,
     units_m, units_o, theirs, mine, hot, back, acc, mix, pre,
 ):
-    nodes, classes = grad.shape
+    nodes, _ = grad.shape
     slots, tb, kt = send.shape[1], tiles.shape[2], tiles.shape[1]
     hid = slope.shape[1]
     for m, (d, returned) in enumerate(zip(send_order(meta), (t0, t1, t2, t3))):
@@ -238,6 +238,14 @@
     theirs[:, hid:] = dot(units_o[0], mix[...], 0, 0).astype(BF)
 
 
+def join_kernel(meta, mine, other, grad_hidden, grad_classes):
+    half, hid = mine.shape[0], grad_hidden.shape[1]
+    for ref, part in ((mine, meta[0]), (other, 1 - meta[0])):
+        at = pl.ds(pl.multiple_of(part * half, half), half)
+        grad_hidden[at, :] = ref[:, :hid].astype(F32)
+        grad_classes[at, :] = ref[:, hid:].astype(F32)
+
+
 def call(kernel, scalars, arrays, outs, scratch, specs=None):
     def whole(x):
         return pl.BlockSpec(x.shape, lambda *_, n=len(x.shape): (0,) * n)
@@ -255,11 +263,10 @@
         ),
         out_shape=outs,
         interpret=INTERPRET,
-        name=kernel.__name__,
     )(*scalars, *arrays)
 
 
-def local(
+def work(
     features,
     adj_tiles,
     col_block,
@@ -293,7 +300,7 @@
     )
     arrived = trade(out)
     w_mine = [w_mine] + [turn(w_mine, "af", k) for k in range(1, n_af)]
-    w_other = [w_other] + [lax.ppermute(w, "core", swap) for w in w_mine[1:]]
+    w_other = [w_other] + [lax.ppermute(w_mine[k], "core", swap) for k in range(1, n_af)]
     top, bottom = call(
         mix_kernel,
         (meta, col_block),
@@ -326,10 +333,9 @@
         [((nodes, 4 * slots), BF), ((4 * slots, 2 * classes), BF), ((slots, nodes), BF)],
     )
     returned = trade(out)
-    pick_hid = jnp.stack([af * 2 + core, af * 2 + 1 - core]).astype(jnp.int32)
     theirs, mine = call(
         grads_kernel,
-        (meta, col_block, send_counts, pick_hid),
+        (meta, col_block, send_counts),
         (adj_tiles, grad, *returned, send_rows, w_cls, slope, top, bottom, hidden, hidden),
         [((half, both), BF), ((half, both), F32)],
         [
@@ -340,8 +346,8 @@
             ((nodes, hid), BF),
         ],
         {
-            11: pl.BlockSpec((1, nodes, LANES), lambda i, a, b, c, s: (s[0], 0, 0)),
-            12: pl.BlockSpec((1, nodes, LANES), lambda i, a, b, c, s: (s[1], 0, 0)),
+            11: pl.BlockSpec((1, nodes, LANES), lambda i, m, c, n: (m[2] * 2 + m[0], 0, 0)),
+            12: pl.BlockSpec((1, nodes, LANES), lambda i, m, c, n: (m[2] * 2 + 1 - m[0], 0, 0)),
         },
     )
     total = mine + lax.ppermute(theirs, "core", swap).astype(F32)
@@ -352,10 +358,14 @@
         jnp.broadcast_to(piece[None], (n_plane,) + piece.shape), PLANE, 0, 0, tiled=True
     ).reshape(half, both)
     other = lax.ppermute(mine, "core", swap)
-    first = jnp.where(core == 0, mine, other)
-    second = jnp.where(core == 0, other, mine)
-    whole = jnp.concatenate([first, second], axis=0).astype(F32)
-    return (whole[:, :hid], whole[:, hid:])
+    grad_hidden, grad_classes = call(
+        join_kernel,
+        (meta,),
+        (mine, other),
+        [((2 * half, hid), F32), ((2 * half, classes), F32)],
+        [],
+    )
+    return (grad_hidden, grad_classes)
 
 
 def solution(mesh):
@@ -377,5 +387,9 @@
         P("af", None),
     )
     return jax.shard_map(
-        local, mesh=split, in_specs=placed, out_specs=(P("af", None), P("af", None)), check_vma=False
-    )
+        work,
+        mesh=split,
+        in_specs=placed,
+        out_specs=(P("af", None), P("af", None)),
+        check_vma=False,
+    )

time: 148 us -> 149 us (level)
  Pallas kernels: 33.4 us -> 36.3 us
    pallas_call x5 -> x6, Pallas kernels: 33.4 us -> 36.3 us  [call(): pl.pallas_call(kernel, grid_spec=pltpu.PrefetchScalarGridSpec(num_scalar_...]
    unnamed x49 -> x53, local copies, waits for them, and re-layouts: 4.71 us -> 5.42 us
where the time goes in v5:
time: 149 us
  blocking collectives  40.5 us (27%)
  starting transfers between devices  36.6 us (25%)
  Pallas kernels  36.3 us (24%)
  waiting for transfers between devices  26.8 us (18%)
  local copies, waits for them, and re-layouts  5.65 us (4%)
  other arithmetic  1.88 us (1%)
    pallas_call x6, Pallas kernels, call(): pl.pallas_call(kernel, grid_spec=pltpu.PrefetchScalarGridSpec(num_scalar_...  36.3 us
    all_to_all x1, blocking collectives, work(): pieces = lax.all_to_all(pieces, PLANE, 0, 0, tiled=True)  25.3 us
    ppermute x9, waiting for transfers between devices, turn(): lax.ppermute(field, axis, [(i, (i + move) % count) for i in range(count)])  19.1 us
    all_to_all x1, blocking collectives, work(): lax.all_to_all(jnp.broadcast_to(piece[None], (n_plane,) + piece.shape), P...  15.2 us
    ppermute x3, starting transfers between devices, trade(): lax.ppermute(fields[1], ROWS, pairs_at(rows, 1))  10.5 us
    ppermute x3, starting transfers between devices, trade(): lax.ppermute(fields[2], 'gy', pairs_at(cols, 0))  8.05 us
    ppermute x9, starting transfers between devices, turn(): lax.ppermute(field, axis, [(i, (i + move) % count) for i in range(count)])  6.74 us
    unnamed x53, local copies, waits for them, and re-layouts  5.42 us
  transfers between devices with their start and end apart: 26, of which 11 were waited for; matrix products, arithmetic and copies ran while one was open for 1% of the time, Pallas kernels for 4%

profile of v5, /device:TPU:1, one launch (start us, length us, event | category | flops | bytes accessed | tf_op | source)
XLA Modules:
  0.0 148.7 jit_solution(14899816083948819760)
XLA Ops:
  0.6 0.6 pad_add_fusion.meta
  1.2 4.4 %shard_map.113 = (bf16[384,256]{1,0:T(8,128)(2,1)}, bf16[384,256]{1,0:T(8,128)(2,1)}, bf16[384,256]{1,0:T(8,128)(2,1)}, bf16[384,256]{1,0:T(8,128)(2,1)}, bf16[1...) custom-call(s32[3]{0:T(128)} %pad_add_fusion.meta, s32[4]{0:T(128)} %counts.5, bf16[1024,256]{1,0:T(8,128)(2,1)} %feat.3, ...), custom_call_target="tpu_custom_call" | custom-call | tf_op jit(solution)/shard_map/pallas_call | solution.py:255
  5.6 3.2 %collective-permute-start = (bf16[384,256]{1,0:T(8,128)(2,1)}, bf16[384,256]{1,0:T(8,128)(2,1)S(1)}, u32[]{:S(2)}, u32[]{:S(2)}) collective-permute-start(bf16[384,256]{1,0:T(8,128)(2,1)} %get-tuple-element.25), channel_id=1, source_target_pairs={{0,16},{16,0},{1,17},{17,1},{2,18},{18,2},{3,19},{19,3},{4,20},{20... | collective-permute-start | bytes 589832 | tf_op jit(solution)/shard_map/ppermute | solution.py:37
  8.8 1.0 collective-permute-start.12
  9.8 0.3 collective-permute-start.11
  10.2 4.0 %collective-permute-start.1 = (bf16[384,256]{1,0:T(8,128)(2,1)}, bf16[384,256]{1,0:T(8,128)(2,1)S(1)}, u32[]{:S(2)}, u32[]{:S(2)}) collective-permute-start(bf16[384,256]{1,0:T(8,128)(2,1)} %get-tuple-element.26), channel_id=1, source_target_pairs={{16,32},{32,16},{48,64},{64,48},{80,96},{96,80},{112,128},{128,112... | collective-permute-start | bytes 589832 | tf_op jit(solution)/shard_map/ppermute | solution.py:38
  14.2 1.3 collective-permute-start.2
  15.5 0.7 collective-permute-start.3
  16.2 1.9 %collective-permute-done.1.r1 = bf16[384,256]{1,0:T(8,128)(2,1)S(1)} collective-permute-done((bf16[384,256]{1,0:T(8,128)(2,1)}, bf16[384,256]{1,0:T(8,128)(2,1)S(1)}, u32[]{:S(2)}, u32[]{:S(2)}) %collective-permute-start.1) | collective-permute-done | bytes 196640 | tf_op jit(solution)/shard_map/ppermute | solution.py:38
  18.0 0.4 collective-permute-start.10
  18.4 1.3 copy.14.col
  19.8 0.7 copy-done.16
  20.5 0.7 copy-done.17
  21.2 5.6 %shard_map.114 = (bf16[512,256]{1,0:T(8,128)(2,1)}, bf16[512,256]{1,0:T(8,128)(2,1)}) custom-call(s32[3]{0:T(128)} %pad_add_fusion.meta, s32[8,4]{1,0:T(8,128)} %copy.14.col, bf16[1024,256]{1,0:T(8,128)(2,1)} %feat.3, bf16[8,4,128,128]{3,2,1,0:T(8,128)(2,1)} %tiles.5, bf16[384,256]{1,0:T(8,128)(2,1)} %copy-done.14, bf16[384,256]{1,0:T(8,128)(2,1)} %copy-done.15, ...), custom_call_target="tpu_custom_call" | custom-call | tf_op jit(solution)/shard_map/pallas_call | solution.py:255
  26.7 2.3 %collective-permute-start.6 = (bf16[512,256]{1,0:T(8,128)(2,1)}, bf16[512,256]{1,0:T(8,128)(2,1)S(1)}, u32[]{:S(2)}, u32[]{:S(2)}) collective-permute-start(bf16[512,256]{1,0:T(8,128)(2,1)} %get-tuple-element.29.own_t.top), channel_id=1, source_target_pairs={{0,3},{1,0},{2,1},{3,2},{4,7},{5,4},{6,5},{7,6},{8,11},{9,8},{10,9... | collective-permute-start | bytes 786440 | tf_op jit(solution)/shard_map/ppermute | solution.py:24
  29.0 2.7 %collective-permute-start.7 = (bf16[512,256]{1,0:T(8,128)(2,1)}, bf16[512,256]{1,0:T(8,128)(2,1)S(1)}, u32[]{:S(2)}, u32[]{:S(2)}) collective-permute-start(bf16[512,256]{1,0:T(8,128)(2,1)} %get-tuple-element.30.own_b.bottom), channel_id=1, source_target_pairs={{0,3},{1,0},{2,1},{3,2},{4,7},{5,4},{6,5},{7,6},{8,11},{9,8},{10,9... | collective-permute-start | bytes 786440 | tf_op jit(solution)/shard_map/ppermute | solution.py:24
  31.7 0.3 collective-permute-start.15
  32.0 3.5 %collective-permute-done.6.hi_t = bf16[512,256]{1,0:T(8,128)(2,1)S(1)} collective-permute-done((bf16[512,256]{1,0:T(8,128)(2,1)}, bf16[512,256]{1,0:T(8,128)(2,1)S(1)}, u32[]{:S(2)}, u32[]{:S(2)}) %collective-permute-start.6) | collective-permute-done | bytes 262176 | tf_op jit(solution)/shard_map/ppermute | solution.py:24
  35.5 3.2 %collective-permute-done.4.lo_t = bf16[512,256]{1,0:T(8,128)(2,1)S(1)} collective-permute-done((bf16[512,256]{1,0:T(8,128)(2,1)}, bf16[512,256]{1,0:T(8,128)(2,1)S(1)}, u32[]{:S(2)}, u32[]{:S(2)}) %collective-permute-start.4) | collective-permute-done | bytes 262176 | tf_op jit(solution)/shard_map/ppermute | solution.py:24
  38.7 0.5 collective-permute-start.13
  39.2 1.6 %collective-permute-done.7.hi_b = bf16[512,256]{1,0:T(8,128)(2,1)S(1)} collective-permute-done((bf16[512,256]{1,0:T(8,128)(2,1)}, bf16[512,256]{1,0:T(8,128)(2,1)S(1)}, u32[]{:S(2)}, u32[]{:S(2)}) %collective-permute-start.7) | collective-permute-done | bytes 262176 | tf_op jit(solution)/shard_map/ppermute | solution.py:24
  40.9 3.4 %collective-permute-done.5.lo_b = bf16[512,256]{1,0:T(8,128)(2,1)S(1)} collective-permute-done((bf16[512,256]{1,0:T(8,128)(2,1)}, bf16[512,256]{1,0:T(8,128)(2,1)S(1)}, u32[]{:S(2)}, u32[]{:S(2)}) %collective-permute-start.5) | collective-permute-done | bytes 262176 | tf_op jit(solution)/shard_map/ppermute | solution.py:24
  44.4 5.9 %collective-permute-done.8.far_t = bf16[512,256]{1,0:T(8,128)(2,1)S(1)} collective-permute-done((bf16[512,256]{1,0:T(8,128)(2,1)S(1)}, bf16[512,256]{1,0:T(8,128)(2,1)S(1)}, u32[]{:S(2)}, u32[]{:S(2)}) %collective-permute-start.8) | collective-permute-done | bytes 262176 | tf_op jit(solution)/shard_map/ppermute | solution.py:24
  50.3 1.4 collective-permute-done.9.far_b
  51.8 0.6 copy-done.13
  52.4 9.4 %shard_map.115 = (bf16[8,1024,128]{2,1,0:T(8,128)(2,1)}, bf16[1024,1024]{1,0:T(8,128)(2,1)}, bf16[1024,256]{1,0:T(8,128)(2,1)}, bf16[1024,128]{1,0:T(8,128)(2,1)...) custom-call(s32[3]{0:T(128)} %pad_add_fusion.meta, ...), custom_call_target="tpu_custom_call" | custom-call | tf_op jit(solution)/shard_map/pallas_call | solution.py:255
  61.8 1.4 collective-permute-start.16
  63.2 2.3 %collective-permute-start.17 = (bf16[384,128]{1,0:T(8,128)(2,1)}, bf16[384,128]{1,0:T(8,128)(2,1)S(1)}, u32[]{:S(2)}, u32[]{:S(2)}) collective-permute-start(bf16[384,128]{1,0:T(8,128)(2,1)} %get-tuple-element.35), channel_id=1, source_target_pairs={{16,32},{32,16},{48,64},{64,48},{80,96},{96,80},{112,128},{128,112... | collective-permute-start | bytes 294920 | tf_op jit(solution)/shard_map/ppermute | solution.py:38
  65.5 3.1 %collective-permute-start.18 = (bf16[384,128]{1,0:T(8,128)(2,1)}, bf16[384,128]{1,0:T(8,128)(2,1)S(1)}, u32[]{:S(2)}, u32[]{:S(2)}) collective-permute-start(bf16[384,128]{1,0:T(8,128)(2,1)} %get-tuple-element.36), channel_id=1, source_target_pairs={{0,4},{4,0},{8,12},{12,8},{1,5},{5,1},{9,13},{13,9},{2,6},{6,2},{1... | collective-permute-start | bytes 294920 | tf_op jit(solution)/shard_map/ppermute | solution.py:39
  68.7 0.7 collective-permute-start.19
  69.4 1.5 %collective-permute-done.18.r2 = bf16[384,128]{1,0:T(8,128)(2,1)S(1)} collective-permute-done((bf16[384,128]{1,0:T(8,128)(2,1)}, bf16[384,128]{1,0:T(8,128)(2,1)S(1)}, u32[]{:S(2)}, u32[]{:S(2)}) %collective-permute-start.18) | collective-permute-done | bytes 98336 | tf_op jit(solution)/shard_map/ppermute | solution.py:39
  70.9 0.6 copy-done.24
  71.6 6.4 %shard_map.116 = (bf16[1024,128]{1,0:T(8,128)(2,1)}, bf16[384,128]{1,0:T(8,128)(2,1)}, bf16[384,128]{1,0:T(8,128)(2,1)}, bf16[384,128]{1,0:T(8,128)(2,1)}, bf16[384,128]{1,0:T(8,128)(2,1)}) custom-call(s32[3]{0:T(128)} %pad_add_fusion.meta, s32[8,4]{1,0:T(8,128)} %copy.14.col, bf16[8,4,128,128]{3,2,1,0:T(8,128)(2,1)} %tiles.5, ...), custom_call_target="tpu_custom_call" | custom-call | tf_op jit(solution)/shard_map/pallas_call | solution.py:255
  78.0 4.2 %collective-permute-start.21 = (bf16[384,128]{1,0:T(8,128)(2,1)}, bf16[384,128]{1,0:T(8,128)(2,1)S(1)}, u32[]{:S(2)}, u32[]{:S(2)}) collective-permute-start(bf16[384,128]{1,0:T(8,128)(2,1)} %get-tuple-element.40), channel_id=1, source_target_pairs={{16,32},{32,16},{48,64},{64,48},{80,96},{96,80},{112,128},{128,112... | collective-permute-start | bytes 294920 | tf_op jit(solution)/shard_map/ppermute | solution.py:38
  82.2 3.6 %collective-permute-start.22 = (bf16[384,128]{1,0:T(8,128)(2,1)}, bf16[384,128]{1,0:T(8,128)(2,1)S(1)}, u32[]{:S(2)}, u32[]{:S(2)}) collective-permute-start(bf16[384,128]{1,0:T(8,128)(2,1)} %get-tuple-element.41), channel_id=1, source_target_pairs={{0,4},{4,0},{8,12},{12,8},{1,5},{5,1},{9,13},{13,9},{2,6},{6,2},{1... | collective-permute-start | bytes 294920 | tf_op jit(solution)/shard_map/ppermute | solution.py:39
  85.8 0.9 collective-permute-start.23
  86.7 1.3 collective-permute-done.22.t2
  88.0 0.6 copy-done.20
  88.7 7.7 %shard_map.117 = (bf16[128,1152]{1,0:T(8,128)(2,1)}, f32[128,1152]{1,0:T(8,128)}) custom-call(s32[3]{0:T(128)} %pad_add_fusion.meta, s32[8,4]{1,0:T(8,128)} %copy.14.col, s32[4]{0:T(128)} %counts.5, bf16[8,4,128,128]{3,2,1,0:T(8,128)(2,1)} %tiles.5, bf16[1024,128]{1,0:T(8,128)(2,1)} %get-tuple-element.38.grad, bf16[384,128]{1,0:T(8,128)(2,1)} %copy-done.18, ...), custom_call_target="tpu_custom_call" | custom-call | tf_op jit(solution)/shard_map/pallas_call | solution.py:255
  96.4 1.8 %collective-permute-done.24 = bf16[128,1152]{1,0:T(8,128)(2,1)S(1)} collective-permute-done((bf16[128,1152]{1,0:T(8,128)(2,1)}, bf16[128,1152]{1,0:T(8,128)(2,1)S(1)}, u32[]{:S(2)}, u32[]{:S(2)}) %collective-permute-start.24) | collective-permute-done | bytes 294944 | tf_op jit(solution)/shard_map/ppermute | solution.py:353
  98.2 1.1 add_convert_fusion
  99.4 25.3 %all_to_all.10 = bf16[32,4,1152]{2,1,0:T(4,128)(2,1)S(1)} all-to-all(bf16[32,4,1152]{2,1,0:T(4,128)(2,1)S(1)} %reshape.15), channel_id=1, replica_groups=mesh['z'=8,'core'=2,'gy'=4,'af'=4] {'z','gy'}, dimensions={0} | all-to-all | bytes 589824 | tf_op jit(solution)/shard_map/all_to_all | solution.py:355
  124.7 0.1 reduce_sum.12
  124.9 15.2 %all_to_all.11 = bf16[32,4,1152]{2,1,0:T(4,128)(2,1)S(1)} all-to-all(bf16[32,4,1152]{2,1,0:T(4,128)(2,1)S(1)} %broadcast_in_dim.2), channel_id=1, replica_groups=mesh['z'=8,'core'=2,'gy'=4,'af'=4] {'z','gy'}, dimensions={0} | all-to-all | bytes 589824 | tf_op jit(solution)/shard_map/all_to_all | solution.py:357
  140.2 3.7 %collective-permute-start.25 = (bf16[128,1152]{1,0:T(8,128)(2,1)S(1)}, bf16[128,1152]{1,0:T(8,128)(2,1)S(1)}, u32[]{:S(2)}, u32[]{:S(2)}) collective-permute-start(bf16[128,1152]{1,0:T(8,128)(2,1)S(1)} %reshape.16.mine), channel_id=1, source_target_pairs={{0,16},{16,0},{1,17},{17,1},{2,18},{18,2},{3,19},{19,3},{4,20},{20... | collective-permute-start | bytes 884744 | tf_op jit(solution)/shard_map/ppermute | solution.py:360
  143.9 1.2 collective-permute-done.25.other
  145.1 0.7 copy-done.1
  145.9 2.8 %shard_map.118 = (f32[256,1024]{1,0:T(8,128)}, f32[256,128]{1,0:T(8,128)}) custom-call(s32[3]{0:T(128)} %pad_add_fusion.meta, bf16[128,1152]{1,0:T(8,128)(2,1)} %copy-done, bf16[128,1152]{1,0:T(8,128)(2,1)} %copy-done.1), custom_call_target="tpu_custom_call" | custom-call | tf_op jit(solution)/shard_map/pallas_call | solution.py:255
  (71 shorter events, 0.5 us)
Async XLA Ops:
  5.6 9.9 %collective-permute-start = (bf16[384,256]{1,0:T(8,128)(2,1)}, bf16[384,256]{1,0:T(8,128)(2,1)S(1)}, u32[]{:S(2)}, u32[]{:S(2)}) collective-permute-start(bf16[384,256]{1,0:T(8,128)(2,1)} %get-tuple-element.25), channel_id=1, source_target_pairs={{0,16},{16,0},{1,17},{17,1},{2,18},{18,2},{3,19},{19,3},{4,20},{20... | collective-permute-start | bytes 589832 | tf_op jit(solution)/shard_map/ppermute | solution.py:37
  8.8 20.2 %collective-permute-start.12 = (bf16[128,1152]{1,0:T(8,128)(2,1)}, bf16[128,1152]{1,0:T(8,128)(2,1)S(1)}, u32[]{:S(2)}, u32[]{:S(2)}) collective-permute-start(bf16[128,1152]{1,0:T(8,128)(2,1)} %get-tuple-element.31.m0), channel_id=1, source_target_pairs={{0,3},{1,0},{2,1},{3,2},{4,7},{5,4},{6,5},{7,6},{8,11},{9,8},{10,9... | collective-permute-start | bytes 884744 | tf_op jit(solution)/shard_map/ppermute | solution.py:24
  9.8 21.9 %collective-permute-start.11 = (bf16[128,1152]{1,0:T(8,128)(2,1)}, bf16[128,1152]{1,0:T(8,128)(2,1)S(1)}, u32[]{:S(2)}, u32[]{:S(2)}) collective-permute-start(bf16[128,1152]{1,0:T(8,128)(2,1)} %get-tuple-element.31.m0), channel_id=1, source_target_pairs={{0,2},{1,3},{2,0},{3,1},{4,6},{5,7},{6,4},{7,5},{8,10},{9,11},{10,... | collective-permute-start | bytes 884744 | tf_op jit(solution)/shard_map/ppermute | solution.py:24
  10.2 7.9 %collective-permute-start.1 = (bf16[384,256]{1,0:T(8,128)(2,1)}, bf16[384,256]{1,0:T(8,128)(2,1)S(1)}, u32[]{:S(2)}, u32[]{:S(2)}) collective-permute-start(bf16[384,256]{1,0:T(8,128)(2,1)} %get-tuple-element.26), channel_id=1, source_target_pairs={{16,32},{32,16},{48,64},{64,48},{80,96},{96,80},{112,128},{128,112... | collective-permute-start | bytes 589832 | tf_op jit(solution)/shard_map/ppermute | solution.py:38
  14.2 5.6 %collective-permute-start.2 = (bf16[384,256]{1,0:T(8,128)(2,1)}, bf16[384,256]{1,0:T(8,128)(2,1)S(1)}, u32[]{:S(2)}, u32[]{:S(2)}) collective-permute-start(bf16[384,256]{1,0:T(8,128)(2,1)} %get-tuple-element.27), channel_id=1, source_target_pairs={{0,4},{4,0},{8,12},{12,8},{1,5},{5,1},{9,13},{13,9},{2,6},{6,2},{1... | collective-permute-start | bytes 589832 | tf_op jit(solution)/shard_map/ppermute | solution.py:39
  15.5 4.3 %copy-start.14 = (bf16[384,256]{1,0:T(8,128)(2,1)}, bf16[384,256]{1,0:T(8,128)(2,1)S(1)}, u32[]{:S(2)}) copy-start(bf16[384,256]{1,0:T(8,128)(2,1)S(1)} %collective-permute-done.r0) | copy-start | bytes 589828
  15.5 4.3 %collective-permute-start.3 = (bf16[384,256]{1,0:T(8,128)(2,1)}, bf16[384,256]{1,0:T(8,128)(2,1)S(1)}, u32[]{:S(2)}, u32[]{:S(2)}) collective-permute-start(bf16[384,256]{1,0:T(8,128)(2,1)} %get-tuple-element.28), channel_id=1, source_target_pairs={{4,8},{8,4},{5,9},{9,5},{6,10},{10,6},{7,11},{11,7},{20,24},{24,20... | collective-permute-start | bytes 589832 | tf_op jit(solution)/shard_map/ppermute | solution.py:40
  18.0 1.8 %copy-start.15 = (bf16[384,256]{1,0:T(8,128)(2,1)}, bf16[384,256]{1,0:T(8,128)(2,1)S(1)}, u32[]{:S(2)}) copy-start(bf16[384,256]{1,0:T(8,128)(2,1)S(1)} %collective-permute-done.1.r1) | copy-start | bytes 589828
  18.0 13.7 %collective-permute-start.10 = (bf16[128,1152]{1,0:T(8,128)(2,1)}, bf16[128,1152]{1,0:T(8,128)(2,1)S(1)}, u32[]{:S(2)}, u32[]{:S(2)}) collective-permute-start(bf16[128,1152]{1,0:T(8,128)(2,1)} %get-tuple-element.31.m0), channel_id=1, source_target_pairs={{0,1},{1,2},{2,3},{3,0},{4,5},{5,6},{6,7},{7,4},{8,9},{9,10},{10,1... | collective-permute-start | bytes 884744 | tf_op jit(solution)/shard_map/ppermute | solution.py:24
  19.8 0.7 copy-start.16
  20.5 0.7 copy-start.17
  26.7 8.7 %collective-permute-start.6 = (bf16[512,256]{1,0:T(8,128)(2,1)}, bf16[512,256]{1,0:T(8,128)(2,1)S(1)}, u32[]{:S(2)}, u32[]{:S(2)}) collective-permute-start(bf16[512,256]{1,0:T(8,128)(2,1)} %get-tuple-element.29.own_t.top), channel_id=1, source_target_pairs={{0,3},{1,0},{2,1},{3,2},{4,7},{5,4},{6,5},{7,6},{8,11},{9,8},{10,9... | collective-permute-start | bytes 786440 | tf_op jit(solution)/shard_map/ppermute | solution.py:24
  29.0 9.7 %collective-permute-start.4 = (bf16[512,256]{1,0:T(8,128)(2,1)}, bf16[512,256]{1,0:T(8,128)(2,1)S(1)}, u32[]{:S(2)}, u32[]{:S(2)}) collective-permute-start(bf16[512,256]{1,0:T(8,128)(2,1)} %get-tuple-element.29.own_t.top), channel_id=1, source_target_pairs={{0,1},{1,2},{2,3},{3,0},{4,5},{5,6},{6,7},{7,4},{8,9},{9,10},{10,1... | collective-permute-start | bytes 786440 | tf_op jit(solution)/shard_map/ppermute | solution.py:24
  29.0 22.7 %copy-start.2 = (bf16[128,1152]{1,0:T(8,128)(2,1)}, bf16[128,1152]{1,0:T(8,128)(2,1)S(1)}, u32[]{:S(2)}) copy-start(bf16[128,1152]{1,0:T(8,128)(2,1)S(1)} %collective-permute-done.12.m3) | copy-start | bytes 884740
  29.0 11.8 %collective-permute-start.7 = (bf16[512,256]{1,0:T(8,128)(2,1)}, bf16[512,256]{1,0:T(8,128)(2,1)S(1)}, u32[]{:S(2)}, u32[]{:S(2)}) collective-permute-start(bf16[512,256]{1,0:T(8,128)(2,1)} %get-tuple-element.30.own_b.bottom), channel_id=1, source_target_pairs={{0,3},{1,0},{2,1},{3,2},{4,7},{5,4},{6,5},{7,6},{8,11},{9,8},{10,9... | collective-permute-start | bytes 786440 | tf_op jit(solution)/shard_map/ppermute | solution.py:24
  31.7 20.0 %copy-start.3 = (bf16[128,1152]{1,0:T(8,128)(2,1)}, bf16[128,1152]{1,0:T(8,128)(2,1)S(1)}, u32[]{:S(2)}) copy-start(bf16[128,1152]{1,0:T(8,128)(2,1)S(1)} %collective-permute-done.11.m2) | copy-start | bytes 884740
  31.7 12.6 %collective-permute-start.5 = (bf16[512,256]{1,0:T(8,128)(2,1)}, bf16[512,256]{1,0:T(8,128)(2,1)S(1)}, u32[]{:S(2)}, u32[]{:S(2)}) collective-permute-start(bf16[512,256]{1,0:T(8,128)(2,1)} %get-tuple-element.30.own_b.bottom), channel_id=1, source_target_pairs={{0,1},{1,2},{2,3},{3,0},{4,5},{5,6},{6,7},{7,4},{8,9},{9,10},{10,1... | collective-permute-start | bytes 786440 | tf_op jit(solution)/shard_map/ppermute | solution.py:24
  31.7 20.0 %copy-start.4 = (bf16[128,1152]{1,0:T(8,128)(2,1)}, bf16[128,1152]{1,0:T(8,128)(2,1)S(1)}, u32[]{:S(2)}) copy-start(bf16[128,1152]{1,0:T(8,128)(2,1)S(1)} %collective-permute-done.10.m1) | copy-start | bytes 884740
  31.7 12.6 %collective-permute-start.15 = (bf16[128,1152]{1,0:T(8,128)(2,1)S(1)}, bf16[128,1152]{1,0:T(8,128)(2,1)S(1)}, u32[]{:S(2)}, u32[]{:S(2)}) collective-permute-start(bf16[128,1152]{1,0:T(8,128)(2,1)S(1)} %collective-permute-done.12.m3), channel_id=1, source_target_pairs={{0,16},{16,0},{1,17},{17,1},{2,18},{18,2},{3,19},{19,3},{4,20},{20... | collective-permute-start | bytes 884744 | tf_op jit(solution)/shard_map/ppermute | solution.py:303
  35.5 16.3 %copy-start.8 = (bf16[512,256]{1,0:T(8,128)(2,1)}, bf16[512,256]{1,0:T(8,128)(2,1)S(1)}, u32[]{:S(2)}) copy-start(bf16[512,256]{1,0:T(8,128)(2,1)S(1)} %collective-permute-done.6.hi_t) | copy-start | bytes 786436
  35.5 8.9 %collective-permute-start.14 = (bf16[128,1152]{1,0:T(8,128)(2,1)S(1)}, bf16[128,1152]{1,0:T(8,128)(2,1)S(1)}, u32[]{:S(2)}, u32[]{:S(2)}) collective-permute-start(bf16[128,1152]{1,0:T(8,128)(2,1)S(1)} %collective-permute-done.11.m2), channel_id=1, source_target_pairs={{0,16},{16,0},{1,17},{17,1},{2,18},{18,2},{3,19},{19,3},{4,20},{20... | collective-permute-start | bytes 884744 | tf_op jit(solution)/shard_map/ppermute | solution.py:303
  38.7 13.0 %copy-start.9 = (bf16[512,256]{1,0:T(8,128)(2,1)}, bf16[512,256]{1,0:T(8,128)(2,1)S(1)}, u32[]{:S(2)}) copy-start(bf16[512,256]{1,0:T(8,128)(2,1)S(1)} %collective-permute-done.4.lo_t) | copy-start | bytes 786436
  38.7 5.7 %collective-permute-start.13 = (bf16[128,1152]{1,0:T(8,128)(2,1)S(1)}, bf16[128,1152]{1,0:T(8,128)(2,1)S(1)}, u32[]{:S(2)}, u32[]{:S(2)}) collective-permute-start(bf16[128,1152]{1,0:T(8,128)(2,1)S(1)} %collective-permute-done.10.m1), channel_id=1, source_target_pairs={{0,16},{16,0},{1,17},{17,1},{2,18},{18,2},{3,19},{19,3},{4,20},{20... | collective-permute-start | bytes 884744 | tf_op jit(solution)/shard_map/ppermute | solution.py:303
  40.9 10.9 %copy-start.10 = (bf16[512,256]{1,0:T(8,128)(2,1)}, bf16[512,256]{1,0:T(8,128)(2,1)S(1)}, u32[]{:S(2)}) copy-start(bf16[512,256]{1,0:T(8,128)(2,1)S(1)} %collective-permute-done.7.hi_b) | copy-start | bytes 786436
  40.9 9.4 %collective-permute-start.8 = (bf16[512,256]{1,0:T(8,128)(2,1)S(1)}, bf16[512,256]{1,0:T(8,128)(2,1)S(1)}, u32[]{:S(2)}, u32[]{:S(2)}) collective-permute-start(bf16[512,256]{1,0:T(8,128)(2,1)S(1)} %collective-permute-done.4.lo_t), channel_id=1, source_target_pairs={{0,1},{1,2},{2,3},{3,0},{4,5},{5,6},{6,7},{7,4},{8,9},{9,10},{10,1... | collective-permute-start | bytes 786440 | tf_op jit(solution)/shard_map/ppermute | solution.py:24
  44.3 7.4 %copy-start.11 = (bf16[512,256]{1,0:T(8,128)(2,1)}, bf16[512,256]{1,0:T(8,128)(2,1)S(1)}, u32[]{:S(2)}) copy-start(bf16[512,256]{1,0:T(8,128)(2,1)S(1)} %collective-permute-done.5.lo_b) | copy-start | bytes 786436
  44.3 7.4 %collective-permute-start.9 = (bf16[512,256]{1,0:T(8,128)(2,1)S(1)}, bf16[512,256]{1,0:T(8,128)(2,1)S(1)}, u32[]{:S(2)}, u32[]{:S(2)}) collective-permute-start(bf16[512,256]{1,0:T(8,128)(2,1)S(1)} %collective-permute-done.7.hi_b), channel_id=1, source_target_pairs={{0,3},{1,0},{2,1},{3,2},{4,7},{5,4},{6,5},{7,6},{8,11},{9,8},{10,9... | collective-permute-start | bytes 786440 | tf_op jit(solution)/shard_map/ppermute | solution.py:24
  44.3 7.4 %copy-start.5 = (bf16[128,1152]{1,0:T(8,128)(2,1)}, bf16[128,1152]{1,0:T(8,128)(2,1)S(1)}, u32[]{:S(2)}) copy-start(bf16[128,1152]{1,0:T(8,128)(2,1)S(1)} %collective-permute-done.15.v3) | copy-start | bytes 884740
  44.3 7.4 %copy-start.6 = (bf16[128,1152]{1,0:T(8,128)(2,1)}, bf16[128,1152]{1,0:T(8,128)(2,1)S(1)}, u32[]{:S(2)}) copy-start(bf16[128,1152]{1,0:T(8,128)(2,1)S(1)} %collective-permute-done.14.v2) | copy-start | bytes 884740
  44.4 7.4 %copy-start.7 = (bf16[128,1152]{1,0:T(8,128)(2,1)}, bf16[128,1152]{1,0:T(8,128)(2,1)S(1)}, u32[]{:S(2)}) copy-start(bf16[128,1152]{1,0:T(8,128)(2,1)S(1)} %collective-permute-done.13.v1) | copy-start | bytes 884740
  50.3 1.5 %copy-start.12 = (bf16[512,256]{1,0:T(8,128)(2,1)}, bf16[512,256]{1,0:T(8,128)(2,1)S(1)}, u32[]{:S(2)}) copy-start(bf16[512,256]{1,0:T(8,128)(2,1)S(1)} %collective-permute-done.8.far_t) | copy-start | bytes 786436
  51.7 0.7 copy-start.13
  61.8 7.5 %collective-permute-start.16 = (bf16[384,128]{1,0:T(8,128)(2,1)}, bf16[384,128]{1,0:T(8,128)(2,1)S(1)}, u32[]{:S(2)}, u32[]{:S(2)}) collective-permute-start(bf16[384,128]{1,0:T(8,128)(2,1)} %get-tuple-element.34), channel_id=1, source_target_pairs={{0,16},{16,0},{1,17},{17,1},{2,18},{18,2},{3,19},{19,3},{4,20},{20... | collective-permute-start | bytes 294920 | tf_op jit(solution)/shard_map/ppermute | solution.py:37
  63.2 6.1 %collective-permute-start.17 = (bf16[384,128]{1,0:T(8,128)(2,1)}, bf16[384,128]{1,0:T(8,128)(2,1)S(1)}, u32[]{:S(2)}, u32[]{:S(2)}) collective-permute-start(bf16[384,128]{1,0:T(8,128)(2,1)} %get-tuple-element.35), channel_id=1, source_target_pairs={{16,32},{32,16},{48,64},{64,48},{80,96},{96,80},{112,128},{128,112... | collective-permute-start | bytes 294920 | tf_op jit(solution)/shard_map/ppermute | solution.py:38
  65.5 5.4 %collective-permute-start.18 = (bf16[384,128]{1,0:T(8,128)(2,1)}, bf16[384,128]{1,0:T(8,128)(2,1)S(1)}, u32[]{:S(2)}, u32[]{:S(2)}) collective-permute-start(bf16[384,128]{1,0:T(8,128)(2,1)} %get-tuple-element.36), channel_id=1, source_target_pairs={{0,4},{4,0},{8,12},{12,8},{1,5},{5,1},{9,13},{13,9},{2,6},{6,2},{1... | collective-permute-start | bytes 294920 | tf_op jit(solution)/shard_map/ppermute | solution.py:39
  68.7 2.2 %collective-permute-start.19 = (bf16[384,128]{1,0:T(8,128)(2,1)}, bf16[384,128]{1,0:T(8,128)(2,1)S(1)}, u32[]{:S(2)}, u32[]{:S(2)}) collective-permute-start(bf16[384,128]{1,0:T(8,128)(2,1)} %get-tuple-element.37), channel_id=1, source_target_pairs={{4,8},{8,4},{5,9},{9,5},{6,10},{10,6},{7,11},{11,7},{20,24},{24,20... | collective-permute-start | bytes 294920 | tf_op jit(solution)/shard_map/ppermute | solution.py:40
  69.3 1.6 %copy-start.22 = (bf16[384,128]{1,0:T(8,128)(2,1)}, bf16[384,128]{1,0:T(8,128)(2,1)S(1)}, u32[]{:S(2)}) copy-start(bf16[384,128]{1,0:T(8,128)(2,1)S(1)} %collective-permute-done.16.r0) | copy-start | bytes 294916
  69.4 1.5 %copy-start.23 = (bf16[384,128]{1,0:T(8,128)(2,1)}, bf16[384,128]{1,0:T(8,128)(2,1)S(1)}, u32[]{:S(2)}) copy-start(bf16[384,128]{1,0:T(8,128)(2,1)S(1)} %collective-permute-done.17.r1) | copy-start | bytes 294916
  78.0 8.7 %collective-permute-start.20 = (bf16[384,128]{1,0:T(8,128)(2,1)}, bf16[384,128]{1,0:T(8,128)(2,1)S(1)}, u32[]{:S(2)}, u32[]{:S(2)}) collective-permute-start(bf16[384,128]{1,0:T(8,128)(2,1)} %get-tuple-element.39), channel_id=1, source_target_pairs={{0,16},{16,0},{1,17},{17,1},{2,18},{18,2},{3,19},{19,3},{4,20},{20... | collective-permute-start | bytes 294920 | tf_op jit(solution)/shard_map/ppermute | solution.py:37
  78.0 8.7 %collective-permute-start.21 = (bf16[384,128]{1,0:T(8,128)(2,1)}, bf16[384,128]{1,0:T(8,128)(2,1)S(1)}, u32[]{:S(2)}, u32[]{:S(2)}) collective-permute-start(bf16[384,128]{1,0:T(8,128)(2,1)} %get-tuple-element.40), channel_id=1, source_target_pairs={{16,32},{32,16},{48,64},{64,48},{80,96},{96,80},{112,128},{128,112... | collective-permute-start | bytes 294920 | tf_op jit(solution)/shard_map/ppermute | solution.py:38
  82.2 5.8 %collective-permute-start.22 = (bf16[384,128]{1,0:T(8,128)(2,1)}, bf16[384,128]{1,0:T(8,128)(2,1)S(1)}, u32[]{:S(2)}, u32[]{:S(2)}) collective-permute-start(bf16[384,128]{1,0:T(8,128)(2,1)} %get-tuple-element.41), channel_id=1, source_target_pairs={{0,4},{4,0},{8,12},{12,8},{1,5},{5,1},{9,13},{13,9},{2,6},{6,2},{1... | collective-permute-start | bytes 294920 | tf_op jit(solution)/shard_map/ppermute | solution.py:39
  85.8 2.2 %collective-permute-start.23 = (bf16[384,128]{1,0:T(8,128)(2,1)}, bf16[384,128]{1,0:T(8,128)(2,1)S(1)}, u32[]{:S(2)}, u32[]{:S(2)}) collective-permute-start(bf16[384,128]{1,0:T(8,128)(2,1)} %get-tuple-element.42), channel_id=1, source_target_pairs={{4,8},{8,4},{5,9},{9,5},{6,10},{10,6},{7,11},{11,7},{20,24},{24,20... | collective-permute-start | bytes 294920 | tf_op jit(solution)/shard_map/ppermute | solution.py:40
  86.7 1.3 copy-start.18
  86.7 1.3 copy-start.19
  96.4 1.8 %collective-permute-start.24 = (bf16[128,1152]{1,0:T(8,128)(2,1)}, bf16[128,1152]{1,0:T(8,128)(2,1)S(1)}, u32[]{:S(2)}, u32[]{:S(2)}) collective-permute-start(bf16[128,1152]{1,0:T(8,128)(2,1)} %get-tuple-element.47), channel_id=1, source_target_pairs={{0,16},{16,0},{1,17},{17,1},{2,18},{18,2},{3,19},{19,3},{4,20},{20... | collective-permute-start | bytes 884744 | tf_op jit(solution)/shard_map/ppermute | solution.py:353
  140.2 4.9 %copy-start = (bf16[128,1152]{1,0:T(8,128)(2,1)}, bf16[128,1152]{1,0:T(8,128)(2,1)S(1)}, u32[]{:S(2)}) copy-start(bf16[128,1152]{1,0:T(8,128)(2,1)S(1)} %reshape.16.mine) | copy-start | bytes 884740
  140.2 4.9 %collective-permute-start.25 = (bf16[128,1152]{1,0:T(8,128)(2,1)S(1)}, bf16[128,1152]{1,0:T(8,128)(2,1)S(1)}, u32[]{:S(2)}, u32[]{:S(2)}) collective-permute-start(bf16[128,1152]{1,0:T(8,128)(2,1)S(1)} %reshape.16.mine), channel_id=1, source_target_pairs={{0,16},{16,0},{1,17},{17,1},{2,18},{18,2},{3,19},{19,3},{4,20},{20... | collective-permute-start | bytes 884744 | tf_op jit(solution)/shard_map/ppermute | solution.py:360
  145.1 0.7 copy-start.1
  (4 other events, 2.6 us)

commit v6 on v5

v6 whole, which is shorter than its diff:
```python
import jax
import jax.numpy as jnp
import numpy as np
from jax import lax
from jax.experimental import pallas as pl
from jax.experimental.pallas import tpu as pltpu
from jax.sharding import Mesh
from jax.sharding import PartitionSpec as P

BF = jnp.bfloat16
F32 = jnp.float32
ROWS = ("z", "core")
PLANE = ("z", "gy")
LANES = 128
INTERPRET = False


def dot(lhs, rhs, lhs_dim=1, rhs_dim=0):
    return lax.dot_general(lhs, rhs, (((lhs_dim,), (rhs_dim,)), ((), ())), preferred_element_type=F32)


def turn(field, axis, move):
    count = lax.axis_size(axis)
    return lax.ppermute(field, axis, [(i, (i + move) % count) for i in range(count)])


def pairs_at(count, first):
    pairs = []
    for i in range(first, count - 1, 2):
        pairs += [(i, i + 1), (i + 1, i)]
    return pairs


def trade(fields):
    rows, cols = lax.axis_size(ROWS), lax.axis_size("gy")
    return (
        lax.ppermute(fields[0], "core", [(0, 1), (1, 0)]),
        lax.ppermute(fields[1], ROWS, pairs_at(rows, 1)),
        lax.ppermute(fields[2], "gy", pairs_at(cols, 0)),
        lax.ppermute(fields[3], "gy", pairs_at(cols, 1)),
    )


def send_order(meta):
    core, odd = meta[0], lax.rem(meta[1], 2)
    return (core, 1 - core, 2 + odd, 3 - odd)


def recv_order(meta):
    core, odd = meta[0], lax.rem(meta[1], 2)
    return (1 - core, core, 3 - odd, 2 + odd)


def down(row):
    return jnp.transpose(jnp.broadcast_to(row.astype(F32), (LANES, LANES)))


def halves(row):
    high = jnp.floor(row.astype(F32) * (1.0 / LANES))
    return high, row.astype(F32) - high * LANES


def pick(row, nodes, out_ref):
    lane = lax.broadcasted_iota(jnp.int32, (LANES, LANES), 1).astype(F32)
    high, low = halves(row)
    none = jnp.zeros((LANES, LANES), BF)
    for b in range(row.shape[1] // LANES):
        at = slice(b * LANES, (b + 1) * LANES)
        match = jnp.where(down(low[:, at]) == lane, 1.0, 0.0).astype(BF)
        block = down(high[:, at]).astype(BF)
        for j in range(nodes // LANES):
            out_ref[at, j * LANES : (j + 1) * LANES] = jnp.where(
                block == jnp.asarray(j, BF), match, none
            )


def put(row, nodes, out_ref, base):
    slots = row.shape[1]
    high, low = halves(row)
    ids = lax.broadcasted_iota(jnp.int32, (LANES, slots), 0).astype(F32)
    match = jnp.where(low == ids, 1.0, 0.0).astype(BF)
    block = jnp.broadcast_to(high, (LANES, slots)).astype(BF)
    none = jnp.zeros((LANES, slots), BF)
    for j in range(nodes // LANES):
        out_ref[j * LANES : (j + 1) * LANES, base : base + slots] = jnp.where(
            block == jnp.asarray(j, BF), match, none
        )


def live_row(send_ref, counts, d):
    row = send_ref[pl.ds(d, 1), :]
    slot = lax.broadcasted_iota(jnp.int32, row.shape, 1)
    return jnp.where(slot < counts[d], row, -1)


def weigh(arrived, weight_row, rhs_ref, base):
    width = arrived.shape[1]
    for b in range(weight_row.shape[1] // LANES):
        w = down(weight_row[:, b * LANES : (b + 1) * LANES])
        w = jnp.concatenate([w] * (width // LANES), axis=1)
        value = arrived[b * LANES : (b + 1) * LANES, :].astype(F32) * w
        high = value.astype(BF)
        low = (value - high.astype(F32)).astype(BF)
        rhs_ref[pl.ds(base + b * LANES, LANES), :width] = high
        rhs_ref[pl.ds(base + b * LANES, LANES), width:] = low


class Mover:
    def __init__(self, sems):
        self.sems, self.used, self.left = sems, 0, []

    def start(self, source, target):
        copy = pltpu.make_async_copy(source, target, self.sems.at[self.used])
        self.used += 1
        copy.start()
        self.left.append(copy)
        return copy

    def wait(self, *copies):
        for copy in copies:
            if any(copy is other for other in self.left):
                self.left = [other for other in self.left if other is not copy]
                copy.wait()

    def finish(self):
        self.wait(*list(self.left))


def send_kernel(
    meta, counts, feat_in, send_in, w_hid, w_cls, o0, o1, o2, o3, mine, other,
    feat, send, hot, out, sems,
):
    nodes = feat.shape[0]
    half, hid = w_hid.shape[0] // 2, w_hid.shape[1]
    mover = Mover(sems)
    got_send = mover.start(send_in, send)
    got_feat = mover.start(feat_in, feat)
    for ref, part in ((mine, meta[0]), (other, 1 - meta[0])):
        at = pl.ds(pl.multiple_of(part * half, half), half)
        mover.start(w_hid.at[at, :], ref.at[:, :hid])
        mover.start(w_cls.at[at, :], ref.at[:, hid:])
    mover.wait(got_send)
    for m, (d, ref) in enumerate(zip(send_order(meta), (o0, o1, o2, o3))):
        pick(live_row(send, counts, d), nodes, hot)
        mover.wait(got_feat)
        out[m] = dot(hot[...], feat[...]).astype(BF)
        mover.start(out.at[m], ref)
    mover.finish()


def near(tiles, col, field, block, tb):
    lhs = jnp.concatenate([tiles[block, k] for k in range(tiles.shape[1])], axis=1)
    rhs = jnp.concatenate(
        [
            field[pl.ds(pl.multiple_of(col[block, k] * tb, tb), tb), :]
            for k in range(tiles.shape[1])
        ],
        axis=0,
    )
    return dot(lhs, rhs)


def mix_kernel(
    meta, col, feat_in, tiles_in, r0, r1, r2, r3, recv_in, weight_in, top, bottom,
    feat, tiles, come, recv, weight, hot, rhs, base, out, sems,
):
    nodes, width = feat.shape
    slots, tb = recv.shape[1], tiles.shape[2]
    order = recv_order(meta)
    mover = Mover(sems)
    first = [mover.start(recv_in, recv), mover.start(weight_in, weight)]
    second = [mover.start(feat_in, feat), mover.start(tiles_in, tiles)]
    third = [mover.start(ref, come.at[m]) for m, ref in enumerate((r0, r1, r2, r3))]
    mover.wait(*first)
    for m, d in enumerate(order):
        put(recv[pl.ds(d, 1), :], nodes, hot, m * slots)
    mover.wait(*second)
    for r in range(nodes // tb):
        base[r * tb : (r + 1) * tb, :] = near(tiles, col, feat, r, tb)
    for m, d in enumerate(order):
        mover.wait(third[m])
        weigh(come[m], weight[pl.ds(d, 1), :], rhs, m * slots)
    part = nodes // 2
    straight = meta[0] == 0
    for h, ref in enumerate((top, bottom)):
        at = slice(h * part, (h + 1) * part)
        far = dot(hot[at, :], rhs[...])
        got = base[at, :] + far[:, :width] + far[:, width:]
        turned = jnp.concatenate([got[:, width // 2 :], got[:, : width // 2]], axis=1)
        out[at, :] = jnp.where(straight, got, turned).astype(BF)
        mover.start(out.at[at, :], ref)
    mover.finish()


def hidden_kernel(
    meta, counts, send_in, own_t, own_b, lo_t, lo_b, hi_t, hi_b, far_t, far_b,
    m0, m1, m2, m3, v0, v1, v2, v3,
    hidden_out, slope_out, z_out, cls_out, o0, o1, o2, o3,
    send, fields, w_all, w_cls, hidden, slope, z_pair, hot, out, sems,
):
    nodes, classes = z_out.shape[0], cls_out.shape[1]
    half, width = m0.shape[0], own_t.shape[1]
    hid = w_all.shape[1]
    n_af = w_all.shape[0] // (2 * half)
    part = nodes // 2
    mover = Mover(sems)
    first = []
    for i, (k, mine, other) in enumerate(((0, m0, v0), (1, m1, v1), (3, m3, v3), (2, m2, v2))):
        at = lax.rem(meta[2] + n_af - k, n_af) * 2
        for ref, row, to in (
            (mine, 2 * i * half, at + meta[0]),
            (other, (2 * i + 1) * half, at + 1 - meta[0]),
        ):
            to = pl.ds(pl.multiple_of(to * half, half), half)
            first.append(mover.start(ref.at[:, :hid], w_all.at[row : row + half, :]))
            first.append(mover.start(ref.at[:, hid:], w_cls.at[to, :]))
    sides = []
    for h, refs in enumerate(((own_t, lo_t, hi_t, far_t), (own_b, lo_b, hi_b, far_b))):
        rows = slice(h * part, (h + 1) * part)
        sides.append(
            [
                mover.start(ref, fields.at[rows, i * width : (i + 1) * width])
                for i, ref in enumerate(refs)
            ]
        )
    got_send = mover.start(send_in, send)
    mover.wait(*first)
    mover.start(w_cls, cls_out)
    rows = 256

    def block(i, carry):
        at = pl.ds(pl.multiple_of(i * rows, rows), rows)
        pre = dot(fields[at, :], w_all[...])
        sig = jax.nn.sigmoid(pre)
        act = (pre * sig).astype(BF)
        slope[at, :] = (sig * (1.0 + pre * (1.0 - sig))).astype(BF)
        for j in range(hid // LANES):
            hidden[j, at, :] = act[:, j * LANES : (j + 1) * LANES]
        z = dot(act, w_cls[...])
        high = z.astype(BF)
        z_pair[at, :classes] = high
        z_pair[at, classes:] = (z - high.astype(F32)).astype(BF)
        return carry

    for h in range(2):
        mover.wait(*sides[h])
        lax.fori_loop(h * part // rows, (h + 1) * part // rows, block, 0)
        at = slice(h * part, (h + 1) * part)
        mover.start(hidden.at[:, at, :], hidden_out.at[:, at, :])
        mover.start(slope.at[at, :], slope_out.at[at, :])
    mover.start(z_pair, z_out)
    mover.wait(got_send)
    for m, (d, ref) in enumerate(zip(send_order(meta), (o0, o1, o2, o3))):
        pick(live_row(send, counts, d), nodes, hot)
        out[m] = dot(hot[...], z_pair[:, :classes]).astype(BF)
        mover.start(out.at[m], ref)
    mover.finish()


def loss_kernel(
    meta, col, tiles_in, z_in, r0, r1, r2, r3, recv_in, weight_in, labels_in,
    grad_out, b0, b1, b2, b3,
    tiles, z_pair, come, recv, weight, labels, hot, rhs, cols, base, grad, out, sems,
):
    nodes, classes = grad.shape
    slots, tb = recv.shape[1], tiles.shape[2]
    order = recv_order(meta)
    mover = Mover(sems)
    first = [mover.start(recv_in, recv), mover.start(weight_in, weight)]
    second = [mover.start(z_in, z_pair), mover.start(tiles_in, tiles)]
    third = [mover.start(ref, come.at[m]) for m, ref in enumerate((r0, r1, r2, r3))]
    last = mover.start(labels_in, labels)
    mover.wait(*first)
    for m, d in enumerate(order):
        put(recv[pl.ds(d, 1), :], nodes, hot, m * slots)
        pick(recv[pl.ds(d, 1), :], nodes, cols.at[m])
    mover.wait(*second)
    for r in range(nodes // tb):
        got = near(tiles, col, z_pair, r, tb)
        base[r * tb : (r + 1) * tb, :] = got[:, :classes] + got[:, classes:]
    for m, d in enumerate(order):
        mover.wait(third[m])
        weigh(come[m], weight[pl.ds(d, 1), :], rhs, m * slots)
    mover.wait(last)
    lane = lax.broadcasted_iota(jnp.int32, (tb, classes), 1).astype(F32)
    part = nodes // 2
    for h in range(2):
        far = dot(hot[h * part : (h + 1) * part, :], rhs[...])
        for b in range(part // tb):
            r = h * (part // tb) + b
            at = slice(r * tb, (r + 1) * tb)
            logit = far[b * tb : (b + 1) * tb, :]
            logit = base[at, :] + logit[:, :classes] + logit[:, classes:]
            exponent = jnp.exp(logit - jnp.max(logit, axis=1, keepdims=True))
            probability = exponent / jnp.sum(exponent, axis=1, keepdims=True)
            onehot = jnp.where(down(labels[r : r + 1, :]) == lane, 1.0, 0.0)
            grad[at, :] = ((probability - onehot) * (1.0 / 64.0)).astype(BF)
    mover.start(grad, grad_out)
    for m, (d, ref) in enumerate(zip(order, (b0, b1, b2, b3))):
        taken = dot(cols[m], grad[...])
        row = weight[pl.ds(d, 1), :]
        for b in range(slots // LANES):
            at = slice(b * LANES, (b + 1) * LANES)
            out[m, at, :] = (taken[at, :] * down(row[:, at])).astype(BF)
        mover.start(out.at[m], ref)
    mover.finish()


def grads_kernel(
    meta, col, counts, tiles_in, grad_in, t0, t1, t2, t3, send_in, cls_in, slope_in, top, bottom,
    hidden, theirs_out, mine_out,
    tiles, grad, send, w_cls, slope, lhs, units, hot, back, acc, mix, pre, theirs, mine, sems,
):
    nodes, _ = grad.shape
    slots, tb, kt = send.shape[1], tiles.shape[2], tiles.shape[1]
    hid = slope.shape[1]
    part = nodes // 2
    mover = Mover(sems)
    first = mover.start(send_in, send)
    second = [mover.start(grad_in, grad), mover.start(tiles_in, tiles)]
    third = [
        mover.start(ref, back.at[m * slots : (m + 1) * slots, :])
        for m, ref in enumerate((t0, t1, t2, t3))
    ]
    fourth = [mover.start(cls_in, w_cls), mover.start(slope_in, slope)]
    own = meta[2] * 2
    last = [
        mover.start(top, lhs.at[:part, :]),
        mover.start(bottom, lhs.at[part:, :]),
        mover.start(hidden.at[own + meta[0]], units.at[0]),
        mover.start(hidden.at[own + 1 - meta[0]], units.at[1]),
    ]
    mover.wait(first)
    for m, d in enumerate(send_order(meta)):
        put(live_row(send, counts, d), nodes, hot, m * slots)
    mover.wait(*third)
    acc[...] = dot(hot[...], back[...])
    mover.wait(*second)
    for r in range(tiles.shape[0]):
        rows = jnp.concatenate([tiles[r, k] for k in range(kt)], axis=1)
        spread = dot(rows, grad[r * tb : (r + 1) * tb, :], 0, 0)
        for k in range(kt):
            at = pl.ds(pl.multiple_of(col[r, k] * tb, tb), tb)
            acc[at, :] += spread[k * tb : (k + 1) * tb, :]
    mix[...] = acc[...].astype(BF)
    mover.wait(*fourth)
    rows = 256

    def block(i, carry):
        at = pl.ds(pl.multiple_of(i * rows, rows), rows)
        act = dot(mix[at, :], w_cls[...], 1, 1)
        pre[at, :] = (act * slope[at, :].astype(F32)).astype(BF)
        return carry

    lax.fori_loop(0, nodes // rows, block, 0)
    mover.wait(*last)
    half = theirs.shape[0]
    theirs[:, :hid] = dot(lhs[:, half:], pre[...], 0, 0).astype(BF)
    theirs[:, hid:] = dot(units[1], mix[...], 0, 0).astype(BF)
    mover.start(theirs, theirs_out)
    mine[:, :hid] = dot(lhs[:, :half], pre[...], 0, 0)
    mine[:, hid:] = dot(units[0], mix[...], 0, 0)
    mover.start(mine, mine_out)
    mover.finish()


def call(kernel, scalars, arrays, outs, scratch, copies):
    outs = [jax.ShapeDtypeStruct(s, t) for s, t in outs]
    return pl.pallas_call(
        kernel,
        in_specs=[pl.BlockSpec(memory_space=pltpu.SMEM) for _ in scalars]
        + [pl.BlockSpec(memory_space=pl.ANY) for _ in arrays],
        out_specs=[pl.BlockSpec(memory_space=pl.ANY) for _ in outs],
        scratch_shapes=[pltpu.VMEM(s, t) for s, t in scratch]
        + [pltpu.SemaphoreType.DMA((copies,))],
        out_shape=outs,
        interpret=INTERPRET,
    )(*scalars, *arrays)


def work(
    features,
    adj_tiles,
    col_block,
    send_rows,
    send_counts,
    recv_target,
    edge_weight,
    labels,
    w_hidden,
    w_classes,
):
    nodes, width = features.shape
    slots = send_rows.shape[1]
    hid, classes = w_hidden.shape[1], w_classes.shape[1]
    half = w_hidden.shape[0] // 2
    n_af = lax.axis_size("af")
    n_plane = lax.axis_size("z") * lax.axis_size("gy")
    core = lax.axis_index("core")
    af = lax.axis_index("af")
    meta = jnp.stack([core, lax.axis_index("gy"), af]).astype(jnp.int32)
    swap = [(0, 1), (1, 0)]
    both = hid + classes
    part = nodes // 2

    nodes_by = (nodes, 4 * slots)
    index_shape = ((4, slots), jnp.int32)
    weight_shape = ((4, slots), F32)
    tiles_shape = (adj_tiles.shape, BF)
    *out, w_mine, w_other = call(
        send_kernel,
        (meta, send_counts),
        (features, send_rows, w_hidden, w_classes),
        [((slots, width), BF)] * 4 + [((half, both), BF)] * 2,
        [(features.shape, BF), index_shape, ((slots, nodes), BF), ((4, slots, width), BF)],
        10,
    )
    arrived = trade(out)
    w_mine = [w_mine] + [turn(w_mine, "af", k) for k in range(1, n_af)]
    w_other = [w_other] + [
        lax.ppermute(w_mine[k], "core", swap) for k in range(1, n_af)
    ]
    top, bottom = call(
        mix_kernel,
        (meta, col_block),
        (features, adj_tiles, *arrived, recv_target, edge_weight),
        [((part, width), BF)] * 2,
        [
            (features.shape, BF),
            tiles_shape,
            ((4, slots, width), BF),
            index_shape,
            weight_shape,
            (nodes_by, BF),
            ((4 * slots, 2 * width), BF),
            ((nodes, width), F32),
            ((nodes, width), BF),
        ],
        10,
    )
    lo_t, hi_b = turn(top, "af", 1), turn(bottom, "af", -1)
    lo_b, hi_t = turn(bottom, "af", 1), turn(top, "af", -1)
    far_t, far_b = turn(lo_t, "af", 1), turn(hi_b, "af", -1)
    hidden, slope, z_pair, w_cls, *out = call(
        hidden_kernel,
        (meta, send_counts),
        (send_rows, top, bottom, lo_t, lo_b, hi_t, hi_b, far_t, far_b, *w_mine, *w_other),
        [
            ((hid // LANES, nodes, LANES), BF),
            ((nodes, hid), BF),
            ((nodes, 2 * classes), BF),
            ((hid, classes), BF),
        ]
        + [((slots, classes), BF)] * 4,
        [
            index_shape,
            ((nodes, n_af * width), BF),
            ((n_af * 2 * half, hid), BF),
            ((hid, classes), BF),
            ((hid // LANES, nodes, LANES), BF),
            ((nodes, hid), BF),
            ((nodes, 2 * classes), BF),
            ((slots, nodes), BF),
            ((4, slots, classes), BF),
        ],
        35,
    )
    arrived = trade(out)
    grad, *out = call(
        loss_kernel,
        (meta, col_block),
        (adj_tiles, z_pair, *arrived, recv_target, edge_weight, labels.reshape(-1, LANES)),
        [((nodes, classes), BF)] + [((slots, classes), BF)] * 4,
        [
            tiles_shape,
            ((nodes, 2 * classes), BF),
            ((4, slots, classes), BF),
            index_shape,
            weight_shape,
            ((nodes // LANES, LANES), jnp.int32),
            (nodes_by, BF),
            ((4 * slots, 2 * classes), BF),
            ((4, slots, nodes), BF),
            ((nodes, classes), F32),
            ((nodes, classes), BF),
            ((4, slots, classes), BF),
        ],
        14,
    )
    returned = trade(out)
    theirs, mine = call(
        grads_kernel,
        (meta, col_block, send_counts),
        (adj_tiles, grad, *returned, send_rows, w_cls, slope, top, bottom, hidden),
        [((half, both), BF), ((half, both), F32)],
        [
            tiles_shape,
            ((nodes, classes), BF),
            index_shape,
            ((hid, classes), BF),
            ((nodes, hid), BF),
            ((nodes, width), BF),
            ((2, nodes, LANES), BF),
            (nodes_by, BF),
            ((4 * slots, classes), BF),
            ((nodes, classes), F32),
            ((nodes, classes), BF),
            ((nodes, hid), BF),
            ((half, both), BF),
            ((half, both), F32),
        ],
        16,
    )
    total = mine + lax.ppermute(theirs, "core", swap).astype(F32)
    pieces = total.astype(BF).reshape(n_plane, half // n_plane, both)
    pieces = lax.all_to_all(pieces, PLANE, 0, 0, tiled=True)
    piece = jnp.sum(pieces.astype(F32), axis=0).astype(BF)
    mine = lax.all_to_all(
        jnp.broadcast_to(piece[None], (n_plane,) + piece.shape), PLANE, 0, 0, tiled=True
    ).reshape(half, both)
    other = lax.ppermute(mine, "core", swap)
    first = jnp.where(core == 0, mine, other)
    second = jnp.where(core == 0, other, mine)
    return (
        jnp.concatenate([first[:, :hid], second[:, :hid]], axis=0).astype(F32),
        jnp.concatenate([first[:, hid:], second[:, hid:]], axis=0).astype(F32),
    )


def solution(mesh):
    shape = mesh.devices.shape
    split = Mesh(
        np.reshape(mesh.devices, (shape[0] // 2, 2) + shape[1:]), ("z", "core", "gy", "af")
    )
    parts = ("z", "core", "gy")
    placed = (
        P(parts, "af"),
        P(parts, None, None, None),
        P(parts, None),
        P(parts, None),
        P(parts),
        P(parts, None),
        P(parts, None),
        P(parts),
        P("af", None),
        P("af", None),
    )
    return jax.shard_map(
        work,
        mesh=split,
        in_specs=placed,
        out_specs=(P("af", None), P("af", None)),
        check_vma=False,
    )
```

time: 149 us -> 163 us (1.094)
  Pallas kernels: 36.3 us -> 48.1 us
  other arithmetic: 1.88 us -> 3.69 us
    pallas_call x6 -> x5, Pallas kernels: 36.3 us -> 48.1 us  [call(): pl.pallas_call(kernel, in_specs=[pl.BlockSpec(memory_space=pltpu.SMEM) fo...]
    convert_element_type x0 -> x2, other arithmetic: none -> 1.75 us  [the longest x1 1.08 us: work(): jnp.concatenate([first[:, :hid], second[:, :hid]], axis=0).astype(F32)]
    unnamed x53 -> x49, local copies, waits for them, and re-layouts: 5.42 us -> 4.69 us
  transfers between devices with their start and end apart: 26 -> 26, of which waited for: 11 -> 11; matrix products, arithmetic and copies ran while one was open for 1% -> 1% of each run, Pallas kernels for 4% -> 3%
where the time goes in v6:
time: 163 us; the launch traced here: 162 us
  Pallas kernels  48.1 us (30%)
  blocking collectives  40.5 us (25%)
  starting transfers between devices  37 us (23%)
  waiting for transfers between devices  26.8 us (16%)
  local copies, waits for them, and re-layouts  4.96 us (3%)
  other arithmetic  3.69 us (2%)
    pallas_call x5, Pallas kernels, call(): pl.pallas_call(kernel, in_specs=[pl.BlockSpec(memory_space=pltpu.SMEM) fo...  48.1 us
    all_to_all x1, blocking collectives, work(): pieces = lax.all_to_all(pieces, PLANE, 0, 0, tiled=True)  25.2 us
    ppermute x9, waiting for transfers between devices, turn(): lax.ppermute(field, axis, [(i, (i + move) % count) for i in range(count)])  19.1 us
    all_to_all x1, blocking collectives, work(): lax.all_to_all(jnp.broadcast_to(piece[None], (n_plane,) + piece.shape), P...  15.2 us
    ppermute x3, starting transfers between devices, trade(): lax.ppermute(fields[1], ROWS, pairs_at(rows, 1))  10.4 us
    ppermute x3, starting transfers between devices, trade(): lax.ppermute(fields[2], 'gy', pairs_at(cols, 0))  8.17 us
    ppermute x9, starting transfers between devices, turn(): lax.ppermute(field, axis, [(i, (i + move) % count) for i in range(count)])  6.81 us
    ppermute x3, starting transfers between devices, trade(): lax.ppermute(fields[0], 'core', [(0, 1), (1, 0)])  4.78 us
  transfers between devices with their start and end apart: 26, of which 11 were waited for; matrix products, arithmetic and copies ran while one was open for 1% of the time, Pallas kernels for 3%

profile of v6, /device:TPU:1, one launch (start us, length us, event | category | flops | bytes accessed | tf_op | source)
XLA Modules:
  0.0 162.1 jit_solution(15912288069184092488)
XLA Ops:
  0.6 0.6 pad_add_fusion.meta
  1.2 19.7 %shard_map.113 = (bf16[384,256]{1,0:T(8,128)(2,1)}, bf16[384,256]{1,0:T(8,128)(2,1)}, bf16[384,256]{1,0:T(8,128)(2,1)}, bf16[384,256]{1,0:T(8,128)(2,1)}, bf16[1...) custom-call(s32[3]{0:T(128)} %pad_add_fusion.meta, s32[4]{0:T(128)} %counts.5, bf16[1024,256]{1,0:T(8,128)(2,1)} %feat_in.3, ...), custom_call_target="tpu_custom_call" | custom-call | tf_op jit(solution)/shard_map/pallas_call | solution.py:369
  21.0 3.3 %collective-permute-start = (bf16[384,256]{1,0:T(8,128)(2,1)}, bf16[384,256]{1,0:T(8,128)(2,1)S(1)}, u32[]{:S(2)}, u32[]{:S(2)}) collective-permute-start(bf16[384,256]{1,0:T(8,128)(2,1)} %get-tuple-element.25), channel_id=1, source_target_pairs={{0,16},{16,0},{1,17},{17,1},{2,18},{18,2},{3,19},{19,3},{4,20},{20... | collective-permute-start | bytes 589832 | tf_op jit(solution)/shard_map/ppermute | solution.py:37
  24.3 1.0 collective-permute-start.12
  25.3 0.3 collective-permute-start.11
  25.7 4.1 %collective-permute-start.1 = (bf16[384,256]{1,0:T(8,128)(2,1)}, bf16[384,256]{1,0:T(8,128)(2,1)S(1)}, u32[]{:S(2)}, u32[]{:S(2)}) collective-permute-start(bf16[384,256]{1,0:T(8,128)(2,1)} %get-tuple-element.26), channel_id=1, source_target_pairs={{16,32},{32,16},{48,64},{64,48},{80,96},{96,80},{112,128},{128,112... | collective-permute-start | bytes 589832 | tf_op jit(solution)/shard_map/ppermute | solution.py:38
  29.7 1.3 collective-permute-start.2
  31.0 0.7 collective-permute-start.3
  31.7 1.9 %collective-permute-done.1.r1 = bf16[384,256]{1,0:T(8,128)(2,1)S(1)} collective-permute-done((bf16[384,256]{1,0:T(8,128)(2,1)}, bf16[384,256]{1,0:T(8,128)(2,1)S(1)}, u32[]{:S(2)}, u32[]{:S(2)}) %collective-permute-start.1) | collective-permute-done | bytes 196640 | tf_op jit(solution)/shard_map/ppermute | solution.py:38
  33.6 0.4 collective-permute-start.10
  34.0 1.3 copy.14.col
  35.4 0.7 copy-done.14
  36.0 0.7 copy-done.15
  36.7 5.6 %shard_map.114 = (bf16[512,256]{1,0:T(8,128)(2,1)}, bf16[512,256]{1,0:T(8,128)(2,1)}) custom-call(s32[3]{0:T(128)} %pad_add_fusion.meta, s32[8,4]{1,0:T(8,128)} %copy.14.col, bf16[1024,256]{1,0:T(8,128)(2,1)} %feat_in.3, bf16[8,4,128,128]{3,2,1,0:T(8,128)(2,1)} %tiles_in.5, bf16[384,256]{1,0:T(8,128)(2,1)} %copy-done.12, bf16[384,256]{1,0:T(8,128)(2,1)} %copy-done.13, ...), custom_call_target="tpu_custom_call" | custom-call | tf_op jit(solution)/shard_map/pallas_call | solution.py:369
  42.4 2.4 %collective-permute-start.6 = (bf16[512,256]{1,0:T(8,128)(2,1)}, bf16[512,256]{1,0:T(8,128)(2,1)S(1)}, u32[]{:S(2)}, u32[]{:S(2)}) collective-permute-start(bf16[512,256]{1,0:T(8,128)(2,1)} %get-tuple-element.29.own_t.top), channel_id=1, source_target_pairs={{0,3},{1,0},{2,1},{3,2},{4,7},{5,4},{6,5},{7,6},{8,11},{9,8},{10,9... | collective-permute-start | bytes 786440 | tf_op jit(solution)/shard_map/ppermute | solution.py:24
  44.7 2.7 %collective-permute-start.7 = (bf16[512,256]{1,0:T(8,128)(2,1)}, bf16[512,256]{1,0:T(8,128)(2,1)S(1)}, u32[]{:S(2)}, u32[]{:S(2)}) collective-permute-start(bf16[512,256]{1,0:T(8,128)(2,1)} %get-tuple-element.30.own_b.bottom), channel_id=1, source_target_pairs={{0,3},{1,0},{2,1},{3,2},{4,7},{5,4},{6,5},{7,6},{8,11},{9,8},{10,9... | collective-permute-start | bytes 786440 | tf_op jit(solution)/shard_map/ppermute | solution.py:24
  47.4 0.3 collective-permute-start.15
  47.7 3.5 %collective-permute-done.6.hi_t = bf16[512,256]{1,0:T(8,128)(2,1)S(1)} collective-permute-done((bf16[512,256]{1,0:T(8,128)(2,1)}, bf16[512,256]{1,0:T(8,128)(2,1)S(1)}, u32[]{:S(2)}, u32[]{:S(2)}) %collective-permute-start.6) | collective-permute-done | bytes 262176 | tf_op jit(solution)/shard_map/ppermute | solution.py:24
  51.2 3.2 %collective-permute-done.4.lo_t = bf16[512,256]{1,0:T(8,128)(2,1)S(1)} collective-permute-done((bf16[512,256]{1,0:T(8,128)(2,1)}, bf16[512,256]{1,0:T(8,128)(2,1)S(1)}, u32[]{:S(2)}, u32[]{:S(2)}) %collective-permute-start.4) | collective-permute-done | bytes 262176 | tf_op jit(solution)/shard_map/ppermute | solution.py:24
  54.4 0.5 collective-permute-start.13
  54.9 1.6 %collective-permute-done.7.hi_b = bf16[512,256]{1,0:T(8,128)(2,1)S(1)} collective-permute-done((bf16[512,256]{1,0:T(8,128)(2,1)}, bf16[512,256]{1,0:T(8,128)(2,1)S(1)}, u32[]{:S(2)}, u32[]{:S(2)}) %collective-permute-start.7) | collective-permute-done | bytes 262176 | tf_op jit(solution)/shard_map/ppermute | solution.py:24
  56.6 3.4 %collective-permute-done.5.lo_b = bf16[512,256]{1,0:T(8,128)(2,1)S(1)} collective-permute-done((bf16[512,256]{1,0:T(8,128)(2,1)}, bf16[512,256]{1,0:T(8,128)(2,1)S(1)}, u32[]{:S(2)}, u32[]{:S(2)}) %collective-permute-start.5) | collective-permute-done | bytes 262176 | tf_op jit(solution)/shard_map/ppermute | solution.py:24
  60.1 5.9 %collective-permute-done.8.far_t = bf16[512,256]{1,0:T(8,128)(2,1)S(1)} collective-permute-done((bf16[512,256]{1,0:T(8,128)(2,1)S(1)}, bf16[512,256]{1,0:T(8,128)(2,1)S(1)}, u32[]{:S(2)}, u32[]{:S(2)}) %collective-permute-start.8) | collective-permute-done | bytes 262176 | tf_op jit(solution)/shard_map/ppermute | solution.py:24
  66.0 1.4 collective-permute-done.9.far_b
  67.5 0.6 copy-done.11
  68.1 9.0 %shard_map.115 = (bf16[8,1024,128]{2,1,0:T(8,128)(2,1)}, bf16[1024,1024]{1,0:T(8,128)(2,1)}, bf16[1024,256]{1,0:T(8,128)(2,1)}, bf16[1024,128]{1,0:T(8,128)(2,1)...) custom-call(s32[3]{0:T(128)} %pad_add_fusion.meta, ...), custom_call_target="tpu_custom_call" | custom-call | tf_op jit(solution)/shard_map/pallas_call | solution.py:369
  77.1 1.4 collective-permute-start.16
  78.5 2.3 %collective-permute-start.17 = (bf16[384,128]{1,0:T(8,128)(2,1)}, bf16[384,128]{1,0:T(8,128)(2,1)S(1)}, u32[]{:S(2)}, u32[]{:S(2)}) collective-permute-start(bf16[384,128]{1,0:T(8,128)(2,1)} %get-tuple-element.35), channel_id=1, source_target_pairs={{16,32},{32,16},{48,64},{64,48},{80,96},{96,80},{112,128},{128,112... | collective-permute-start | bytes 294920 | tf_op jit(solution)/shard_map/ppermute | solution.py:38
  80.8 3.3 %collective-permute-start.18 = (bf16[384,128]{1,0:T(8,128)(2,1)}, bf16[384,128]{1,0:T(8,128)(2,1)S(1)}, u32[]{:S(2)}, u32[]{:S(2)}) collective-permute-start(bf16[384,128]{1,0:T(8,128)(2,1)} %get-tuple-element.36), channel_id=1, source_target_pairs={{0,4},{4,0},{8,12},{12,8},{1,5},{5,1},{9,13},{13,9},{2,6},{6,2},{1... | collective-permute-start | bytes 294920 | tf_op jit(solution)/shard_map/ppermute | solution.py:39
  84.1 0.7 collective-permute-start.19
  84.8 1.5 collective-permute-done.18.r2
  86.3 0.6 copy-done.18
  86.9 6.6 %shard_map.116 = (bf16[1024,128]{1,0:T(8,128)(2,1)}, bf16[384,128]{1,0:T(8,128)(2,1)}, bf16[384,128]{1,0:T(8,128)(2,1)}, bf16[384,128]{1,0:T(8,128)(2,1)}, bf16[384,128]{1,0:T(8,128)(2,1)}) custom-call(s32[3]{0:T(128)} %pad_add_fusion.meta, s32[8,4]{1,0:T(8,128)} %copy.14.col, bf16[8,4,128,128]{3,2,1,0:T(8,128)(2,1)} %tiles_in.5, ...), custom_call_target="tpu_custom_call" | custom-call | tf_op jit(solution)/shard_map/pallas_call | solution.py:369
  93.6 4.1 %collective-permute-start.21 = (bf16[384,128]{1,0:T(8,128)(2,1)}, bf16[384,128]{1,0:T(8,128)(2,1)S(1)}, u32[]{:S(2)}, u32[]{:S(2)}) collective-permute-start(bf16[384,128]{1,0:T(8,128)(2,1)} %get-tuple-element.40), channel_id=1, source_target_pairs={{16,32},{32,16},{48,64},{64,48},{80,96},{96,80},{112,128},{128,112... | collective-permute-start | bytes 294920 | tf_op jit(solution)/shard_map/ppermute | solution.py:38
  97.7 3.6 %collective-permute-start.22 = (bf16[384,128]{1,0:T(8,128)(2,1)}, bf16[384,128]{1,0:T(8,128)(2,1)S(1)}, u32[]{:S(2)}, u32[]{:S(2)}) collective-permute-start(bf16[384,128]{1,0:T(8,128)(2,1)} %get-tuple-element.41), channel_id=1, source_target_pairs={{0,4},{4,0},{8,12},{12,8},{1,5},{5,1},{9,13},{13,9},{2,6},{6,2},{1... | collective-permute-start | bytes 294920 | tf_op jit(solution)/shard_map/ppermute | solution.py:39
  101.3 0.9 collective-permute-start.23
  102.2 1.3 collective-permute-done.22.t2
  103.6 0.6 copy-done.22
  104.2 7.2 %shard_map.117 = (bf16[128,1152]{1,0:T(8,128)(2,1)}, f32[128,1152]{1,0:T(8,128)}) custom-call(s32[3]{0:T(128)} %pad_add_fusion.meta, s32[8,4]{1,0:T(8,128)} %copy.14.col, s32[4]{0:T(128)} %counts.5, bf16[8,4,128,128]{3,2,1,0:T(8,128)(2,1)} %tiles_in.5, bf16[1024,128]{1,0:T(8,128)(2,1)} %get-tuple-element.38.grad_in, bf16[384,128]{1,0:T(8,128)(2,1)} %copy-done.20, ...), custom_call_target="tpu_custom_call" | custom-call | tf_op jit(solution)/shard_map/pallas_call | solution.py:369
  111.5 1.8 %collective-permute-done.24 = bf16[128,1152]{1,0:T(8,128)(2,1)S(1)} collective-permute-done((bf16[128,1152]{1,0:T(8,128)(2,1)}, bf16[128,1152]{1,0:T(8,128)(2,1)S(1)}, u32[]{:S(2)}, u32[]{:S(2)}) %collective-permute-start.24) | collective-permute-done | bytes 294944 | tf_op jit(solution)/shard_map/ppermute | solution.py:514
  113.3 1.1 add_convert_fusion
  114.5 25.2 %all_to_all.10 = bf16[32,4,1152]{2,1,0:T(4,128)(2,1)S(1)} all-to-all(bf16[32,4,1152]{2,1,0:T(4,128)(2,1)S(1)} %reshape.15), channel_id=1, replica_groups=mesh['z'=8,'core'=2,'gy'=4,'af'=4] {'z','gy'}, dimensions={0} | all-to-all | bytes 589824 | tf_op jit(solution)/shard_map/all_to_all | solution.py:516
  139.7 0.1 reduce_sum.12
  139.9 15.2 %all_to_all.11 = bf16[32,4,1152]{2,1,0:T(4,128)(2,1)S(1)} all-to-all(bf16[32,4,1152]{2,1,0:T(4,128)(2,1)S(1)} %broadcast_in_dim.2), channel_id=1, replica_groups=mesh['z'=8,'core'=2,'gy'=4,'af'=4] {'z','gy'}, dimensions={0} | all-to-all | bytes 589824 | tf_op jit(solution)/shard_map/all_to_all | solution.py:518
  155.3 3.7 %collective-permute-start.25 = (bf16[128,1152]{1,0:T(8,128)(2,1)S(1)}, bf16[128,1152]{1,0:T(8,128)(2,1)S(1)}, u32[]{:S(2)}, u32[]{:S(2)}) collective-permute-start(bf16[128,1152]{1,0:T(8,128)(2,1)S(1)} %reshape.16), channel_id=1, source_target_pairs={{0,16},{16,0},{1,17},{17,1},{2,18},{18,2},{3,19},{19,3},{4,20},{20... | collective-permute-start | bytes 884744 | tf_op jit(solution)/shard_map/ppermute | solution.py:521
  159.0 1.2 collective-permute-done.25
  160.3 0.7 maximum_convert_fusion.1
  161.0 1.1 maximum_convert_fusion
  (73 shorter events, 0.7 us)
Async XLA Ops:
  21.0 10.0 %collective-permute-start = (bf16[384,256]{1,0:T(8,128)(2,1)}, bf16[384,256]{1,0:T(8,128)(2,1)S(1)}, u32[]{:S(2)}, u32[]{:S(2)}) collective-permute-start(bf16[384,256]{1,0:T(8,128)(2,1)} %get-tuple-element.25), channel_id=1, source_target_pairs={{0,16},{16,0},{1,17},{17,1},{2,18},{18,2},{3,19},{19,3},{4,20},{20... | collective-permute-start | bytes 589832 | tf_op jit(solution)/shard_map/ppermute | solution.py:37
  24.3 20.4 %collective-permute-start.12 = (bf16[128,1152]{1,0:T(8,128)(2,1)}, bf16[128,1152]{1,0:T(8,128)(2,1)S(1)}, u32[]{:S(2)}, u32[]{:S(2)}) collective-permute-start(bf16[128,1152]{1,0:T(8,128)(2,1)} %get-tuple-element.31.m0), channel_id=1, source_target_pairs={{0,3},{1,0},{2,1},{3,2},{4,7},{5,4},{6,5},{7,6},{8,11},{9,8},{10,9... | collective-permute-start | bytes 884744 | tf_op jit(solution)/shard_map/ppermute | solution.py:24
  25.3 22.1 %collective-permute-start.11 = (bf16[128,1152]{1,0:T(8,128)(2,1)}, bf16[128,1152]{1,0:T(8,128)(2,1)S(1)}, u32[]{:S(2)}, u32[]{:S(2)}) collective-permute-start(bf16[128,1152]{1,0:T(8,128)(2,1)} %get-tuple-element.31.m0), channel_id=1, source_target_pairs={{0,2},{1,3},{2,0},{3,1},{4,6},{5,7},{6,4},{7,5},{8,10},{9,11},{10,... | collective-permute-start | bytes 884744 | tf_op jit(solution)/shard_map/ppermute | solution.py:24
  25.7 7.9 %collective-permute-start.1 = (bf16[384,256]{1,0:T(8,128)(2,1)}, bf16[384,256]{1,0:T(8,128)(2,1)S(1)}, u32[]{:S(2)}, u32[]{:S(2)}) collective-permute-start(bf16[384,256]{1,0:T(8,128)(2,1)} %get-tuple-element.26), channel_id=1, source_target_pairs={{16,32},{32,16},{48,64},{64,48},{80,96},{96,80},{112,128},{128,112... | collective-permute-start | bytes 589832 | tf_op jit(solution)/shard_map/ppermute | solution.py:38
  29.7 5.6 %collective-permute-start.2 = (bf16[384,256]{1,0:T(8,128)(2,1)}, bf16[384,256]{1,0:T(8,128)(2,1)S(1)}, u32[]{:S(2)}, u32[]{:S(2)}) collective-permute-start(bf16[384,256]{1,0:T(8,128)(2,1)} %get-tuple-element.27), channel_id=1, source_target_pairs={{0,4},{4,0},{8,12},{12,8},{1,5},{5,1},{9,13},{13,9},{2,6},{6,2},{1... | collective-permute-start | bytes 589832 | tf_op jit(solution)/shard_map/ppermute | solution.py:39
  31.0 4.3 %copy-start.12 = (bf16[384,256]{1,0:T(8,128)(2,1)}, bf16[384,256]{1,0:T(8,128)(2,1)S(1)}, u32[]{:S(2)}) copy-start(bf16[384,256]{1,0:T(8,128)(2,1)S(1)} %collective-permute-done.r0) | copy-start | bytes 589828
  31.0 4.3 %collective-permute-start.3 = (bf16[384,256]{1,0:T(8,128)(2,1)}, bf16[384,256]{1,0:T(8,128)(2,1)S(1)}, u32[]{:S(2)}, u32[]{:S(2)}) collective-permute-start(bf16[384,256]{1,0:T(8,128)(2,1)} %get-tuple-element.28), channel_id=1, source_target_pairs={{4,8},{8,4},{5,9},{9,5},{6,10},{10,6},{7,11},{11,7},{20,24},{24,20... | collective-permute-start | bytes 589832 | tf_op jit(solution)/shard_map/ppermute | solution.py:40
  33.6 1.8 %copy-start.13 = (bf16[384,256]{1,0:T(8,128)(2,1)}, bf16[384,256]{1,0:T(8,128)(2,1)S(1)}, u32[]{:S(2)}) copy-start(bf16[384,256]{1,0:T(8,128)(2,1)S(1)} %collective-permute-done.1.r1) | copy-start | bytes 589828
  33.6 13.8 %collective-permute-start.10 = (bf16[128,1152]{1,0:T(8,128)(2,1)}, bf16[128,1152]{1,0:T(8,128)(2,1)S(1)}, u32[]{:S(2)}, u32[]{:S(2)}) collective-permute-start(bf16[128,1152]{1,0:T(8,128)(2,1)} %get-tuple-element.31.m0), channel_id=1, source_target_pairs={{0,1},{1,2},{2,3},{3,0},{4,5},{5,6},{6,7},{7,4},{8,9},{9,10},{10,1... | collective-permute-start | bytes 884744 | tf_op jit(solution)/shard_map/ppermute | solution.py:24
  35.3 0.7 copy-start.14
  36.0 0.7 copy-start.15
  42.4 8.8 %collective-permute-start.6 = (bf16[512,256]{1,0:T(8,128)(2,1)}, bf16[512,256]{1,0:T(8,128)(2,1)S(1)}, u32[]{:S(2)}, u32[]{:S(2)}) collective-permute-start(bf16[512,256]{1,0:T(8,128)(2,1)} %get-tuple-element.29.own_t.top), channel_id=1, source_target_pairs={{0,3},{1,0},{2,1},{3,2},{4,7},{5,4},{6,5},{7,6},{8,11},{9,8},{10,9... | collective-permute-start | bytes 786440 | tf_op jit(solution)/shard_map/ppermute | solution.py:24
  44.7 9.7 %collective-permute-start.4 = (bf16[512,256]{1,0:T(8,128)(2,1)}, bf16[512,256]{1,0:T(8,128)(2,1)S(1)}, u32[]{:S(2)}, u32[]{:S(2)}) collective-permute-start(bf16[512,256]{1,0:T(8,128)(2,1)} %get-tuple-element.29.own_t.top), channel_id=1, source_target_pairs={{0,1},{1,2},{2,3},{3,0},{4,5},{5,6},{6,7},{7,4},{8,9},{9,10},{10,1... | collective-permute-start | bytes 786440 | tf_op jit(solution)/shard_map/ppermute | solution.py:24
  44.7 22.7 %copy-start = (bf16[128,1152]{1,0:T(8,128)(2,1)}, bf16[128,1152]{1,0:T(8,128)(2,1)S(1)}, u32[]{:S(2)}) copy-start(bf16[128,1152]{1,0:T(8,128)(2,1)S(1)} %collective-permute-done.12.m3) | copy-start | bytes 884740
  44.7 11.8 %collective-permute-start.7 = (bf16[512,256]{1,0:T(8,128)(2,1)}, bf16[512,256]{1,0:T(8,128)(2,1)S(1)}, u32[]{:S(2)}, u32[]{:S(2)}) collective-permute-start(bf16[512,256]{1,0:T(8,128)(2,1)} %get-tuple-element.30.own_b.bottom), channel_id=1, source_target_pairs={{0,3},{1,0},{2,1},{3,2},{4,7},{5,4},{6,5},{7,6},{8,11},{9,8},{10,9... | collective-permute-start | bytes 786440 | tf_op jit(solution)/shard_map/ppermute | solution.py:24
  47.4 20.0 %copy-start.1 = (bf16[128,1152]{1,0:T(8,128)(2,1)}, bf16[128,1152]{1,0:T(8,128)(2,1)S(1)}, u32[]{:S(2)}) copy-start(bf16[128,1152]{1,0:T(8,128)(2,1)S(1)} %collective-permute-done.11.m2) | copy-start | bytes 884740
  47.4 12.6 %collective-permute-start.5 = (bf16[512,256]{1,0:T(8,128)(2,1)}, bf16[512,256]{1,0:T(8,128)(2,1)S(1)}, u32[]{:S(2)}, u32[]{:S(2)}) collective-permute-start(bf16[512,256]{1,0:T(8,128)(2,1)} %get-tuple-element.30.own_b.bottom), channel_id=1, source_target_pairs={{0,1},{1,2},{2,3},{3,0},{4,5},{5,6},{6,7},{7,4},{8,9},{9,10},{10,1... | collective-permute-start | bytes 786440 | tf_op jit(solution)/shard_map/ppermute | solution.py:24
  47.4 20.0 %copy-start.2 = (bf16[128,1152]{1,0:T(8,128)(2,1)}, bf16[128,1152]{1,0:T(8,128)(2,1)S(1)}, u32[]{:S(2)}) copy-start(bf16[128,1152]{1,0:T(8,128)(2,1)S(1)} %collective-permute-done.10.m1) | copy-start | bytes 884740
  47.4 12.6 %collective-permute-start.15 = (bf16[128,1152]{1,0:T(8,128)(2,1)S(1)}, bf16[128,1152]{1,0:T(8,128)(2,1)S(1)}, u32[]{:S(2)}, u32[]{:S(2)}) collective-permute-start(bf16[128,1152]{1,0:T(8,128)(2,1)S(1)} %collective-permute-done.12.m3), channel_id=1, source_target_pairs={{0,16},{16,0},{1,17},{17,1},{2,18},{18,2},{3,19},{19,3},{4,20},{20... | collective-permute-start | bytes 884744 | tf_op jit(solution)/shard_map/ppermute | solution.py:421
  51.2 16.3 %copy-start.6 = (bf16[512,256]{1,0:T(8,128)(2,1)}, bf16[512,256]{1,0:T(8,128)(2,1)S(1)}, u32[]{:S(2)}) copy-start(bf16[512,256]{1,0:T(8,128)(2,1)S(1)} %collective-permute-done.6.hi_t) | copy-start | bytes 786436
  51.2 8.9 %collective-permute-start.14 = (bf16[128,1152]{1,0:T(8,128)(2,1)S(1)}, bf16[128,1152]{1,0:T(8,128)(2,1)S(1)}, u32[]{:S(2)}, u32[]{:S(2)}) collective-permute-start(bf16[128,1152]{1,0:T(8,128)(2,1)S(1)} %collective-permute-done.11.m2), channel_id=1, source_target_pairs={{0,16},{16,0},{1,17},{17,1},{2,18},{18,2},{3,19},{19,3},{4,20},{20... | collective-permute-start | bytes 884744 | tf_op jit(solution)/shard_map/ppermute | solution.py:421
  54.4 13.0 %copy-start.7 = (bf16[512,256]{1,0:T(8,128)(2,1)}, bf16[512,256]{1,0:T(8,128)(2,1)S(1)}, u32[]{:S(2)}) copy-start(bf16[512,256]{1,0:T(8,128)(2,1)S(1)} %collective-permute-done.4.lo_t) | copy-start | bytes 786436
  54.4 5.7 %collective-permute-start.13 = (bf16[128,1152]{1,0:T(8,128)(2,1)S(1)}, bf16[128,1152]{1,0:T(8,128)(2,1)S(1)}, u32[]{:S(2)}, u32[]{:S(2)}) collective-permute-start(bf16[128,1152]{1,0:T(8,128)(2,1)S(1)} %collective-permute-done.10.m1), channel_id=1, source_target_pairs={{0,16},{16,0},{1,17},{17,1},{2,18},{18,2},{3,19},{19,3},{4,20},{20... | collective-permute-start | bytes 884744 | tf_op jit(solution)/shard_map/ppermute | solution.py:421
  56.6 10.9 %copy-start.8 = (bf16[512,256]{1,0:T(8,128)(2,1)}, bf16[512,256]{1,0:T(8,128)(2,1)S(1)}, u32[]{:S(2)}) copy-start(bf16[512,256]{1,0:T(8,128)(2,1)S(1)} %collective-permute-done.7.hi_b) | copy-start | bytes 786436
  56.6 9.4 %collective-permute-start.8 = (bf16[512,256]{1,0:T(8,128)(2,1)S(1)}, bf16[512,256]{1,0:T(8,128)(2,1)S(1)}, u32[]{:S(2)}, u32[]{:S(2)}) collective-permute-start(bf16[512,256]{1,0:T(8,128)(2,1)S(1)} %collective-permute-done.4.lo_t), channel_id=1, source_target_pairs={{0,1},{1,2},{2,3},{3,0},{4,5},{5,6},{6,7},{7,4},{8,9},{9,10},{10,1... | collective-permute-start | bytes 786440 | tf_op jit(solution)/shard_map/ppermute | solution.py:24
  60.0 7.4 %copy-start.9 = (bf16[512,256]{1,0:T(8,128)(2,1)}, bf16[512,256]{1,0:T(8,128)(2,1)S(1)}, u32[]{:S(2)}) copy-start(bf16[512,256]{1,0:T(8,128)(2,1)S(1)} %collective-permute-done.5.lo_b) | copy-start | bytes 786436
  60.0 7.4 %collective-permute-start.9 = (bf16[512,256]{1,0:T(8,128)(2,1)S(1)}, bf16[512,256]{1,0:T(8,128)(2,1)S(1)}, u32[]{:S(2)}, u32[]{:S(2)}) collective-permute-start(bf16[512,256]{1,0:T(8,128)(2,1)S(1)} %collective-permute-done.7.hi_b), channel_id=1, source_target_pairs={{0,3},{1,0},{2,1},{3,2},{4,7},{5,4},{6,5},{7,6},{8,11},{9,8},{10,9... | collective-permute-start | bytes 786440 | tf_op jit(solution)/shard_map/ppermute | solution.py:24
  60.0 7.4 %copy-start.3 = (bf16[128,1152]{1,0:T(8,128)(2,1)}, bf16[128,1152]{1,0:T(8,128)(2,1)S(1)}, u32[]{:S(2)}) copy-start(bf16[128,1152]{1,0:T(8,128)(2,1)S(1)} %collective-permute-done.15.v3) | copy-start | bytes 884740
  60.0 7.4 %copy-start.4 = (bf16[128,1152]{1,0:T(8,128)(2,1)}, bf16[128,1152]{1,0:T(8,128)(2,1)S(1)}, u32[]{:S(2)}) copy-start(bf16[128,1152]{1,0:T(8,128)(2,1)S(1)} %collective-permute-done.14.v2) | copy-start | bytes 884740
  60.1 7.4 %copy-start.5 = (bf16[128,1152]{1,0:T(8,128)(2,1)}, bf16[128,1152]{1,0:T(8,128)(2,1)S(1)}, u32[]{:S(2)}) copy-start(bf16[128,1152]{1,0:T(8,128)(2,1)S(1)} %collective-permute-done.13.v1) | copy-start | bytes 884740
  66.0 1.5 copy-start.10
  67.4 0.7 copy-start.11
  77.1 7.6 %collective-permute-start.16 = (bf16[384,128]{1,0:T(8,128)(2,1)}, bf16[384,128]{1,0:T(8,128)(2,1)S(1)}, u32[]{:S(2)}, u32[]{:S(2)}) collective-permute-start(bf16[384,128]{1,0:T(8,128)(2,1)} %get-tuple-element.34), channel_id=1, source_target_pairs={{0,16},{16,0},{1,17},{17,1},{2,18},{18,2},{3,19},{19,3},{4,20},{20... | collective-permute-start | bytes 294920 | tf_op jit(solution)/shard_map/ppermute | solution.py:37
  78.5 6.2 %collective-permute-start.17 = (bf16[384,128]{1,0:T(8,128)(2,1)}, bf16[384,128]{1,0:T(8,128)(2,1)S(1)}, u32[]{:S(2)}, u32[]{:S(2)}) collective-permute-start(bf16[384,128]{1,0:T(8,128)(2,1)} %get-tuple-element.35), channel_id=1, source_target_pairs={{16,32},{32,16},{48,64},{64,48},{80,96},{96,80},{112,128},{128,112... | collective-permute-start | bytes 294920 | tf_op jit(solution)/shard_map/ppermute | solution.py:38
  80.8 5.5 %collective-permute-start.18 = (bf16[384,128]{1,0:T(8,128)(2,1)}, bf16[384,128]{1,0:T(8,128)(2,1)S(1)}, u32[]{:S(2)}, u32[]{:S(2)}) collective-permute-start(bf16[384,128]{1,0:T(8,128)(2,1)} %get-tuple-element.36), channel_id=1, source_target_pairs={{0,4},{4,0},{8,12},{12,8},{1,5},{5,1},{9,13},{13,9},{2,6},{6,2},{1... | collective-permute-start | bytes 294920 | tf_op jit(solution)/shard_map/ppermute | solution.py:39
  84.1 2.2 %collective-permute-start.19 = (bf16[384,128]{1,0:T(8,128)(2,1)}, bf16[384,128]{1,0:T(8,128)(2,1)S(1)}, u32[]{:S(2)}, u32[]{:S(2)}) collective-permute-start(bf16[384,128]{1,0:T(8,128)(2,1)} %get-tuple-element.37), channel_id=1, source_target_pairs={{4,8},{8,4},{5,9},{9,5},{6,10},{10,6},{7,11},{11,7},{20,24},{24,20... | collective-permute-start | bytes 294920 | tf_op jit(solution)/shard_map/ppermute | solution.py:40
  84.7 1.6 copy-start.16
  84.7 1.5 copy-start.17
  86.3 0.7 copy-start.19
  93.5 8.7 %collective-permute-start.20 = (bf16[384,128]{1,0:T(8,128)(2,1)}, bf16[384,128]{1,0:T(8,128)(2,1)S(1)}, u32[]{:S(2)}, u32[]{:S(2)}) collective-permute-start(bf16[384,128]{1,0:T(8,128)(2,1)} %get-tuple-element.39), channel_id=1, source_target_pairs={{0,16},{16,0},{1,17},{17,1},{2,18},{18,2},{3,19},{19,3},{4,20},{20... | collective-permute-start | bytes 294920 | tf_op jit(solution)/shard_map/ppermute | solution.py:37
  93.6 8.6 %collective-permute-start.21 = (bf16[384,128]{1,0:T(8,128)(2,1)}, bf16[384,128]{1,0:T(8,128)(2,1)S(1)}, u32[]{:S(2)}, u32[]{:S(2)}) collective-permute-start(bf16[384,128]{1,0:T(8,128)(2,1)} %get-tuple-element.40), channel_id=1, source_target_pairs={{16,32},{32,16},{48,64},{64,48},{80,96},{96,80},{112,128},{128,112... | collective-permute-start | bytes 294920 | tf_op jit(solution)/shard_map/ppermute | solution.py:38
  97.7 5.8 %collective-permute-start.22 = (bf16[384,128]{1,0:T(8,128)(2,1)}, bf16[384,128]{1,0:T(8,128)(2,1)S(1)}, u32[]{:S(2)}, u32[]{:S(2)}) collective-permute-start(bf16[384,128]{1,0:T(8,128)(2,1)} %get-tuple-element.41), channel_id=1, source_target_pairs={{0,4},{4,0},{8,12},{12,8},{1,5},{5,1},{9,13},{13,9},{2,6},{6,2},{1... | collective-permute-start | bytes 294920 | tf_op jit(solution)/shard_map/ppermute | solution.py:39
  101.3 2.2 %collective-permute-start.23 = (bf16[384,128]{1,0:T(8,128)(2,1)}, bf16[384,128]{1,0:T(8,128)(2,1)S(1)}, u32[]{:S(2)}, u32[]{:S(2)}) collective-permute-start(bf16[384,128]{1,0:T(8,128)(2,1)} %get-tuple-element.42), channel_id=1, source_target_pairs={{4,8},{8,4},{5,9},{9,5},{6,10},{10,6},{7,11},{11,7},{20,24},{24,20... | collective-permute-start | bytes 294920 | tf_op jit(solution)/shard_map/ppermute | solution.py:40
  102.2 1.3 copy-start.20
  102.2 1.3 copy-start.21
  103.5 0.7 copy-start.23
  111.4 1.9 %collective-permute-start.24 = (bf16[128,1152]{1,0:T(8,128)(2,1)}, bf16[128,1152]{1,0:T(8,128)(2,1)S(1)}, u32[]{:S(2)}, u32[]{:S(2)}) collective-permute-start(bf16[128,1152]{1,0:T(8,128)(2,1)} %get-tuple-element.47), channel_id=1, source_target_pairs={{0,16},{16,0},{1,17},{17,1},{2,18},{18,2},{3,19},{19,3},{4,20},{20... | collective-permute-start | bytes 884744 | tf_op jit(solution)/shard_map/ppermute | solution.py:514
  155.3 4.9 %collective-permute-start.25 = (bf16[128,1152]{1,0:T(8,128)(2,1)S(1)}, bf16[128,1152]{1,0:T(8,128)(2,1)S(1)}, u32[]{:S(2)}, u32[]{:S(2)}) collective-permute-start(bf16[128,1152]{1,0:T(8,128)(2,1)S(1)} %reshape.16), channel_id=1, source_target_pairs={{0,16},{16,0},{1,17},{17,1},{2,18},{18,2},{3,19},{19,3},{4,20},{20... | collective-permute-start | bytes 884744 | tf_op jit(solution)/shard_map/ppermute | solution.py:521
  (2 other events, 1.3 us)

commit v7 on v5

--- a/solution.py
+++ b/solution.py
@@ -204,7 +204,7 @@
 
 def grads_kernel(
     meta, col, counts, tiles, grad, t0, t1, t2, t3, send, w_cls, slope, top, bottom,
-    units_m, units_o, theirs, mine, hot, back, acc, mix, pre,
+    hidden, theirs, mine, hot, back, acc, mix, pre,
 ):
     nodes, _ = grad.shape
     slots, tb, kt = send.shape[1], tiles.shape[2], tiles.shape[1]
@@ -234,34 +234,23 @@
     half = both.shape[0] // 2
     mine[:, :hid] = both[:half]
     theirs[:, :hid] = both[half:].astype(BF)
-    mine[:, hid:] = dot(units_m[0], mix[...], 0, 0)
-    theirs[:, hid:] = dot(units_o[0], mix[...], 0, 0).astype(BF)
-
-
-def join_kernel(meta, mine, other, grad_hidden, grad_classes):
-    half, hid = mine.shape[0], grad_hidden.shape[1]
-    for ref, part in ((mine, meta[0]), (other, 1 - meta[0])):
-        at = pl.ds(pl.multiple_of(part * half, half), half)
-        grad_hidden[at, :] = ref[:, :hid].astype(F32)
-        grad_classes[at, :] = ref[:, hid:].astype(F32)
-
-
-def call(kernel, scalars, arrays, outs, scratch, specs=None):
-    def whole(x):
-        return pl.BlockSpec(x.shape, lambda *_, n=len(x.shape): (0,) * n)
-
-    specs = specs or {}
-    outs = [jax.ShapeDtypeStruct(s, t) for s, t in outs]
+    mine[:, hid:] = dot(hidden[meta[2] * 2 + meta[0]], mix[...], 0, 0)
+    theirs[:, hid:] = dot(hidden[meta[2] * 2 + 1 - meta[0]], mix[...], 0, 0).astype(BF)
+
+
+def call(kernel, scalars, arrays, outs, scratch):
+    if not INTERPRET:
+        arrays = [pltpu.with_memory_space_constraint(x, pltpu.VMEM) for x in arrays]
     return pl.pallas_call(
         kernel,
-        grid_spec=pltpu.PrefetchScalarGridSpec(
-            num_scalar_prefetch=len(scalars),
-            grid=(1,),
-            in_specs=[specs.get(i, whole(x)) for i, x in enumerate(arrays)],
-            out_specs=[whole(x) for x in outs],
-            scratch_shapes=[pltpu.VMEM(s, t) for s, t in scratch],
-        ),
-        out_shape=outs,
+        in_specs=[pl.BlockSpec(memory_space=pltpu.SMEM) for _ in scalars]
+        + [pl.BlockSpec(memory_space=pltpu.VMEM) for _ in arrays],
+        out_specs=[pl.BlockSpec(memory_space=pltpu.VMEM) for _ in outs],
+        scratch_shapes=[pltpu.VMEM(s, t) for s, t in scratch],
+        out_shape=[
+            jax.ShapeDtypeStruct(s, t) if INTERPRET else pltpu.VMEM(s, t) for s, t in outs
+        ],
+        compiler_params=pltpu.CompilerParams(vmem_limit_bytes=24 * 2**20),
         interpret=INTERPRET,
     )(*scalars, *arrays)
 
@@ -336,7 +325,7 @@
     theirs, mine = call(
         grads_kernel,
         (meta, col_block, send_counts),
-        (adj_tiles, grad, *returned, send_rows, w_cls, slope, top, bottom, hidden, hidden),
+        (adj_tiles, grad, *returned, send_rows, w_cls, slope, top, bottom, hidden),
         [((half, both), BF), ((half, both), F32)],
         [
             ((nodes, 4 * slots), BF),
@@ -345,10 +334,6 @@
             ((nodes, classes), BF),
             ((nodes, hid), BF),
         ],
-        {
-            11: pl.BlockSpec((1, nodes, LANES), lambda i, m, c, n: (m[2] * 2 + m[0], 0, 0)),
-            12: pl.BlockSpec((1, nodes, LANES), lambda i, m, c, n: (m[2] * 2 + 1 - m[0], 0, 0)),
-        },
     )
     total = mine + lax.ppermute(theirs, "core", swap).astype(F32)
     pieces = total.astype(BF).reshape(n_plane, half // n_plane, both)
@@ -358,14 +343,12 @@
         jnp.broadcast_to(piece[None], (n_plane,) + piece.shape), PLANE, 0, 0, tiled=True
     ).reshape(half, both)
     other = lax.ppermute(mine, "core", swap)
-    grad_hidden, grad_classes = call(
-        join_kernel,
-        (meta,),
-        (mine, other),
-        [((2 * half, hid), F32), ((2 * half, classes), F32)],
-        [],
-    )
-    return (grad_hidden, grad_classes)
+    first = jnp.where(core == 0, mine, other)
+    second = jnp.where(core == 0, other, mine)
+    return (
+        jnp.concatenate([first[:, :hid], second[:, :hid]], axis=0).astype(F32),
+        jnp.concatenate([first[:, hid:], second[:, hid:]], axis=0).astype(F32),
+    )
 
 
 def solution(mesh):

time: 149 us -> 137 us (0.919)
  Pallas kernels: 36.3 us -> 19.9 us
  starting transfers between devices: 36.6 us -> 41.5 us
  waiting for transfers between devices: 26.8 us -> 22.7 us
  local copies, waits for them, and re-layouts: 5.65 us -> 8.97 us
    pallas_call x6 -> x5, Pallas kernels: 36.3 us -> 19.9 us  [call(): pl.pallas_call(kernel, in_specs=[pl.BlockSpec(memory_space=pltpu.SMEM) fo...]
    ppermute x9, waiting for transfers between devices: 19.1 us -> 15.5 us  [turn(): lax.ppermute(field, axis, [(i, (i + move) % count) for i in range(count)])]
    unnamed x53 -> x27, local copies, waits for them, and re-layouts: 5.42 us -> 8.69 us
    ppermute x3, starting transfers between devices: 0.81 us -> 3.08 us  [work(): lax.ppermute(w_mine[k], 'core', swap)]
    convert_element_type x0 -> x2, other arithmetic: none -> 1.75 us  [the longest x1 1.08 us: work(): jnp.concatenate([first[:, :hid], second[:, :hid]], axis=0).astype(F32)]
  transfers between devices with their start and end apart: 26 -> 26, of which waited for: 11 -> 12; matrix products, arithmetic and copies ran while one was open for 1% -> 1% of each run, Pallas kernels for 4% -> 2%
where the time goes in v7:
time: 137 us; the launch traced here: 136 us
  starting transfers between devices  41.5 us (30%)
  blocking collectives  40.1 us (29%)
  waiting for transfers between devices  22.7 us (17%)
  Pallas kernels  19.9 us (15%)
  local copies, waits for them, and re-layouts  8.97 us (7%)
  other arithmetic  2.08 us (2%)
    all_to_all x1, blocking collectives, work(): pieces = lax.all_to_all(pieces, PLANE, 0, 0, tiled=True)  24.9 us
    pallas_call x5, Pallas kernels, call(): pl.pallas_call(kernel, in_specs=[pl.BlockSpec(memory_space=pltpu.SMEM) fo...  19.9 us
    ppermute x9, waiting for transfers between devices, turn(): lax.ppermute(field, axis, [(i, (i + move) % count) for i in range(count)])  15.5 us
    all_to_all x1, blocking collectives, work(): lax.all_to_all(jnp.broadcast_to(piece[None], (n_plane,) + piece.shape), P...  15.2 us
    ppermute x3, starting transfers between devices, trade(): lax.ppermute(fields[1], ROWS, pairs_at(rows, 1))  11.2 us
    ppermute x3, starting transfers between devices, trade(): lax.ppermute(fields[2], 'gy', pairs_at(cols, 0))  9.08 us
    unnamed x27, local copies, waits for them, and re-layouts  8.69 us
    ppermute x9, starting transfers between devices, turn(): lax.ppermute(field, axis, [(i, (i + move) % count) for i in range(count)])  7.11 us
  transfers between devices with their start and end apart: 26, of which 12 were waited for; matrix products, arithmetic and copies ran while one was open for 1% of the time, Pallas kernels for 2%

profile of v7, /device:TPU:1, one launch (start us, length us, event | category | flops | bytes accessed | tf_op | source)
XLA Modules:
  0.0 136.1 jit_solution(5823261634232717631)
XLA Ops:
  0.7 1.0 copy-done.2
  1.8 1.0 copy-done.4
  2.8 0.8 copy-done.5
  3.7 0.7 copy-done.6
  4.4 0.7 copy-done.10
  5.0 2.1 %shard_map.113 = (bf16[384,256]{1,0:T(8,128)(2,1)S(1)}, bf16[384,256]{1,0:T(8,128)(2,1)S(1)}, bf16[384,256]{1,0:T(8,128)(2,1)S(1)}, bf16[384,256]{1,0:T(8,128)(2...) custom-call(s32[3]{0:T(128)S(1)} %pad_add_fusion.meta, s32[4]{0:T(128)S(1)} %copy-done.10, ...), custom_call_target="tpu_custom_call" | custom-call | tf_op jit(solution)/shard_map/pallas_call | solution.py:244
  7.1 3.3 %collective-permute-start = (bf16[384,256]{1,0:T(8,128)(2,1)S(1)}, bf16[384,256]{1,0:T(8,128)(2,1)S(1)}, u32[]{:S(2)}, u32[]{:S(2)}) collective-permute-start(bf16[384,256]{1,0:T(8,128)(2,1)S(1)} %get-tuple-element.25), channel_id=1, source_target_pairs={{0,16},{16,0},{1,17},{17,1},{2,18},{18,2},{3,19},{19,3},{4,20},{20... | collective-permute-start | bytes 589832 | tf_op jit(solution)/shard_map/ppermute | solution.py:37
  10.4 1.0 collective-permute-start.12
  11.8 4.1 %collective-permute-start.1 = (bf16[384,256]{1,0:T(8,128)(2,1)S(1)}, bf16[384,256]{1,0:T(8,128)(2,1)S(1)}, u32[]{:S(2)}, u32[]{:S(2)}) collective-permute-start(bf16[384,256]{1,0:T(8,128)(2,1)S(1)} %get-tuple-element.26), channel_id=1, source_target_pairs={{16,32},{32,16},{48,64},{64,48},{80,96},{96,80},{112,128},{128,112... | collective-permute-start | bytes 589832 | tf_op jit(solution)/shard_map/ppermute | solution.py:38
  15.9 1.3 collective-permute-start.2
  17.2 0.7 collective-permute-start.3
  17.8 1.7 %collective-permute-done.1.r1 = bf16[384,256]{1,0:T(8,128)(2,1)S(1)} collective-permute-done((bf16[384,256]{1,0:T(8,128)(2,1)S(1)}, bf16[384,256]{1,0:T(8,128)(2,1)S(1)}, u32[]{:S(2)}, u32[]{:S(2)}) %collective-permute-start.1) | collective-permute-done | bytes 196640 | tf_op jit(solution)/shard_map/ppermute | solution.py:38
  19.9 0.8 copy.14.col
  20.8 1.2 copy-done
  22.0 1.0 copy-done.3
  23.0 0.7 copy-done.8
  23.7 0.7 copy-done.9
  24.4 3.1 %shard_map.114 = (bf16[512,256]{1,0:T(8,128)(2,1)S(1)}, bf16[512,256]{1,0:T(8,128)(2,1)S(1)}) custom-call(s32[3]{0:T(128)S(1)} %pad_add_fusion.meta, s32[8,4]{1,0:T(8,128)S(1)} %copy.14.col, bf16[1024,256]{1,0:T(8,128)(2,1)S(1)} %copy-done.3, bf16[8,4,128,128]{3,2,1,0:T(8,128)(2,1)S(1)} %copy-done, bf16[384,256]{1,0:T(8,128)(2,1)S(1)} %collective-permute-done.r0, ...), custom_call_target="tpu_custom_call" | custom-call | tf_op jit(solution)/shard_map/pallas_call | solution.py:244
  27.5 2.4 %collective-permute-start.6 = (bf16[512,256]{1,0:T(8,128)(2,1)S(1)}, bf16[512,256]{1,0:T(8,128)(2,1)S(1)}, u32[]{:S(2)}, u32[]{:S(2)}) collective-permute-start(bf16[512,256]{1,0:T(8,128)(2,1)S(1)} %get-tuple-element.29.own_t.top), channel_id=1, source_target_pairs={{0,3},{1,0},{2,1},{3,2},{4,7},{5,4},{6,5},{7,6},{8,11},{9,8},{10,9... | collective-permute-start | bytes 786440 | tf_op jit(solution)/shard_map/ppermute | solution.py:24
  29.9 2.7 %collective-permute-start.7 = (bf16[512,256]{1,0:T(8,128)(2,1)S(1)}, bf16[512,256]{1,0:T(8,128)(2,1)S(1)}, u32[]{:S(2)}, u32[]{:S(2)}) collective-permute-start(bf16[512,256]{1,0:T(8,128)(2,1)S(1)} %get-tuple-element.30.own_b.bottom), channel_id=1, source_target_pairs={{0,3},{1,0},{2,1},{3,2},{4,7},{5,4},{6,5},{7,6},{8,11},{9,8},{10,9... | collective-permute-start | bytes 786440 | tf_op jit(solution)/shard_map/ppermute | solution.py:24
  32.6 0.7 collective-permute-start.15
  33.3 2.5 %collective-permute-done.6.hi_t = bf16[512,256]{1,0:T(8,128)(2,1)S(1)} collective-permute-done((bf16[512,256]{1,0:T(8,128)(2,1)S(1)}, bf16[512,256]{1,0:T(8,128)(2,1)S(1)}, u32[]{:S(2)}, u32[]{:S(2)}) %collective-permute-start.6) | collective-permute-done | bytes 262176 | tf_op jit(solution)/shard_map/ppermute | solution.py:24
  35.8 0.9 collective-permute-start.14
  36.7 2.2 %collective-permute-done.4.lo_t = bf16[512,256]{1,0:T(8,128)(2,1)S(1)} collective-permute-done((bf16[512,256]{1,0:T(8,128)(2,1)S(1)}, bf16[512,256]{1,0:T(8,128)(2,1)S(1)}, u32[]{:S(2)}, u32[]{:S(2)}) %collective-permute-start.4) | collective-permute-done | bytes 262176 | tf_op jit(solution)/shard_map/ppermute | solution.py:24
  38.9 1.5 %collective-permute-start.13 = (bf16[128,1152]{1,0:T(8,128)(2,1)S(1)}, bf16[128,1152]{1,0:T(8,128)(2,1)S(1)}, u32[]{:S(2)}, u32[]{:S(2)}) collective-permute-start(bf16[128,1152]{1,0:T(8,128)(2,1)S(1)} %collective-permute-done.10.m1), channel_id=1, source_target_pairs={{0,16},{16,0},{1,17},{17,1},{2,18},{18,2},{3,19},{19,3},{4,20},{20... | collective-permute-start | bytes 884744 | tf_op jit(solution)/shard_map/ppermute | solution.py:292
  40.4 1.0 collective-permute-done.7.hi_b
  41.4 3.1 %collective-permute-done.5.lo_b = bf16[512,256]{1,0:T(8,128)(2,1)S(1)} collective-permute-done((bf16[512,256]{1,0:T(8,128)(2,1)S(1)}, bf16[512,256]{1,0:T(8,128)(2,1)S(1)}, u32[]{:S(2)}, u32[]{:S(2)}) %collective-permute-start.5) | collective-permute-done | bytes 262176 | tf_op jit(solution)/shard_map/ppermute | solution.py:24
  44.8 6.0 %collective-permute-done.8.far_t = bf16[512,256]{1,0:T(8,128)(2,1)S(1)} collective-permute-done((bf16[512,256]{1,0:T(8,128)(2,1)S(1)}, bf16[512,256]{1,0:T(8,128)(2,1)S(1)}, u32[]{:S(2)}, u32[]{:S(2)}) %collective-permute-start.8) | collective-permute-done | bytes 262176 | tf_op jit(solution)/shard_map/ppermute | solution.py:24
  50.8 0.6 collective-permute-done.9.far_b
  51.4 6.2 %shard_map.115 = (bf16[8,1024,128]{2,1,0:T(8,128)(2,1)S(1)}, bf16[1024,1024]{1,0:T(8,128)(2,1)S(1)}, bf16[1024,256]{1,0:T(8,128)(2,1)S(1)}, bf16[1024,128]{1,0:T...) custom-call(s32[3]{0:T(128)S(1)} %pad_add_fusion.meta, ...), custom_call_target="tpu_custom_call" | custom-call | tf_op jit(solution)/shard_map/pallas_call | solution.py:244
  57.7 1.9 %collective-permute-start.16 = (bf16[384,128]{1,0:T(8,128)(2,1)S(1)}, bf16[384,128]{1,0:T(8,128)(2,1)S(1)}, u32[]{:S(2)}, u32[]{:S(2)}) collective-permute-start(bf16[384,128]{1,0:T(8,128)(2,1)S(1)} %get-tuple-element.34), channel_id=1, source_target_pairs={{0,16},{16,0},{1,17},{17,1},{2,18},{18,2},{3,19},{19,3},{4,20},{20... | collective-permute-start | bytes 294920 | tf_op jit(solution)/shard_map/ppermute | solution.py:37
  59.6 3.0 %collective-permute-start.17 = (bf16[384,128]{1,0:T(8,128)(2,1)S(1)}, bf16[384,128]{1,0:T(8,128)(2,1)S(1)}, u32[]{:S(2)}, u32[]{:S(2)}) collective-permute-start(bf16[384,128]{1,0:T(8,128)(2,1)S(1)} %get-tuple-element.35), channel_id=1, source_target_pairs={{16,32},{32,16},{48,64},{64,48},{80,96},{96,80},{112,128},{128,112... | collective-permute-start | bytes 294920 | tf_op jit(solution)/shard_map/ppermute | solution.py:38
  62.6 4.1 %collective-permute-start.18 = (bf16[384,128]{1,0:T(8,128)(2,1)S(1)}, bf16[384,128]{1,0:T(8,128)(2,1)S(1)}, u32[]{:S(2)}, u32[]{:S(2)}) collective-permute-start(bf16[384,128]{1,0:T(8,128)(2,1)S(1)} %get-tuple-element.36), channel_id=1, source_target_pairs={{0,4},{4,0},{8,12},{12,8},{1,5},{5,1},{9,13},{13,9},{2,6},{6,2},{1... | collective-permute-start | bytes 294920 | tf_op jit(solution)/shard_map/ppermute | solution.py:39
  66.7 0.7 collective-permute-start.19
  67.4 1.3 collective-permute-done.18.r2
  68.7 4.2 %shard_map.116 = (bf16[1024,128]{1,0:T(8,128)(2,1)S(1)}, bf16[384,128]{1,0:T(8,128)(2,1)S(1)}, bf16[384,128]{1,0:T(8,128)(2,1)S(1)}, bf16[384,128]{1,0:T(8,128)(2,1)S(1)}, bf16[384,128]{1,0:T(8,128)(2,1)S(1)}) custom-call(s32[3]{0:T(128)S(1)} %pad_add_fusion.meta, s32[8,4]{1,0:T(8,128)S(1)} %copy.14.col, bf16[8,4,128,128]{3,2,1,0:T(8,128)(2,1)S(1)} %copy-done.1, ...), custom_call_target="tpu_custom_call" | custom-call | tf_op jit(solution)/shard_map/pallas_call | solution.py:244
  73.0 4.1 %collective-permute-start.21 = (bf16[384,128]{1,0:T(8,128)(2,1)S(1)}, bf16[384,128]{1,0:T(8,128)(2,1)S(1)}, u32[]{:S(2)}, u32[]{:S(2)}) collective-permute-start(bf16[384,128]{1,0:T(8,128)(2,1)S(1)} %get-tuple-element.40), channel_id=1, source_target_pairs={{16,32},{32,16},{48,64},{64,48},{80,96},{96,80},{112,128},{128,112... | collective-permute-start | bytes 294920 | tf_op jit(solution)/shard_map/ppermute | solution.py:38
  77.1 3.6 %collective-permute-start.22 = (bf16[384,128]{1,0:T(8,128)(2,1)S(1)}, bf16[384,128]{1,0:T(8,128)(2,1)S(1)}, u32[]{:S(2)}, u32[]{:S(2)}) collective-permute-start(bf16[384,128]{1,0:T(8,128)(2,1)S(1)} %get-tuple-element.41), channel_id=1, source_target_pairs={{0,4},{4,0},{8,12},{12,8},{1,5},{5,1},{9,13},{13,9},{2,6},{6,2},{1... | collective-permute-start | bytes 294920 | tf_op jit(solution)/shard_map/ppermute | solution.py:39
  80.8 0.7 collective-permute-start.23
  81.5 1.3 collective-permute-done.22.t2
  82.8 4.3 %shard_map.117 = (bf16[128,1152]{1,0:T(8,128)(2,1)S(1)}, f32[128,1152]{1,0:T(8,128)S(1)}) custom-call(s32[3]{0:T(128)S(1)} %pad_add_fusion.meta, s32[8,4]{1,0:T(8,128)S(1)} %copy.14.col, s32[4]{0:T(128)S(1)} %copy-done.11, bf16[8,4,128,128]{3,2,1,0:T(8,128)(2,1)S(1)} %copy-done.1, bf16[1024,128]{1,0:T(8,128)(2,1)S(1)} %get-tuple-element.38.grad, ...), custom_call_target="tpu_custom_call" | custom-call | tf_op jit(solution)/shard_map/pallas_call | solution.py:244
  87.2 1.6 %collective-permute-done.24 = bf16[128,1152]{1,0:T(8,128)(2,1)S(1)} collective-permute-done((bf16[128,1152]{1,0:T(8,128)(2,1)S(1)}, bf16[128,1152]{1,0:T(8,128)(2,1)S(1)}, u32[]{:S(2)}, u32[]{:S(2)}) %collective-permute-start.24) | collective-permute-done | bytes 294944 | tf_op jit(solution)/shard_map/ppermute | solution.py:338
  88.9 24.9 %all_to_all.10 = bf16[32,4,1152]{2,1,0:T(4,128)(2,1)S(1)} all-to-all(bf16[32,4,1152]{2,1,0:T(4,128)(2,1)S(1)} %reshape.15), channel_id=1, replica_groups=mesh['z'=8,'core'=2,'gy'=4,'af'=4] {'z','gy'}, dimensions={0} | all-to-all | bytes 589824 | tf_op jit(solution)/shard_map/all_to_all | solution.py:340
  114.0 15.2 %all_to_all.11 = bf16[32,4,1152]{2,1,0:T(4,128)(2,1)S(1)} all-to-all(bf16[32,4,1152]{2,1,0:T(4,128)(2,1)S(1)} %broadcast_in_dim.2), channel_id=1, replica_groups=mesh['z'=8,'core'=2,'gy'=4,'af'=4] {'z','gy'}, dimensions={0} | all-to-all | bytes 589824 | tf_op jit(solution)/shard_map/all_to_all | solution.py:342
  129.3 3.7 %collective-permute-start.25 = (bf16[128,1152]{1,0:T(8,128)(2,1)S(1)}, bf16[128,1152]{1,0:T(8,128)(2,1)S(1)}, u32[]{:S(2)}, u32[]{:S(2)}) collective-permute-start(bf16[128,1152]{1,0:T(8,128)(2,1)S(1)} %reshape.16), channel_id=1, source_target_pairs={{0,16},{16,0},{1,17},{17,1},{2,18},{18,2},{3,19},{19,3},{4,20},{20... | collective-permute-start | bytes 884744 | tf_op jit(solution)/shard_map/ppermute | solution.py:345
  133.0 1.2 collective-permute-done.25
  134.3 0.7 maximum_convert_fusion.1
  135.0 1.1 maximum_convert_fusion
  (51 shorter events, 2.0 us)
Async XLA Ops:
  0.6 50.8 %copy-start.11 = (s32[4]{0:T(128)S(1)}, s32[4]{0:T(128)}, u32[]{:S(2)}) copy-start(s32[4]{0:T(128)} %counts.5) | copy-start | bytes 52
  0.6 50.8 %copy-start.7 = (s32[4,384]{1,0:T(4,128)S(1)}, s32[4,384]{1,0:T(4,128)}, u32[]{:S(2)}) copy-start(s32[4,384]{1,0:T(4,128)} %send.5) | copy-start | bytes 18436
  0.7 1.0 copy-start.2
  1.8 1.0 copy-start.4
  2.8 0.8 copy-start.5
  3.7 0.7 copy-start.6
  4.4 0.7 copy-start.10
  7.1 10.0 %collective-permute-start = (bf16[384,256]{1,0:T(8,128)(2,1)S(1)}, bf16[384,256]{1,0:T(8,128)(2,1)S(1)}, u32[]{:S(2)}, u32[]{:S(2)}) collective-permute-start(bf16[384,256]{1,0:T(8,128)(2,1)S(1)} %get-tuple-element.25), channel_id=1, source_target_pairs={{0,16},{16,0},{1,17},{17,1},{2,18},{18,2},{3,19},{19,3},{4,20},{20... | collective-permute-start | bytes 589832 | tf_op jit(solution)/shard_map/ppermute | solution.py:37
  10.4 19.5 %collective-permute-start.12 = (bf16[128,1152]{1,0:T(8,128)(2,1)S(1)}, bf16[128,1152]{1,0:T(8,128)(2,1)S(1)}, u32[]{:S(2)}, u32[]{:S(2)}) collective-permute-start(bf16[128,1152]{1,0:T(8,128)(2,1)S(1)} %get-tuple-element.31.m0), channel_id=1, source_target_pairs={{0,3},{1,0},{2,1},{3,2},{4,7},{5,4},{6,5},{7,6},{8,11},{9,8},{10,9... | collective-permute-start | bytes 884744 | tf_op jit(solution)/shard_map/ppermute | solution.py:24
  11.4 21.1 %collective-permute-start.11 = (bf16[128,1152]{1,0:T(8,128)(2,1)S(1)}, bf16[128,1152]{1,0:T(8,128)(2,1)S(1)}, u32[]{:S(2)}, u32[]{:S(2)}) collective-permute-start(bf16[128,1152]{1,0:T(8,128)(2,1)S(1)} %get-tuple-element.31.m0), channel_id=1, source_target_pairs={{0,2},{1,3},{2,0},{3,1},{4,6},{5,7},{6,4},{7,5},{8,10},{9,11},{10,... | collective-permute-start | bytes 884744 | tf_op jit(solution)/shard_map/ppermute | solution.py:24
  11.8 7.7 %collective-permute-start.1 = (bf16[384,256]{1,0:T(8,128)(2,1)S(1)}, bf16[384,256]{1,0:T(8,128)(2,1)S(1)}, u32[]{:S(2)}, u32[]{:S(2)}) collective-permute-start(bf16[384,256]{1,0:T(8,128)(2,1)S(1)} %get-tuple-element.26), channel_id=1, source_target_pairs={{16,32},{32,16},{48,64},{64,48},{80,96},{96,80},{112,128},{128,112... | collective-permute-start | bytes 589832 | tf_op jit(solution)/shard_map/ppermute | solution.py:38
  15.9 4.9 %collective-permute-start.2 = (bf16[384,256]{1,0:T(8,128)(2,1)S(1)}, bf16[384,256]{1,0:T(8,128)(2,1)S(1)}, u32[]{:S(2)}, u32[]{:S(2)}) collective-permute-start(bf16[384,256]{1,0:T(8,128)(2,1)S(1)} %get-tuple-element.27), channel_id=1, source_target_pairs={{0,4},{4,0},{8,12},{12,8},{1,5},{5,1},{9,13},{13,9},{2,6},{6,2},{1... | collective-permute-start | bytes 589832 | tf_op jit(solution)/shard_map/ppermute | solution.py:39
  17.2 3.6 %collective-permute-start.3 = (bf16[384,256]{1,0:T(8,128)(2,1)S(1)}, bf16[384,256]{1,0:T(8,128)(2,1)S(1)}, u32[]{:S(2)}, u32[]{:S(2)}) collective-permute-start(bf16[384,256]{1,0:T(8,128)(2,1)S(1)} %get-tuple-element.28), channel_id=1, source_target_pairs={{4,8},{8,4},{5,9},{9,5},{6,10},{10,6},{7,11},{11,7},{20,24},{24,20... | collective-permute-start | bytes 589832 | tf_op jit(solution)/shard_map/ppermute | solution.py:40
  19.5 13.1 %collective-permute-start.10 = (bf16[128,1152]{1,0:T(8,128)(2,1)S(1)}, bf16[128,1152]{1,0:T(8,128)(2,1)S(1)}, u32[]{:S(2)}, u32[]{:S(2)}) collective-permute-start(bf16[128,1152]{1,0:T(8,128)(2,1)S(1)} %get-tuple-element.31.m0), channel_id=1, source_target_pairs={{0,1},{1,2},{2,3},{3,0},{4,5},{5,6},{6,7},{7,4},{8,9},{9,10},{10,1... | collective-permute-start | bytes 884744 | tf_op jit(solution)/shard_map/ppermute | solution.py:24
  20.8 1.2 copy-start
  22.0 1.0 copy-start.3
  23.0 0.7 copy-start.8
  23.7 0.7 copy-start.9
  27.5 8.3 %collective-permute-start.6 = (bf16[512,256]{1,0:T(8,128)(2,1)S(1)}, bf16[512,256]{1,0:T(8,128)(2,1)S(1)}, u32[]{:S(2)}, u32[]{:S(2)}) collective-permute-start(bf16[512,256]{1,0:T(8,128)(2,1)S(1)} %get-tuple-element.29.own_t.top), channel_id=1, source_target_pairs={{0,3},{1,0},{2,1},{3,2},{4,7},{5,4},{6,5},{7,6},{8,11},{9,8},{10,9... | collective-permute-start | bytes 786440 | tf_op jit(solution)/shard_map/ppermute | solution.py:24
  29.9 9.0 %collective-permute-start.4 = (bf16[512,256]{1,0:T(8,128)(2,1)S(1)}, bf16[512,256]{1,0:T(8,128)(2,1)S(1)}, u32[]{:S(2)}, u32[]{:S(2)}) collective-permute-start(bf16[512,256]{1,0:T(8,128)(2,1)S(1)} %get-tuple-element.29.own_t.top), channel_id=1, source_target_pairs={{0,1},{1,2},{2,3},{3,0},{4,5},{5,6},{6,7},{7,4},{8,9},{9,10},{10,1... | collective-permute-start | bytes 786440 | tf_op jit(solution)/shard_map/ppermute | solution.py:24
  29.9 11.5 %collective-permute-start.7 = (bf16[512,256]{1,0:T(8,128)(2,1)S(1)}, bf16[512,256]{1,0:T(8,128)(2,1)S(1)}, u32[]{:S(2)}, u32[]{:S(2)}) collective-permute-start(bf16[512,256]{1,0:T(8,128)(2,1)S(1)} %get-tuple-element.30.own_b.bottom), channel_id=1, source_target_pairs={{0,3},{1,0},{2,1},{3,2},{4,7},{5,4},{6,5},{7,6},{8,11},{9,8},{10,9... | collective-permute-start | bytes 786440 | tf_op jit(solution)/shard_map/ppermute | solution.py:24
  32.6 11.9 %collective-permute-start.5 = (bf16[512,256]{1,0:T(8,128)(2,1)S(1)}, bf16[512,256]{1,0:T(8,128)(2,1)S(1)}, u32[]{:S(2)}, u32[]{:S(2)}) collective-permute-start(bf16[512,256]{1,0:T(8,128)(2,1)S(1)} %get-tuple-element.30.own_b.bottom), channel_id=1, source_target_pairs={{0,1},{1,2},{2,3},{3,0},{4,5},{5,6},{6,7},{7,4},{8,9},{9,10},{10,1... | collective-permute-start | bytes 786440 | tf_op jit(solution)/shard_map/ppermute | solution.py:24
  32.6 12.2 %collective-permute-start.15 = (bf16[128,1152]{1,0:T(8,128)(2,1)S(1)}, bf16[128,1152]{1,0:T(8,128)(2,1)S(1)}, u32[]{:S(2)}, u32[]{:S(2)}) collective-permute-start(bf16[128,1152]{1,0:T(8,128)(2,1)S(1)} %collective-permute-done.12.m3), channel_id=1, source_target_pairs={{0,16},{16,0},{1,17},{17,1},{2,18},{18,2},{3,19},{19,3},{4,20},{20... | collective-permute-start | bytes 884744 | tf_op jit(solution)/shard_map/ppermute | solution.py:292
  35.8 9.0 %collective-permute-start.14 = (bf16[128,1152]{1,0:T(8,128)(2,1)S(1)}, bf16[128,1152]{1,0:T(8,128)(2,1)S(1)}, u32[]{:S(2)}, u32[]{:S(2)}) collective-permute-start(bf16[128,1152]{1,0:T(8,128)(2,1)S(1)} %collective-permute-done.11.m2), channel_id=1, source_target_pairs={{0,16},{16,0},{1,17},{17,1},{2,18},{18,2},{3,19},{19,3},{4,20},{20... | collective-permute-start | bytes 884744 | tf_op jit(solution)/shard_map/ppermute | solution.py:292
  38.9 5.9 %collective-permute-start.13 = (bf16[128,1152]{1,0:T(8,128)(2,1)S(1)}, bf16[128,1152]{1,0:T(8,128)(2,1)S(1)}, u32[]{:S(2)}, u32[]{:S(2)}) collective-permute-start(bf16[128,1152]{1,0:T(8,128)(2,1)S(1)} %collective-permute-done.10.m1), channel_id=1, source_target_pairs={{0,16},{16,0},{1,17},{17,1},{2,18},{18,2},{3,19},{19,3},{4,20},{20... | collective-permute-start | bytes 884744 | tf_op jit(solution)/shard_map/ppermute | solution.py:292
  41.3 9.4 %collective-permute-start.8 = (bf16[512,256]{1,0:T(8,128)(2,1)S(1)}, bf16[512,256]{1,0:T(8,128)(2,1)S(1)}, u32[]{:S(2)}, u32[]{:S(2)}) collective-permute-start(bf16[512,256]{1,0:T(8,128)(2,1)S(1)} %collective-permute-done.4.lo_t), channel_id=1, source_target_pairs={{0,1},{1,2},{2,3},{3,0},{4,5},{5,6},{6,7},{7,4},{8,9},{9,10},{10,1... | collective-permute-start | bytes 786440 | tf_op jit(solution)/shard_map/ppermute | solution.py:24
  44.5 6.9 %collective-permute-start.9 = (bf16[512,256]{1,0:T(8,128)(2,1)S(1)}, bf16[512,256]{1,0:T(8,128)(2,1)S(1)}, u32[]{:S(2)}, u32[]{:S(2)}) collective-permute-start(bf16[512,256]{1,0:T(8,128)(2,1)S(1)} %collective-permute-done.7.hi_b), channel_id=1, source_target_pairs={{0,3},{1,0},{2,1},{3,2},{4,7},{5,4},{6,5},{7,6},{8,11},{9,8},{10,9... | collective-permute-start | bytes 786440 | tf_op jit(solution)/shard_map/ppermute | solution.py:24
  51.4 17.3 %copy-start.1 = (bf16[8,4,128,128]{3,2,1,0:T(8,128)(2,1)S(1)}, bf16[8,4,128,128]{3,2,1,0:T(8,128)(2,1)}, u32[]{:S(2)}) copy-start(bf16[8,4,128,128]{3,2,1,0:T(8,128)(2,1)} %tiles.5) | copy-start | bytes 3145732
  51.4 17.3 %copy-start.12 = (s32[1024]{0:T(1024)S(1)}, s32[1024]{0:T(1024)}, u32[]{:S(2)}) copy-start(s32[1024]{0:T(1024)} %param.17) | copy-start | bytes 12292
  57.7 9.7 %collective-permute-start.16 = (bf16[384,128]{1,0:T(8,128)(2,1)S(1)}, bf16[384,128]{1,0:T(8,128)(2,1)S(1)}, u32[]{:S(2)}, u32[]{:S(2)}) collective-permute-start(bf16[384,128]{1,0:T(8,128)(2,1)S(1)} %get-tuple-element.34), channel_id=1, source_target_pairs={{0,16},{16,0},{1,17},{17,1},{2,18},{18,2},{3,19},{19,3},{4,20},{20... | collective-permute-start | bytes 294920 | tf_op jit(solution)/shard_map/ppermute | solution.py:37
  59.6 7.8 %collective-permute-start.17 = (bf16[384,128]{1,0:T(8,128)(2,1)S(1)}, bf16[384,128]{1,0:T(8,128)(2,1)S(1)}, u32[]{:S(2)}, u32[]{:S(2)}) collective-permute-start(bf16[384,128]{1,0:T(8,128)(2,1)S(1)} %get-tuple-element.35), channel_id=1, source_target_pairs={{16,32},{32,16},{48,64},{64,48},{80,96},{96,80},{112,128},{128,112... | collective-permute-start | bytes 294920 | tf_op jit(solution)/shard_map/ppermute | solution.py:38
  62.6 6.1 %collective-permute-start.18 = (bf16[384,128]{1,0:T(8,128)(2,1)S(1)}, bf16[384,128]{1,0:T(8,128)(2,1)S(1)}, u32[]{:S(2)}, u32[]{:S(2)}) collective-permute-start(bf16[384,128]{1,0:T(8,128)(2,1)S(1)} %get-tuple-element.36), channel_id=1, source_target_pairs={{0,4},{4,0},{8,12},{12,8},{1,5},{5,1},{9,13},{13,9},{2,6},{6,2},{1... | collective-permute-start | bytes 294920 | tf_op jit(solution)/shard_map/ppermute | solution.py:39
  66.7 2.0 %collective-permute-start.19 = (bf16[384,128]{1,0:T(8,128)(2,1)S(1)}, bf16[384,128]{1,0:T(8,128)(2,1)S(1)}, u32[]{:S(2)}, u32[]{:S(2)}) collective-permute-start(bf16[384,128]{1,0:T(8,128)(2,1)S(1)} %get-tuple-element.37), channel_id=1, source_target_pairs={{4,8},{8,4},{5,9},{9,5},{6,10},{10,6},{7,11},{11,7},{20,24},{24,20... | collective-permute-start | bytes 294920 | tf_op jit(solution)/shard_map/ppermute | solution.py:40
  72.9 8.5 %collective-permute-start.20 = (bf16[384,128]{1,0:T(8,128)(2,1)S(1)}, bf16[384,128]{1,0:T(8,128)(2,1)S(1)}, u32[]{:S(2)}, u32[]{:S(2)}) collective-permute-start(bf16[384,128]{1,0:T(8,128)(2,1)S(1)} %get-tuple-element.39), channel_id=1, source_target_pairs={{0,16},{16,0},{1,17},{17,1},{2,18},{18,2},{3,19},{19,3},{4,20},{20... | collective-permute-start | bytes 294920 | tf_op jit(solution)/shard_map/ppermute | solution.py:37
  73.0 8.4 %collective-permute-start.21 = (bf16[384,128]{1,0:T(8,128)(2,1)S(1)}, bf16[384,128]{1,0:T(8,128)(2,1)S(1)}, u32[]{:S(2)}, u32[]{:S(2)}) collective-permute-start(bf16[384,128]{1,0:T(8,128)(2,1)S(1)} %get-tuple-element.40), channel_id=1, source_target_pairs={{16,32},{32,16},{48,64},{64,48},{80,96},{96,80},{112,128},{128,112... | collective-permute-start | bytes 294920 | tf_op jit(solution)/shard_map/ppermute | solution.py:38
  77.1 5.7 %collective-permute-start.22 = (bf16[384,128]{1,0:T(8,128)(2,1)S(1)}, bf16[384,128]{1,0:T(8,128)(2,1)S(1)}, u32[]{:S(2)}, u32[]{:S(2)}) collective-permute-start(bf16[384,128]{1,0:T(8,128)(2,1)S(1)} %get-tuple-element.41), channel_id=1, source_target_pairs={{0,4},{4,0},{8,12},{12,8},{1,5},{5,1},{9,13},{13,9},{2,6},{6,2},{1... | collective-permute-start | bytes 294920 | tf_op jit(solution)/shard_map/ppermute | solution.py:39
  80.8 2.0 %collective-permute-start.23 = (bf16[384,128]{1,0:T(8,128)(2,1)S(1)}, bf16[384,128]{1,0:T(8,128)(2,1)S(1)}, u32[]{:S(2)}, u32[]{:S(2)}) collective-permute-start(bf16[384,128]{1,0:T(8,128)(2,1)S(1)} %get-tuple-element.42), channel_id=1, source_target_pairs={{4,8},{8,4},{5,9},{9,5},{6,10},{10,6},{7,11},{11,7},{20,24},{24,20... | collective-permute-start | bytes 294920 | tf_op jit(solution)/shard_map/ppermute | solution.py:40
  87.1 1.7 %collective-permute-start.24 = (bf16[128,1152]{1,0:T(8,128)(2,1)S(1)}, bf16[128,1152]{1,0:T(8,128)(2,1)S(1)}, u32[]{:S(2)}, u32[]{:S(2)}) collective-permute-start(bf16[128,1152]{1,0:T(8,128)(2,1)S(1)} %get-tuple-element.47), channel_id=1, source_target_pairs={{0,16},{16,0},{1,17},{17,1},{2,18},{18,2},{3,19},{19,3},{4,20},{20... | collective-permute-start | bytes 884744 | tf_op jit(solution)/shard_map/ppermute | solution.py:338
  129.3 4.9 %collective-permute-start.25 = (bf16[128,1152]{1,0:T(8,128)(2,1)S(1)}, bf16[128,1152]{1,0:T(8,128)(2,1)S(1)}, u32[]{:S(2)}, u32[]{:S(2)}) collective-permute-start(bf16[128,1152]{1,0:T(8,128)(2,1)S(1)} %reshape.16), channel_id=1, source_target_pairs={{0,16},{16,0},{1,17},{17,1},{2,18},{18,2},{3,19},{19,3},{4,20},{20... | collective-permute-start | bytes 884744 | tf_op jit(solution)/shard_map/ppermute | solution.py:345

commit v8 on v7

--- a/solution.py
+++ b/solution.py
@@ -70,10 +70,10 @@
     return jnp.where(ids == row, 1.0, 0.0).astype(BF)
 
 
-def live_row(send_ref, counts, d):
+def live_row(send_ref, meta, d):
     row = send_ref[pl.ds(d, 1), :]
     slot = lax.broadcasted_iota(jnp.int32, row.shape, 1)
-    return jnp.where(slot < counts[d], row, -1)
+    return jnp.where(slot < meta[3 + d], row, -1)
 
 
 def weigh(arrived, weight_row, rhs_ref, base):
@@ -88,23 +88,35 @@
         rhs_ref[pl.ds(base + b * LANES, LANES), width:] = low
 
 
-def send_kernel(meta, counts, feat, send, w_hid, w_cls, o0, o1, o2, o3, mine, other, hot):
+def send_kernel(
+    meta, feat_in, send_in, w_hid, w_cls, tiles_in, recv_in, weight_in, labels_in,
+    o0, o1, o2, o3, mine, other, feat, send, tiles, recv, weight, labels, hot, sems,
+):
     nodes = feat.shape[0]
     half, hid = w_hid.shape[0] // 2, w_hid.shape[1]
+    moves = [(send_in, send), (feat_in, feat)]
     for ref, part in ((mine, meta[0]), (other, 1 - meta[0])):
-        at = pl.multiple_of(part * half, half)
-        ref[:, :hid] = w_hid[pl.ds(at, half), :]
-        ref[:, hid:] = w_cls[pl.ds(at, half), :]
+        at = pl.ds(pl.multiple_of(part * half, half), half)
+        moves.append((w_hid.at[at, :], ref.at[:, :hid]))
+        moves.append((w_cls.at[at, :], ref.at[:, hid:]))
+    moves += [(tiles_in, tiles), (recv_in, recv), (weight_in, weight), (labels_in, labels)]
+    copies = [pltpu.make_async_copy(x, y, sems.at[i]) for i, (x, y) in enumerate(moves)]
+    for copy in copies:
+        copy.start()
+    copies[0].wait()
+    copies[1].wait()
     for d, out in zip(send_order(meta), (o0, o1, o2, o3)):
-        pick(live_row(send, counts, d), nodes, hot)
+        pick(live_row(send, meta, d), nodes, hot)
         out[...] = dot(hot[...], feat[...]).astype(BF)
+    for copy in copies[2:]:
+        copy.wait()
 
 
 def near(tiles, col, field, block, tb):
     lhs = jnp.concatenate([tiles[block, k] for k in range(tiles.shape[1])], axis=1)
     rhs = jnp.concatenate(
         [
-            field[pl.ds(pl.multiple_of(col[block, k] * tb, tb), tb), :]
+            field[pl.ds(pl.multiple_of(col[k, block] * tb, tb), tb), :]
             for k in range(tiles.shape[1])
         ],
         axis=0,
@@ -130,7 +142,7 @@
 
 
 def hidden_kernel(
-    meta, counts, send, own_t, own_b, lo_t, lo_b, hi_t, hi_b, far_t, far_b,
+    meta, send, own_t, own_b, lo_t, lo_b, hi_t, hi_b, far_t, far_b,
     m0, m1, m2, m3, v0, v1, v2, v3,
     hidden, slope, z_pair, w_cls, o0, o1, o2, o3, w_all, hot,
 ):
@@ -167,7 +179,7 @@
 
         lax.fori_loop(0, part // rows, block, 0)
     for d, out in zip(send_order(meta), (o0, o1, o2, o3)):
-        pick(live_row(send, counts, d), nodes, hot)
+        pick(live_row(send, meta, d), nodes, hot)
         out[...] = dot(hot[...], z_pair[:, :classes]).astype(BF)
 
 
@@ -203,21 +215,21 @@
 
 
 def grads_kernel(
-    meta, col, counts, tiles, grad, t0, t1, t2, t3, send, w_cls, slope, top, bottom,
+    meta, col, tiles, grad, t0, t1, t2, t3, send, w_cls, slope, top, bottom,
     hidden, theirs, mine, hot, back, acc, mix, pre,
 ):
     nodes, _ = grad.shape
     slots, tb, kt = send.shape[1], tiles.shape[2], tiles.shape[1]
     hid = slope.shape[1]
     for m, (d, returned) in enumerate(zip(send_order(meta), (t0, t1, t2, t3))):
-        hot[:, m * slots : (m + 1) * slots] = put(live_row(send, counts, d), nodes)
+        hot[:, m * slots : (m + 1) * slots] = put(live_row(send, meta, d), nodes)
         back[m * slots : (m + 1) * slots, :] = returned[...]
     acc[...] = dot(hot[...], back[...])
     for r in range(tiles.shape[0]):
         lhs = jnp.concatenate([tiles[r, k] for k in range(kt)], axis=1)
         spread = dot(lhs, grad[r * tb : (r + 1) * tb, :], 0, 0)
         for k in range(kt):
-            at = pl.ds(pl.multiple_of(col[r, k] * tb, tb), tb)
+            at = pl.ds(pl.multiple_of(col[k, r] * tb, tb), tb)
             acc[at, :] += spread[k * tb : (k + 1) * tb, :]
     mix[...] = acc[...].astype(BF)
     rows = 256
@@ -238,15 +250,19 @@
     theirs[:, hid:] = dot(hidden[meta[2] * 2 + 1 - meta[0]], mix[...], 0, 0).astype(BF)
 
 
-def call(kernel, scalars, arrays, outs, scratch):
-    if not INTERPRET:
-        arrays = [pltpu.with_memory_space_constraint(x, pltpu.VMEM) for x in arrays]
+def call(kernel, scalars, arrays, outs, scratch, copies=0):
+    space = pltpu.HBM if copies else pltpu.VMEM
+    if INTERPRET:
+        space = pl.ANY if copies else pltpu.VMEM
+    else:
+        arrays = [pltpu.with_memory_space_constraint(x, space) for x in arrays]
+    sems = [pltpu.SemaphoreType.DMA((copies,))] if copies else []
     return pl.pallas_call(
         kernel,
         in_specs=[pl.BlockSpec(memory_space=pltpu.SMEM) for _ in scalars]
-        + [pl.BlockSpec(memory_space=pltpu.VMEM) for _ in arrays],
+        + [pl.BlockSpec(memory_space=space) for _ in arrays],
         out_specs=[pl.BlockSpec(memory_space=pltpu.VMEM) for _ in outs],
-        scratch_shapes=[pltpu.VMEM(s, t) for s, t in scratch],
+        scratch_shapes=[pltpu.VMEM(s, t) for s, t in scratch] + sems,
         out_shape=[
             jax.ShapeDtypeStruct(s, t) if INTERPRET else pltpu.VMEM(s, t) for s, t in outs
         ],
@@ -275,24 +291,39 @@
     n_plane = lax.axis_size("z") * lax.axis_size("gy")
     core = lax.axis_index("core")
     af = lax.axis_index("af")
-    meta = jnp.stack([core, lax.axis_index("gy"), af]).astype(jnp.int32)
+    place = jnp.stack([core, lax.axis_index("gy"), af]).astype(jnp.int32)
+    meta = jnp.concatenate([place, send_counts])
+    columns = col_block.T
     swap = [(0, 1), (1, 0)]
     both = hid + classes
     part = nodes // 2
 
-    *out, w_mine, w_other = call(
+    taken = (
+        features,
+        send_rows,
+        w_hidden,
+        w_classes,
+        adj_tiles,
+        recv_target,
+        edge_weight,
+        labels.reshape(-1, LANES),
+    )
+    *out, w_mine, w_other, features, send_rows, adj_tiles, recv_target, edge_weight, labels = call(
         send_kernel,
-        (meta, send_counts),
-        (features, send_rows, w_hidden, w_classes),
-        [((slots, width), BF)] * 4 + [((half, both), BF)] * 2,
+        (meta,),
+        taken,
+        [((slots, width), BF)] * 4
+        + [((half, both), BF)] * 2
+        + [(taken[i].shape, taken[i].dtype) for i in (0, 1, 4, 5, 6, 7)],
         [((slots, nodes), BF)],
+        10,
     )
     arrived = trade(out)
     w_mine = [w_mine] + [turn(w_mine, "af", k) for k in range(1, n_af)]
     w_other = [w_other] + [lax.ppermute(w_mine[k], "core", swap) for k in range(1, n_af)]
     top, bottom = call(
         mix_kernel,
-        (meta, col_block),
+        (meta, columns),
         (features, adj_tiles, *arrived, recv_target, edge_weight),
         [((part, width), BF)] * 2,
         [((nodes, 4 * slots), BF), ((4 * slots, 2 * width), BF)],
@@ -302,7 +333,7 @@
     far_t, far_b = turn(lo_t, "af", 1), turn(hi_b, "af", -1)
     hidden, slope, z_pair, w_cls, *out = call(
         hidden_kernel,
-        (meta, send_counts),
+        (meta,),
         (send_rows, top, bottom, lo_t, lo_b, hi_t, hi_b, far_t, far_b, *w_mine, *w_other),
         [
             ((hid // LANES, nodes, LANES), BF),
@@ -316,15 +347,15 @@
     arrived = trade(out)
     grad, *out = call(
         loss_kernel,
-        (meta, col_block),
-        (adj_tiles, z_pair, *arrived, recv_target, edge_weight, labels.reshape(-1, LANES)),
+        (meta, columns),
+        (adj_tiles, z_pair, *arrived, recv_target, edge_weight, labels),
         [((nodes, classes), BF)] + [((slots, classes), BF)] * 4,
         [((nodes, 4 * slots), BF), ((4 * slots, 2 * classes), BF), ((slots, nodes), BF)],
     )
     returned = trade(out)
     theirs, mine = call(
         grads_kernel,
-        (meta, col_block, send_counts),
+        (meta, columns),
         (adj_tiles, grad, *returned, send_rows, w_cls, slope, top, bottom, hidden),
         [((half, both), BF), ((half, both), F32)],
         [

time: 137 us -> 130 us (0.949)
  local copies, waits for them, and re-layouts: 8.97 us -> 0.28 us
    unnamed x27 -> x2, local copies, waits for them, and re-layouts: 8.69 us -> 0.01 us
  transfers between devices with their start and end apart: 26 -> 26, of which waited for: 12 -> 12; matrix products, arithmetic and copies ran while one was open for 1% -> 0% of each run, Pallas kernels for 2% -> 2%
where the time goes in v8:
time: 130 us
  starting transfers between devices  41.3 us (32%)
  blocking collectives  40.1 us (31%)
  waiting for transfers between devices  23.6 us (18%)
  Pallas kernels  21 us (16%)
  other arithmetic  2.74 us (2%)
    all_to_all x1, blocking collectives, work(): pieces = lax.all_to_all(pieces, PLANE, 0, 0, tiled=True)  24.9 us
    pallas_call x5, Pallas kernels, call(): pl.pallas_call(kernel, in_specs=[pl.BlockSpec(memory_space=pltpu.SMEM) fo...  21 us
    ppermute x9, waiting for transfers between devices, turn(): lax.ppermute(field, axis, [(i, (i + move) % count) for i in range(count)])  15.6 us
    all_to_all x1, blocking collectives, work(): lax.all_to_all(jnp.broadcast_to(piece[None], (n_plane,) + piece.shape), P...  15.2 us
    ppermute x3, starting transfers between devices, trade(): lax.ppermute(fields[1], ROWS, pairs_at(rows, 1))  11.2 us
    ppermute x3, starting transfers between devices, trade(): lax.ppermute(fields[2], 'gy', pairs_at(cols, 0))  9.07 us
    ppermute x9, starting transfers between devices, turn(): lax.ppermute(field, axis, [(i, (i + move) % count) for i in range(count)])  7.11 us
    ppermute x3, starting transfers between devices, trade(): lax.ppermute(fields[0], 'core', [(0, 1), (1, 0)])  5.27 us
  transfers between devices with their start and end apart: 26, of which 12 were waited for; matrix products, arithmetic and copies ran while one was open for 0% of the time, Pallas kernels for 2%

profile of v8, /device:TPU:1, one launch (start us, length us, event | category | flops | bytes accessed | tf_op | source)
XLA Modules:
  0.0 129.8 jit_solution(10792120415255984707)
XLA Ops:
  0.6 0.7 pad_add_fusion.meta
  1.4 3.3 %shard_map.113 = (bf16[384,256]{1,0:T(8,128)(2,1)S(1)}, bf16[384,256]{1,0:T(8,128)(2,1)S(1)}, bf16[384,256]{1,0:T(8,128)(2,1)S(1)}, bf16[384,256]{1,0:T(8,128)(2...) custom-call(s32[7]{0:T(128)S(1)} %pad_add_fusion.meta, ...), custom_call_target="tpu_custom_call" | custom-call | tf_op jit(solution)/shard_map/pallas_call | solution.py:260
  4.7 3.3 %collective-permute-start = (bf16[384,256]{1,0:T(8,128)(2,1)S(1)}, bf16[384,256]{1,0:T(8,128)(2,1)S(1)}, u32[]{:S(2)}, u32[]{:S(2)}) collective-permute-start(bf16[384,256]{1,0:T(8,128)(2,1)S(1)} %get-tuple-element.34), channel_id=1, source_target_pairs={{0,16},{16,0},{1,17},{17,1},{2,18},{18,2},{3,19},{19,3},{4,20},{20... | collective-permute-start | bytes 589832 | tf_op jit(solution)/shard_map/ppermute | solution.py:37
  7.9 1.0 collective-permute-start.12
  9.0 0.3 collective-permute-start.11
  9.3 4.1 %collective-permute-start.1 = (bf16[384,256]{1,0:T(8,128)(2,1)S(1)}, bf16[384,256]{1,0:T(8,128)(2,1)S(1)}, u32[]{:S(2)}, u32[]{:S(2)}) collective-permute-start(bf16[384,256]{1,0:T(8,128)(2,1)S(1)} %get-tuple-element.35), channel_id=1, source_target_pairs={{16,32},{32,16},{48,64},{64,48},{80,96},{96,80},{112,128},{128,112... | collective-permute-start | bytes 589832 | tf_op jit(solution)/shard_map/ppermute | solution.py:38
  13.4 1.3 %collective-permute-start.2 = (bf16[384,256]{1,0:T(8,128)(2,1)S(1)}, bf16[384,256]{1,0:T(8,128)(2,1)S(1)}, u32[]{:S(2)}, u32[]{:S(2)}) collective-permute-start(bf16[384,256]{1,0:T(8,128)(2,1)S(1)} %get-tuple-element.36), channel_id=1, source_target_pairs={{0,4},{4,0},{8,12},{12,8},{1,5},{5,1},{9,13},{13,9},{2,6},{6,2},{1... | collective-permute-start | bytes 589832 | tf_op jit(solution)/shard_map/ppermute | solution.py:39
  14.7 0.7 collective-permute-start.3
  15.4 1.7 %collective-permute-done.1.r1 = bf16[384,256]{1,0:T(8,128)(2,1)S(1)} collective-permute-done((bf16[384,256]{1,0:T(8,128)(2,1)S(1)}, bf16[384,256]{1,0:T(8,128)(2,1)S(1)}, u32[]{:S(2)}, u32[]{:S(2)}) %collective-permute-start.1) | collective-permute-done | bytes 196640 | tf_op jit(solution)/shard_map/ppermute | solution.py:38
  17.0 0.4 collective-permute-start.10
  17.4 0.9 collective-permute-done.2.r2
  18.3 3.0 %shard_map.114 = (bf16[512,256]{1,0:T(8,128)(2,1)S(1)}, bf16[512,256]{1,0:T(8,128)(2,1)S(1)}) custom-call(s32[7]{0:T(128)S(1)} %pad_add_fusion.meta, s32[4,8]{1,0:T(4,128)S(1)} %bitcast.5, bf16[1024,256]{1,0:T(8,128)(2,1)S(1)} %get-tuple-element.33.feat, bf16[8,4,128,128]{3,2,1,0:T(8,128)(2,1)S(1)} %get-tuple-element.31.tiles, ...), custom_call_target="tpu_custom_call" | custom-call | tf_op jit(solution)/shard_map/pallas_call | solution.py:260
  21.4 2.4 %collective-permute-start.6 = (bf16[512,256]{1,0:T(8,128)(2,1)S(1)}, bf16[512,256]{1,0:T(8,128)(2,1)S(1)}, u32[]{:S(2)}, u32[]{:S(2)}) collective-permute-start(bf16[512,256]{1,0:T(8,128)(2,1)S(1)} %get-tuple-element.40.own_t.top), channel_id=1, source_target_pairs={{0,3},{1,0},{2,1},{3,2},{4,7},{5,4},{6,5},{7,6},{8,11},{9,8},{10,9... | collective-permute-start | bytes 786440 | tf_op jit(solution)/shard_map/ppermute | solution.py:24
  23.7 2.7 %collective-permute-start.7 = (bf16[512,256]{1,0:T(8,128)(2,1)S(1)}, bf16[512,256]{1,0:T(8,128)(2,1)S(1)}, u32[]{:S(2)}, u32[]{:S(2)}) collective-permute-start(bf16[512,256]{1,0:T(8,128)(2,1)S(1)} %get-tuple-element.41.own_b.bottom), channel_id=1, source_target_pairs={{0,3},{1,0},{2,1},{3,2},{4,7},{5,4},{6,5},{7,6},{8,11},{9,8},{10,9... | collective-permute-start | bytes 786440 | tf_op jit(solution)/shard_map/ppermute | solution.py:24
  26.4 0.7 collective-permute-start.15
  27.2 2.6 %collective-permute-done.6.hi_t = bf16[512,256]{1,0:T(8,128)(2,1)S(1)} collective-permute-done((bf16[512,256]{1,0:T(8,128)(2,1)S(1)}, bf16[512,256]{1,0:T(8,128)(2,1)S(1)}, u32[]{:S(2)}, u32[]{:S(2)}) %collective-permute-start.6) | collective-permute-done | bytes 262176 | tf_op jit(solution)/shard_map/ppermute | solution.py:24
  29.8 0.7 collective-permute-start.14
  30.5 2.2 %collective-permute-done.4.lo_t = bf16[512,256]{1,0:T(8,128)(2,1)S(1)} collective-permute-done((bf16[512,256]{1,0:T(8,128)(2,1)S(1)}, bf16[512,256]{1,0:T(8,128)(2,1)S(1)}, u32[]{:S(2)}, u32[]{:S(2)}) %collective-permute-start.4) | collective-permute-done | bytes 262176 | tf_op jit(solution)/shard_map/ppermute | solution.py:24
  32.7 1.5 %collective-permute-start.13 = (bf16[128,1152]{1,0:T(8,128)(2,1)S(1)}, bf16[128,1152]{1,0:T(8,128)(2,1)S(1)}, u32[]{:S(2)}, u32[]{:S(2)}) collective-permute-start(bf16[128,1152]{1,0:T(8,128)(2,1)S(1)} %collective-permute-done.10.m1), channel_id=1, source_target_pairs={{0,16},{16,0},{1,17},{17,1},{2,18},{18,2},{3,19},{19,3},{4,20},{20... | collective-permute-start | bytes 884744 | tf_op jit(solution)/shard_map/ppermute | solution.py:323
  34.2 1.0 collective-permute-done.7.hi_b
  35.2 3.1 %collective-permute-done.5.lo_b = bf16[512,256]{1,0:T(8,128)(2,1)S(1)} collective-permute-done((bf16[512,256]{1,0:T(8,128)(2,1)S(1)}, bf16[512,256]{1,0:T(8,128)(2,1)S(1)}, u32[]{:S(2)}, u32[]{:S(2)}) %collective-permute-start.5) | collective-permute-done | bytes 262176 | tf_op jit(solution)/shard_map/ppermute | solution.py:24
  38.3 0.3 collective-permute-start.9
  38.6 6.0 %collective-permute-done.8.far_t = bf16[512,256]{1,0:T(8,128)(2,1)S(1)} collective-permute-done((bf16[512,256]{1,0:T(8,128)(2,1)S(1)}, bf16[512,256]{1,0:T(8,128)(2,1)S(1)}, u32[]{:S(2)}, u32[]{:S(2)}) %collective-permute-start.8) | collective-permute-done | bytes 262176 | tf_op jit(solution)/shard_map/ppermute | solution.py:24
  44.6 0.6 collective-permute-done.9.far_b
  45.3 6.2 %shard_map.115 = (bf16[8,1024,128]{2,1,0:T(8,128)(2,1)S(1)}, bf16[1024,1024]{1,0:T(8,128)(2,1)S(1)}, bf16[1024,256]{1,0:T(8,128)(2,1)S(1)}, bf16[1024,128]{1,0:T...) custom-call(s32[7]{0:T(128)S(1)} %pad_add_fusion.meta, ...), custom_call_target="tpu_custom_call" | custom-call | tf_op jit(solution)/shard_map/pallas_call | solution.py:260
  51.5 1.9 %collective-permute-start.16 = (bf16[384,128]{1,0:T(8,128)(2,1)S(1)}, bf16[384,128]{1,0:T(8,128)(2,1)S(1)}, u32[]{:S(2)}, u32[]{:S(2)}) collective-permute-start(bf16[384,128]{1,0:T(8,128)(2,1)S(1)} %get-tuple-element.45), channel_id=1, source_target_pairs={{0,16},{16,0},{1,17},{17,1},{2,18},{18,2},{3,19},{19,3},{4,20},{20... | collective-permute-start | bytes 294920 | tf_op jit(solution)/shard_map/ppermute | solution.py:37
  53.4 3.0 %collective-permute-start.17 = (bf16[384,128]{1,0:T(8,128)(2,1)S(1)}, bf16[384,128]{1,0:T(8,128)(2,1)S(1)}, u32[]{:S(2)}, u32[]{:S(2)}) collective-permute-start(bf16[384,128]{1,0:T(8,128)(2,1)S(1)} %get-tuple-element.46), channel_id=1, source_target_pairs={{16,32},{32,16},{48,64},{64,48},{80,96},{96,80},{112,128},{128,112... | collective-permute-start | bytes 294920 | tf_op jit(solution)/shard_map/ppermute | solution.py:38
  56.4 4.1 %collective-permute-start.18 = (bf16[384,128]{1,0:T(8,128)(2,1)S(1)}, bf16[384,128]{1,0:T(8,128)(2,1)S(1)}, u32[]{:S(2)}, u32[]{:S(2)}) collective-permute-start(bf16[384,128]{1,0:T(8,128)(2,1)S(1)} %get-tuple-element.47), channel_id=1, source_target_pairs={{0,4},{4,0},{8,12},{12,8},{1,5},{5,1},{9,13},{13,9},{2,6},{6,2},{1... | collective-permute-start | bytes 294920 | tf_op jit(solution)/shard_map/ppermute | solution.py:39
  60.5 0.7 collective-permute-start.19
  61.2 1.3 %collective-permute-done.18.r2 = bf16[384,128]{1,0:T(8,128)(2,1)S(1)} collective-permute-done((bf16[384,128]{1,0:T(8,128)(2,1)S(1)}, bf16[384,128]{1,0:T(8,128)(2,1)S(1)}, u32[]{:S(2)}, u32[]{:S(2)}) %collective-permute-start.18) | collective-permute-done | bytes 98336 | tf_op jit(solution)/shard_map/ppermute | solution.py:39
  62.5 4.2 %shard_map.116 = (bf16[1024,128]{1,0:T(8,128)(2,1)S(1)}, bf16[384,128]{1,0:T(8,128)(2,1)S(1)}, bf16[384,128]{1,0:T(8,128)(2,1)S(1)}, bf16[384,128]{1,0:T(8,128)(2,1)S(1)}, bf16[384,128]{1,0:T(8,128)(2,1)S(1)}) custom-call(s32[7]{0:T(128)S(1)} %pad_add_fusion.meta, s32[4,8]{1,0:T(4,128)S(1)} %bitcast.6, bf16[8,4,128,128]{3,2,1,0:T(8,128)(2,1)S(1)} %get-tuple-element.31.tiles, ...), custom_call_target="tpu_custom_call" | custom-call | tf_op jit(solution)/shard_map/pallas_call | solution.py:260
  66.7 0.1 collective-permute-start.20
  66.8 4.1 %collective-permute-start.21 = (bf16[384,128]{1,0:T(8,128)(2,1)S(1)}, bf16[384,128]{1,0:T(8,128)(2,1)S(1)}, u32[]{:S(2)}, u32[]{:S(2)}) collective-permute-start(bf16[384,128]{1,0:T(8,128)(2,1)S(1)} %get-tuple-element.52), channel_id=1, source_target_pairs={{16,32},{32,16},{48,64},{64,48},{80,96},{96,80},{112,128},{128,112... | collective-permute-start | bytes 294920 | tf_op jit(solution)/shard_map/ppermute | solution.py:38
  70.9 3.7 %collective-permute-start.22 = (bf16[384,128]{1,0:T(8,128)(2,1)S(1)}, bf16[384,128]{1,0:T(8,128)(2,1)S(1)}, u32[]{:S(2)}, u32[]{:S(2)}) collective-permute-start(bf16[384,128]{1,0:T(8,128)(2,1)S(1)} %get-tuple-element.53), channel_id=1, source_target_pairs={{0,4},{4,0},{8,12},{12,8},{1,5},{5,1},{9,13},{13,9},{2,6},{6,2},{1... | collective-permute-start | bytes 294920 | tf_op jit(solution)/shard_map/ppermute | solution.py:39
  74.6 0.7 collective-permute-start.23
  75.3 1.3 %collective-permute-done.22.t2 = bf16[384,128]{1,0:T(8,128)(2,1)S(1)} collective-permute-done((bf16[384,128]{1,0:T(8,128)(2,1)S(1)}, bf16[384,128]{1,0:T(8,128)(2,1)S(1)}, u32[]{:S(2)}, u32[]{:S(2)}) %collective-permute-start.22) | collective-permute-done | bytes 98336 | tf_op jit(solution)/shard_map/ppermute | solution.py:39
  76.6 4.2 %shard_map.117 = (bf16[128,1152]{1,0:T(8,128)(2,1)S(1)}, f32[128,1152]{1,0:T(8,128)S(1)}) custom-call(s32[7]{0:T(128)S(1)} %pad_add_fusion.meta, s32[4,8]{1,0:T(4,128)S(1)} %bitcast.7, bf16[8,4,128,128]{3,2,1,0:T(8,128)(2,1)S(1)} %get-tuple-element.31.tiles, bf16[1024,128]{1,0:T(8,128)(2,1)S(1)} %get-tuple-element.50.grad, ...), custom_call_target="tpu_custom_call" | custom-call | tf_op jit(solution)/shard_map/pallas_call | solution.py:260
  80.8 0.1 collective-permute-start.24
  80.9 1.6 %collective-permute-done.24 = bf16[128,1152]{1,0:T(8,128)(2,1)S(1)} collective-permute-done((bf16[128,1152]{1,0:T(8,128)(2,1)S(1)}, bf16[128,1152]{1,0:T(8,128)(2,1)S(1)}, u32[]{:S(2)}, u32[]{:S(2)}) %collective-permute-start.24) | collective-permute-done | bytes 294944 | tf_op jit(solution)/shard_map/ppermute | solution.py:369
  82.6 0.1 reshape.15
  82.6 24.9 %all_to_all.10 = bf16[32,4,1152]{2,1,0:T(4,128)(2,1)S(1)} all-to-all(bf16[32,4,1152]{2,1,0:T(4,128)(2,1)S(1)} %reshape.15), channel_id=1, replica_groups=mesh['z'=8,'core'=2,'gy'=4,'af'=4] {'z','gy'}, dimensions={0} | all-to-all | bytes 589824 | tf_op jit(solution)/shard_map/all_to_all | solution.py:371
  107.5 0.1 reduce_sum.12
  107.6 0.1 broadcast_in_dim.2
  107.7 15.2 %all_to_all.11 = bf16[32,4,1152]{2,1,0:T(4,128)(2,1)S(1)} all-to-all(bf16[32,4,1152]{2,1,0:T(4,128)(2,1)S(1)} %broadcast_in_dim.2), channel_id=1, replica_groups=mesh['z'=8,'core'=2,'gy'=4,'af'=4] {'z','gy'}, dimensions={0} | all-to-all | bytes 589824 | tf_op jit(solution)/shard_map/all_to_all | solution.py:373
  123.0 3.7 %collective-permute-start.25 = (bf16[128,1152]{1,0:T(8,128)(2,1)S(1)}, bf16[128,1152]{1,0:T(8,128)(2,1)S(1)}, u32[]{:S(2)}, u32[]{:S(2)}) collective-permute-start(bf16[128,1152]{1,0:T(8,128)(2,1)S(1)} %reshape.16), channel_id=1, source_target_pairs={{0,16},{16,0},{1,17},{17,1},{2,18},{18,2},{3,19},{19,3},{4,20},{20... | collective-permute-start | bytes 884744 | tf_op jit(solution)/shard_map/ppermute | solution.py:376
  126.7 1.2 collective-permute-done.25
  128.1 0.7 maximum_convert_fusion.1
  128.8 1.1 maximum_convert_fusion
  (26 shorter events, 0.3 us)
Async XLA Ops:
  0.6 17.7 %copy-start = (s32[8,4]{0,1:T(4,128)S(1)}, s32[8,4]{0,1:T(4,128)}, u32[]{:S(2)}) copy-start(s32[8,4]{0,1:T(4,128)} %param.12) | copy-start | bytes 388
  4.7 10.0 %collective-permute-start = (bf16[384,256]{1,0:T(8,128)(2,1)S(1)}, bf16[384,256]{1,0:T(8,128)(2,1)S(1)}, u32[]{:S(2)}, u32[]{:S(2)}) collective-permute-start(bf16[384,256]{1,0:T(8,128)(2,1)S(1)} %get-tuple-element.34), channel_id=1, source_target_pairs={{0,16},{16,0},{1,17},{17,1},{2,18},{18,2},{3,19},{19,3},{4,20},{20... | collective-permute-start | bytes 589832 | tf_op jit(solution)/shard_map/ppermute | solution.py:37
  7.9 15.8 %collective-permute-start.12 = (bf16[128,1152]{1,0:T(8,128)(2,1)S(1)}, bf16[128,1152]{1,0:T(8,128)(2,1)S(1)}, u32[]{:S(2)}, u32[]{:S(2)}) collective-permute-start(bf16[128,1152]{1,0:T(8,128)(2,1)S(1)} %get-tuple-element.42.m0), channel_id=1, source_target_pairs={{0,3},{1,0},{2,1},{3,2},{4,7},{5,4},{6,5},{7,6},{8,11},{9,8},{10,9... | collective-permute-start | bytes 884744 | tf_op jit(solution)/shard_map/ppermute | solution.py:24
  9.0 17.4 %collective-permute-start.11 = (bf16[128,1152]{1,0:T(8,128)(2,1)S(1)}, bf16[128,1152]{1,0:T(8,128)(2,1)S(1)}, u32[]{:S(2)}, u32[]{:S(2)}) collective-permute-start(bf16[128,1152]{1,0:T(8,128)(2,1)S(1)} %get-tuple-element.42.m0), channel_id=1, source_target_pairs={{0,2},{1,3},{2,0},{3,1},{4,6},{5,7},{6,4},{7,5},{8,10},{9,11},{10,... | collective-permute-start | bytes 884744 | tf_op jit(solution)/shard_map/ppermute | solution.py:24
  9.3 7.7 %collective-permute-start.1 = (bf16[384,256]{1,0:T(8,128)(2,1)S(1)}, bf16[384,256]{1,0:T(8,128)(2,1)S(1)}, u32[]{:S(2)}, u32[]{:S(2)}) collective-permute-start(bf16[384,256]{1,0:T(8,128)(2,1)S(1)} %get-tuple-element.35), channel_id=1, source_target_pairs={{16,32},{32,16},{48,64},{64,48},{80,96},{96,80},{112,128},{128,112... | collective-permute-start | bytes 589832 | tf_op jit(solution)/shard_map/ppermute | solution.py:38
  13.4 4.9 %collective-permute-start.2 = (bf16[384,256]{1,0:T(8,128)(2,1)S(1)}, bf16[384,256]{1,0:T(8,128)(2,1)S(1)}, u32[]{:S(2)}, u32[]{:S(2)}) collective-permute-start(bf16[384,256]{1,0:T(8,128)(2,1)S(1)} %get-tuple-element.36), channel_id=1, source_target_pairs={{0,4},{4,0},{8,12},{12,8},{1,5},{5,1},{9,13},{13,9},{2,6},{6,2},{1... | collective-permute-start | bytes 589832 | tf_op jit(solution)/shard_map/ppermute | solution.py:39
  14.7 3.6 %collective-permute-start.3 = (bf16[384,256]{1,0:T(8,128)(2,1)S(1)}, bf16[384,256]{1,0:T(8,128)(2,1)S(1)}, u32[]{:S(2)}, u32[]{:S(2)}) collective-permute-start(bf16[384,256]{1,0:T(8,128)(2,1)S(1)} %get-tuple-element.37), channel_id=1, source_target_pairs={{4,8},{8,4},{5,9},{9,5},{6,10},{10,6},{7,11},{11,7},{20,24},{24,20... | collective-permute-start | bytes 589832 | tf_op jit(solution)/shard_map/ppermute | solution.py:40
  17.0 9.4 %collective-permute-start.10 = (bf16[128,1152]{1,0:T(8,128)(2,1)S(1)}, bf16[128,1152]{1,0:T(8,128)(2,1)S(1)}, u32[]{:S(2)}, u32[]{:S(2)}) collective-permute-start(bf16[128,1152]{1,0:T(8,128)(2,1)S(1)} %get-tuple-element.42.m0), channel_id=1, source_target_pairs={{0,1},{1,2},{2,3},{3,0},{4,5},{5,6},{6,7},{7,4},{8,9},{9,10},{10,1... | collective-permute-start | bytes 884744 | tf_op jit(solution)/shard_map/ppermute | solution.py:24
  21.4 8.4 %collective-permute-start.6 = (bf16[512,256]{1,0:T(8,128)(2,1)S(1)}, bf16[512,256]{1,0:T(8,128)(2,1)S(1)}, u32[]{:S(2)}, u32[]{:S(2)}) collective-permute-start(bf16[512,256]{1,0:T(8,128)(2,1)S(1)} %get-tuple-element.40.own_t.top), channel_id=1, source_target_pairs={{0,3},{1,0},{2,1},{3,2},{4,7},{5,4},{6,5},{7,6},{8,11},{9,8},{10,9... | collective-permute-start | bytes 786440 | tf_op jit(solution)/shard_map/ppermute | solution.py:24
  23.7 9.0 %collective-permute-start.4 = (bf16[512,256]{1,0:T(8,128)(2,1)S(1)}, bf16[512,256]{1,0:T(8,128)(2,1)S(1)}, u32[]{:S(2)}, u32[]{:S(2)}) collective-permute-start(bf16[512,256]{1,0:T(8,128)(2,1)S(1)} %get-tuple-element.40.own_t.top), channel_id=1, source_target_pairs={{0,1},{1,2},{2,3},{3,0},{4,5},{5,6},{6,7},{7,4},{8,9},{9,10},{10,1... | collective-permute-start | bytes 786440 | tf_op jit(solution)/shard_map/ppermute | solution.py:24
  23.7 11.5 %collective-permute-start.7 = (bf16[512,256]{1,0:T(8,128)(2,1)S(1)}, bf16[512,256]{1,0:T(8,128)(2,1)S(1)}, u32[]{:S(2)}, u32[]{:S(2)}) collective-permute-start(bf16[512,256]{1,0:T(8,128)(2,1)S(1)} %get-tuple-element.41.own_b.bottom), channel_id=1, source_target_pairs={{0,3},{1,0},{2,1},{3,2},{4,7},{5,4},{6,5},{7,6},{8,11},{9,8},{10,9... | collective-permute-start | bytes 786440 | tf_op jit(solution)/shard_map/ppermute | solution.py:24
  26.4 11.9 %collective-permute-start.5 = (bf16[512,256]{1,0:T(8,128)(2,1)S(1)}, bf16[512,256]{1,0:T(8,128)(2,1)S(1)}, u32[]{:S(2)}, u32[]{:S(2)}) collective-permute-start(bf16[512,256]{1,0:T(8,128)(2,1)S(1)} %get-tuple-element.41.own_b.bottom), channel_id=1, source_target_pairs={{0,1},{1,2},{2,3},{3,0},{4,5},{5,6},{6,7},{7,4},{8,9},{9,10},{10,1... | collective-permute-start | bytes 786440 | tf_op jit(solution)/shard_map/ppermute | solution.py:24
  26.4 12.2 %collective-permute-start.15 = (bf16[128,1152]{1,0:T(8,128)(2,1)S(1)}, bf16[128,1152]{1,0:T(8,128)(2,1)S(1)}, u32[]{:S(2)}, u32[]{:S(2)}) collective-permute-start(bf16[128,1152]{1,0:T(8,128)(2,1)S(1)} %collective-permute-done.12.m3), channel_id=1, source_target_pairs={{0,16},{16,0},{1,17},{17,1},{2,18},{18,2},{3,19},{19,3},{4,20},{20... | collective-permute-start | bytes 884744 | tf_op jit(solution)/shard_map/ppermute | solution.py:323
  29.8 8.9 %collective-permute-start.14 = (bf16[128,1152]{1,0:T(8,128)(2,1)S(1)}, bf16[128,1152]{1,0:T(8,128)(2,1)S(1)}, u32[]{:S(2)}, u32[]{:S(2)}) collective-permute-start(bf16[128,1152]{1,0:T(8,128)(2,1)S(1)} %collective-permute-done.11.m2), channel_id=1, source_target_pairs={{0,16},{16,0},{1,17},{17,1},{2,18},{18,2},{3,19},{19,3},{4,20},{20... | collective-permute-start | bytes 884744 | tf_op jit(solution)/shard_map/ppermute | solution.py:323
  32.7 5.9 %collective-permute-start.13 = (bf16[128,1152]{1,0:T(8,128)(2,1)S(1)}, bf16[128,1152]{1,0:T(8,128)(2,1)S(1)}, u32[]{:S(2)}, u32[]{:S(2)}) collective-permute-start(bf16[128,1152]{1,0:T(8,128)(2,1)S(1)} %collective-permute-done.10.m1), channel_id=1, source_target_pairs={{0,16},{16,0},{1,17},{17,1},{2,18},{18,2},{3,19},{19,3},{4,20},{20... | collective-permute-start | bytes 884744 | tf_op jit(solution)/shard_map/ppermute | solution.py:323
  35.2 9.4 %collective-permute-start.8 = (bf16[512,256]{1,0:T(8,128)(2,1)S(1)}, bf16[512,256]{1,0:T(8,128)(2,1)S(1)}, u32[]{:S(2)}, u32[]{:S(2)}) collective-permute-start(bf16[512,256]{1,0:T(8,128)(2,1)S(1)} %collective-permute-done.4.lo_t), channel_id=1, source_target_pairs={{0,1},{1,2},{2,3},{3,0},{4,5},{5,6},{6,7},{7,4},{8,9},{9,10},{10,1... | collective-permute-start | bytes 786440 | tf_op jit(solution)/shard_map/ppermute | solution.py:24
  38.3 6.9 %collective-permute-start.9 = (bf16[512,256]{1,0:T(8,128)(2,1)S(1)}, bf16[512,256]{1,0:T(8,128)(2,1)S(1)}, u32[]{:S(2)}, u32[]{:S(2)}) collective-permute-start(bf16[512,256]{1,0:T(8,128)(2,1)S(1)} %collective-permute-done.7.hi_b), channel_id=1, source_target_pairs={{0,3},{1,0},{2,1},{3,2},{4,7},{5,4},{6,5},{7,6},{8,11},{9,8},{10,9... | collective-permute-start | bytes 786440 | tf_op jit(solution)/shard_map/ppermute | solution.py:24
  51.5 9.7 %collective-permute-start.16 = (bf16[384,128]{1,0:T(8,128)(2,1)S(1)}, bf16[384,128]{1,0:T(8,128)(2,1)S(1)}, u32[]{:S(2)}, u32[]{:S(2)}) collective-permute-start(bf16[384,128]{1,0:T(8,128)(2,1)S(1)} %get-tuple-element.45), channel_id=1, source_target_pairs={{0,16},{16,0},{1,17},{17,1},{2,18},{18,2},{3,19},{19,3},{4,20},{20... | collective-permute-start | bytes 294920 | tf_op jit(solution)/shard_map/ppermute | solution.py:37
  53.4 7.8 %collective-permute-start.17 = (bf16[384,128]{1,0:T(8,128)(2,1)S(1)}, bf16[384,128]{1,0:T(8,128)(2,1)S(1)}, u32[]{:S(2)}, u32[]{:S(2)}) collective-permute-start(bf16[384,128]{1,0:T(8,128)(2,1)S(1)} %get-tuple-element.46), channel_id=1, source_target_pairs={{16,32},{32,16},{48,64},{64,48},{80,96},{96,80},{112,128},{128,112... | collective-permute-start | bytes 294920 | tf_op jit(solution)/shard_map/ppermute | solution.py:38
  56.4 6.1 %collective-permute-start.18 = (bf16[384,128]{1,0:T(8,128)(2,1)S(1)}, bf16[384,128]{1,0:T(8,128)(2,1)S(1)}, u32[]{:S(2)}, u32[]{:S(2)}) collective-permute-start(bf16[384,128]{1,0:T(8,128)(2,1)S(1)} %get-tuple-element.47), channel_id=1, source_target_pairs={{0,4},{4,0},{8,12},{12,8},{1,5},{5,1},{9,13},{13,9},{2,6},{6,2},{1... | collective-permute-start | bytes 294920 | tf_op jit(solution)/shard_map/ppermute | solution.py:39
  60.5 2.0 %collective-permute-start.19 = (bf16[384,128]{1,0:T(8,128)(2,1)S(1)}, bf16[384,128]{1,0:T(8,128)(2,1)S(1)}, u32[]{:S(2)}, u32[]{:S(2)}) collective-permute-start(bf16[384,128]{1,0:T(8,128)(2,1)S(1)} %get-tuple-element.48), channel_id=1, source_target_pairs={{4,8},{8,4},{5,9},{9,5},{6,10},{10,6},{7,11},{11,7},{20,24},{24,20... | collective-permute-start | bytes 294920 | tf_op jit(solution)/shard_map/ppermute | solution.py:40
  66.7 8.5 %collective-permute-start.20 = (bf16[384,128]{1,0:T(8,128)(2,1)S(1)}, bf16[384,128]{1,0:T(8,128)(2,1)S(1)}, u32[]{:S(2)}, u32[]{:S(2)}) collective-permute-start(bf16[384,128]{1,0:T(8,128)(2,1)S(1)} %get-tuple-element.51), channel_id=1, source_target_pairs={{0,16},{16,0},{1,17},{17,1},{2,18},{18,2},{3,19},{19,3},{4,20},{20... | collective-permute-start | bytes 294920 | tf_op jit(solution)/shard_map/ppermute | solution.py:37
  66.8 8.4 %collective-permute-start.21 = (bf16[384,128]{1,0:T(8,128)(2,1)S(1)}, bf16[384,128]{1,0:T(8,128)(2,1)S(1)}, u32[]{:S(2)}, u32[]{:S(2)}) collective-permute-start(bf16[384,128]{1,0:T(8,128)(2,1)S(1)} %get-tuple-element.52), channel_id=1, source_target_pairs={{16,32},{32,16},{48,64},{64,48},{80,96},{96,80},{112,128},{128,112... | collective-permute-start | bytes 294920 | tf_op jit(solution)/shard_map/ppermute | solution.py:38
  70.9 5.7 %collective-permute-start.22 = (bf16[384,128]{1,0:T(8,128)(2,1)S(1)}, bf16[384,128]{1,0:T(8,128)(2,1)S(1)}, u32[]{:S(2)}, u32[]{:S(2)}) collective-permute-start(bf16[384,128]{1,0:T(8,128)(2,1)S(1)} %get-tuple-element.53), channel_id=1, source_target_pairs={{0,4},{4,0},{8,12},{12,8},{1,5},{5,1},{9,13},{13,9},{2,6},{6,2},{1... | collective-permute-start | bytes 294920 | tf_op jit(solution)/shard_map/ppermute | solution.py:39
  74.6 2.0 %collective-permute-start.23 = (bf16[384,128]{1,0:T(8,128)(2,1)S(1)}, bf16[384,128]{1,0:T(8,128)(2,1)S(1)}, u32[]{:S(2)}, u32[]{:S(2)}) collective-permute-start(bf16[384,128]{1,0:T(8,128)(2,1)S(1)} %get-tuple-element.54), channel_id=1, source_target_pairs={{4,8},{8,4},{5,9},{9,5},{6,10},{10,6},{7,11},{11,7},{20,24},{24,20... | collective-permute-start | bytes 294920 | tf_op jit(solution)/shard_map/ppermute | solution.py:40
  80.8 1.7 %collective-permute-start.24 = (bf16[128,1152]{1,0:T(8,128)(2,1)S(1)}, bf16[128,1152]{1,0:T(8,128)(2,1)S(1)}, u32[]{:S(2)}, u32[]{:S(2)}) collective-permute-start(bf16[128,1152]{1,0:T(8,128)(2,1)S(1)} %get-tuple-element.59), channel_id=1, source_target_pairs={{0,16},{16,0},{1,17},{17,1},{2,18},{18,2},{3,19},{19,3},{4,20},{20... | collective-permute-start | bytes 884744 | tf_op jit(solution)/shard_map/ppermute | solution.py:369
  123.0 4.9 %collective-permute-start.25 = (bf16[128,1152]{1,0:T(8,128)(2,1)S(1)}, bf16[128,1152]{1,0:T(8,128)(2,1)S(1)}, u32[]{:S(2)}, u32[]{:S(2)}) collective-permute-start(bf16[128,1152]{1,0:T(8,128)(2,1)S(1)} %reshape.16), channel_id=1, source_target_pairs={{0,16},{16,0},{1,17},{17,1},{2,18},{18,2},{3,19},{19,3},{4,20},{20... | collective-permute-start | bytes 884744 | tf_op jit(solution)/shard_map/ppermute | solution.py:376

commit v9 on v8

--- a/solution.py
+++ b/solution.py
@@ -90,7 +90,7 @@
 
 def send_kernel(
     meta, feat_in, send_in, w_hid, w_cls, tiles_in, recv_in, weight_in, labels_in,
-    o0, o1, o2, o3, mine, other, feat, send, tiles, recv, weight, labels, hot, sems,
+    o0, o1, o2, o3, mine, other, quarter, feat, send, tiles, recv, weight, labels, hot, sems,
 ):
     nodes = feat.shape[0]
     half, hid = w_hid.shape[0] // 2, w_hid.shape[1]
@@ -99,6 +99,10 @@
         at = pl.ds(pl.multiple_of(part * half, half), half)
         moves.append((w_hid.at[at, :], ref.at[:, :hid]))
         moves.append((w_cls.at[at, :], ref.at[:, hid:]))
+    rows = half // 2
+    at = pl.ds(pl.multiple_of(meta[0] * half + lax.rem(meta[1], 2) * rows, rows), rows)
+    moves.append((w_hid.at[at, :], quarter.at[:, :hid]))
+    moves.append((w_cls.at[at, :], quarter.at[:, hid:]))
     moves += [(tiles_in, tiles), (recv_in, recv), (weight_in, weight), (labels_in, labels)]
     copies = [pltpu.make_async_copy(x, y, sems.at[i]) for i, (x, y) in enumerate(moves)]
     for copy in copies:
@@ -143,20 +147,30 @@
 
 def hidden_kernel(
     meta, send, own_t, own_b, lo_t, lo_b, hi_t, hi_b, far_t, far_b,
-    m0, m1, m2, m3, v0, v1, v2, v3,
+    mine, other, near_w, far_w,
     hidden, slope, z_pair, w_cls, o0, o1, o2, o3, w_all, hot,
 ):
     nodes = z_pair.shape[0]
-    half = m0.shape[0]
+    half = mine.shape[0]
     hid = w_all.shape[1]
     classes = w_cls.shape[1]
     n_af = w_cls.shape[0] // (2 * half)
-    for i, (k, mine, other) in enumerate(((0, m0, v0), (1, m1, v1), (3, m3, v3), (2, m2, v2))):
-        w_all[2 * i * half : (2 * i + 1) * half, :] = mine[:, :hid]
-        w_all[(2 * i + 1) * half : (2 * i + 2) * half, :] = other[:, :hid]
+    rows = half // 2
+    odd = lax.rem(meta[1], 2)
+    for i, k in enumerate((0, 1, 3, 2)):
         base = lax.rem(meta[2] + n_af - k, n_af) * 2
-        w_cls[pl.ds(pl.multiple_of((base + meta[0]) * half, half), half), :] = mine[:, hid:]
-        w_cls[pl.ds(pl.multiple_of((base + 1 - meta[0]) * half, half), half), :] = other[:, hid:]
+        for c, (whole, pieces) in enumerate(((mine, near_w), (other, far_w))):
+            to_all = (2 * i + c) * half
+            to_cls = (base + (meta[0] if c == 0 else 1 - meta[0])) * half
+            if k == 0:
+                w_all[to_all : to_all + half, :] = whole[:, :hid]
+                w_cls[pl.ds(pl.multiple_of(to_cls, half), half), :] = whole[:, hid:]
+                continue
+            for place, start in ((odd, (k - 1) * rows), (1 - odd, (k + n_af - 2) * rows)):
+                piece = pieces[start : start + rows, :]
+                step = place * rows
+                w_all[pl.ds(pl.multiple_of(to_all + step, rows), rows), :] = piece[:, :hid]
+                w_cls[pl.ds(pl.multiple_of(to_cls + step, rows), rows), :] = piece[:, hid:]
     part = nodes // 2
     rows = 256
     for h, refs in enumerate(((own_t, lo_t, hi_t, far_t), (own_b, lo_b, hi_b, far_b))):
@@ -308,19 +322,19 @@
         edge_weight,
         labels.reshape(-1, LANES),
     )
-    *out, w_mine, w_other, features, send_rows, adj_tiles, recv_target, edge_weight, labels = call(
+    *out, w_mine, w_other, w_part, features, send_rows, adj_tiles, recv_target, edge_weight, labels = call(
         send_kernel,
         (meta,),
         taken,
         [((slots, width), BF)] * 4
         + [((half, both), BF)] * 2
+        + [((half // 2, both), BF)]
         + [(taken[i].shape, taken[i].dtype) for i in (0, 1, 4, 5, 6, 7)],
         [((slots, nodes), BF)],
-        10,
+        12,
     )
     arrived = trade(out)
-    w_mine = [w_mine] + [turn(w_mine, "af", k) for k in range(1, n_af)]
-    w_other = [w_other] + [lax.ppermute(w_mine[k], "core", swap) for k in range(1, n_af)]
+    near_w = [turn(w_part, "af", k) for k in range(1, n_af)]
     top, bottom = call(
         mix_kernel,
         (meta, columns),
@@ -328,13 +342,18 @@
         [((part, width), BF)] * 2,
         [((nodes, 4 * slots), BF), ((4 * slots, 2 * width), BF)],
     )
+    near_w, _ = lax.optimization_barrier((near_w, top))
+    near_w = jnp.concatenate(near_w, axis=0)
+    across = lax.ppermute(near_w, "gy", pairs_at(lax.axis_size("gy"), 0))
+    near_w = jnp.concatenate([near_w, across], axis=0)
+    far_w = lax.ppermute(near_w, "core", swap)
     lo_t, hi_b = turn(top, "af", 1), turn(bottom, "af", -1)
     lo_b, hi_t = turn(bottom, "af", 1), turn(top, "af", -1)
     far_t, far_b = turn(lo_t, "af", 1), turn(hi_b, "af", -1)
     hidden, slope, z_pair, w_cls, *out = call(
         hidden_kernel,
         (meta,),
-        (send_rows, top, bottom, lo_t, lo_b, hi_t, hi_b, far_t, far_b, *w_mine, *w_other),
+        (send_rows, top, bottom, lo_t, lo_b, hi_t, hi_b, far_t, far_b, w_mine, w_other, near_w, far_w),
         [
             ((hid // LANES, nodes, LANES), BF),
             ((nodes, hid), BF),

time: 130 us -> 141 us (1.085)
  waiting for transfers between devices: 23.6 us -> 34.8 us
    ppermute x3 -> x2, waiting for transfers between devices: 0.01 us -> 10.1 us  [the longest x1 10.1 us: work(): across = lax.ppermute(near_w, 'gy', pairs_at(lax.axis_size('gy'), 0))]
    ppermute x9, waiting for transfers between devices: 15.6 us -> 18.6 us  [turn(): lax.ppermute(field, axis, [(i, (i + move) % count) for i in range(count)])]
    ppermute x3, starting transfers between devices: 9.07 us -> 6.38 us  [trade(): lax.ppermute(fields[2], 'gy', pairs_at(cols, 0))]
    ppermute x3 -> x2, starting transfers between devices: 2.96 us -> 4.98 us  [the longest x1 3.93 us: work(): across = lax.ppermute(near_w, 'gy', pairs_at(lax.axis_size('gy'), 0))]
    ppermute x9, starting transfers between devices: 7.11 us -> 9.1 us  [turn(): lax.ppermute(field, axis, [(i, (i + move) % count) for i in range(count)])]
  transfers between devices with their start and end apart: 26 -> 25, of which waited for: 12 -> 15; matrix products, arithmetic and copies ran while one was open for 0% -> 0% of each run, Pallas kernels for 2% -> 2%
where the time goes in v9:
time: 141 us; the launch traced here: 140 us
  starting transfers between devices  41.8 us (30%)
  blocking collectives  38.8 us (28%)
  waiting for transfers between devices  34.8 us (25%)
  Pallas kernels  21 us (15%)
  other arithmetic  2.78 us (2%)
    all_to_all x1, blocking collectives, work(): pieces = lax.all_to_all(pieces, PLANE, 0, 0, tiled=True)  23.5 us
    pallas_call x5, Pallas kernels, call(): pl.pallas_call(kernel, in_specs=[pl.BlockSpec(memory_space=pltpu.SMEM) fo...  21 us
    ppermute x9, waiting for transfers between devices, turn(): lax.ppermute(field, axis, [(i, (i + move) % count) for i in range(count)])  18.6 us
    all_to_all x1, blocking collectives, work(): lax.all_to_all(jnp.broadcast_to(piece[None], (n_plane,) + piece.shape), P...  15.2 us
    ppermute x3, starting transfers between devices, trade(): lax.ppermute(fields[1], ROWS, pairs_at(rows, 1))  11.1 us
    ppermute x1, waiting for transfers between devices, work(): across = lax.ppermute(near_w, 'gy', pairs_at(lax.axis_size('gy'), 0))  10.1 us
    ppermute x9, starting transfers between devices, turn(): lax.ppermute(field, axis, [(i, (i + move) % count) for i in range(count)])  9.1 us
    ppermute x3, starting transfers between devices, trade(): lax.ppermute(fields[2], 'gy', pairs_at(cols, 0))  6.38 us
  transfers between devices with their start and end apart: 25, of which 15 were waited for; matrix products, arithmetic and copies ran while one was open for 0% of the time, Pallas kernels for 2%

profile of v9, /device:TPU:1, one launch (start us, length us, event | category | flops | bytes accessed | tf_op | source)
XLA Modules:
  0.0 140.4 jit_solution(7714399545519790378)
XLA Ops:
  0.6 0.7 pad_add_fusion.meta
  1.4 3.3 %shard_map.113 = (bf16[384,256]{1,0:T(8,128)(2,1)S(1)}, bf16[384,256]{1,0:T(8,128)(2,1)S(1)}, bf16[384,256]{1,0:T(8,128)(2,1)S(1)}, bf16[384,256]{1,0:T(8,128)(2...) custom-call(s32[7]{0:T(128)S(1)} %pad_add_fusion.meta, ...), custom_call_target="tpu_custom_call" | custom-call | tf_op jit(solution)/shard_map/pallas_call | solution.py:274
  4.7 3.3 %collective-permute-start = (bf16[384,256]{1,0:T(8,128)(2,1)S(1)}, bf16[384,256]{1,0:T(8,128)(2,1)S(1)}, u32[]{:S(2)}, u32[]{:S(2)}) collective-permute-start(bf16[384,256]{1,0:T(8,128)(2,1)S(1)} %get-tuple-element.38), channel_id=1, source_target_pairs={{0,16},{16,0},{1,17},{17,1},{2,18},{18,2},{3,19},{19,3},{4,20},{20... | collective-permute-start | bytes 589832 | tf_op jit(solution)/shard_map/ppermute | solution.py:37
  8.0 1.9 %collective-permute-start.1 = (bf16[384,256]{1,0:T(8,128)(2,1)S(1)}, bf16[384,256]{1,0:T(8,128)(2,1)S(1)}, u32[]{:S(2)}, u32[]{:S(2)}) collective-permute-start(bf16[384,256]{1,0:T(8,128)(2,1)S(1)} %get-tuple-element.39), channel_id=1, source_target_pairs={{16,32},{32,16},{48,64},{64,48},{80,96},{96,80},{112,128},{128,112... | collective-permute-start | bytes 589832 | tf_op jit(solution)/shard_map/ppermute | solution.py:38
  9.9 1.1 collective-permute-start.2
  11.0 0.7 collective-permute-start.3
  11.7 2.8 %collective-permute-start.12 = (bf16[64,1152]{1,0:T(8,128)(2,1)S(1)}, bf16[64,1152]{1,0:T(8,128)(2,1)S(1)}, u32[]{:S(2)}, u32[]{:S(2)}) collective-permute-start(bf16[64,1152]{1,0:T(8,128)(2,1)S(1)} %get-tuple-element.48), channel_id=1, source_target_pairs={{0,3},{1,0},{2,1},{3,2},{4,7},{5,4},{6,5},{7,6},{8,11},{9,8},{10,9... | collective-permute-start | bytes 442376 | tf_op jit(solution)/shard_map/ppermute | solution.py:24
  14.5 0.3 collective-permute-start.11
  14.8 0.4 collective-permute-done.1.r1
  15.2 0.3 collective-permute-start.10
  15.5 0.3 collective-permute-done.2.r2
  15.8 3.1 %shard_map.114 = (bf16[512,256]{1,0:T(8,128)(2,1)S(1)}, bf16[512,256]{1,0:T(8,128)(2,1)S(1)}) custom-call(s32[7]{0:T(128)S(1)} %pad_add_fusion.meta, s32[4,8]{1,0:T(4,128)S(1)} %bitcast.5, bf16[1024,256]{1,0:T(8,128)(2,1)S(1)} %get-tuple-element.37.feat, bf16[8,4,128,128]{3,2,1,0:T(8,128)(2,1)S(1)} %get-tuple-element.35.tiles, ...), custom_call_target="tpu_custom_call" | custom-call | tf_op jit(solution)/shard_map/pallas_call | solution.py:274
  18.9 0.4 collective-permute-done.12
  19.3 2.1 %collective-permute-done.11 = bf16[64,1152]{1,0:T(8,128)(2,1)S(1)} collective-permute-done((bf16[64,1152]{1,0:T(8,128)(2,1)S(1)}, bf16[64,1152]{1,0:T(8,128)(2,1)S(1)}, u32[]{:S(2)}, u32[]{:S(2)}) %collective-permute-start.11) | collective-permute-done | bytes 147488 | tf_op jit(solution)/shard_map/ppermute | solution.py:24
  21.4 1.6 %collective-permute-done.10 = bf16[64,1152]{1,0:T(8,128)(2,1)S(1)} collective-permute-done((bf16[64,1152]{1,0:T(8,128)(2,1)S(1)}, bf16[64,1152]{1,0:T(8,128)(2,1)S(1)}, u32[]{:S(2)}, u32[]{:S(2)}) %collective-permute-start.10) | collective-permute-done | bytes 147488 | tf_op jit(solution)/shard_map/ppermute | solution.py:24
  23.0 3.9 %collective-permute-start.13 = (bf16[192,1152]{1,0:T(8,128)(2,1)S(1)}, bf16[192,1152]{1,0:T(8,128)(2,1)S(1)}, u32[]{:S(2)}, u32[]{:S(2)}) collective-permute-start(bf16[192,1152]{1,0:T(8,128)(2,1)S(1)} %pad_maximum_fusion), channel_id=1, source_target_pairs={{0,4},{4,0},{8,12},{12,8},{1,5},{5,1},{9,13},{13,9},{2,6},{6,2},{1... | collective-permute-start | bytes 1327112 | tf_op jit(solution)/shard_map/ppermute | solution.py:347
  27.0 10.1 %collective-permute-done.13 = bf16[192,1152]{1,0:T(8,128)(2,1)S(1)} collective-permute-done((bf16[192,1152]{1,0:T(8,128)(2,1)S(1)}, bf16[192,1152]{1,0:T(8,128)(2,1)S(1)}, u32[]{:S(2)}, u32[]{:S(2)}) %collective-permute-start.13) | collective-permute-done | bytes 442400 | tf_op jit(solution)/shard_map/ppermute | solution.py:347
  37.2 1.1 collective-permute-start.14
  38.2 1.5 %collective-permute-start.4 = (bf16[512,256]{1,0:T(8,128)(2,1)S(1)}, bf16[512,256]{1,0:T(8,128)(2,1)S(1)}, u32[]{:S(2)}, u32[]{:S(2)}) collective-permute-start(bf16[512,256]{1,0:T(8,128)(2,1)S(1)} %get-tuple-element.44.own_t.top), channel_id=1, source_target_pairs={{0,1},{1,2},{2,3},{3,0},{4,5},{5,6},{6,7},{7,4},{8,9},{9,10},{10,1... | collective-permute-start | bytes 786440 | tf_op jit(solution)/shard_map/ppermute | solution.py:24
  39.7 2.7 %collective-permute-start.6 = (bf16[512,256]{1,0:T(8,128)(2,1)S(1)}, bf16[512,256]{1,0:T(8,128)(2,1)S(1)}, u32[]{:S(2)}, u32[]{:S(2)}) collective-permute-start(bf16[512,256]{1,0:T(8,128)(2,1)S(1)} %get-tuple-element.44.own_t.top), channel_id=1, source_target_pairs={{0,3},{1,0},{2,1},{3,2},{4,7},{5,4},{6,5},{7,6},{8,11},{9,8},{10,9... | collective-permute-start | bytes 786440 | tf_op jit(solution)/shard_map/ppermute | solution.py:24
  42.4 3.6 %collective-permute-done.7.hi_b = bf16[512,256]{1,0:T(8,128)(2,1)S(1)} collective-permute-done((bf16[512,256]{1,0:T(8,128)(2,1)S(1)}, bf16[512,256]{1,0:T(8,128)(2,1)S(1)}, u32[]{:S(2)}, u32[]{:S(2)}) %collective-permute-start.7) | collective-permute-done | bytes 262176 | tf_op jit(solution)/shard_map/ppermute | solution.py:24
  46.0 1.5 %collective-permute-start.9 = (bf16[512,256]{1,0:T(8,128)(2,1)S(1)}, bf16[512,256]{1,0:T(8,128)(2,1)S(1)}, u32[]{:S(2)}, u32[]{:S(2)}) collective-permute-start(bf16[512,256]{1,0:T(8,128)(2,1)S(1)} %collective-permute-done.7.hi_b), channel_id=1, source_target_pairs={{0,3},{1,0},{2,1},{3,2},{4,7},{5,4},{6,5},{7,6},{8,11},{9,8},{10,9... | collective-permute-start | bytes 786440 | tf_op jit(solution)/shard_map/ppermute | solution.py:24
  47.5 5.2 %collective-permute-done.5.lo_b = bf16[512,256]{1,0:T(8,128)(2,1)S(1)} collective-permute-done((bf16[512,256]{1,0:T(8,128)(2,1)S(1)}, bf16[512,256]{1,0:T(8,128)(2,1)S(1)}, u32[]{:S(2)}, u32[]{:S(2)}) %collective-permute-start.5) | collective-permute-done | bytes 262176 | tf_op jit(solution)/shard_map/ppermute | solution.py:24
  52.8 4.5 %collective-permute-done.9.far_b = bf16[512,256]{1,0:T(8,128)(2,1)S(1)} collective-permute-done((bf16[512,256]{1,0:T(8,128)(2,1)S(1)}, bf16[512,256]{1,0:T(8,128)(2,1)S(1)}, u32[]{:S(2)}, u32[]{:S(2)}) %collective-permute-start.9) | collective-permute-done | bytes 262176 | tf_op jit(solution)/shard_map/ppermute | solution.py:24
  57.2 1.1 collective-permute-done.8.far_t
  58.4 6.3 %shard_map.115 = (bf16[8,1024,128]{2,1,0:T(8,128)(2,1)S(1)}, bf16[1024,1024]{1,0:T(8,128)(2,1)S(1)}, bf16[1024,256]{1,0:T(8,128)(2,1)S(1)}, bf16[1024,128]{1,0:T...) custom-call(s32[7]{0:T(128)S(1)} %pad_add_fusion.meta, ...), custom_call_target="tpu_custom_call" | custom-call | tf_op jit(solution)/shard_map/pallas_call | solution.py:274
  64.6 1.1 collective-permute-start.15
  65.8 5.3 %collective-permute-start.16 = (bf16[384,128]{1,0:T(8,128)(2,1)S(1)}, bf16[384,128]{1,0:T(8,128)(2,1)S(1)}, u32[]{:S(2)}, u32[]{:S(2)}) collective-permute-start(bf16[384,128]{1,0:T(8,128)(2,1)S(1)} %get-tuple-element.54), channel_id=1, source_target_pairs={{16,32},{32,16},{48,64},{64,48},{80,96},{96,80},{112,128},{128,112... | collective-permute-start | bytes 294920 | tf_op jit(solution)/shard_map/ppermute | solution.py:38
  71.0 1.5 %collective-permute-start.17 = (bf16[384,128]{1,0:T(8,128)(2,1)S(1)}, bf16[384,128]{1,0:T(8,128)(2,1)S(1)}, u32[]{:S(2)}, u32[]{:S(2)}) collective-permute-start(bf16[384,128]{1,0:T(8,128)(2,1)S(1)} %get-tuple-element.55), channel_id=1, source_target_pairs={{0,4},{4,0},{8,12},{12,8},{1,5},{5,1},{9,13},{13,9},{2,6},{6,2},{1... | collective-permute-start | bytes 294920 | tf_op jit(solution)/shard_map/ppermute | solution.py:39
  72.6 0.7 collective-permute-start.18
  73.3 1.3 collective-permute-done.17.r2
  74.6 4.2 %shard_map.116 = (bf16[1024,128]{1,0:T(8,128)(2,1)S(1)}, bf16[384,128]{1,0:T(8,128)(2,1)S(1)}, bf16[384,128]{1,0:T(8,128)(2,1)S(1)}, bf16[384,128]{1,0:T(8,128)(2,1)S(1)}, bf16[384,128]{1,0:T(8,128)(2,1)S(1)}) custom-call(s32[7]{0:T(128)S(1)} %pad_add_fusion.meta, s32[4,8]{1,0:T(4,128)S(1)} %bitcast.6, bf16[8,4,128,128]{3,2,1,0:T(8,128)(2,1)S(1)} %get-tuple-element.35.tiles, ...), custom_call_target="tpu_custom_call" | custom-call | tf_op jit(solution)/shard_map/pallas_call | solution.py:274
  78.8 0.1 collective-permute-start.19
  78.9 3.9 %collective-permute-start.20 = (bf16[384,128]{1,0:T(8,128)(2,1)S(1)}, bf16[384,128]{1,0:T(8,128)(2,1)S(1)}, u32[]{:S(2)}, u32[]{:S(2)}) collective-permute-start(bf16[384,128]{1,0:T(8,128)(2,1)S(1)} %get-tuple-element.60), channel_id=1, source_target_pairs={{16,32},{32,16},{48,64},{64,48},{80,96},{96,80},{112,128},{128,112... | collective-permute-start | bytes 294920 | tf_op jit(solution)/shard_map/ppermute | solution.py:38
  82.8 3.7 %collective-permute-start.21 = (bf16[384,128]{1,0:T(8,128)(2,1)S(1)}, bf16[384,128]{1,0:T(8,128)(2,1)S(1)}, u32[]{:S(2)}, u32[]{:S(2)}) collective-permute-start(bf16[384,128]{1,0:T(8,128)(2,1)S(1)} %get-tuple-element.61), channel_id=1, source_target_pairs={{0,4},{4,0},{8,12},{12,8},{1,5},{5,1},{9,13},{13,9},{2,6},{6,2},{1... | collective-permute-start | bytes 294920 | tf_op jit(solution)/shard_map/ppermute | solution.py:39
  86.5 0.7 collective-permute-start.22
  87.2 1.3 collective-permute-done.21.t2
  88.5 4.2 %shard_map.117 = (bf16[128,1152]{1,0:T(8,128)(2,1)S(1)}, f32[128,1152]{1,0:T(8,128)S(1)}) custom-call(s32[7]{0:T(128)S(1)} %pad_add_fusion.meta, s32[4,8]{1,0:T(4,128)S(1)} %bitcast.7, bf16[8,4,128,128]{3,2,1,0:T(8,128)(2,1)S(1)} %get-tuple-element.35.tiles, bf16[1024,128]{1,0:T(8,128)(2,1)S(1)} %get-tuple-element.58.grad, ...), custom_call_target="tpu_custom_call" | custom-call | tf_op jit(solution)/shard_map/pallas_call | solution.py:274
  92.8 0.1 collective-permute-start.23
  92.9 1.6 %collective-permute-done.23 = bf16[128,1152]{1,0:T(8,128)(2,1)S(1)} collective-permute-done((bf16[128,1152]{1,0:T(8,128)(2,1)S(1)}, bf16[128,1152]{1,0:T(8,128)(2,1)S(1)}, u32[]{:S(2)}, u32[]{:S(2)}) %collective-permute-start.23) | collective-permute-done | bytes 294944 | tf_op jit(solution)/shard_map/ppermute | solution.py:388
  94.6 23.5 %all_to_all.10 = bf16[32,4,1152]{2,1,0:T(4,128)(2,1)S(1)} all-to-all(bf16[32,4,1152]{2,1,0:T(4,128)(2,1)S(1)} %reshape.15), channel_id=1, replica_groups=mesh['z'=8,'core'=2,'gy'=4,'af'=4] {'z','gy'}, dimensions={0} | all-to-all | bytes 589824 | tf_op jit(solution)/shard_map/all_to_all | solution.py:390
  118.1 0.1 reduce_sum.12
  118.2 0.1 broadcast_in_dim.2
  118.3 15.2 %all_to_all.11 = bf16[32,4,1152]{2,1,0:T(4,128)(2,1)S(1)} all-to-all(bf16[32,4,1152]{2,1,0:T(4,128)(2,1)S(1)} %broadcast_in_dim.2), channel_id=1, replica_groups=mesh['z'=8,'core'=2,'gy'=4,'af'=4] {'z','gy'}, dimensions={0} | all-to-all | bytes 589824 | tf_op jit(solution)/shard_map/all_to_all | solution.py:392
  133.7 3.7 %collective-permute-start.24 = (bf16[128,1152]{1,0:T(8,128)(2,1)S(1)}, bf16[128,1152]{1,0:T(8,128)(2,1)S(1)}, u32[]{:S(2)}, u32[]{:S(2)}) collective-permute-start(bf16[128,1152]{1,0:T(8,128)(2,1)S(1)} %reshape.16), channel_id=1, source_target_pairs={{0,16},{16,0},{1,17},{17,1},{2,18},{18,2},{3,19},{19,3},{4,20},{20... | collective-permute-start | bytes 884744 | tf_op jit(solution)/shard_map/ppermute | solution.py:395
  137.3 1.2 collective-permute-done.24
  138.7 0.7 maximum_convert_fusion.1
  139.4 1.1 maximum_convert_fusion
  (29 shorter events, 0.6 us)
Async XLA Ops:
  0.6 15.2 %copy-start = (s32[8,4]{0,1:T(4,128)S(1)}, s32[8,4]{0,1:T(4,128)}, u32[]{:S(2)}) copy-start(s32[8,4]{0,1:T(4,128)} %param.12) | copy-start | bytes 388
  4.7 9.8 %collective-permute-start = (bf16[384,256]{1,0:T(8,128)(2,1)S(1)}, bf16[384,256]{1,0:T(8,128)(2,1)S(1)}, u32[]{:S(2)}, u32[]{:S(2)}) collective-permute-start(bf16[384,256]{1,0:T(8,128)(2,1)S(1)} %get-tuple-element.38), channel_id=1, source_target_pairs={{0,16},{16,0},{1,17},{17,1},{2,18},{18,2},{3,19},{19,3},{4,20},{20... | collective-permute-start | bytes 589832 | tf_op jit(solution)/shard_map/ppermute | solution.py:37
  8.0 7.3 %collective-permute-start.1 = (bf16[384,256]{1,0:T(8,128)(2,1)S(1)}, bf16[384,256]{1,0:T(8,128)(2,1)S(1)}, u32[]{:S(2)}, u32[]{:S(2)}) collective-permute-start(bf16[384,256]{1,0:T(8,128)(2,1)S(1)} %get-tuple-element.39), channel_id=1, source_target_pairs={{16,32},{32,16},{48,64},{64,48},{80,96},{96,80},{112,128},{128,112... | collective-permute-start | bytes 589832 | tf_op jit(solution)/shard_map/ppermute | solution.py:38
  9.9 6.0 %collective-permute-start.2 = (bf16[384,256]{1,0:T(8,128)(2,1)S(1)}, bf16[384,256]{1,0:T(8,128)(2,1)S(1)}, u32[]{:S(2)}, u32[]{:S(2)}) collective-permute-start(bf16[384,256]{1,0:T(8,128)(2,1)S(1)} %get-tuple-element.40), channel_id=1, source_target_pairs={{0,4},{4,0},{8,12},{12,8},{1,5},{5,1},{9,13},{13,9},{2,6},{6,2},{1... | collective-permute-start | bytes 589832 | tf_op jit(solution)/shard_map/ppermute | solution.py:39
  11.0 4.8 %collective-permute-start.3 = (bf16[384,256]{1,0:T(8,128)(2,1)S(1)}, bf16[384,256]{1,0:T(8,128)(2,1)S(1)}, u32[]{:S(2)}, u32[]{:S(2)}) collective-permute-start(bf16[384,256]{1,0:T(8,128)(2,1)S(1)} %get-tuple-element.41), channel_id=1, source_target_pairs={{4,8},{8,4},{5,9},{9,5},{6,10},{10,6},{7,11},{11,7},{20,24},{24,20... | collective-permute-start | bytes 589832 | tf_op jit(solution)/shard_map/ppermute | solution.py:40
  11.7 7.6 %collective-permute-start.12 = (bf16[64,1152]{1,0:T(8,128)(2,1)S(1)}, bf16[64,1152]{1,0:T(8,128)(2,1)S(1)}, u32[]{:S(2)}, u32[]{:S(2)}) collective-permute-start(bf16[64,1152]{1,0:T(8,128)(2,1)S(1)} %get-tuple-element.48), channel_id=1, source_target_pairs={{0,3},{1,0},{2,1},{3,2},{4,7},{5,4},{6,5},{7,6},{8,11},{9,8},{10,9... | collective-permute-start | bytes 442376 | tf_op jit(solution)/shard_map/ppermute | solution.py:24
  14.5 6.9 %collective-permute-start.11 = (bf16[64,1152]{1,0:T(8,128)(2,1)S(1)}, bf16[64,1152]{1,0:T(8,128)(2,1)S(1)}, u32[]{:S(2)}, u32[]{:S(2)}) collective-permute-start(bf16[64,1152]{1,0:T(8,128)(2,1)S(1)} %get-tuple-element.48), channel_id=1, source_target_pairs={{0,2},{1,3},{2,0},{3,1},{4,6},{5,7},{6,4},{7,5},{8,10},{9,11},{10,... | collective-permute-start | bytes 442376 | tf_op jit(solution)/shard_map/ppermute | solution.py:24
  15.2 7.8 %collective-permute-start.10 = (bf16[64,1152]{1,0:T(8,128)(2,1)S(1)}, bf16[64,1152]{1,0:T(8,128)(2,1)S(1)}, u32[]{:S(2)}, u32[]{:S(2)}) collective-permute-start(bf16[64,1152]{1,0:T(8,128)(2,1)S(1)} %get-tuple-element.48), channel_id=1, source_target_pairs={{0,1},{1,2},{2,3},{3,0},{4,5},{5,6},{6,7},{7,4},{8,9},{9,10},{10,1... | collective-permute-start | bytes 442376 | tf_op jit(solution)/shard_map/ppermute | solution.py:24
  23.0 14.1 %collective-permute-start.13 = (bf16[192,1152]{1,0:T(8,128)(2,1)S(1)}, bf16[192,1152]{1,0:T(8,128)(2,1)S(1)}, u32[]{:S(2)}, u32[]{:S(2)}) collective-permute-start(bf16[192,1152]{1,0:T(8,128)(2,1)S(1)} %pad_maximum_fusion), channel_id=1, source_target_pairs={{0,4},{4,0},{8,12},{12,8},{1,5},{5,1},{9,13},{13,9},{2,6},{6,2},{1... | collective-permute-start | bytes 1327112 | tf_op jit(solution)/shard_map/ppermute | solution.py:347
  37.2 21.2 %collective-permute-start.14 = (bf16[384,1152]{1,0:T(8,128)(2,1)S(1)}, bf16[384,1152]{1,0:T(8,128)(2,1)S(1)}, u32[]{:S(2)}, u32[]{:S(2)}) collective-permute-start(bf16[384,1152]{1,0:T(8,128)(2,1)S(1)} %constant_dynamic-update-slice_fusion.near_w), channel_id=1, source_target_pairs={{0,16},{16,0},{1,17},{17,1},{2,18},{18,2},{3,19},{19,3},{4,20},{20... | collective-permute-start | bytes 2654216 | tf_op jit(solution)/shard_map/ppermute | solution.py:349
  38.2 7.8 %collective-permute-start.7 = (bf16[512,256]{1,0:T(8,128)(2,1)S(1)}, bf16[512,256]{1,0:T(8,128)(2,1)S(1)}, u32[]{:S(2)}, u32[]{:S(2)}) collective-permute-start(bf16[512,256]{1,0:T(8,128)(2,1)S(1)} %get-tuple-element.45.own_b.bottom), channel_id=1, source_target_pairs={{0,3},{1,0},{2,1},{3,2},{4,7},{5,4},{6,5},{7,6},{8,11},{9,8},{10,9... | collective-permute-start | bytes 786440 | tf_op jit(solution)/shard_map/ppermute | solution.py:24
  38.2 9.3 %collective-permute-start.4 = (bf16[512,256]{1,0:T(8,128)(2,1)S(1)}, bf16[512,256]{1,0:T(8,128)(2,1)S(1)}, u32[]{:S(2)}, u32[]{:S(2)}) collective-permute-start(bf16[512,256]{1,0:T(8,128)(2,1)S(1)} %get-tuple-element.44.own_t.top), channel_id=1, source_target_pairs={{0,1},{1,2},{2,3},{3,0},{4,5},{5,6},{6,7},{7,4},{8,9},{9,10},{10,1... | collective-permute-start | bytes 786440 | tf_op jit(solution)/shard_map/ppermute | solution.py:24
  39.7 13.0 %collective-permute-start.5 = (bf16[512,256]{1,0:T(8,128)(2,1)S(1)}, bf16[512,256]{1,0:T(8,128)(2,1)S(1)}, u32[]{:S(2)}, u32[]{:S(2)}) collective-permute-start(bf16[512,256]{1,0:T(8,128)(2,1)S(1)} %get-tuple-element.45.own_b.bottom), channel_id=1, source_target_pairs={{0,1},{1,2},{2,3},{3,0},{4,5},{5,6},{6,7},{7,4},{8,9},{9,10},{10,1... | collective-permute-start | bytes 786440 | tf_op jit(solution)/shard_map/ppermute | solution.py:24
  39.7 13.0 %collective-permute-start.6 = (bf16[512,256]{1,0:T(8,128)(2,1)S(1)}, bf16[512,256]{1,0:T(8,128)(2,1)S(1)}, u32[]{:S(2)}, u32[]{:S(2)}) collective-permute-start(bf16[512,256]{1,0:T(8,128)(2,1)S(1)} %get-tuple-element.44.own_t.top), channel_id=1, source_target_pairs={{0,3},{1,0},{2,1},{3,2},{4,7},{5,4},{6,5},{7,6},{8,11},{9,8},{10,9... | collective-permute-start | bytes 786440 | tf_op jit(solution)/shard_map/ppermute | solution.py:24
  46.0 11.2 %collective-permute-start.9 = (bf16[512,256]{1,0:T(8,128)(2,1)S(1)}, bf16[512,256]{1,0:T(8,128)(2,1)S(1)}, u32[]{:S(2)}, u32[]{:S(2)}) collective-permute-start(bf16[512,256]{1,0:T(8,128)(2,1)S(1)} %collective-permute-done.7.hi_b), channel_id=1, source_target_pairs={{0,3},{1,0},{2,1},{3,2},{4,7},{5,4},{6,5},{7,6},{8,11},{9,8},{10,9... | collective-permute-start | bytes 786440 | tf_op jit(solution)/shard_map/ppermute | solution.py:24
  47.5 10.9 %collective-permute-start.8 = (bf16[512,256]{1,0:T(8,128)(2,1)S(1)}, bf16[512,256]{1,0:T(8,128)(2,1)S(1)}, u32[]{:S(2)}, u32[]{:S(2)}) collective-permute-start(bf16[512,256]{1,0:T(8,128)(2,1)S(1)} %collective-permute-done.4.lo_t), channel_id=1, source_target_pairs={{0,1},{1,2},{2,3},{3,0},{4,5},{5,6},{6,7},{7,4},{8,9},{9,10},{10,1... | collective-permute-start | bytes 786440 | tf_op jit(solution)/shard_map/ppermute | solution.py:24
  64.6 8.6 %collective-permute-start.15 = (bf16[384,128]{1,0:T(8,128)(2,1)S(1)}, bf16[384,128]{1,0:T(8,128)(2,1)S(1)}, u32[]{:S(2)}, u32[]{:S(2)}) collective-permute-start(bf16[384,128]{1,0:T(8,128)(2,1)S(1)} %get-tuple-element.53), channel_id=1, source_target_pairs={{0,16},{16,0},{1,17},{17,1},{2,18},{18,2},{3,19},{19,3},{4,20},{20... | collective-permute-start | bytes 294920 | tf_op jit(solution)/shard_map/ppermute | solution.py:37
  65.8 7.6 %collective-permute-start.16 = (bf16[384,128]{1,0:T(8,128)(2,1)S(1)}, bf16[384,128]{1,0:T(8,128)(2,1)S(1)}, u32[]{:S(2)}, u32[]{:S(2)}) collective-permute-start(bf16[384,128]{1,0:T(8,128)(2,1)S(1)} %get-tuple-element.54), channel_id=1, source_target_pairs={{16,32},{32,16},{48,64},{64,48},{80,96},{96,80},{112,128},{128,112... | collective-permute-start | bytes 294920 | tf_op jit(solution)/shard_map/ppermute | solution.py:38
  71.0 3.6 %collective-permute-start.17 = (bf16[384,128]{1,0:T(8,128)(2,1)S(1)}, bf16[384,128]{1,0:T(8,128)(2,1)S(1)}, u32[]{:S(2)}, u32[]{:S(2)}) collective-permute-start(bf16[384,128]{1,0:T(8,128)(2,1)S(1)} %get-tuple-element.55), channel_id=1, source_target_pairs={{0,4},{4,0},{8,12},{12,8},{1,5},{5,1},{9,13},{13,9},{2,6},{6,2},{1... | collective-permute-start | bytes 294920 | tf_op jit(solution)/shard_map/ppermute | solution.py:39
  72.6 2.0 %collective-permute-start.18 = (bf16[384,128]{1,0:T(8,128)(2,1)S(1)}, bf16[384,128]{1,0:T(8,128)(2,1)S(1)}, u32[]{:S(2)}, u32[]{:S(2)}) collective-permute-start(bf16[384,128]{1,0:T(8,128)(2,1)S(1)} %get-tuple-element.56), channel_id=1, source_target_pairs={{4,8},{8,4},{5,9},{9,5},{6,10},{10,6},{7,11},{11,7},{20,24},{24,20... | collective-permute-start | bytes 294920 | tf_op jit(solution)/shard_map/ppermute | solution.py:40
  78.8 8.4 %collective-permute-start.19 = (bf16[384,128]{1,0:T(8,128)(2,1)S(1)}, bf16[384,128]{1,0:T(8,128)(2,1)S(1)}, u32[]{:S(2)}, u32[]{:S(2)}) collective-permute-start(bf16[384,128]{1,0:T(8,128)(2,1)S(1)} %get-tuple-element.59), channel_id=1, source_target_pairs={{0,16},{16,0},{1,17},{17,1},{2,18},{18,2},{3,19},{19,3},{4,20},{20... | collective-permute-start | bytes 294920 | tf_op jit(solution)/shard_map/ppermute | solution.py:37
  78.9 8.3 %collective-permute-start.20 = (bf16[384,128]{1,0:T(8,128)(2,1)S(1)}, bf16[384,128]{1,0:T(8,128)(2,1)S(1)}, u32[]{:S(2)}, u32[]{:S(2)}) collective-permute-start(bf16[384,128]{1,0:T(8,128)(2,1)S(1)} %get-tuple-element.60), channel_id=1, source_target_pairs={{16,32},{32,16},{48,64},{64,48},{80,96},{96,80},{112,128},{128,112... | collective-permute-start | bytes 294920 | tf_op jit(solution)/shard_map/ppermute | solution.py:38
  82.8 5.7 %collective-permute-start.21 = (bf16[384,128]{1,0:T(8,128)(2,1)S(1)}, bf16[384,128]{1,0:T(8,128)(2,1)S(1)}, u32[]{:S(2)}, u32[]{:S(2)}) collective-permute-start(bf16[384,128]{1,0:T(8,128)(2,1)S(1)} %get-tuple-element.61), channel_id=1, source_target_pairs={{0,4},{4,0},{8,12},{12,8},{1,5},{5,1},{9,13},{13,9},{2,6},{6,2},{1... | collective-permute-start | bytes 294920 | tf_op jit(solution)/shard_map/ppermute | solution.py:39
  86.5 2.0 %collective-permute-start.22 = (bf16[384,128]{1,0:T(8,128)(2,1)S(1)}, bf16[384,128]{1,0:T(8,128)(2,1)S(1)}, u32[]{:S(2)}, u32[]{:S(2)}) collective-permute-start(bf16[384,128]{1,0:T(8,128)(2,1)S(1)} %get-tuple-element.62), channel_id=1, source_target_pairs={{4,8},{8,4},{5,9},{9,5},{6,10},{10,6},{7,11},{11,7},{20,24},{24,20... | collective-permute-start | bytes 294920 | tf_op jit(solution)/shard_map/ppermute | solution.py:40
  92.8 1.7 %collective-permute-start.23 = (bf16[128,1152]{1,0:T(8,128)(2,1)S(1)}, bf16[128,1152]{1,0:T(8,128)(2,1)S(1)}, u32[]{:S(2)}, u32[]{:S(2)}) collective-permute-start(bf16[128,1152]{1,0:T(8,128)(2,1)S(1)} %get-tuple-element.67), channel_id=1, source_target_pairs={{0,16},{16,0},{1,17},{17,1},{2,18},{18,2},{3,19},{19,3},{4,20},{20... | collective-permute-start | bytes 884744 | tf_op jit(solution)/shard_map/ppermute | solution.py:388
  133.7 4.9 %collective-permute-start.24 = (bf16[128,1152]{1,0:T(8,128)(2,1)S(1)}, bf16[128,1152]{1,0:T(8,128)(2,1)S(1)}, u32[]{:S(2)}, u32[]{:S(2)}) collective-permute-start(bf16[128,1152]{1,0:T(8,128)(2,1)S(1)} %reshape.16), channel_id=1, source_target_pairs={{0,16},{16,0},{1,17},{17,1},{2,18},{18,2},{3,19},{19,3},{4,20},{20... | collective-permute-start | bytes 884744 | tf_op jit(solution)/shard_map/ppermute | solution.py:395
